TPU v7x, 32 devices: a whole 2x2x4 slice. The times are simulated.
32 devices in a mesh: dp: 8 (over y, x, core), tensor: 4 (over z).
Axes of the slice: x: 2, y: 2, z: 4, core: 2. Of those that a mesh axis runs over, the one named last changes fastest.
Arguments:
- inputs: bfloat16 [2, 16384, 1024], P(None, ('dp', 'tensor')), may hold values from -6 to 6
- segment_ids: int32 [2, 8, 2048], P(None, 'dp'), may hold values from 0 to 3, never falling along the last dimension, each value on 1 to 1024 neighbouring positions
- token_valid: int32 [2, 8, 2048], P(None, 'dp'), may hold values from 0 to 1, as said below
- qkv_weight: bfloat16 [3, 1024, 1024], P(None, 'dp', 'tensor'), may hold values from -0.1875 to 0.1875
- qv_bias: float32 [2, 1024], P(None, 'tensor'), may hold values from -3 to 3
- out_weight: bfloat16 [1024, 1024], P('tensor', 'dp'), may hold values from -1.5 to 1.5
- norm_gains: float32 [2, 1024], replicated, may hold values from 0.25 to 1.75
- row_biases: float32 [4, 1024], replicated, may hold values from -3 to 3
- up_weight: bfloat16 [1024, 4096], P('dp', 'tensor'), may hold values from -0.1875 to 0.1875
- up_bias: float32 [4096], P('tensor'), may hold values from -3 to 3
- down_weight: bfloat16 [4096, 1024], P('tensor', 'dp'), may hold values from -0.09375 to 0.09375
- out_grad: bfloat16 [2, 16384, 1024], P(None, ('dp', 'tensor')), may hold values from -6 to 6
Outputs:
- layer_out: bfloat16 [2, 16384, 1024], P(None, ('dp', 'tensor'))
- input_grad: float32 [2, 16384, 1024], P(None, ('dp', 'tensor'))
- qkv_grad: float32 [3, 1024, 1024], P(None, 'dp', 'tensor')
- qv_bias_grad: float32 [2, 1024], P(None, 'tensor')
- out_weight_grad: float32 [1024, 1024], P('tensor', 'dp')
- gain_grad: float32 [2, 1024], replicated
- row_bias_grad: float32 [4, 1024], replicated
- up_weight_grad: float32 [1024, 4096], P('dp', 'tensor')
- up_bias_grad: float32 [4096], P('tensor')
- down_weight_grad: float32 [4096, 1024], P('tensor', 'dp')
Inputs may be any that keep to these rules, and one draw needn't show every extreme that they name: `segment_ids`: segment numbers never fall along a sequence. `token_valid`: in each sequence the ones form a prefix of at least three quarters of it, and its last token is padding.
All inputs are finite; a program needn't handle non-finite values.
Results may differ from a plain program's by a relative error of at most 0.019.
Values may be sent and summed in bfloat16 or wider, within the bound.
A program may use at most 256 MiB of HBM per device.

v0:
```python
import jax
import jax.numpy as jnp
from jax import lax
from jax.sharding import PartitionSpec as P

HEAD = 64


NEG_FILL = -1e30


def exact_gelu(values):
    return jax.nn.gelu(values, approximate=False)


def norm_forward(values, norm_gain, norm_shift):
    center = values - jnp.mean(values, axis=-1, keepdims=True)
    inverse = lax.rsqrt(jnp.mean(center * center, axis=-1, keepdims=True) + 1e-05)
    normed = center * inverse
    return (normed * norm_gain + norm_shift, normed, inverse)


def norm_backward(incoming, normed, inverse, norm_gain):
    scaled = incoming * norm_gain
    return inverse * (
        scaled
        - jnp.mean(scaled, axis=-1, keepdims=True)
        - normed * jnp.mean(scaled * normed, axis=-1, keepdims=True)
    )


def block_scores(queries, key_rows, segment, valid_keys, first_row, row_count):
    query_blk = lax.dynamic_slice_in_dim(queries, first_row, row_count, 0)
    scores = jnp.einsum(
        "qhe,khe->hqk", query_blk, key_rows, preferred_element_type=jnp.float32
    ) * queries.shape[2] ** (-0.5)
    key_pos = jnp.arange(segment.shape[0], dtype=jnp.int32)
    query_pos = first_row + jnp.arange(row_count, dtype=jnp.int32)
    query_seg = lax.dynamic_slice_in_dim(segment, first_row, row_count)
    allowed = (query_seg[:, None] == segment[None, :]) & (
        (valid_keys[None, :] > 0) | (query_pos[:, None] == key_pos[None, :])
    )
    return jnp.where(allowed[None], scores, NEG_FILL)


def attend_forward(queries, key_rows, value_rows, segment, valid_keys):
    length, head_local, head_size = queries.shape
    block_rows = min(512, length)

    def one_block(block_index):
        first_row = block_index * block_rows
        scores = block_scores(queries, key_rows, segment, valid_keys, first_row, block_rows)
        top_score = jnp.max(scores, axis=-1, keepdims=True)
        raised = jnp.exp(scores - top_score)
        row_total = jnp.sum(raised, axis=-1, keepdims=True)
        attention = (raised / row_total).astype(jnp.bfloat16)
        context = jnp.einsum(
            "hqk,khe->qhe", attention, value_rows, preferred_element_type=jnp.float32
        )
        return (context.astype(jnp.bfloat16), (top_score + jnp.log(row_total))[:, :, 0])

    context, log_total = lax.map(one_block, jnp.arange(length // block_rows, dtype=jnp.int32))
    return (context.reshape(length, head_local * head_size), log_total)


def attend_backward(queries, key_rows, value_rows, context_grad, log_total, segment, valid_keys):
    length, head_local, head_size = queries.shape
    block_rows = min(512, length)
    score_scale = head_size ** (-0.5)

    def one_block(totals, block_index):
        key_grad, value_grad = totals
        first_row = block_index * block_rows
        query_blk = lax.dynamic_slice_in_dim(queries, first_row, block_rows, 0)
        grad_blk = lax.dynamic_slice_in_dim(context_grad, first_row, block_rows, 0)
        scores = block_scores(queries, key_rows, segment, valid_keys, first_row, block_rows)
        attention = jnp.exp(scores - log_total[block_index][:, :, None])
        value_grad = value_grad + jnp.einsum(
            "hqk,qhe->khe",
            attention.astype(jnp.bfloat16),
            grad_blk,
            preferred_element_type=jnp.float32,
        )
        attn_grad = jnp.einsum(
            "qhe,khe->hqk", grad_blk, value_rows, preferred_element_type=jnp.float32
        )
        row_dot = jnp.sum(attention * attn_grad, axis=-1, keepdims=True)
        score_grad = (attention * (attn_grad - row_dot)).astype(jnp.bfloat16)
        query_grad = (
            jnp.einsum("hqk,khe->qhe", score_grad, key_rows, preferred_element_type=jnp.float32)
            * score_scale
        )
        key_grad = (
            key_grad
            + jnp.einsum("hqk,qhe->khe", score_grad, query_blk, preferred_element_type=jnp.float32)
            * score_scale
        )
        return ((key_grad, value_grad), query_grad.astype(jnp.bfloat16))

    zero_grad = jnp.zeros(key_rows.shape, jnp.float32)
    (key_grad, value_grad), query_grad = lax.scan(
        one_block, (zero_grad, zero_grad), jnp.arange(length // block_rows, dtype=jnp.int32)
    )
    flat = head_local * head_size
    return (
        query_grad.reshape(length, flat),
        key_grad.astype(jnp.bfloat16).reshape(length, flat),
        value_grad.astype(jnp.bfloat16).reshape(length, flat),
    )


def body(
    inputs,
    segment_ids,
    token_valid,
    qkv_weight,
    qv_bias,
    out_weight,
    norm_gains,
    row_biases,
    up_weight,
    up_bias,
    down_weight,
    out_grad,
):
    micro_count = inputs.shape[0]
    model_width = inputs.shape[2]
    local_cols = qkv_weight.shape[2]
    local_hidden = up_weight.shape[1]
    head_local = local_cols // HEAD
    tensor_rank = lax.axis_index("tensor")
    bias_three = jnp.stack([qv_bias[0], jnp.zeros_like(qv_bias[0]), qv_bias[1]])
    outputs_list = []
    input_list = []
    weight_totals = None
    small_totals = None
    for micro_index in range(micro_count):
        full_qkv, full_out, full_up, full_down = (
            lax.all_gather(qkv_weight, "dp", axis=1, tiled=True),
            lax.all_gather(out_weight, "dp", axis=1, tiled=True),
            lax.all_gather(up_weight, "dp", axis=0, tiled=True),
            lax.all_gather(down_weight, "dp", axis=1, tiled=True),
        )
        tokens = inputs[micro_index]
        segment = segment_ids[micro_index, 0]
        valid_keys = token_valid[micro_index, 0]
        gathered = lax.all_gather(tokens, "tensor", axis=0, tiled=True)
        length = gathered.shape[0]
        projected = (
            jnp.einsum("td,cdf->ctf", gathered, full_qkv, preferred_element_type=jnp.float32)
            + bias_three[:, None, :]
        )
        projected = projected.astype(jnp.bfloat16)
        heads_view = projected.reshape(3, length, head_local, HEAD)
        context, log_total = attend_forward(
            heads_view[0], heads_view[1], heads_view[2], segment, valid_keys
        )
        attn_rows = lax.psum_scatter(
            jnp.dot(context, full_out, preferred_element_type=jnp.float32).astype(jnp.bfloat16),
            "tensor",
            scatter_dimension=0,
            tiled=True,
        ).astype(jnp.float32)
        mixed_rows = tokens.astype(jnp.float32) + attn_rows + row_biases[0]
        hidden, normed_one, inverse_one = norm_forward(mixed_rows, norm_gains[0], row_biases[1])
        hidden_all = lax.all_gather(hidden.astype(jnp.bfloat16), "tensor", axis=0, tiled=True)
        pre_act = jnp.dot(hidden_all, full_up, preferred_element_type=jnp.float32) + up_bias
        active, gelu_pull = jax.vjp(exact_gelu, pre_act)
        active_low = active.astype(jnp.bfloat16)
        ffn_rows = lax.psum_scatter(
            jnp.dot(active_low, full_down, preferred_element_type=jnp.float32).astype(jnp.bfloat16),
            "tensor",
            scatter_dimension=0,
            tiled=True,
        ).astype(jnp.float32)
        summed = hidden + ffn_rows + row_biases[2]
        layer_rows, normed_two, inverse_two = norm_forward(summed, norm_gains[1], row_biases[3])
        outputs_list.append(layer_rows.astype(jnp.bfloat16))
        incoming = out_grad[micro_index].astype(jnp.float32)
        gain_two = jnp.sum(incoming * normed_two, axis=0)
        shift_two = jnp.sum(incoming, axis=0)
        summed_grad = norm_backward(incoming, normed_two, inverse_two, norm_gains[1])
        ffn_bias = jnp.sum(summed_grad, axis=0)
        ffn_grad_all = lax.all_gather(
            summed_grad.astype(jnp.bfloat16), "tensor", axis=0, tiled=True
        )
        down_grad = jnp.einsum(
            "tf,td->fd", active_low, ffn_grad_all, preferred_element_type=jnp.float32
        )
        active_grad = jnp.einsum(
            "td,fd->tf", ffn_grad_all, full_down, preferred_element_type=jnp.float32
        )
        pre_grad = gelu_pull(active_grad)[0].astype(jnp.bfloat16)
        up_bias_part = jnp.sum(pre_grad.astype(jnp.float32), axis=0)
        up_grad = jnp.einsum("td,tf->df", hidden_all, pre_grad, preferred_element_type=jnp.float32)
        hidden_grad = (
            lax.psum_scatter(
                jnp.einsum(
                    "tf,df->td", pre_grad, full_up, preferred_element_type=jnp.float32
                ).astype(jnp.bfloat16),
                "tensor",
                scatter_dimension=0,
                tiled=True,
            ).astype(jnp.float32)
            + summed_grad
        )
        gain_one = jnp.sum(hidden_grad * normed_one, axis=0)
        shift_one = jnp.sum(hidden_grad, axis=0)
        mixed_grad = norm_backward(hidden_grad, normed_one, inverse_one, norm_gains[0])
        attn_bias = jnp.sum(mixed_grad, axis=0)
        attn_grad_all = lax.all_gather(
            mixed_grad.astype(jnp.bfloat16), "tensor", axis=0, tiled=True
        )
        out_w_grad = jnp.einsum(
            "tc,td->cd", context, attn_grad_all, preferred_element_type=jnp.float32
        )
        context_grad = jnp.einsum(
            "td,cd->tc", attn_grad_all, full_out, preferred_element_type=jnp.float32
        ).astype(jnp.bfloat16)
        query_grad, key_grad, value_grad = attend_backward(
            heads_view[0],
            heads_view[1],
            heads_view[2],
            context_grad.reshape(length, head_local, HEAD),
            log_total,
            segment,
            valid_keys,
        )
        proj_grad = jnp.stack([query_grad, key_grad, value_grad])
        qkv_w_grad = jnp.einsum(
            "td,ctf->cdf", gathered, proj_grad, preferred_element_type=jnp.float32
        )
        proj_bias = jnp.sum(proj_grad.astype(jnp.float32), axis=1)
        input_rows = (
            lax.psum_scatter(
                jnp.einsum(
                    "ctf,cdf->td", proj_grad, full_qkv, preferred_element_type=jnp.float32
                ).astype(jnp.bfloat16),
                "tensor",
                scatter_dimension=0,
                tiled=True,
            ).astype(jnp.float32)
            + mixed_grad
        )
        input_list.append(input_rows)
        qv_padded = lax.dynamic_update_slice(
            jnp.zeros((2, model_width), jnp.float32),
            jnp.stack([proj_bias[0], proj_bias[2]]),
            (jnp.zeros((), jnp.int32), tensor_rank * local_cols),
        )
        up_padded = lax.dynamic_update_slice(
            jnp.zeros((local_hidden * lax.axis_size("tensor"),), jnp.float32),
            up_bias_part,
            (tensor_rank * local_hidden,),
        )
        small_part = (
            jnp.stack([gain_one, gain_two]),
            jnp.stack([attn_bias, shift_one, ffn_bias, shift_two]),
            qv_padded,
            up_padded,
        )
        small_totals = (
            small_part if small_totals is None else jax.tree.map(jnp.add, small_totals, small_part)
        )
        local_grads = (qkv_w_grad, out_w_grad, up_grad, down_grad)
        reduced = (
            lax.psum_scatter(local_grads[0], "dp", scatter_dimension=1, tiled=True),
            lax.psum_scatter(local_grads[1], "dp", scatter_dimension=1, tiled=True),
            lax.psum_scatter(local_grads[2], "dp", scatter_dimension=0, tiled=True),
            lax.psum_scatter(local_grads[3], "dp", scatter_dimension=1, tiled=True),
        )
        weight_totals = (
            reduced if weight_totals is None else jax.tree.map(jnp.add, weight_totals, reduced)
        )
    gain_sum, bias_sum, qv_sum, up_sum = lax.psum(small_totals, ("dp", "tensor"))
    qv_bias_grad = lax.dynamic_slice_in_dim(qv_sum, tensor_rank * local_cols, local_cols, 1)
    up_bias_grad = lax.dynamic_slice_in_dim(up_sum, tensor_rank * local_hidden, local_hidden, 0)
    qkv_total, out_total, up_total, down_total = weight_totals
    return (
        jnp.stack(outputs_list),
        jnp.stack(input_list),
        qkv_total,
        qv_bias_grad,
        out_total,
        gain_sum,
        bias_sum,
        up_total,
        up_bias_grad,
        down_total,
    )


def solution(mesh):
    return jax.shard_map(
        body,
        mesh=mesh,
        in_specs=(
            P(None, ("dp", "tensor"), None),
            P(None, "dp", None),
            P(None, "dp", None),
            P(None, "dp", "tensor"),
            P(None, "tensor"),
            P("tensor", "dp"),
            P(),
            P(),
            P("dp", "tensor"),
            P("tensor"),
            P("tensor", "dp"),
            P(None, ("dp", "tensor"), None),
        ),
        out_specs=(
            P(None, ("dp", "tensor"), None),
            P(None, ("dp", "tensor"), None),
            P(None, "dp", "tensor"),
            P(None, "tensor"),
            P("tensor", "dp"),
            P(),
            P(),
            P("dp", "tensor"),
            P("tensor"),
            P("tensor", "dp"),
        ),
        check_vma=False,
    )
```

profile of v0, /device:TPU:0, one launch (start us, length us, event | category | flops | bytes accessed | tf_op | source)
XLA Modules:
  0.0 2160.7 jit_solution(6602268979720648420)
XLA Ops:
  12.9 13.7 all_gather.42
  27.4 12.3 all-gather.14.cloned.1.call-done
  39.7 82.9 %all-gather.32.cloned.1.call-done = bf16[1,2048,1024]{2,1,0:T(8,128)(2,1)} async-done(((bf16[1,512,1024]{2,1,0:T(8,128)(2,1)}), bf16[1,2048,1024]{2,1,0:T(8,128)(2,1)}) %all-gather.32.cloned.1.call-update) | async-done | bytes 4194320 | tf_op jit(solution)/shard_map/all_gather | solution.py:147
  130.1 65.7 %while.54 = (s32[]{:T(128)}, bf16[4,512,4,64]{1,3,2,0:T(8,128)(2,1)}, f32[4,4,512]{2,1,0:T(4,128)S(1)}, s32[4]{0:T(128)S(1)}, s32[2048]{0:T(1024)S(1)}, /*index=...) while((s32[]{:T(128)}, ...), condition=%wide.region_3.4_spmd, body=%wide.region_0.3_spmd.sunk | while | flops 1128399360 | bytes 57244364 | solution.py:62
  212.2 65.5 %while.55 = (s32[]{:T(128)}, bf16[4,512,4,64]{1,3,2,0:T(8,128)(2,1)}, f32[4,4,512]{2,1,0:T(4,128)S(1)}, s32[4]{0:T(128)S(1)}, s32[2048]{0:T(1024)S(1)}, /*index=...) while((s32[]{:T(128)}, ...), condition=%wide.region_13.14_spmd, body=%wide.region_10.13_spmd.sunk | while | flops 1128399360 | bytes 57244364 | solution.py:62
  289.2 71.8 %reduce-scatter.17.cloned.1.call-done = bf16[512,1024]{1,0:T(8,128)(2,1)} async-done(((bf16[2048,1024]{1,0:T(8,128)(2,1)}), bf16[512,1024]{1,0:T(8,128)(2,1)}) %reduce-scatter.17.cloned.1.call-update) | async-done | bytes 1048592 | tf_op jit(solution)/shard_map/reduce_scatter | solution.py:158
  368.1 22.9 %all-gather.18.cloned.1.call-done = bf16[1024,1024]{1,0:T(8,128)(2,1)} async-done(((bf16[128,1024]{1,0:T(8,128)(2,1)}), bf16[1024,1024]{1,0:T(8,128)(2,1)}) %all-gather.18.cloned.1.call-update) | async-done | bytes 2097168 | tf_op jit(solution)/shard_map/all_gather | solution.py:141
  391.0 82.9 %all-gather.22.cloned.1.call-done = bf16[2048,1024]{1,0:T(8,128)(2,1)} async-done(((bf16[512,1024]{1,0:T(8,128)(2,1)}), bf16[2048,1024]{1,0:T(8,128)(2,1)}) %all-gather.22.cloned.1.call-update) | async-done | bytes 4194320 | tf_op jit(solution)/shard_map/all_gather | solution.py:166
  473.9 10.9 fusion.161
  484.9 70.5 %all-gather.16.cloned.1.call-done = bf16[2048,1024]{1,0:T(8,128)(2,1)} async-done(((bf16[512,1024]{1,0:T(8,128)(2,1)}), bf16[2048,1024]{1,0:T(8,128)(2,1)}) %all-gather.16.cloned.1.call-update) | async-done | bytes 4194320 | tf_op jit(solution)/shard_map/all_gather | solution.py:166
  555.4 44.6 %multiply_convert_fusion.3 = (bf16[2048,1024]{1,0:T(8,128)(2,1)}, f32[2048,1024]{1,0:T(8,128)}, bf16[2048,1024]{1,0:T(8,128)(2,1)}, f32[2048,1024]{1,0:T(8,128)}, f32[2048,1024]{1,0:T(8,128)}) fusion(f32[1024]{0:T(1024)S(1)} %copy-done.106, f32[2048,1024]{1,0:T(8,128)} %fusion.161, bf16[2048,1024]{1,0:T(8,128)(2,1)} %all-gather.16.cloned.1.call-done, ...), kind=kOutput, calls=%fused_computation.129 | convolution fusion | flops 4571791360 | bytes 48238592 | tf_op jit(solution)/shard_map/dot_general | solution.py:167
  600.0 9.5 convolution_convert_fusion.5
  611.1 8.3 convolution_convert_fusion.4
  619.6 65.4 %reduce-scatter.15.cloned.1.call-done = bf16[512,1024]{1,0:T(8,128)(2,1)} async-done(((bf16[2048,1024]{1,0:T(8,128)(2,1)}), bf16[512,1024]{1,0:T(8,128)(2,1)}) %reduce-scatter.15.cloned.1.call-update) | async-done | bytes 1048592 | tf_op jit(solution)/shard_map/reduce_scatter | solution.py:170
  685.0 79.6 %reduce-scatter.19.cloned.1.call-done = bf16[512,1024]{1,0:T(8,128)(2,1)} async-done(((bf16[2048,1024]{1,0:T(8,128)(2,1)}), bf16[512,1024]{1,0:T(8,128)(2,1)}) %reduce-scatter.19.cloned.1.call-update) | async-done | bytes 1048592 | tf_op jit(solution)/shard_map/reduce_scatter | solution.py:170
  780.0 78.5 %all-gather.24.cloned.1.call-done = bf16[2048,1024]{1,0:T(8,128)(2,1)} async-done(((bf16[512,1024]{1,0:T(8,128)(2,1)}), bf16[2048,1024]{1,0:T(8,128)(2,1)}) %all-gather.24.cloned.1.call-update) | async-done | bytes 4194320 | tf_op jit(solution)/shard_map/all_gather | solution.py:184
  858.5 10.8 fusion.162
  869.3 70.0 %all-gather.28.cloned.1.call-done = bf16[2048,1024]{1,0:T(8,128)(2,1)} async-done(((bf16[512,1024]{1,0:T(8,128)(2,1)}), bf16[2048,1024]{1,0:T(8,128)(2,1)}) %all-gather.28.cloned.1.call-update) | async-done | bytes 4194320 | tf_op jit(solution)/shard_map/all_gather | solution.py:184
  939.3 22.7 %convert_reduce_fusion = (f32[1024]{0:T(1024)}, bf16[2048,1024]{1,0:T(8,128)(2,1)S(1)}, f32[1024]{0:T(1024)}, bf16[2048,1024]{1,0:T(8,128)(2,1)}) fusion(f32[2048,1024]{1,0:T(8,128)} %get-tuple-element.553, f32[2048,1024]{1,0:T(8,128)} %fusion.161, f32[1024]{0:T(1024)S(1)} %copy-done.106, f32[2048,1024]{1,0:T(8,128)} %fusion.162, ...), kind=kOutput, calls=%fused_computation.112 | convolution fusion | flops 4366268416 | bytes 56635392 | tf_op jit(solution)/shard_map/td,fd->tf/dot_general | solution.py:190
  970.6 9.4 convolution_convert_fusion.3
  980.1 65.9 %reduce-scatter.25.cloned.1.call-done = bf16[512,1024]{1,0:T(8,128)(2,1)} async-done(((bf16[2048,1024]{1,0:T(8,128)(2,1)}), bf16[512,1024]{1,0:T(8,128)(2,1)}) %reduce-scatter.25.cloned.1.call-update) | async-done | bytes 1048592 | tf_op jit(solution)/shard_map/reduce_scatter | solution.py:197
  1045.9 79.5 %reduce-scatter.21.cloned.1.call-done = bf16[512,1024]{1,0:T(8,128)(2,1)} async-done(((bf16[2048,1024]{1,0:T(8,128)(2,1)}), bf16[512,1024]{1,0:T(8,128)(2,1)}) %reduce-scatter.21.cloned.1.call-update) | async-done | bytes 1048592 | tf_op jit(solution)/shard_map/reduce_scatter | solution.py:197
  1139.6 80.1 %all-gather.30.cloned.1.call-done = bf16[2048,1024]{1,0:T(8,128)(2,1)} async-done(((bf16[512,1024]{1,0:T(8,128)(2,1)}), bf16[2048,1024]{1,0:T(8,128)(2,1)}) %all-gather.30.cloned.1.call-update) | async-done | bytes 4194320 | tf_op jit(solution)/shard_map/all_gather | solution.py:211
  1225.2 269.2 %while.57 = (s32[]{:T(128)}, f32[2048,4,64]{0,2,1:T(8,128)}, f32[2048,4,64]{0,2,1:T(8,128)}, bf16[4,512,4,64]{1,3,2,0:T(8,128)(2,1)}, s32[4]{0:T(128)S(1)}, /*in...) while((s32[]{:T(128)}, f32[2048,4,64]{0,2,1:T(8,128)}, ...), condition=%wide.region_36.37_spmd.clone, body=%wide.region_34.36_spmd.clone.sunk | while | flops 2754347520 | bytes 231037904 | solution.py:101
  1230.5 9.1 fusion.295
  1242.4 15.6 multiply_reduce_fusion.15
  1259.3 10.8 multiply_convert_fusion.7
  1280.1 11.8 fusion.298
  1296.9 9.1 fusion.295
  1308.7 15.6 multiply_reduce_fusion.15
  1325.6 10.8 multiply_convert_fusion.7
  1346.9 12.3 fusion.298
  1364.3 9.1 fusion.295
  1376.2 15.6 multiply_reduce_fusion.15
  1393.0 10.8 multiply_convert_fusion.7
  1414.3 12.3 fusion.298
  1431.7 9.1 fusion.295
  1443.6 15.6 multiply_reduce_fusion.15
  1460.4 10.8 multiply_convert_fusion.7
  1481.7 12.3 fusion.298
  1513.2 260.0 %while.56 = (s32[]{:T(128)}, f32[2048,4,64]{0,2,1:T(8,128)}, f32[2048,4,64]{0,2,1:T(8,128)}, bf16[4,512,4,64]{1,3,2,0:T(8,128)(2,1)}, s32[4]{0:T(128)S(1)}, /*in...) while((s32[]{:T(128)}, f32[2048,4,64]{0,2,1:T(8,128)}, ...), condition=%wide.region_27.28_spmd.clone, body=%wide.region_25.27_spmd.clone.sunk | while | flops 2754347520 | bytes 231103504 | solution.py:101
  1516.0 9.1 fusion.281
  1527.8 15.6 multiply_reduce_fusion.14
  1544.6 10.8 multiply_convert_fusion.6
  1565.3 11.9 fusion.284
  1580.1 9.1 fusion.281
  1591.9 15.6 multiply_reduce_fusion.14
  1608.7 10.8 multiply_convert_fusion.6
  1630.0 12.5 fusion.284
  1645.4 9.1 fusion.281
  1657.1 15.6 multiply_reduce_fusion.14
  1674.0 10.8 multiply_convert_fusion.6
  1695.2 12.5 fusion.284
  1710.6 9.1 fusion.281
  1722.4 15.6 multiply_reduce_fusion.14
  1739.2 10.8 multiply_convert_fusion.6
  1760.5 12.5 fusion.284
  1814.7 7.9 fusion.165
  1856.2 44.0 %all-reduce = (f32[2,1024]{1,0:T(2,128)S(1)}, f32[2,1024]{1,0:T(2,128)}, f32[4,1024]{1,0:T(4,128)}, f32[4096]{0:T(1024)S(1)}) all-reduce(f32[2,1024]{1,0:T(2,128)S(1)} %fusion.138, f32[2,1024]{1,0:T(2,128)S(1)} %maximum_add_fusion.1, f32[4,1024]{1,0:T(4,128)S(1)} %maximum_add_fusion, ...), channel_id=1, replica_groups=mesh['dp'=8,'tensor'=4] {'dp','tensor'}, use_global_device_ids=true, to_apply=%region_42.43 | all-reduce | flops 12288 | bytes 98304 | tf_op jit(solution)/shard_map/psum | solution.py:275
  1903.3 20.8 reduce-scatter.23.cloned.1.call-done
  1927.7 75.8 %reduce-scatter.27.cloned.1.call-done = bf16[512,1024]{1,0:T(8,128)(2,1)} async-done(((bf16[2048,1024]{1,0:T(8,128)(2,1)}), bf16[512,1024]{1,0:T(8,128)(2,1)}) %reduce-scatter.27.cloned.1.call-update) | async-done | bytes 1048592 | tf_op jit(solution)/shard_map/reduce_scatter | solution.py:235
  2007.8 51.3 %reduce-scatter.35.cloned.1.call-done = f32[1024,128]{1,0:T(8,128)} async-done(((f32[1024,1024]{1,0:T(8,128)}), f32[1024,128]{1,0:T(8,128)}) %reduce-scatter.35.cloned.1.call-update) | async-done | bytes 524304 | tf_op jit(solution)/shard_map/reduce_scatter | solution.py:270
  2059.1 55.1 %reduce-scatter.33.cloned.1.call-done = f32[128,1024]{1,0:T(8,128)} async-done(((f32[1024,1024]{1,0:T(8,128)}), f32[128,1024]{1,0:T(8,128)}) %reduce-scatter.33.cloned.1.call-update) | async-done | bytes 524304 | tf_op jit(solution)/shard_map/reduce_scatter | solution.py:269
  2114.2 39.8 %reduce-scatter.31.cloned.1.call-done = f32[256,128]{1,0:T(8,128)} async-done(((f32[256,1024]{1,0:T(8,128)}), f32[256,128]{1,0:T(8,128)}) %reduce-scatter.31.cloned.1.call-update) | async-done | bytes 131088 | tf_op jit(solution)/shard_map/reduce_scatter | solution.py:268
  (615 shorter events, 447.5 us)
Async XLA Ops:
  7.2 19.5 copy-start.90
  7.2 19.5 copy-start.89
  7.2 32.5 %all-gather.14.cloned.1.call-start = ((), (), s32[]{:S(2)}) async-start(), calls=%async_computation.12 | async-start | bytes 1769472 | tf_op jit(solution)/shard_map/all_gather | solution.py:139
  9.0 113.6 %all-gather.32.cloned.1.call-start = ((), (), s32[]{:S(2)}) async-start(), calls=%async_computation.29 | async-start | bytes 5242880 | tf_op jit(solution)/shard_map/all_gather | solution.py:147
  12.1 191.3 %all-gather.34.cloned.1.call-start = ((), (), s32[]{:S(2)}) async-start(), calls=%async_computation.30 | async-start | bytes 5242880 | tf_op jit(solution)/shard_map/all_gather | solution.py:147
  12.9 274.5 %reduce-scatter.13.cloned.1.call-start = ((), (), s32[]{:S(2)}) async-start(), calls=%async_computation.13 | async-start | bytes 5242880 | tf_op jit(solution)/shard_map/reduce_scatter | solution.py:158
  27.4 95.2 %copy-start.96 = (f32[3,256]{1,0:T(4,128)}, f32[3,256]{1,0:T(4,128)S(1)}, u32[]{:S(2)}) copy-start(f32[3,256]{1,0:T(4,128)S(1)} %pad_maximum_fusion.4) | copy-start | bytes 9220
  203.3 157.6 %reduce-scatter.17.cloned.1.call-start = ((), (), s32[]{:S(2)}) async-start(), calls=%async_computation.18 | async-start | bytes 5242880 | tf_op jit(solution)/shard_map/reduce_scatter | solution.py:158
  285.1 105.9 %all-gather.18.cloned.1.call-start = ((), (), s32[]{:S(2)}) async-start(), calls=%async_computation.15 | async-start | bytes 2359296 | tf_op jit(solution)/shard_map/all_gather | solution.py:141
  285.7 188.2 %all-gather.22.cloned.1.call-start = ((), (), s32[]{:S(2)}) async-start(), calls=%async_computation.19 | async-start | bytes 5242880 | tf_op jit(solution)/shard_map/all_gather | solution.py:166
  286.8 77.4 %copy-start.64 = (f32[1,1024]{1,0:T(1,128)}, f32[1,1024]{1,0:T(1,128)S(1)}, u32[]{:S(2)}) copy-start(f32[1,1024]{1,0:T(1,128)S(1)} %get-tuple-element.545) | copy-start | bytes 12292
  287.4 76.8 %copy-start.60 = (f32[1,1024]{1,0:T(1,128)}, f32[1,1024]{1,0:T(1,128)S(1)}, u32[]{:S(2)}) copy-start(f32[1,1024]{1,0:T(1,128)S(1)} %get-tuple-element.538) | copy-start | bytes 12292
  287.4 76.8 %copy-start.76 = (f32[1,1024]{1,0:T(1,128)}, f32[1,1024]{1,0:T(1,128)S(1)}, u32[]{:S(2)}) copy-start(f32[1,1024]{1,0:T(1,128)S(1)} %get-tuple-element.537) | copy-start | bytes 12292
  287.4 76.8 %copy-start.14 = (bf16[512,1024]{1,0:T(8,128)(2,1)S(1)}, bf16[512,1024]{1,0:T(8,128)(2,1)}, u32[]{:S(2)}) copy-start(bf16[512,1024]{1,0:T(8,128)(2,1)} %reduce-scatter.13.cloned.1.call-done) | copy-start | bytes 3145732
  289.1 77.4 %copy-start.66 = (f32[512]{0:T(512)}, f32[512]{0:T(512)S(1)}, u32[]{:S(2)}) copy-start(f32[512]{0:T(512)S(1)} %broadcast_multiply_fusion.11) | copy-start | bytes 6148
  366.6 188.8 %all-gather.16.cloned.1.call-start = ((), (), s32[]{:S(2)}) async-start(), calls=%async_computation.14 | async-start | bytes 5242880 | tf_op jit(solution)/shard_map/all_gather | solution.py:166
  367.3 232.7 %all-gather.20.cloned.1.call-start = ((), (), s32[]{:S(2)}) async-start(), calls=%async_computation.16 | async-start | bytes 2359296 | tf_op jit(solution)/shard_map/all_gather | solution.py:142
  368.1 187.3 %copy-start.106 = (f32[1024]{0:T(1024)S(1)}, f32[1024]{0:T(1024)}, u32[]{:S(2)}) copy-start(f32[1024]{0:T(1024)} %param.29) | copy-start | bytes 12292
  368.1 316.9 %reduce-scatter.15.cloned.1.call-start = ((), (), s32[]{:S(2)}) async-start(), calls=%async_computation.17 | async-start | bytes 5242880 | tf_op jit(solution)/shard_map/reduce_scatter | solution.py:170
  391.0 164.3 %copy-start.102 = (bf16[1024,1024]{1,0:T(8,128)(2,1)S(1)}, bf16[1024,1024]{1,0:T(8,128)(2,1)}, u32[]{:S(2)}) copy-start(bf16[1024,1024]{1,0:T(8,128)(2,1)} %all-gather.18.cloned.1.call-done) | copy-start | bytes 6291460
  609.5 155.1 %reduce-scatter.19.cloned.1.call-start = ((), (), s32[]{:S(2)}) async-start(), calls=%async_computation.20 | async-start | bytes 5242880 | tf_op jit(solution)/shard_map/reduce_scatter | solution.py:170
  619.4 145.2 %copy-start.9 = (bf16[2,512,1024]{2,1,0:T(8,128)(2,1)S(1)}, bf16[2,512,1024]{2,1,0:T(8,128)(2,1)}, u32[]{:S(2)}) copy-start(bf16[2,512,1024]{2,1,0:T(8,128)(2,1)} %param.20) | copy-start | bytes 6291460
  619.4 145.2 %copy-start.15 = (bf16[512,1024]{1,0:T(8,128)(2,1)S(1)}, bf16[512,1024]{1,0:T(8,128)(2,1)}, u32[]{:S(2)}) copy-start(bf16[512,1024]{1,0:T(8,128)(2,1)} %reduce-scatter.13.cloned.1.call-done) | copy-start | bytes 3145732
  619.4 145.2 %copy-start.61 = (f32[1,1024]{1,0:T(1,128)S(1)}, f32[1,1024]{1,0:T(1,128)}, u32[]{:S(2)}) copy-start(f32[1,1024]{1,0:T(1,128)} %copy-done.60) | copy-start | bytes 12292
  619.4 145.2 %copy-start.65 = (f32[1,1024]{1,0:T(1,128)S(1)}, f32[1,1024]{1,0:T(1,128)}, u32[]{:S(2)}) copy-start(f32[1,1024]{1,0:T(1,128)} %copy-done.64) | copy-start | bytes 12292
  619.4 145.2 %copy-start.67 = (f32[512]{0:T(512)S(1)}, f32[512]{0:T(512)}, u32[]{:S(2)}) copy-start(f32[512]{0:T(512)} %copy-done.66) | copy-start | bytes 6148
  619.5 145.2 %copy-start.69 = (f32[512]{0:T(512)S(1)}, f32[512]{0:T(512)}, u32[]{:S(2)}) copy-start(f32[512]{0:T(512)} %copy-done.68) | copy-start | bytes 6148
  619.5 145.2 %copy-start.72 = (f32[512]{0:T(512)S(1)}, f32[512]{0:T(512)}, u32[]{:S(2)}) copy-start(f32[512]{0:T(512)} %copy-done.71) | copy-start | bytes 6148
  619.5 145.2 %copy-start.74 = (f32[512]{0:T(512)S(1)}, f32[512]{0:T(512)}, u32[]{:S(2)}) copy-start(f32[512]{0:T(512)} %copy-done.73) | copy-start | bytes 6148
  619.5 145.2 %copy-start.77 = (f32[1,1024]{1,0:T(1,128)S(1)}, f32[1,1024]{1,0:T(1,128)}, u32[]{:S(2)}) copy-start(f32[1,1024]{1,0:T(1,128)} %copy-done.76) | copy-start | bytes 12292
  619.5 145.2 %copy-start.87 = (f32[1,1024]{1,0:T(1,128)S(1)}, f32[1,1024]{1,0:T(1,128)}, u32[]{:S(2)}) copy-start(f32[1,1024]{1,0:T(1,128)} %get-tuple-element.539) | copy-start | bytes 12292
  619.5 238.9 %all-gather.24.cloned.1.call-start = ((), (), s32[]{:S(2)}) async-start(), calls=%async_computation.21 | async-start | bytes 5242880 | tf_op jit(solution)/shard_map/all_gather | solution.py:184
  777.1 162.2 %all-gather.28.cloned.1.call-start = ((), (), s32[]{:S(2)}) async-start(), calls=%async_computation.25 | async-start | bytes 5242880 | tf_op jit(solution)/shard_map/all_gather | solution.py:184
  780.0 266.0 %reduce-scatter.25.cloned.1.call-start = ((), (), s32[]{:S(2)}) async-start(), calls=%async_computation.26 | async-start | bytes 5242880 | tf_op jit(solution)/shard_map/reduce_scatter | solution.py:197
  939.3 24.8 %copy-start.103 = (bf16[1024,1024]{1,0:T(8,128)(2,1)S(1)}, bf16[1024,1024]{1,0:T(8,128)(2,1)}, u32[]{:S(2)}) copy-start(bf16[1024,1024]{1,0:T(8,128)(2,1)} %all-gather.18.cloned.1.call-done) | copy-start | bytes 6291460
  970.5 154.9 %reduce-scatter.21.cloned.1.call-start = ((), (), s32[]{:S(2)}) async-start(), calls=%async_computation.22 | async-start | bytes 5242880 | tf_op jit(solution)/shard_map/reduce_scatter | solution.py:197
  980.0 239.7 %all-gather.30.cloned.1.call-start = ((), (), s32[]{:S(2)}) async-start(), calls=%async_computation.27 | async-start | bytes 5242880 | tf_op jit(solution)/shard_map/all_gather | solution.py:211
  1137.1 82.6 %copy-start.34 = (bf16[256,1024]{1,0:T(8,128)(2,1)S(1)}, bf16[256,1024]{1,0:T(8,128)(2,1)}, u32[]{:S(2)}) copy-start(bf16[256,1024]{1,0:T(8,128)(2,1)} %all_gather.42) | copy-start | bytes 1572868
  1138.3 369.3 %all-gather.26.cloned.1.call-start = ((), (), s32[]{:S(2)}) async-start(), calls=%async_computation.23 | async-start | bytes 5242880 | tf_op jit(solution)/shard_map/all_gather | solution.py:211
  1139.5 85.7 %copy-start.6 = (bf16[2048,4,64]{0,2,1:T(8,128)(2,1)S(1)}, bf16[2048,4,64]{0,2,1:T(8,128)(2,1)}, u32[]{:S(2)}) copy-start(bf16[2048,4,64]{0,2,1:T(8,128)(2,1)} %copy-done.5) | copy-start | bytes 3145732
  1139.6 761.8 %reduce-scatter.29.cloned.1.call-start = ((), (), s32[]{:S(2)}) async-start(), calls=%async_computation.31 | async-start | bytes 3538944 | tf_op jit(solution)/shard_map/reduce_scatter | solution.py:267
  1242.3 15.7 slice-start
  1242.3 15.7 slice-start.1
  1242.3 15.7 slice-start.2
  1242.4 17.0 slice-start.3
  1308.7 16.8 slice-start.3
  1376.2 16.8 slice-start.3
  1443.6 16.8 slice-start.3
  1527.8 15.6 slice-start.6
  1527.8 16.8 slice-start.7
  1591.9 16.8 slice-start.7
  1657.1 15.6 slice-start.4
  1657.1 15.6 slice-start.5
  1657.1 15.6 slice-start.6
  1657.1 16.8 slice-start.7
  1722.4 15.6 slice-start.5
  1722.4 15.6 slice-start.6
  1722.4 16.8 slice-start.7
  1799.2 124.9 %reduce-scatter.23.cloned.1.call-start = ((), (), s32[]{:S(2)}) async-start(), calls=%async_computation.24 | async-start | bytes 5242880 | tf_op jit(solution)/shard_map/reduce_scatter | solution.py:235
  1806.8 196.8 %reduce-scatter.27.cloned.1.call-start = ((), (), s32[]{:S(2)}) async-start(), calls=%async_computation.28 | async-start | bytes 5242880 | tf_op jit(solution)/shard_map/reduce_scatter | solution.py:235
  1814.6 244.5 %reduce-scatter.35.cloned.1.call-start = ((), (), s32[]{:S(2)}) async-start(), calls=%async_computation.34 | async-start | bytes 4718592 | tf_op jit(solution)/shard_map/reduce_scatter | solution.py:270
  1828.8 285.4 %reduce-scatter.33.cloned.1.call-start = ((), (), s32[]{:S(2)}) async-start(), calls=%async_computation.33 | async-start | bytes 4718592 | tf_op jit(solution)/shard_map/reduce_scatter | solution.py:269
  1843.0 310.9 %reduce-scatter.31.cloned.1.call-start = ((), (), s32[]{:S(2)}) async-start(), calls=%async_computation.32 | async-start | bytes 1179648 | tf_op jit(solution)/shard_map/reduce_scatter | solution.py:268
  1854.0 149.6 %copy-start.22 = (f32[512,1024]{1,0:T(8,128)S(1)}, f32[512,1024]{1,0:T(8,128)}, u32[]{:S(2)}) copy-start(f32[512,1024]{1,0:T(8,128)} %copy-done.21) | copy-start | bytes 6291460
  (116 other events, 799.2 us)
Sparse Core Ops, SparseCore 0:
  10.5 29.1 all-gather.13
  41.9 80.7 all-gather.31
  124.2 79.2 all-gather.33
  206.2 75.2 reduce-scatter.12
  285.3 75.6 reduce-scatter.16
  362.7 28.2 all-gather.17
  393.2 80.7 all-gather.21
  476.1 79.2 all-gather.15
  557.2 26.5 all-gather.19
  609.7 75.2 reduce-scatter.14
  687.3 77.2 reduce-scatter.18
  777.2 81.2 all-gather.23
  860.0 79.2 all-gather.27
  970.6 75.2 reduce-scatter.24
  1048.1 77.2 reduce-scatter.20
  1138.4 81.2 all-gather.29
  1221.1 79.2 all-gather.25
  1799.4 44.5 reduce-scatter.28
  1846.2 77.8 reduce-scatter.22
  1926.3 77.2 reduce-scatter.26
  2007.5 51.5 reduce-scatter.34
  2063.0 51.1 reduce-scatter.32
  2118.0 35.9 reduce-scatter.30
where the time goes:
time: 2170 us; the launch traced here: 2160 us
  waiting for transfers between devices  1110 us (51%)
  matrix products  659 us (30%)
  other arithmetic  204 us (9%)
  local copies, waits for them, and re-layouts  87.2 us (4%)
  blocking collectives  57.7 us (3%)
  loops' own time  27.9 us (1%)
    all_gather x2, waiting for transfers between devices, body(): lax.all_gather(hidden.astype(jnp.bfloat16), 'tensor', axis=0, tiled=True)  153 us
    all_gather x2, waiting for transfers between devices, body(): lax.all_gather(summed_grad.astype(jnp.bfloat16), 'tensor', axis=0, tiled=...  148 us
    reduce_scatter x2, waiting for transfers between devices, body(): lax.psum_scatter(jnp.einsum('tf,df->td', pre_grad, full_up, preferred_ele...  145 us
    reduce_scatter x2, waiting for transfers between devices, body(): lax.psum_scatter(jnp.dot(active_low, full_down, preferred_element_type=jn...  145 us
    dot_general x8, matrix products, one_block(): jnp.einsum('qhe,khe->hqk', grad_blk, value_rows, preferred_element_type=j...  125 us
    dot_general x16, matrix products, block_scores(): jnp.einsum('qhe,khe->hqk', query_blk, key_rows, preferred_element_type=jn...  98.7 us
    dot_general x8, matrix products, one_block(): jnp.einsum('hqk,qhe->khe', attention.astype(jnp.bfloat16), grad_blk, pref...  98.2 us
    reduce_scatter x2, waiting for transfers between devices, body(): lax.psum_scatter(jnp.einsum('ctf,cdf->td', proj_grad, full_qkv, preferred...  96.7 us
  transfers between devices with their start and end apart: 23, of which 19 were waited for; matrix products, arithmetic and copies ran while one was open for 27% of the time, Pallas kernels for 0%

commit v1 on v0

v1 whole, which is shorter than its diff:
```python
import functools
import math
import jax
import jax.numpy as jnp
from jax import lax
from jax.sharding import PartitionSpec as P
from jax.experimental import pallas as pl
from jax.experimental.pallas import tpu as pltpu

HEAD = 64
PAIR = 2 * HEAD
NEG_FILL = -1e30
F32 = jnp.float32
BF16 = jnp.bfloat16
NT = (((1,), (1,)), ((), ()))
NN = (((1,), (0,)), ((), ()))
TN = (((0,), (0,)), ((), ()))


def dot(a, b, dims=NN, precision=None):
    return lax.dot_general(a, b, dims, preferred_element_type=F32, precision=precision)


def head_lanes(rows, which):
    lane = lax.broadcasted_iota(jnp.int32, (rows, PAIR), 1)
    return (lane < HEAD) if which == 0 else (lane >= HEAD)


def attend_fwd_kernel(bk, lo_ref, hi_ref, pad_ref, q_ref, k_ref, v_ref, qcode_ref, kcode_ref, o_ref, lse_ref):
    i = pl.program_id(1)
    bq = q_ref.shape[0]
    q = q_ref[...] * jnp.asarray(0.125, BF16)
    heads = [jnp.where(head_lanes(bq, w), q, jnp.zeros_like(q)) for w in (0, 1)]
    qcode = jnp.tile(qcode_ref[...], (1, bk // 128))
    first = i * bq

    def run(diagonal):
        def step(t, carry):
            at = pl.multiple_of(t * bk, bk)
            k = k_ref[pl.ds(at, bk), :]
            v = v_ref[pl.ds(at, bk), :]
            mask = qcode == kcode_ref[:, pl.ds(at, bk)]
            if diagonal:
                gap = lax.broadcasted_iota(jnp.int32, (bq, bk), 1) - lax.broadcasted_iota(jnp.int32, (bq, bk), 0)
                mask = mask | (gap == first - at)
            out = []
            for h in (0, 1):
                top, total, acc = carry[3 * h : 3 * h + 3]
                s = jnp.where(mask, dot(heads[h], k, NT), NEG_FILL)
                new = jnp.maximum(top, jnp.max(s, axis=1, keepdims=True))
                p = jnp.exp(s - new)
                old = jnp.exp(top - new)
                out += [
                    new,
                    total * old + jnp.sum(p, axis=1, keepdims=True),
                    acc * old + dot(p.astype(BF16), v),
                ]
            return tuple(out)

        one = (jnp.full((bq, 1), NEG_FILL, F32), jnp.zeros((bq, 1), F32), jnp.zeros((bq, PAIR), F32))
        ma, la, aa, mb, lb, ab = lax.fori_loop(lo_ref[i], hi_ref[i], step, one + one)
        o_ref[...] = jnp.where(head_lanes(bq, 0), aa / la, ab / lb).astype(BF16)
        lane = lax.broadcasted_iota(jnp.int32, (bq, PAIR), 1)
        wide = jnp.where(lane == 0, ma + jnp.log(la), mb + jnp.log(lb))
        lse_ref[...] = wide.T[0:8, :]

    pl.when(pad_ref[i] > 0)(lambda: run(True))
    pl.when(pad_ref[i] == 0)(lambda: run(False))


def attend_bwd_kernel(
    bq, lo_ref, hi_ref, pad_ref, q_ref, k_ref, v_ref, c_ref, dc_ref, lse_ref, qcode_ref, kcode_ref,
    dq_ref, dk_ref, dv_ref, dq_acc, delta,
):
    i = pl.program_id(1)
    bk = k_ref.shape[0]
    first = i * bk

    @pl.when(i == 0)
    def _():
        dq_acc[...] = jnp.zeros_like(dq_acc)
        row = lax.broadcasted_iota(jnp.int32, (8, PAIR), 0)
        lane = lax.broadcasted_iota(jnp.int32, (8, PAIR), 1)
        pick = jnp.where(lane // HEAD == row, 1.0, 0.0).astype(F32)
        prod = dc_ref[...].astype(F32) * c_ref[...].astype(F32)
        delta[...] = dot(pick, prod, NT, lax.Precision.HIGHEST)

    k = k_ref[...] * jnp.asarray(0.125, BF16)
    v = v_ref[...]
    kh = [jnp.where(head_lanes(bk, w), k, jnp.zeros_like(k)) for w in (0, 1)]
    vh = [jnp.where(head_lanes(bk, w), v, jnp.zeros_like(v)) for w in (0, 1)]
    kcode = jnp.tile(kcode_ref[...], (1, bq // 128))

    def run(diagonal):
        def step(t, carry):
            dk, dv = carry
            at = pl.multiple_of(t * bq, bq)
            rows = pl.ds(at, bq)
            q = q_ref[rows, :]
            dc = dc_ref[rows, :]
            mask = kcode == qcode_ref[:, rows]
            if diagonal:
                gap = lax.broadcasted_iota(jnp.int32, (bk, bq), 1) - lax.broadcasted_iota(jnp.int32, (bk, bq), 0)
                mask = mask | (gap == first - at)
            dq = jnp.zeros((bq, PAIR), F32)
            for h in (0, 1):
                s = dot(kh[h], q, NT)
                p = jnp.exp(jnp.where(mask, s - lse_ref[h : h + 1, rows], NEG_FILL))
                dp = dot(vh[h], dc, NT)
                ds = (p * (dp - delta[h : h + 1, rows])).astype(BF16)
                own = head_lanes(bq, h)
                dv = dv + dot(p.astype(BF16), jnp.where(own, dc, jnp.zeros_like(dc)))
                dk = dk + dot(ds, jnp.where(own, q, jnp.zeros_like(q)))
                dq = dq + dot(ds, kh[h], TN)
            dq_acc[rows, :] += dq
            return dk, dv

        zero = jnp.zeros((bk, PAIR), F32)
        dk, dv = lax.fori_loop(lo_ref[i], hi_ref[i], step, (zero, zero))
        dk_ref[...] = (dk * 0.125).astype(BF16)
        dv_ref[...] = dv.astype(BF16)

    pl.when(pad_ref[i] > 0)(lambda: run(True))
    pl.when(pad_ref[i] == 0)(lambda: run(False))

    @pl.when(i == pl.num_programs(1) - 1)
    def _():
        dq_ref[...] = dq_acc[...].astype(BF16)


def block_bounds(segment, valid, block, other):
    length = segment.shape[0]
    blocks = segment.reshape(length // block, block)
    lo = jnp.sum((segment[None, :] < blocks[:, :1]).astype(jnp.int32), axis=1) // other
    hi = (jnp.sum((segment[None, :] <= blocks[:, -1:]).astype(jnp.int32), axis=1) + other - 1) // other
    pad = jnp.sum((valid.reshape(length // block, block) == 0).astype(jnp.int32), axis=1)
    return lo, hi, pad


def attention_codes(segment, valid):
    kcode = jnp.where(valid > 0, segment, -1)
    qcode = segment
    wide = lambda a: jnp.broadcast_to(a[:, None], (a.shape[0], 128))
    return qcode, kcode, wide(qcode), wide(kcode)


def attend_fwd(qkv, segment, valid, bq=256, bk=256):
    length, width = qkv.shape
    pairs = width // 3 // PAIR
    lo, hi, pad = block_bounds(segment, valid, bq, bk)
    qcode, kcode, qwide, kwide = attention_codes(segment, valid)
    return pl.pallas_call(
        functools.partial(attend_fwd_kernel, bk),
        grid_spec=pltpu.PrefetchScalarGridSpec(
            num_scalar_prefetch=3,
            grid=(pairs, length // bq),
            in_specs=[
                pl.BlockSpec((bq, PAIR), lambda h, i, *_: (i, h)),
                pl.BlockSpec((length, PAIR), lambda h, i, *_: (0, pairs + h)),
                pl.BlockSpec((length, PAIR), lambda h, i, *_: (0, 2 * pairs + h)),
                pl.BlockSpec((bq, 128), lambda h, i, *_: (i, 0)),
                pl.BlockSpec((1, length), lambda h, i, *_: (0, 0)),
            ],
            out_specs=[
                pl.BlockSpec((bq, PAIR), lambda h, i, *_: (i, h)),
                pl.BlockSpec((8, bq), lambda h, i, *_: (h, i)),
            ],
        ),
        out_shape=[
            jax.ShapeDtypeStruct((length, pairs * PAIR), BF16),
            jax.ShapeDtypeStruct((pairs * 8, length), F32),
        ],
        compiler_params=pltpu.CompilerParams(dimension_semantics=("arbitrary", "arbitrary")),
        cost_estimate=pl.CostEstimate(flops=8 * 2 * length * length * PAIR, bytes_accessed=8 * length * width, transcendentals=4 * length * length),
    )(lo, hi, pad, qkv, qkv, qkv, qwide, kcode[None, :])


def attend_bwd(qkv, context, context_grad, lse, segment, valid, bq=256, bk=256):
    length, width = qkv.shape
    pairs = width // 3 // PAIR
    lo, hi, pad = block_bounds(segment, valid, bk, bq)
    qcode, kcode, qwide, kwide = attention_codes(segment, valid)
    whole = lambda at: pl.BlockSpec((length, PAIR), lambda h, i, *_: (0, at * pairs + h))
    part = lambda at: pl.BlockSpec((bk, PAIR), lambda h, i, *_: (i, at * pairs + h))
    shape = jax.ShapeDtypeStruct((length, pairs * PAIR), BF16)
    return pl.pallas_call(
        functools.partial(attend_bwd_kernel, bq),
        grid_spec=pltpu.PrefetchScalarGridSpec(
            num_scalar_prefetch=3,
            grid=(pairs, length // bk),
            in_specs=[
                whole(0), part(1), part(2), whole(0), whole(0),
                pl.BlockSpec((8, length), lambda h, i, *_: (h, 0)),
                pl.BlockSpec((1, length), lambda h, i, *_: (0, 0)),
                pl.BlockSpec((bk, 128), lambda h, i, *_: (i, 0)),
            ],
            out_specs=[whole(0), part(0), part(0)],
            scratch_shapes=[pltpu.VMEM((length, PAIR), F32), pltpu.VMEM((8, length), F32)],
        ),
        out_shape=[shape, shape, shape],
        compiler_params=pltpu.CompilerParams(dimension_semantics=("arbitrary", "arbitrary")),
        cost_estimate=pl.CostEstimate(flops=20 * 2 * length * length * PAIR, bytes_accessed=16 * length * width, transcendentals=4 * length * length),
    )(lo, hi, pad, qkv, qkv, qkv, context, context_grad, lse, qcode[None, :], kwide)


def norm_stats(values):
    center = values - jnp.mean(values, axis=1, keepdims=True)
    inverse = lax.rsqrt(jnp.mean(center * center, axis=1, keepdims=True) + 1e-05)
    return center * inverse, inverse


def norm_pull(incoming, normed, inverse, gain):
    scaled = incoming * gain
    return inverse * (
        scaled - jnp.mean(scaled, axis=1, keepdims=True) - normed * jnp.mean(scaled * normed, axis=1, keepdims=True)
    )


def col_sum(values):
    return jnp.sum(values, axis=0, keepdims=True)


def add_sums(ref, parts):
    @pl.when(pl.program_id(0) == 0)
    def _():
        ref[...] = jnp.zeros_like(ref)

    for at, part in enumerate(parts):
        ref[at : at + 1, :] += col_sum(part)


def mix_kernel(x_ref, c_ref, w_ref, bias_ref, gain_ref, hl_ref, n_ref, r_ref):
    mixed = x_ref[...].astype(F32) + dot(c_ref[...], w_ref[...]) + bias_ref[0:1, :]
    normed, inverse = norm_stats(mixed)
    hl_ref[...] = (normed * gain_ref[0:1, :] + bias_ref[1:2, :]).astype(BF16)
    n_ref[...] = normed
    r_ref[...] = jnp.broadcast_to(inverse, r_ref.shape)


def up_kernel(h_ref, w_ref, bias_ref, g_ref, slope_ref):
    u = dot(h_ref[...], w_ref[...]) + bias_ref[...]
    cdf = 0.5 + 0.5 * lax.erf(u * (1.0 / math.sqrt(2.0)))
    g_ref[...] = (u * cdf).astype(BF16)
    slope_ref[...] = (cdf + u * (jnp.exp(-0.5 * u * u) * (1.0 / math.sqrt(2.0 * math.pi)))).astype(BF16)


def down_kernel(g_ref, w_ref, n_ref, e_ref, bias_ref, gain_ref, out_ref, dr_ref, dz_ref, sum_ref):
    hidden = n_ref[...] * gain_ref[0:1, :] + bias_ref[1:2, :]
    normed, inverse = norm_stats(hidden + dot(g_ref[...], w_ref[...]) + bias_ref[2:3, :])
    out_ref[...] = (normed * gain_ref[1:2, :] + bias_ref[3:4, :]).astype(BF16)
    e = e_ref[...].astype(F32)
    dr = norm_pull(e, normed, inverse, gain_ref[1:2, :])
    dr_ref[...] = dr
    dz_ref[...] = dr.astype(BF16)
    add_sums(sum_ref, (e * normed, dr, e))


def slope_kernel(dz_ref, w_ref, slope_ref, du_ref, sum_ref):
    du = (dot(dz_ref[...], w_ref[...], NT) * slope_ref[...].astype(F32)).astype(BF16)
    du_ref[...] = du

    @pl.when(pl.program_id(1) == 0)
    def _():
        sum_ref[...] = jnp.zeros_like(sum_ref)

    sum_ref[0:1, :] += col_sum(du.astype(F32))


def mix_pull_kernel(du_ref, w_ref, dr_ref, n_ref, r_ref, gain_ref, dm_ref, da_ref, sum_ref):
    dh = dr_ref[...] + dot(du_ref[...], w_ref[...], NT)
    normed = n_ref[...]
    dm = norm_pull(dh, normed, r_ref[:, 0:1], gain_ref[0:1, :])
    dm_ref[...] = dm
    da_ref[...] = dm.astype(BF16)
    add_sums(sum_ref, (dh * normed, dm, dh))


def call(kernel, grid, ins, outs, flops, nbytes, *args):
    return pl.pallas_call(
        kernel,
        grid=grid,
        in_specs=ins,
        out_specs=outs[0],
        out_shape=outs[1],
        compiler_params=pltpu.CompilerParams(dimension_semantics=("arbitrary",) * len(grid)),
        cost_estimate=pl.CostEstimate(flops=flops, bytes_accessed=nbytes, transcendentals=0),
    )(*args)


def rows(block, width):
    return pl.BlockSpec((block, width), lambda i: (i, 0))


def held(shape):
    return pl.BlockSpec(shape, lambda i: (0, 0))


def once(shape):
    return pl.BlockSpec(shape, lambda i: (0, 0), pipeline_mode=pl.Buffered(1))


def sds(shape, dtype=BF16):
    return jax.ShapeDtypeStruct(shape, dtype)


def mix(x, c, w, biases, gains, block=256):
    n, d = x.shape
    r = functools.partial(rows, block)
    return call(
        mix_kernel, (n // block,),
        [r(d), r(c.shape[1]), once(w.shape), held(biases.shape), held(gains.shape)],
        ([r(d), r(d), r(128)], [sds((n, d)), sds((n, d), F32), sds((n, 128), F32)]),
        2 * n * d * d, 12 * n * d, x, c, w, biases, gains,
    )


def up(h, w, bias, block=256, cols=1024):
    n, d = h.shape
    f = w.shape[1]
    cols = min(cols, f)
    tile = pl.BlockSpec((block, cols), lambda j, i: (i, j))
    return call(
        up_kernel, (f // cols, n // block),
        [pl.BlockSpec((block, d), lambda j, i: (i, 0)), pl.BlockSpec((d, cols), lambda j, i: (0, j)), pl.BlockSpec((1, cols), lambda j, i: (0, j))],
        ([tile, tile], [sds((n, f)), sds((n, f))]),
        2 * n * d * f, 4 * n * f + 2 * d * f, h, w, bias,
    )


def down(g, w, normed, e, biases, gains, block=256):
    n, f = g.shape
    d = w.shape[1]
    r = functools.partial(rows, block)
    return call(
        down_kernel, (n // block,),
        [r(f), once(w.shape), r(d), r(d), held(biases.shape), held(gains.shape)],
        ([r(d), r(d), r(d), held((8, d))], [sds((n, d)), sds((n, d), F32), sds((n, d)), sds((8, d), F32)]),
        2 * n * d * f, 2 * n * f + 2 * d * f, g, w, normed, e, biases, gains,
    )


def slope_pull(dz, w, slope, block=256, cols=1024):
    n, d = dz.shape
    f = w.shape[0]
    tile = pl.BlockSpec((block, cols), lambda j, i: (i, j))
    return call(
        slope_kernel, (f // cols, n // block),
        [pl.BlockSpec((block, d), lambda j, i: (i, 0)), pl.BlockSpec((cols, d), lambda j, i: (j, 0)), tile],
        ([tile, pl.BlockSpec((8, cols), lambda j, i: (0, j))], [sds((n, f)), sds((8, f), F32)]),
        2 * n * d * f, 4 * n * f + 2 * d * f, dz, w, slope,
    )


def mix_pull(du, w, dr, normed, inverse, gains, block=256):
    n, f = du.shape
    d = w.shape[0]
    r = functools.partial(rows, block)
    return call(
        mix_pull_kernel, (n // block,),
        [r(f), once(w.shape), r(d), r(d), r(128), held(gains.shape)],
        ([r(d), r(d), held((8, d))], [sds((n, d), F32), sds((n, d)), sds((8, d), F32)]),
        2 * n * d * f, 2 * n * f + 2 * d * f, du, w, dr, normed, inverse, gains,
    )


def swap_cores(value):
    return lax.ppermute(value, "core", [(0, 1), (1, 0)])


def column_routes(tensor_size):
    first, second = [], []
    for core in range(2):
        for t in range(tensor_size):
            at = core * tensor_size + t
            first.append((at, (t >> 1) * tensor_size + 2 * core + (t & 1)))
            second.append((at, (t >> 1) * tensor_size + 2 * core + 1 - (t & 1)))
    return first, second


def back(route):
    return [(b, a) for a, b in route]


def by_core(core, mine, other, axis):
    return jnp.where(
        core == 0, jnp.concatenate([mine, other], axis=axis), jnp.concatenate([other, mine], axis=axis)
    )


def body(
    inputs, segment_ids, token_valid, qkv_weight, qv_bias, out_weight, norm_gains, row_biases,
    up_weight, up_bias, down_weight, out_grad,
):
    COL = ("core", "tensor")
    ALL = ("p", "core", "tensor")
    core, tensor = lax.axis_index("core"), lax.axis_index("tensor")
    n_p, n_t = lax.axis_size("p"), lax.axis_size("tensor")
    n_dp = 2 * n_p
    micro, held_rows, width = inputs.shape
    assert micro == 2 and n_t == 4
    odd = tensor & 1
    route_a, route_b = column_routes(n_t)

    def bring(value):
        a = lax.ppermute(value[odd], COL, route_a)
        b = lax.ppermute(value[1 - odd], COL, route_b)
        return jnp.where(odd == 0, jnp.concatenate([a, b]), jnp.concatenate([b, a]))

    def give(value):
        a = lax.ppermute(lax.dynamic_slice_in_dim(value, odd * held_rows, held_rows), COL, back(route_a))
        b = lax.ppermute(lax.dynamic_slice_in_dim(value, (1 - odd) * held_rows, held_rows), COL, back(route_b))
        return jnp.where(odd == 0, jnp.stack([a, b]), jnp.stack([b, a]))

    def gathered(weight):
        got = lax.all_gather(weight, ALL, axis=0, tiled=False)
        return got.reshape((n_dp, n_t) + weight.shape)

    x_own = bring(inputs)
    rows = x_own.shape[0]
    labels = jnp.stack([segment_ids[:, 0], token_valid[:, 0]], axis=1)[odd]
    labels = jnp.where((tensor >> 1) == core, labels, swap_cores(labels))
    segment, valid = labels[0], labels[1]

    bias_all = lax.all_gather(jnp.concatenate([qv_bias.reshape(-1), up_bias]), "tensor")
    n_qv = qv_bias.size
    qv_all = bias_all[:, :n_qv].reshape(n_t, 2, -1).transpose(1, 0, 2).reshape(2, -1)
    up_bias_all = bias_all[:, n_qv:].reshape(1, -1)

    w_qkv = gathered(qkv_weight)
    w_qkv = lax.dynamic_slice_in_dim(w_qkv, 2 * core, 2, 1)
    w_qkv = w_qkv.transpose(0, 3, 2, 1, 4).reshape(width, -1)
    own = w_qkv.shape[1] // 3
    w_out = gathered(out_weight).transpose(1, 2, 0, 3).reshape(-1, width)
    w_up = gathered(up_weight).transpose(0, 2, 1, 3).reshape(width, -1)
    w_down = gathered(down_weight).transpose(1, 2, 0, 3).reshape(-1, width)

    x_full = by_core(core, x_own, swap_cores(x_own), 0)
    qv_own = lax.dynamic_slice_in_dim(qv_all, core * own, own, 1)
    bias = jnp.concatenate([qv_own[0], jnp.zeros_like(qv_own[0]), qv_own[1]])
    qkv = (jnp.dot(x_full, w_qkv, preferred_element_type=F32) + bias).astype(BF16)
    context, lse = attend_fwd(qkv, segment, valid, 512, 512)
    mine = lax.dynamic_slice_in_dim(context, core * rows, rows)
    other = lax.dynamic_slice_in_dim(context, (1 - core) * rows, rows)
    c_own = by_core(core, mine, swap_cores(other), 1)
    hl, normed, inverse = mix(x_own, c_own, w_out, row_biases, norm_gains)
    active, slope = up(hl, w_up, up_bias_all)
    grad_own = bring(out_grad)
    layer, dr, dz, sums_two = down(active, w_down, normed, grad_own, row_biases, norm_gains)
    layer_out = give(layer)

    du, up_sum = slope_pull(dz, w_down, slope)
    dm, da, sums_one = mix_pull(du, w_up, dr, normed, inverse, norm_gains)
    g_down = dot(active, dz, TN).astype(BF16)
    g_up = dot(hl, du, TN).astype(BF16)
    g_out = dot(c_own, da, TN).astype(BF16)
    dc = dot(da, w_out, NT).astype(BF16)
    mine = lax.dynamic_slice_in_dim(dc, core * own, own, 1)
    other = lax.dynamic_slice_in_dim(dc, (1 - core) * own, own, 1)
    dc_full = by_core(core, mine, swap_cores(other), 0)
    dq, dk, dv = attend_bwd(qkv, context, dc_full, lse, segment, valid, 256, 512)
    dqkv = jnp.concatenate([dq, dk, dv], axis=1)
    g_qkv = dot(x_full, dqkv, TN).astype(BF16)
    qv_sum = jnp.stack([jnp.sum(dq.astype(F32), axis=0), jnp.sum(dv.astype(F32), axis=0)])
    dx = dot(dqkv, w_qkv, NT)
    mine = lax.dynamic_slice_in_dim(dx, core * rows, rows)
    other = lax.dynamic_slice_in_dim(dx, (1 - core) * rows, rows).astype(BF16)
    dx_own = mine + swap_cores(other).astype(F32) + dm
    input_grad = give(dx_own.astype(BF16)).astype(F32)

    def owner_sum(parts, join):
        keep = lax.dynamic_index_in_dim(parts, core, 1, keepdims=False)
        send = lax.dynamic_index_in_dim(parts, 1 - core, 1, keepdims=False)
        both = join(keep, swap_cores(send))
        some = lax.psum_scatter(both, "p", scatter_dimension=0, tiled=False)
        return lax.psum_scatter(some, "tensor", scatter_dimension=0, tiled=False).astype(F32)

    plus = lambda a, b: (a.astype(F32) + b.astype(F32)).astype(BF16)
    beside = lambda a, b: by_core(core, a, b, 1)
    down_total = owner_sum(g_down.reshape(n_t, -1, n_p, 2, down_weight.shape[1]).transpose(2, 3, 0, 1, 4), plus)
    up_total = owner_sum(g_up.reshape(n_p, 2, -1, n_t, up_weight.shape[1]).transpose(0, 1, 3, 2, 4), plus)
    out_total = owner_sum(g_out.reshape(n_t, -1, n_p, 2, out_weight.shape[1]).transpose(2, 3, 0, 1, 4), plus)
    qkv_total = owner_sum(
        g_qkv.reshape(n_p, 2, -1, 3, 2, qkv_weight.shape[2]).transpose(0, 1, 4, 3, 2, 5), beside
    )

    qv_pad = lax.dynamic_update_slice(jnp.zeros((2, width), F32), qv_sum, (0, core * own))
    small = jnp.concatenate(
        [
            jnp.stack([sums_one[0], sums_two[0], sums_one[1], sums_one[2], sums_two[1], sums_two[2]]).reshape(-1),
            qv_pad.reshape(-1),
            up_sum[0],
        ]
    )
    small = lax.psum(small, ALL)
    gain_sum = small[: 2 * width].reshape(2, width)
    bias_sum = small[2 * width : 6 * width].reshape(4, width)
    qv_total = lax.dynamic_slice_in_dim(small[6 * width : 8 * width].reshape(2, width), tensor * qv_bias.shape[1], qv_bias.shape[1], 1)
    up_bias_total = lax.dynamic_slice_in_dim(small[8 * width :], tensor * up_bias.shape[0], up_bias.shape[0])
    return (
        layer_out, input_grad, qkv_total, qv_total, out_total, gain_sum, bias_sum, up_total, up_bias_total, down_total,
    )


def solution(mesh):
    dp, tensor = mesh.devices.shape
    split = jax.sharding.Mesh(mesh.devices.reshape(dp // 2, 2, tensor), ("p", "core", "tensor"))
    pc = ("p", "core")
    tokens = P(None, ("p", "core", "tensor"), None)
    return jax.shard_map(
        body,
        mesh=split,
        in_specs=(
            tokens, P(None, pc, None), P(None, pc, None), P(None, pc, "tensor"), P(None, "tensor"), P("tensor", pc),
            P(), P(), P(pc, "tensor"), P("tensor"), P("tensor", pc), tokens,
        ),
        out_specs=(
            tokens, tokens, P(None, pc, "tensor"), P(None, "tensor"), P("tensor", pc), P(), P(), P(pc, "tensor"),
            P("tensor"), P("tensor", pc),
        ),
        check_vma=False,
    )
```

time: 2170 us -> 905 us (0.42)
  waiting for transfers between devices: 1110 us -> 94.6 us
  matrix products: 659 us -> 70.5 us
  Pallas kernels: 0 us -> 258 us
  other arithmetic: 204 us -> 50.1 us
  blocking collectives: 57.7 us -> 157 us
  local copies, waits for them, and re-layouts: 87.2 us -> 182 us
  starting transfers between devices: 1.35 us -> 71 us
  loops' own time: 27.9 us -> 0 us
    reduce_scatter x12 -> x4, waiting for transfers between devices: 605 us -> 0.01 us  [owner_sum(): lax.psum_scatter(some, 'tensor', scatter_dimension=0, tiled=False)]
    dot_general x80 -> x7, matrix products: 659 us -> 70.5 us  [the longest x6 56.6 us: dot(): lax.dot_general(a, b, dims, preferred_element_type=F32, precision=precision)]
    all_gather x11 -> x4, waiting for transfers between devices: 500 us -> 32.2 us  [gathered(): got = lax.all_gather(weight, ALL, axis=0, tiled=False)]
    pallas_call x0 -> x7, Pallas kernels: none -> 258 us  [the longest x5 92.1 us: call(): pl.pallas_call(kernel, grid=grid, in_specs=ins, out_specs=outs[0], out_sh...]
    convert_element_type x17 -> x10, other arithmetic: 103 us -> 24.6 us  [the longest x3 10.6 us: body(): plus = lambda a, b: (a.astype(F32) + b.astype(F32)).astype(BF16)]
    ppermute x0 -> x17, starting transfers between devices: none -> 70.5 us  [the longest x9 36.8 us: swap_cores(): return lax.ppermute(value, 'core', [(0, 1), (1, 0)])]
    reshape x0 -> x9, local copies, waits for them, and re-layouts: none -> 65.6 us  [the longest x3 27.1 us: gathered(): return got.reshape((n_dp, n_t) + weight.shape)]
    psum x1, blocking collectives: 44 us -> 109 us  [body(): small = lax.psum(small, ALL)]
  transfers between devices with their start and end apart: 23 -> 29, of which waited for: 19 -> 6; matrix products, arithmetic and copies ran while one was open for 27% -> 29% of each run, Pallas kernels for 0% -> 19%
where the time goes in v1:
time: 905 us; the launch traced here: 899 us
  Pallas kernels  258 us (29%)
  local copies, waits for them, and re-layouts  182 us (20%)
  blocking collectives  157 us (17%)
  waiting for transfers between devices  94.6 us (10%)
  starting transfers between devices  71 us (8%)
  matrix products  70.5 us (8%)
  other arithmetic  50.1 us (6%)
  between operations  14.9 us (2%)
    psum x1, blocking collectives, body(): small = lax.psum(small, ALL)  109 us
    pallas_call x5, Pallas kernels, call(): pl.pallas_call(kernel, grid=grid, in_specs=ins, out_specs=outs[0], out_sh...  92.1 us
    pallas_call x1, Pallas kernels, attend_bwd(): pl.pallas_call(functools.partial(attend_bwd_kernel, bq), grid_spec=pltpu....  92.1 us
    pallas_call x1, Pallas kernels, attend_fwd(): pl.pallas_call(functools.partial(attend_fwd_kernel, bk), grid_spec=pltpu....  74.2 us
    dot_general x6, matrix products, dot(): lax.dot_general(a, b, dims, preferred_element_type=F32, precision=precision)  56.6 us
    unnamed x53, local copies, waits for them, and re-layouts  52.8 us
    all_gather x1, blocking collectives, body(): lax.all_gather(jnp.concatenate([qv_bias.reshape(-1), up_bias]), 'tensor')  48.3 us
    ppermute x9, starting transfers between devices, swap_cores(): return lax.ppermute(value, 'core', [(0, 1), (1, 0)])  36.8 us
  transfers between devices with their start and end apart: 29, of which 6 were waited for; matrix products, arithmetic and copies ran while one was open for 29% of the time, Pallas kernels for 19%

profile of v1, /device:TPU:0, one launch (start us, length us, event | category | flops | bytes accessed | tf_op | source)
XLA Modules:
  0.0 898.6 jit_solution(15893002144514096118)
XLA Ops:
  10.0 3.0 dynamic-slice_bitcast_fusion.3
  13.1 3.1 collective-permute-start.1
  16.2 9.4 %collective-permute-start = (bf16[512,1024]{1,0:T(8,128)(2,1)}, bf16[512,1024]{1,0:T(8,128)(2,1)}, u32[]{:S(2)}, u32[]{:S(2)}) collective-permute-start(bf16[512,1024]{1,0:T(8,128)(2,1)} %get-tuple-element.70), channel_id=1, source_target_pairs={{0,0},{1,1},{2,4},{3,5},{4,2},{5,3},{6,6},{7,7},{8,8},{9,9},{10,12... | collective-permute-start | bytes 3145736 | tf_op jit(solution)/shard_map/ppermute | solution.py:405
  25.6 19.0 %collective-permute-done.1 = bf16[512,1024]{1,0:T(8,128)(2,1)S(1)} collective-permute-done((bf16[512,1024]{1,0:T(8,128)(2,1)}, bf16[512,1024]{1,0:T(8,128)(2,1)S(1)}, u32[]{:S(2)}, u32[]{:S(2)}) %collective-permute-start.1) | collective-permute-done | bytes 1048608 | tf_op jit(solution)/shard_map/ppermute | solution.py:406
  44.6 4.0 maximum_select_fusion.2.x_ref
  48.6 34.4 %collective-permute-start.3 = (bf16[1024,1024]{1,0:T(8,128)(2,1)}, bf16[1024,1024]{1,0:T(8,128)(2,1)}, u32[]{:S(2)}, u32[]{:S(2)}) collective-permute-start(bf16[1024,1024]{1,0:T(8,128)(2,1)} %maximum_select_fusion.2.x_ref), channel_id=1, source_target_pairs={{0,4},{4,0},{1,5},{5,1},{2,6},{6,2},{3,7},{7,3},{8,12},{12,8},{9,1... | collective-permute-start | bytes 6291464 | tf_op jit(solution)/shard_map/ppermute | solution.py:367
  84.6 4.8 collective-permute-start.6
  89.4 9.5 %collective-permute-start.5 = (bf16[512,1024]{1,0:T(8,128)(2,1)}, bf16[512,1024]{1,0:T(8,128)(2,1)}, u32[]{:S(2)}, u32[]{:S(2)}) collective-permute-start(bf16[512,1024]{1,0:T(8,128)(2,1)} %get-tuple-element.66), channel_id=1, source_target_pairs={{0,0},{1,1},{2,4},{3,5},{4,2},{5,3},{6,6},{7,7},{8,8},{9,9},{10,12... | collective-permute-start | bytes 3145736 | tf_op jit(solution)/shard_map/ppermute | solution.py:405
  98.9 48.3 %all-gather.5 = f32[4,1,1536]{2,1,0:T(1,128)S(1)} all-gather(f32[1,1,1536]{2,1,0:T(1,128)S(1)} %reshape.168), channel_id=3, replica_groups=mesh['p'=4,'core'=2,'tensor'=4] {'tensor'}, dimensions={0}, use_global_device_ids=true | all-gather | bytes 30720 | tf_op jit(solution)/shard_map/all_gather | solution.py:424
  149.8 2.1 constant_dynamic-slice_fusion.18
  151.9 3.4 copy.80
  155.3 13.9 %add_convert_fusion.q_ref.k_ref.v_ref = bf16[2048,1536]{1,0:T(8,128)(2,1)} fusion(f32[1536]{0:T(1024)S(1)} %pad_maximum_fusion.3, bf16[192,8,8,128]{3,2,1,0:T(8,128)(2,1)} %bitcast.151, bf16[1024,1024]{1,0:T(8,128)(2,1)} %collective-permute-done.3, bf16[1024,1024]{1,0:T(8,128)(2,1)} %maximum_select_fusion.2.x_ref, pred[]{:T(512)S(6)} %eq.25), kind=kOutput, calls=%fused_computation | convolution fusion | flops 6467616768 | bytes 13637633 | tf_op jit(solution)/shard_map/dot_general | solution.py:440
  170.5 74.2 %shard_map.195 = (bf16[2048,512]{1,0:T(8,128)(2,1)}, f32[32,2048]{1,0:T(8,128)}) custom-call(s32[4]{0:T(128)} %get-tuple-element.86.lo_ref, s32[4]{0:T(128)} %get-tuple-element.83.hi_ref, s32[4]{0:T(128)} %reduce_sum.48.pad_ref, bf16[2048,1536]{1,0:T(8,128)(2,1)} %add_convert_fusion.q_ref.k_ref.v_ref, bf16[2048,1536]{1,0:T(8,128)(2,1)} %add_convert_fusion.q_ref.k_ref.v_ref, ...), custom_call_target="tpu_custom_call" | custom-call | flops 8589934592 | bytes 25165824 | tf_op jit(solution)/shard_map/pallas_call | solution.py:152
  244.7 2.8 constant_dynamic-slice_fusion.17
  248.1 4.7 maximum_select_fusion.4.e_ref
  252.8 2.9 copy.66
  255.8 1.9 copy.120
  257.7 3.7 maximum_select_fusion.3.c_ref
  261.4 8.2 shard_map.196
  269.6 12.1 %copy.67 = bf16[8,4,128,1024]{3,1,2,0:T(4,128)(2,1)} copy(bf16[8,4,128,1024]{3,2,1,0:T(8,128)(2,1)} %bitcast.140) | data formatting | bytes 16777216 | tf_op jit(solution)/shard_map/reshape | solution.py:416
  281.7 12.2 %copy.92 = bf16[128,8,4,1024]{3,1,2,0:T(8,128)(2,1)} copy(bf16[128,8,4,1024]{3,2,1,0:T(4,128)(2,1)} %bitcast.138) | data formatting | bytes 16777216
  293.9 32.2 %all-gather.17.cloned.1.call-done = bf16[32768,128]{1,0:T(8,128)(2,1)} async-done(((bf16[1024,128]{1,0:T(8,128)(2,1)}), bf16[32768,128]{1,0:T(8,128)(2,1)}) %all-gather.17.cloned.1.call-update) | async-done | bytes 8388624 | tf_op jit(solution)/shard_map/all_gather | solution.py:415
  326.1 12.0 %copy.68 = bf16[8,4,1024,128]{3,0,2,1:T(8,128)(2,1)} copy(bf16[8,4,1024,128]{3,2,1,0:T(8,128)(2,1)} %bitcast.141) | data formatting | bytes 16777216 | tf_op jit(solution)/shard_map/reshape | solution.py:416
  338.1 9.0 copy.117
  347.1 24.8 %shard_map.197 = (bf16[1024,4096]{1,0:T(8,128)(2,1)}, bf16[1024,4096]{1,0:T(8,128)(2,1)}) custom-call(bf16[1024,1024]{1,0:T(8,128)(2,1)} %get-tuple-element.30.h_ref, bf16[1024,4096]{1,0:T(8,128)(2,1)} %bitcast.142, f32[1,4096]{1,0:T(1,128)} %bitcast.172), custom_call_target="tpu_custom_call" | custom-call | flops 8589934592 | bytes 25165824 | tf_op jit(solution)/shard_map/pallas_call | solution.py:279
  371.9 19.3 %shard_map.198 = (bf16[1024,1024]{1,0:T(8,128)(2,1)}, f32[1024,1024]{1,0:T(8,128)}, bf16[1024,1024]{1,0:T(8,128)(2,1)}, f32[8,1024]{1,0:T(8,128)}) custom-call(bf16[1024,4096]{1,0:T(8,128)(2,1)} %get-tuple-element.31.g_ref, bf16[4096,1024]{1,0:T(8,128)(2,1)} %bitcast.144, f32[1024,1024]{1,0:T(8,128)} %get-tuple-element.32.n_ref, ...), custom_call_target="tpu_custom_call" | custom-call | flops 8589934592 | bytes 16777216 | tf_op jit(solution)/shard_map/pallas_call | solution.py:279
  391.2 22.0 %shard_map.199 = (bf16[1024,4096]{1,0:T(8,128)(2,1)}, f32[8,4096]{1,0:T(8,128)}) custom-call(bf16[1024,1024]{1,0:T(8,128)(2,1)} %get-tuple-element.34.dz_ref, bf16[4096,1024]{1,0:T(8,128)(2,1)} %bitcast.145, bf16[1024,4096]{1,0:T(8,128)(2,1)} %get-tuple-element.35.slope_ref), custom_call_target="tpu_custom_call" | custom-call | flops 8589934592 | bytes 25165824 | tf_op jit(solution)/shard_map/pallas_call | solution.py:279
  413.2 17.8 %shard_map.200 = (f32[1024,1024]{1,0:T(8,128)}, bf16[1024,1024]{1,0:T(8,128)(2,1)}, f32[8,1024]{1,0:T(8,128)}) custom-call(bf16[1024,4096]{1,0:T(8,128)(2,1)} %get-tuple-element.36.du_ref, bf16[1024,4096]{1,0:T(8,128)(2,1)} %bitcast.143, f32[1024,1024]{1,0:T(8,128)} %get-tuple-element.37.dr_ref, f32[1024,1024]{1,0:T(8,128)} %get-tuple-element.32.n_ref, ...), custom_call_target="tpu_custom_call" | custom-call | flops 8589934592 | bytes 16777216 | tf_op jit(solution)/shard_map/pallas_call | solution.py:279
  431.0 4.0 convolution_convert_fusion.4
  437.5 3.8 convolution_convert_fusion.3
  441.3 3.2 reshape.148
  444.6 5.7 constant_dynamic-slice_fusion.6
  451.7 3.4 maximum_select_fusion.6.dc_ref
  456.5 92.1 %shard_map.201 = (bf16[2048,512]{1,0:T(8,128)(2,1)}, bf16[2048,512]{1,0:T(8,128)(2,1)}, bf16[2048,512]{1,0:T(8,128)(2,1)}) custom-call(s32[4]{0:T(128)} %get-tuple-element.87.lo_ref, s32[4]{0:T(128)} %get-tuple-element.82.hi_ref, s32[4]{0:T(128)} %reduce_sum.48.pad_ref, bf16[2048,1536]{1,0:T(8,128)(2,1)} %add_convert_fusion.q_ref.k_ref.v_ref, ...), custom_call_target="tpu_custom_call" | custom-call | flops 21474836480 | bytes 50331648 | tf_op jit(solution)/shard_map/pallas_call | solution.py:186
  548.6 1.9 constant_dynamic-update-slice_fusion.2
  552.3 2.7 copy-done.8
  555.0 10.5 %convolution_convert_fusion.2 = bf16[1024,1536]{1,0:T(8,128)(2,1)} fusion(bf16[2048,1536]{1,0:T(8,128)(2,1)S(1)} %constant_dynamic-update-slice_fusion, bf16[1024,1024]{1,0:T(8,128)(2,1)} %collective-permute-done.3, bf16[1024,1024]{1,0:T(8,128)(2,1)} %maximum_select_fusion.2.x_ref, pred[]{:T(512)S(6)} %eq.25), kind=kOutput, calls=%fused_computation.15 | convolution fusion | flops 6462898176 | bytes 13631489 | tf_op jit(solution)/shard_map/dot_general | solution.py:21
  565.5 6.2 reshape.145
  571.7 3.2 fusion.8
  575.0 2.2 constant_dynamic-slice_fusion.9
  578.1 2.8 collective-permute-done.13
  580.9 1.9 maximum_select_fusion.1
  584.4 14.9 %convolution_convert_fusion.1 = bf16[1024,4096]{1,0:T(8,128)(2,1)} fusion(bf16[1024,1024]{1,0:T(8,128)(2,1)S(1)} %copy-done.14, bf16[1024,4096]{1,0:T(8,128)(2,1)} %get-tuple-element.36.du_ref), kind=kOutput, calls=%fused_computation.7 | convolution fusion | flops 8594128896 | bytes 18874368 | tf_op jit(solution)/shard_map/dot_general | solution.py:21
  599.3 14.6 %reshape.149 = bf16[4,2,128,4,1024]{4,3,2,1,0:T(4,128)(2,1)} reshape(bf16[1024,4096]{1,0:T(8,128)(2,1)} %convolution_convert_fusion.1) | data formatting | bytes 16777216 | tf_op jit(solution)/shard_map/reshape | solution.py:480
  613.9 9.5 %constant_dynamic-slice_fusion.4 = (bf16[4,1,128,4,1024]{4,3,2,1,0:T(4,128)(2,1)S(1)}, bf16[4,1,128,4,1024]{4,3,2,1,0:T(4,128)(2,1)}) fusion(bf16[4,2,128,4,1024]{4,3,2,1,0:T(4,128)(2,1)} %reshape.149, s32[]{:T(128)S(6)} %select_n.176, s32[]{:T(128)S(6)} %select_n.177), kind=kLoop, calls=%fused_computation.70 | loop fusion | bytes 16777224 | tf_op jit(solution)/shard_map/jit(dynamic_index_in_dim)/dynamic_slice | solution.py:471
  623.4 3.7 copy.119
  627.7 6.8 collective-permute-done.15
  634.5 4.3 fusion.1
  640.4 14.7 %convolution_convert_fusion = bf16[4096,1024]{1,0:T(8,128)(2,1)} fusion(bf16[1024,4096]{1,0:T(8,128)(2,1)} %get-tuple-element.31.g_ref, bf16[1024,1024]{1,0:T(8,128)(2,1)S(1)} %copy-done.16), kind=kOutput, calls=%fused_computation.6 | convolution fusion | flops 8594128896 | bytes 18874368 | tf_op jit(solution)/shard_map/dot_general | solution.py:21
  655.1 14.5 %reshape.150 = bf16[4,1024,4,2,128]{4,3,2,1,0:T(2,128)(2,1)} reshape(bf16[4096,1024]{1,0:T(8,128)(2,1)} %convolution_convert_fusion) | data formatting | bytes 16777216 | tf_op jit(solution)/shard_map/reshape | solution.py:479
  669.6 20.2 %constant_dynamic-slice_fusion.2 = (bf16[4,1024,4,1,128]{4,3,2,1,0:T(2,128)(2,1)S(1)}, bf16[4,1024,4,1,128]{4,3,2,1,0:T(2,128)(2,1)}) fusion(bf16[4,1024,4,2,128]{4,3,2,1,0:T(2,128)(2,1)} %reshape.150, s32[]{:T(128)S(6)} %select_n.176, s32[]{:T(128)S(6)} %select_n.177), kind=kLoop, calls=%fused_computation.68 | loop fusion | bytes 16777224 | tf_op jit(solution)/shard_map/jit(dynamic_index_in_dim)/dynamic_slice | solution.py:471
  689.8 5.2 copy.118
  695.5 6.8 collective-permute-done.16
  702.3 3.1 fusion
  707.4 8.7 fusion.2
  716.1 3.3 copy-done.2
  724.5 3.0 constant_dynamic-slice_fusion.15
  729.3 1.9 collective-permute-start.7
  732.2 2.1 convert_reduce_fusion
  735.1 4.2 add_convert_fusion.1
  739.3 23.1 %reduce-scatter.31.cloned.1.call-done = bf16[1,4,1024,128]{3,2,1,0:T(8,128)(2,1)} async-done(((bf16[4,4,1024,128]{3,2,1,0:T(8,128)(2,1)}), bf16[1,4,1024,128]{3,2,1,0:T(8,128)(2,1)}) %reduce-scatter.31.cloned.1.call-update) | async-done | bytes 1048592
  767.2 108.7 %psum.7 = f32[12288]{0:T(1024)S(1)} all-reduce(f32[12288]{0:T(1024)S(1)} %pad_maximum_fusion), channel_id=1, replica_groups=mesh['p'=4,'core'=2,'tensor'=4] {'p','core','tensor'}, use_global_device_ids=true, to_apply=%region_7.8 | all-reduce | flops 12288 | bytes 98304 | tf_op jit(solution)/shard_map/psum | solution.py:494
  878.4 3.9 maximum_select_fusion.5
  883.8 2.4 fusion.7
  (148 shorter events, 46.0 us)
Async XLA Ops:
  7.2 142.6 %all-gather.11.cloned.1.call-start = ((), (), s32[]{:S(2)}) async-start(), calls=%async_computation.12 | async-start | bytes 6488064 | tf_op jit(solution)/shard_map/all_gather | solution.py:415
  7.9 244.9 %all-gather.13.cloned.1.call-start = ((), (), s32[]{:S(2)}) async-start(), calls=%async_computation.13 | async-start | bytes 2162688 | tf_op jit(solution)/shard_map/all_gather | solution.py:415
  8.7 260.9 %all-gather.15.cloned.1.call-start = ((), (), s32[]{:S(2)}) async-start(), calls=%async_computation.14 | async-start | bytes 8650752 | tf_op jit(solution)/shard_map/all_gather | solution.py:415
  9.4 316.7 %all-gather.17.cloned.1.call-start = ((), (), s32[]{:S(2)}) async-start(), calls=%async_computation.15 | async-start | bytes 8650752 | tf_op jit(solution)/shard_map/all_gather | solution.py:415
  10.0 695.5 %reduce-scatter.27.cloned.1.call-start = ((), (), s32[]{:S(2)}) async-start(), calls=%async_computation.17 | async-start | bytes 1310720
  13.1 70.0 %copy-start.10 = (s32[2,1,2048]{2,1,0:T(1,128)S(1)}, s32[2,1,2048]{2,1,0:T(1,128)}, u32[]{:S(2)}) copy-start(s32[2,1,2048]{2,1,0:T(1,128)} %param.13) | copy-start | bytes 49156
  13.1 70.0 %copy-start.11 = (s32[2,1,2048]{2,1,0:T(1,128)S(1)}, s32[2,1,2048]{2,1,0:T(1,128)}, u32[]{:S(2)}) copy-start(s32[2,1,2048]{2,1,0:T(1,128)} %param.14) | copy-start | bytes 49156
  13.1 70.1 %copy-start.5 = (bf16[2,512,1024]{2,1,0:T(8,128)(2,1)S(1)}, bf16[2,512,1024]{2,1,0:T(8,128)(2,1)}, u32[]{:S(2)}) copy-start(bf16[2,512,1024]{2,1,0:T(8,128)(2,1)} %param.23) | copy-start | bytes 6291460
  13.1 31.6 %collective-permute-start.1 = (bf16[512,1024]{1,0:T(8,128)(2,1)}, bf16[512,1024]{1,0:T(8,128)(2,1)S(1)}, u32[]{:S(2)}, u32[]{:S(2)}) collective-permute-start(bf16[512,1024]{1,0:T(8,128)(2,1)} %get-tuple-element.71), channel_id=1, source_target_pairs={{0,1},{1,0},{2,5},{3,4},{4,3},{5,2},{6,7},{7,6},{8,9},{9,8},{10,13... | collective-permute-start | bytes 3145736 | tf_op jit(solution)/shard_map/ppermute | solution.py:406
  16.2 28.5 %collective-permute-start = (bf16[512,1024]{1,0:T(8,128)(2,1)}, bf16[512,1024]{1,0:T(8,128)(2,1)}, u32[]{:S(2)}, u32[]{:S(2)}) collective-permute-start(bf16[512,1024]{1,0:T(8,128)(2,1)} %get-tuple-element.70), channel_id=1, source_target_pairs={{0,0},{1,1},{2,4},{3,5},{4,2},{5,3},{6,6},{7,7},{8,8},{9,9},{10,12... | collective-permute-start | bytes 3145736 | tf_op jit(solution)/shard_map/ppermute | solution.py:405
  48.6 50.3 %copy-start.13 = (f32[2,256]{1,0:T(2,128)S(1)}, f32[2,256]{1,0:T(2,128)}, u32[]{:S(2)}) copy-start(f32[2,256]{1,0:T(2,128)} %param.16) | copy-start | bytes 6148
  48.6 50.3 %copy-start.12 = (f32[1024]{0:T(1024)S(1)}, f32[1024]{0:T(1024)}, u32[]{:S(2)}) copy-start(f32[1024]{0:T(1024)} %param.21) | copy-start | bytes 12292
  48.6 106.7 %collective-permute-start.3 = (bf16[1024,1024]{1,0:T(8,128)(2,1)}, bf16[1024,1024]{1,0:T(8,128)(2,1)}, u32[]{:S(2)}, u32[]{:S(2)}) collective-permute-start(bf16[1024,1024]{1,0:T(8,128)(2,1)} %maximum_select_fusion.2.x_ref), channel_id=1, source_target_pairs={{0,4},{4,0},{1,5},{5,1},{2,6},{6,2},{3,7},{7,3},{8,12},{12,8},{9,1... | collective-permute-start | bytes 6291464 | tf_op jit(solution)/shard_map/ppermute | solution.py:367
  83.0 64.4 %collective-permute-start.2 = (s32[2,2048]{1,0:T(2,128)S(1)}, s32[2,2048]{1,0:T(2,128)S(1)}, u32[]{:S(2)}, u32[]{:S(2)}) collective-permute-start(s32[2,2048]{1,0:T(2,128)S(1)} %fusion.10), channel_id=1, source_target_pairs={{0,4},{4,0},{1,5},{5,1},{2,6},{6,2},{3,7},{7,3},{8,12},{12,8},{9,1... | collective-permute-start | bytes 49160 | tf_op jit(solution)/shard_map/ppermute | solution.py:367
  84.6 163.5 %collective-permute-start.6 = (bf16[512,1024]{1,0:T(8,128)(2,1)}, bf16[512,1024]{1,0:T(8,128)(2,1)}, u32[]{:S(2)}, u32[]{:S(2)}) collective-permute-start(bf16[512,1024]{1,0:T(8,128)(2,1)} %get-tuple-element.67), channel_id=1, source_target_pairs={{0,1},{1,0},{2,5},{3,4},{4,3},{5,2},{6,7},{7,6},{8,9},{9,8},{10,13... | collective-permute-start | bytes 3145736 | tf_op jit(solution)/shard_map/ppermute | solution.py:406
  89.4 158.7 %collective-permute-start.5 = (bf16[512,1024]{1,0:T(8,128)(2,1)}, bf16[512,1024]{1,0:T(8,128)(2,1)}, u32[]{:S(2)}, u32[]{:S(2)}) collective-permute-start(bf16[512,1024]{1,0:T(8,128)(2,1)} %get-tuple-element.66), channel_id=1, source_target_pairs={{0,0},{1,1},{2,4},{3,5},{4,2},{5,3},{6,6},{7,7},{8,8},{9,9},{10,12... | collective-permute-start | bytes 3145736 | tf_op jit(solution)/shard_map/ppermute | solution.py:405
  148.0 288.4 %copy-start.9 = (s32[1,2048]{1,0:T(1,128)}, s32[1,2048]{1,0:T(1,128)S(1)}, u32[]{:S(2)}) copy-start(s32[1,2048]{1,0:T(1,128)S(1)} %get-tuple-element.77.qcode_ref) | copy-start | bytes 24580
  247.4 10.3 %collective-permute-start.4 = (bf16[1024,512]{1,0:T(8,128)(2,1)}, bf16[1024,512]{1,0:T(8,128)(2,1)}, u32[]{:S(2)}, u32[]{:S(2)}) collective-permute-start(bf16[1024,512]{1,0:T(8,128)(2,1)} %get-tuple-element.69), channel_id=1, source_target_pairs={{0,4},{4,0},{1,5},{5,1},{2,6},{6,2},{3,7},{7,3},{8,12},{12,8},{9,1... | collective-permute-start | bytes 3145736 | tf_op jit(solution)/shard_map/ppermute | solution.py:367
  434.9 2.0 copy-start.6
  434.9 2.6 copy-start.15
  436.2 15.5 %collective-permute-start.9 = (bf16[1024,512]{1,0:T(8,128)(2,1)}, bf16[1024,512]{1,0:T(8,128)(2,1)}, u32[]{:S(2)}, u32[]{:S(2)}) collective-permute-start(bf16[1024,512]{1,0:T(8,128)(2,1)} %get-tuple-element.63), channel_id=1, source_target_pairs={{0,4},{4,0},{1,5},{5,1},{2,6},{6,2},{3,7},{7,3},{8,12},{12,8},{9,1... | collective-permute-start | bytes 3145736 | tf_op jit(solution)/shard_map/ppermute | solution.py:367
  451.5 120.2 %collective-permute-start.14 = (bf16[4,4,256,128]{3,2,1,0:T(8,128)(2,1)}, bf16[4,4,256,128]{3,2,1,0:T(8,128)(2,1)}, u32[]{:S(2)}, u32[]{:S(2)}) collective-permute-start(bf16[4,4,256,128]{3,2,1,0:T(8,128)(2,1)} %bitcast.135), channel_id=1, source_target_pairs={{0,4},{4,0},{1,5},{5,1},{2,6},{6,2},{3,7},{7,3},{8,12},{12,8},{9,1... | collective-permute-start | bytes 3145736 | tf_op jit(solution)/shard_map/ppermute | solution.py:367
  548.5 2.2 copy-start.7
  550.4 1.7 copy-start.1
  552.3 2.7 copy-start.8
  574.9 131.3 %reduce-scatter.25.cloned.1.call-start = ((), (), s32[]{:S(2)}) async-start(), calls=%async_computation.16 | async-start | bytes 3932160
  577.4 3.5 collective-permute-start.13
  582.8 1.6 copy-start.14
  582.8 138.6 %reduce-scatter.29.cloned.1.call-start = ((), (), s32[]{:S(2)}) async-start(), calls=%async_computation.18 | async-start | bytes 5242880
  627.1 7.4 collective-permute-start.15
  638.8 1.6 copy-start.16
  638.8 123.6 %reduce-scatter.31.cloned.1.call-start = ((), (), s32[]{:S(2)}) async-start(), calls=%async_computation.19 | async-start | bytes 5242880
  695.0 7.3 collective-permute-start.16
  705.4 2.0 copy-start.4
  705.4 176.8 %reduce-scatter.19.cloned.1.call-start = ((), (), s32[]{:S(2)}) async-start(), calls=%async_computation.9 | async-start | bytes 327680 | tf_op jit(solution)/shard_map/reduce_scatter | solution.py:475
  706.2 180.0 %reduce-scatter.17.cloned.1.call-start = ((), (), s32[]{:S(2)}) async-start(), calls=%async_computation.8 | async-start | bytes 983040 | tf_op jit(solution)/shard_map/reduce_scatter | solution.py:475
  706.8 181.1 %reduce-scatter.21.cloned.1.call-start = ((), (), s32[]{:S(2)}) async-start(), calls=%async_computation.10 | async-start | bytes 1310720 | tf_op jit(solution)/shard_map/reduce_scatter | solution.py:475
  716.1 3.3 copy-start.2
  721.0 13.6 %collective-permute-start.10 = (bf16[1024,1024]{1,0:T(8,128)(2,1)}, bf16[1024,1024]{1,0:T(8,128)(2,1)}, u32[]{:S(2)}, u32[]{:S(2)}) collective-permute-start(bf16[1024,1024]{1,0:T(8,128)(2,1)} %dynamic-slice_convert_fusion), channel_id=1, source_target_pairs={{0,4},{4,0},{1,5},{5,1},{2,6},{6,2},{3,7},{7,3},{8,12},{12,8},{9,1... | collective-permute-start | bytes 6291464 | tf_op jit(solution)/shard_map/ppermute | solution.py:367
  721.4 168.3 %reduce-scatter.23.cloned.1.call-start = ((), (), s32[]{:S(2)}) async-start(), calls=%async_computation.11 | async-start | bytes 1310720 | tf_op jit(solution)/shard_map/reduce_scatter | solution.py:475
  724.5 9.7 %copy-start = (bf16[2048,512]{1,0:T(8,128)(2,1)S(1)}, bf16[2048,512]{1,0:T(8,128)(2,1)}, u32[]{:S(2)}) copy-start(bf16[2048,512]{1,0:T(8,128)(2,1)} %get-tuple-element.41) | copy-start | bytes 6291460
  727.5 150.8 %collective-permute-start.8 = (bf16[512,1024]{1,0:T(8,128)(2,1)}, bf16[512,1024]{1,0:T(8,128)(2,1)}, u32[]{:S(2)}, u32[]{:S(2)}) collective-permute-start(bf16[512,1024]{1,0:T(8,128)(2,1)} %get-tuple-element.65), channel_id=1, source_target_pairs={{1,0},{0,1},{5,2},{4,3},{3,4},{2,5},{7,6},{6,7},{9,8},{8,9},{13,10... | collective-permute-start | bytes 3145736 | tf_op jit(solution)/shard_map/ppermute | solution.py:411
  729.3 149.1 %collective-permute-start.7 = (bf16[512,1024]{1,0:T(8,128)(2,1)S(1)}, bf16[512,1024]{1,0:T(8,128)(2,1)}, u32[]{:S(2)}, u32[]{:S(2)}) collective-permute-start(bf16[512,1024]{1,0:T(8,128)(2,1)S(1)} %get-tuple-element.64), channel_id=1, source_target_pairs={{0,0},{1,1},{4,2},{5,3},{2,4},{3,5},{6,6},{7,7},{8,8},{9,9},{12,10... | collective-permute-start | bytes 3145736 | tf_op jit(solution)/shard_map/ppermute | solution.py:410
  732.2 2.9 copy-start.3
  763.9 119.9 %collective-permute-start.12 = (bf16[512,1024]{1,0:T(8,128)(2,1)}, bf16[512,1024]{1,0:T(8,128)(2,1)S(1)}, u32[]{:S(2)}, u32[]{:S(2)}) collective-permute-start(bf16[512,1024]{1,0:T(8,128)(2,1)} %get-tuple-element.61), channel_id=1, source_target_pairs={{1,0},{0,1},{5,2},{4,3},{3,4},{2,5},{7,6},{6,7},{9,8},{8,9},{13,10... | collective-permute-start | bytes 3145736 | tf_op jit(solution)/shard_map/ppermute | solution.py:411
  765.4 118.4 %collective-permute-start.11 = (bf16[512,1024]{1,0:T(8,128)(2,1)}, bf16[512,1024]{1,0:T(8,128)(2,1)S(1)}, u32[]{:S(2)}, u32[]{:S(2)}) collective-permute-start(bf16[512,1024]{1,0:T(8,128)(2,1)} %get-tuple-element.60), channel_id=1, source_target_pairs={{0,0},{1,1},{4,2},{5,3},{2,4},{3,5},{6,6},{7,7},{8,8},{9,9},{12,10... | collective-permute-start | bytes 3145736 | tf_op jit(solution)/shard_map/ppermute | solution.py:410
Sparse Core Ops, SparseCore 0:
  10.9 87.2 all-gather.10
  101.0 67.6 all-gather.12
  171.6 75.9 all-gather.14
  250.4 75.6 all-gather.16
  575.0 28.7 reduce-scatter.26
  606.7 43.8 reduce-scatter.24
  654.1 52.5 reduce-scatter.28
  709.7 52.5 reduce-scatter.30
  764.6 28.2 reduce-scatter.18
  795.0 27.0 reduce-scatter.16
  824.4 30.9 reduce-scatter.20
  857.5 26.1 reduce-scatter.22

commit v2 on v1

--- a/solution.py
+++ b/solution.py
@@ -363,6 +363,201 @@
     )
 
 
+def split_columns(acc, keep_ref, send_ref):
+    n_p, c = keep_ref.shape[0], keep_ref.shape[3]
+    for bit in (0, 1):
+
+        @pl.when(lax.axis_index("core") == bit)
+        def _():
+            for p in range(n_p):
+                at, to = (2 * p + bit) * c, (2 * p + 1 - bit) * c
+                keep_ref[p, 0] = acc[:, at : at + c]
+                send_ref[p, 0] = acc[:, to : to + c]
+
+
+def split_rows(acc, place, keep_ref, send_ref):
+    n_p, r = keep_ref.shape[0], keep_ref.shape[-2]
+    for bit in (0, 1):
+
+        @pl.when(lax.axis_index("core") == bit)
+        def _():
+            for p in range(n_p):
+                at, to = (2 * p + bit) * r, (2 * p + 1 - bit) * r
+                for cb in range(acc.shape[1] // 128):
+                    keep_ref[(p, 0) + place + (cb,)] = acc[at : at + r, cb * 128 : cb * 128 + 128]
+                    send_ref[(p, 0) + place + (cb,)] = acc[to : to + r, cb * 128 : cb * 128 + 128]
+
+
+def col_grad_kernel(a_ref, b_ref, keep_ref, send_ref, acc):
+    acc[...] = dot(a_ref[...], b_ref[...], TN).astype(BF16)
+    split_columns(acc, keep_ref, send_ref)
+
+
+def row_grad_kernel(a_ref, b_ref, keep_ref, send_ref, turned, acc):
+    @pl.when(pl.program_id(0) == 0)
+    def _():
+        turned[...] = a_ref[...].T
+
+    acc[...] = dot(turned[...], b_ref[...]).astype(BF16)
+    split_rows(acc, (), keep_ref, send_ref)
+
+
+def qkv_grad_kernel(x_ref, dq_ref, dk_ref, dv_ref, keep_ref, send_ref, sum_ref, turned, acc):
+    @pl.when(pl.program_id(0) == 0)
+    def _():
+        turned[...] = x_ref[...].T
+
+    for at, ref in enumerate((dq_ref, dk_ref, dv_ref)):
+        acc[...] = dot(turned[...], ref[...]).astype(BF16)
+        split_rows(acc, (at,), keep_ref, send_ref)
+    sum_ref[0:1, :] = col_sum(dq_ref[...].astype(F32))
+    sum_ref[1:2, :] = col_sum(dv_ref[...].astype(F32))
+
+
+def grad_call(kernel, grid, ins, outs, scratch, flops, *args):
+    return pl.pallas_call(
+        kernel,
+        grid=grid,
+        in_specs=ins,
+        out_specs=outs[0],
+        out_shape=outs[1],
+        scratch_shapes=scratch,
+        compiler_params=pltpu.CompilerParams(dimension_semantics=("arbitrary",) * len(grid)),
+        cost_estimate=pl.CostEstimate(flops=flops, bytes_accessed=flops // 512, transcendentals=0),
+    )(*args)
+
+
+def col_grad(a, b, n_p, n_t, block=512):
+    n, f = a.shape
+    d = b.shape[1]
+    per_t, c = f // n_t, d // (2 * n_p)
+    block = min(block, per_t)
+    steps = per_t // block
+    spec = pl.BlockSpec((n_p, 1, block, c), lambda i: (0, i // steps, i % steps, 0))
+    shape = sds((n_p, n_t, per_t, c))
+    return grad_call(
+        col_grad_kernel, (f // block,),
+        [pl.BlockSpec((n, block), lambda i: (0, i)), once((n, d))],
+        ([spec, spec], [shape, shape]), [pltpu.VMEM((block, d), BF16)], 2 * n * f * d, a, b,
+    )
+
+
+def row_grad(a, b, n_p, n_t, block=512):
+    n, d = a.shape
+    f = b.shape[1]
+    per_t, r = f // n_t, d // (2 * n_p)
+    steps = per_t // block
+    spec = pl.BlockSpec((n_p, 1, block // 128, r, 128), lambda i: (0, i // steps, i % steps, 0, 0))
+    shape = sds((n_p, n_t, per_t // 128, r, 128))
+    return grad_call(
+        row_grad_kernel, (f // block,),
+        [once((n, d)), pl.BlockSpec((n, block), lambda i: (0, i))],
+        ([spec, spec], [shape, shape]),
+        [pltpu.VMEM((d, n), BF16), pltpu.VMEM((d, block), BF16)], 2 * n * f * d, a, b,
+    )
+
+
+def qkv_grad(x, dq, dk, dv, n_p, n_t):
+    n, d = x.shape
+    f = dq.shape[1]
+    half, r = f // (n_t // 2), d // (2 * n_p)
+    spec = pl.BlockSpec((n_p, 1, 3, half // 128, r, 128), lambda i: (0, i, 0, 0, 0, 0))
+    shape = sds((n_p, n_t // 2, 3, half // 128, r, 128))
+    cols = pl.BlockSpec((n, half), lambda i: (0, i))
+    return grad_call(
+        qkv_grad_kernel, (n_t // 2,),
+        [once((n, d)), cols, cols, cols],
+        ([spec, spec, pl.BlockSpec((8, half), lambda i: (0, i))], [shape, shape, sds((8, f), F32)]),
+        [pltpu.VMEM((d, n), BF16), pltpu.VMEM((d, half), BF16)], 6 * n * f * d, x, dq, dk, dv,
+    )
+
+
+def input_pull_kernel(core_ref, dq_ref, dk_ref, dv_ref, w_ref, *refs):
+    f = dq_ref.shape[1]
+    total = dot(dq_ref[...], w_ref[:, :f], NT)
+    total = total + dot(dk_ref[...], w_ref[:, f : 2 * f], NT)
+    total = total + dot(dv_ref[...], w_ref[:, 2 * f :], NT)
+    if len(refs) == 2:
+        total = total + refs[0][...]
+    refs[-1][...] = total.astype(refs[-1].dtype)
+
+
+def input_pull(part, dq, dk, dv, w, dm=None, block=256):
+    n, f = dq.shape
+    d = w.shape[0]
+    steps = n // 2 // block
+    cols = pl.BlockSpec((block, f), lambda i, at: (at[0] * steps + i, 0))
+    own = pl.BlockSpec((block, d), lambda i, at: (i, 0))
+    extra = [] if dm is None else [dm]
+    return pl.pallas_call(
+        input_pull_kernel,
+        grid_spec=pltpu.PrefetchScalarGridSpec(
+            num_scalar_prefetch=1,
+            grid=(steps,),
+            in_specs=[cols, cols, cols, pl.BlockSpec(w.shape, lambda i, at: (0, 0), pipeline_mode=pl.Buffered(1))]
+            + [own] * len(extra),
+            out_specs=own,
+        ),
+        out_shape=sds((n // 2, d), BF16 if dm is None else F32),
+        compiler_params=pltpu.CompilerParams(dimension_semantics=("arbitrary",)),
+        cost_estimate=pl.CostEstimate(flops=3 * n * f * d, bytes_accessed=8 * n * d, transcendentals=0),
+    )(jnp.reshape(part, (1,)).astype(jnp.int32), dq, dk, dv, w, *extra)
+
+
+def small_sum_kernel(n_p, n_t, in_ref, out_ref, pair, pair_sum, plane, plane_sum, column, send_sems, recv_sems):
+    p, core, t = lax.axis_index("p"), lax.axis_index("core"), lax.axis_index("tensor")
+    peers = [{"core": 1 - core}] + [{"p": lax.rem(p + r, n_p)} for r in range(1, n_p)]
+    peers += [{"tensor": lax.rem(t + r, n_t)} for r in range(1, n_t)]
+    barrier = pltpu.get_barrier_semaphore()
+    for peer in peers:
+        pl.semaphore_signal(barrier, inc=1, device_id=peer, device_id_type=pl.DeviceIdType.MESH)
+    pl.semaphore_wait(barrier, len(peers))
+
+    def exchange(first, count, source, slots, at):
+        copies = []
+        for j in range(count):
+            copy = pltpu.make_async_remote_copy(
+                src_ref=source, dst_ref=slots.at[at], send_sem=send_sems.at[first + j], recv_sem=recv_sems.at[first + j],
+                device_id=peers[first + j], device_id_type=pl.DeviceIdType.MESH,
+            )
+            copy.start()
+            copies.append(copy)
+        for copy in copies:
+            copy.wait()
+
+    exchange(0, 1, in_ref, pair, 0)
+    pair_sum[...] = in_ref[...] + pair[0]
+    exchange(1, n_p - 1, pair_sum, plane, p)
+    plane[p] = pair_sum[...]
+    total = plane[0]
+    for j in range(1, n_p):
+        total = total + plane[j]
+    plane_sum[...] = total
+    exchange(n_p, n_t - 1, plane_sum, column, t)
+    column[t] = plane_sum[...]
+    total = column[0]
+    for j in range(1, n_t):
+        total = total + column[j]
+    out_ref[...] = total
+
+
+def small_sum(values, n_p, n_t):
+    rows_ = values.shape[0]
+    count = n_p + n_t - 1
+    return pl.pallas_call(
+        functools.partial(small_sum_kernel, n_p, n_t),
+        out_shape=sds(values.shape, F32),
+        in_specs=[pl.BlockSpec(memory_space=pltpu.VMEM)],
+        out_specs=pl.BlockSpec(memory_space=pltpu.VMEM),
+        scratch_shapes=[
+            pltpu.VMEM((1, rows_, 128), F32), pltpu.VMEM((rows_, 128), F32), pltpu.VMEM((n_p, rows_, 128), F32),
+            pltpu.VMEM((rows_, 128), F32), pltpu.VMEM((n_t, rows_, 128), F32),
+            pltpu.SemaphoreType.DMA((count,)), pltpu.SemaphoreType.DMA((count,)),
+        ],
+        compiler_params=pltpu.CompilerParams(collective_id=0, has_side_effects=True),
+    )(values)
+
+
 def swap_cores(value):
     return lax.ppermute(value, "core", [(0, 1), (1, 0)])
 
@@ -450,40 +645,60 @@
 
     du, up_sum = slope_pull(dz, w_down, slope)
     dm, da, sums_one = mix_pull(du, w_up, dr, normed, inverse, norm_gains)
-    g_down = dot(active, dz, TN).astype(BF16)
-    g_up = dot(hl, du, TN).astype(BF16)
-    g_out = dot(c_own, da, TN).astype(BF16)
+    down_keep, down_send = col_grad(active, dz, n_p, n_t)
+    down_recv = swap_cores(down_send)
+    up_keep, up_send = row_grad(hl, du, n_p, n_t)
+    up_recv = swap_cores(up_send)
+    out_keep, out_send = col_grad(c_own, da, n_p, n_t)
+    out_recv = swap_cores(out_send)
     dc = dot(da, w_out, NT).astype(BF16)
     mine = lax.dynamic_slice_in_dim(dc, core * own, own, 1)
     other = lax.dynamic_slice_in_dim(dc, (1 - core) * own, own, 1)
     dc_full = by_core(core, mine, swap_cores(other), 0)
+
+    def flat(values):
+        return values.reshape(-1, values.shape[-1])
+
+    def totals(axis, size, at, parts, dtype):
+        widths = sorted({part.shape[-1] for part in parts})
+        done = [None] * len(parts)
+        for lanes in widths:
+            index = [j for j, part in enumerate(parts) if part.shape[-1] == lanes]
+            pick = lambda to: jnp.concatenate(
+                [flat(lax.dynamic_index_in_dim(parts[j], to, 0, keepdims=False)) for j in index]
+            )
+            total = pick(at).astype(F32)
+            for r in range(1, size):
+                moved = lax.ppermute(pick((at + r) % size), axis, [(i, (i + r) % size) for i in range(size)])
+                total = total + moved.astype(F32)
+            total = total.astype(dtype)
+            first = 0
+            for j in index:
+                shape = parts[j].shape[1:]
+                count = math.prod(shape) // lanes
+                done[j] = total[first : first + count].reshape(shape)
+                first += count
+        return done
+
+    p_at = lax.axis_index("p")
+    plus = lambda a, b: (a.astype(F32) + b.astype(F32)).astype(BF16)
+    ffn_parts = [plus(down_keep, down_recv), plus(up_keep, up_recv), plus(out_keep, out_recv)]
+    *ffn_parts, dc_full = lax.optimization_barrier((*ffn_parts, dc_full))
+    ffn_parts = totals("p", n_p, p_at, ffn_parts, BF16)
+
     dq, dk, dv = attend_bwd(qkv, context, dc_full, lse, segment, valid, 256, 512)
-    dqkv = jnp.concatenate([dq, dk, dv], axis=1)
-    g_qkv = dot(x_full, dqkv, TN).astype(BF16)
-    qv_sum = jnp.stack([jnp.sum(dq.astype(F32), axis=0), jnp.sum(dv.astype(F32), axis=0)])
-    dx = dot(dqkv, w_qkv, NT)
-    mine = lax.dynamic_slice_in_dim(dx, core * rows, rows)
-    other = lax.dynamic_slice_in_dim(dx, (1 - core) * rows, rows).astype(BF16)
-    dx_own = mine + swap_cores(other).astype(F32) + dm
-    input_grad = give(dx_own.astype(BF16)).astype(F32)
-
-    def owner_sum(parts, join):
-        keep = lax.dynamic_index_in_dim(parts, core, 1, keepdims=False)
-        send = lax.dynamic_index_in_dim(parts, 1 - core, 1, keepdims=False)
-        both = join(keep, swap_cores(send))
-        some = lax.psum_scatter(both, "p", scatter_dimension=0, tiled=False)
-        return lax.psum_scatter(some, "tensor", scatter_dimension=0, tiled=False).astype(F32)
-
-    plus = lambda a, b: (a.astype(F32) + b.astype(F32)).astype(BF16)
-    beside = lambda a, b: by_core(core, a, b, 1)
-    down_total = owner_sum(g_down.reshape(n_t, -1, n_p, 2, down_weight.shape[1]).transpose(2, 3, 0, 1, 4), plus)
-    up_total = owner_sum(g_up.reshape(n_p, 2, -1, n_t, up_weight.shape[1]).transpose(0, 1, 3, 2, 4), plus)
-    out_total = owner_sum(g_out.reshape(n_t, -1, n_p, 2, out_weight.shape[1]).transpose(2, 3, 0, 1, 4), plus)
-    qkv_total = owner_sum(
-        g_qkv.reshape(n_p, 2, -1, 3, 2, qkv_weight.shape[2]).transpose(0, 1, 4, 3, 2, 5), beside
-    )
-
-    qv_pad = lax.dynamic_update_slice(jnp.zeros((2, width), F32), qv_sum, (0, core * own))
+    dx_other = swap_cores(input_pull(1 - core, dq, dk, dv, w_qkv))
+    qkv_keep, qkv_send, qv_sum = qkv_grad(x_full, dq, dk, dv, n_p, n_t)
+    qkv_recv = swap_cores(qkv_send)
+    dx_mine = input_pull(core, dq, dk, dv, w_qkv, dm)
+    input_grad = give((dx_mine + dx_other.astype(F32)).astype(BF16)).astype(F32)
+    qkv_parts = totals("p", n_p, p_at, [by_core(core, qkv_keep, qkv_recv, 1)], BF16)
+    down_total, up_total, out_total = totals("tensor", n_t, tensor, ffn_parts, F32)
+    (qkv_total,) = totals("tensor", n_t, tensor, qkv_parts, F32)
+    up_total = up_total.transpose(1, 0, 2).reshape(up_weight.shape)
+    qkv_total = qkv_total.transpose(0, 2, 1, 3).reshape(qkv_weight.shape)
+
+    qv_pad = lax.dynamic_update_slice(jnp.zeros((2, width), F32), qv_sum[0:2], (0, core * own))
     small = jnp.concatenate(
         [
             jnp.stack([sums_one[0], sums_two[0], sums_one[1], sums_one[2], sums_two[1], sums_two[2]]).reshape(-1),
@@ -491,7 +706,7 @@
             up_sum[0],
         ]
     )
-    small = lax.psum(small, ALL)
+    small = small_sum(small.reshape(-1, 128), n_p, n_t).reshape(-1)
     gain_sum = small[: 2 * width].reshape(2, width)
     bias_sum = small[2 * width : 6 * width].reshape(4, width)
     qv_total = lax.dynamic_slice_in_dim(small[6 * width : 8 * width].reshape(2, width), tensor * qv_bias.shape[1], qv_bias.shape[1], 1)

time: 905 us -> 859 us (0.949)
  the two profiles are of different devices: /device:TPU:0 before, /device:TPU:3 now
where the time goes in v2:
time: 859 us; the launch traced here: 852 us
  Pallas kernels  324 us (38%)
  waiting for transfers between devices  159 us (19%)
  other arithmetic  106 us (12%)
  local copies, waits for them, and re-layouts  92.3 us (11%)
  starting transfers between devices  87.1 us (10%)
  blocking collectives  53.3 us (6%)
  matrix products  15.9 us (2%)
  between operations  14.6 us (2%)
    pallas_call x5, Pallas kernels, call(): pl.pallas_call(kernel, grid=grid, in_specs=ins, out_specs=outs[0], out_sh...  92 us
    pallas_call x1, Pallas kernels, attend_bwd(): pl.pallas_call(functools.partial(attend_bwd_kernel, bq), grid_spec=pltpu....  65.8 us
    pallas_call x4, Pallas kernels, grad_call(): pl.pallas_call(kernel, grid=grid, in_specs=ins, out_specs=outs[0], out_sh...  56.3 us
    pallas_call x1, Pallas kernels, attend_fwd(): pl.pallas_call(functools.partial(attend_fwd_kernel, bk), grid_spec=pltpu....  53.9 us
    all_gather x1, blocking collectives, body(): lax.all_gather(jnp.concatenate([qv_bias.reshape(-1), up_bias]), 'tensor')  53.3 us
    ppermute x12, starting transfers between devices, totals(): lax.ppermute(pick((at + r) % size), axis, [(i, (i + r) % size) for i in r...  47.8 us
    all_gather x4, waiting for transfers between devices, gathered(): got = lax.all_gather(weight, ALL, axis=0, tiled=False)  43.7 us
    concatenate x6, other arithmetic, totals(): jnp.concatenate([flat(lax.dynamic_index_in_dim(parts[j], to, 0, keepdims=...  43.6 us
  transfers between devices with their start and end apart: 33, of which 8 were waited for; matrix products, arithmetic and copies ran while one was open for 22% of the time, Pallas kernels for 31%

profile of v2, /device:TPU:3, one launch (start us, length us, event | category | flops | bytes accessed | tf_op | source)
XLA Modules:
  0.0 852.1 jit_solution(1324032079185823139)
XLA Ops:
  11.7 3.9 collective-permute-start.1
  15.7 1.9 collective-permute-start
  17.6 26.6 %collective-permute-done.1 = bf16[512,1024]{1,0:T(8,128)(2,1)S(1)} collective-permute-done((bf16[512,1024]{1,0:T(8,128)(2,1)S(1)}, bf16[512,1024]{1,0:T(8,128)(2,1)S(1)}, u32[]{:S(2)}, u32[]{:S(2)}) %collective-permute-start.1) | collective-permute-done | bytes 1048608 | tf_op jit(solution)/shard_map/ppermute | solution.py:601
  44.2 29.4 %collective-permute-done = bf16[512,1024]{1,0:T(8,128)(2,1)} collective-permute-done((bf16[512,1024]{1,0:T(8,128)(2,1)S(1)}, bf16[512,1024]{1,0:T(8,128)(2,1)}, u32[]{:S(2)}, u32[]{:S(2)}) %collective-permute-start) | collective-permute-done | bytes 1048608 | tf_op jit(solution)/shard_map/ppermute | solution.py:600
  73.7 2.6 maximum_select_fusion.2.x_ref
  77.0 3.1 dynamic-slice_bitcast_fusion.1
  80.1 6.6 collective-permute-start.6
  86.7 1.9 collective-permute-start.5
  88.7 53.3 %all-gather.5 = f32[4,1,1536]{2,1,0:T(1,128)S(1)} all-gather(f32[1,1,1536]{2,1,0:T(1,128)S(1)} %reshape.288), channel_id=3, replica_groups=mesh['p'=4,'core'=2,'tensor'=4] {'tensor'}, dimensions={0}, use_global_device_ids=true | all-gather | bytes 30720 | tf_op jit(solution)/shard_map/all_gather | solution.py:619
  144.6 4.8 maximum_select_fusion.x_ref
  149.4 2.1 constant_dynamic-slice_fusion.34
  151.5 4.8 copy.82
  156.3 6.8 reshape.227.w_ref
  163.1 12.0 %add_convert_fusion.q_ref.k_ref.v_ref = bf16[2048,1536]{1,0:T(8,128)(2,1)} fusion(bf16[2048,1024]{1,0:T(8,128)(2,1)} %maximum_select_fusion.x_ref, bf16[1024,1536]{1,0:T(8,128)(2,1)S(1)} %reshape.227.w_ref, f32[1536]{0:T(1024)S(1)} %pad_maximum_fusion.8), kind=kOutput, calls=%fused_computation | convolution fusion | flops 6448742400 | bytes 13637632 | tf_op jit(solution)/shard_map/dot_general | solution.py:635
  176.4 53.9 %shard_map.195 = (bf16[2048,512]{1,0:T(8,128)(2,1)}, f32[32,2048]{1,0:T(8,128)}) custom-call(s32[4]{0:T(128)} %get-tuple-element.170.lo_ref, s32[4]{0:T(128)} %get-tuple-element.167.hi_ref, s32[4]{0:T(128)} %reduce_sum.29.pad_ref, bf16[2048,1536]{1,0:T(8,128)(2,1)} %add_convert_fusion.q_ref.k_ref.v_ref, ...), custom_call_target="tpu_custom_call" | custom-call | flops 8589934592 | bytes 25165824 | tf_op jit(solution)/shard_map/pallas_call | solution.py:152
  230.3 2.7 constant_dynamic-slice_fusion.33
  234.8 4.8 maximum_select_fusion.4.e_ref
  239.6 3.0 copy.57
  242.6 2.0 copy.83
  244.6 3.7 maximum_select_fusion.3.c_ref.a_ref
  248.3 8.2 shard_map.196
  256.4 12.6 %copy.58 = bf16[8,4,128,1024]{3,1,2,0:T(4,128)(2,1)} copy(bf16[8,4,128,1024]{3,2,1,0:T(8,128)(2,1)} %bitcast.131) | data formatting | bytes 16777216 | tf_op jit(solution)/shard_map/reshape | solution.py:611
  269.0 12.2 %copy.70 = bf16[128,8,4,1024]{3,1,2,0:T(8,128)(2,1)} copy(bf16[128,8,4,1024]{3,2,1,0:T(4,128)(2,1)} %bitcast.128) | data formatting | bytes 16777216
  281.2 43.6 %all-gather.17.cloned.1.call-done = bf16[32768,128]{1,0:T(8,128)(2,1)} async-done(((bf16[1024,128]{1,0:T(8,128)(2,1)}), bf16[32768,128]{1,0:T(8,128)(2,1)}) %all-gather.17.cloned.1.call-update) | async-done | bytes 8388624 | tf_op jit(solution)/shard_map/all_gather | solution.py:610
  324.8 12.0 %copy.59 = bf16[8,4,1024,128]{3,0,2,1:T(8,128)(2,1)} copy(bf16[8,4,1024,128]{3,2,1,0:T(8,128)(2,1)} %bitcast.132) | data formatting | bytes 16777216 | tf_op jit(solution)/shard_map/reshape | solution.py:611
  336.8 9.0 %copy.81 = bf16[512,8,8,128]{3,1,2,0:T(8,128)(2,1)} copy(bf16[512,8,8,128]{3,2,1,0:T(8,128)(2,1)} %bitcast.129) | data formatting | bytes 16777216
  345.9 24.8 %shard_map.197 = (bf16[1024,4096]{1,0:T(8,128)(2,1)}, bf16[1024,4096]{1,0:T(8,128)(2,1)}) custom-call(bf16[1024,1024]{1,0:T(8,128)(2,1)} %get-tuple-element.43.h_ref.a_ref, bf16[1024,4096]{1,0:T(8,128)(2,1)} %bitcast.133, f32[1,4096]{1,0:T(1,128)} %bitcast.182), custom_call_target="tpu_custom_call" | custom-call | flops 8589934592 | bytes 25165824 | tf_op jit(solution)/shard_map/pallas_call | solution.py:279
  370.6 19.2 %shard_map.198 = (bf16[1024,1024]{1,0:T(8,128)(2,1)}, f32[1024,1024]{1,0:T(8,128)}, bf16[1024,1024]{1,0:T(8,128)(2,1)}, f32[8,1024]{1,0:T(8,128)}) custom-call(bf16[1024,4096]{1,0:T(8,128)(2,1)} %get-tuple-element.44.g_ref.a_ref, bf16[4096,1024]{1,0:T(8,128)(2,1)} %bitcast.135, f32[1024,1024]{1,0:T(8,128)} %get-tuple-element.45.n_ref, ...), custom_call_target="tpu_custom_call" | custom-call | flops 8589934592 | bytes 16777216 | tf_op jit(solution)/shard_map/pallas_call | solution.py:279
  389.9 15.2 %shard_map.199 = (bf16[4,4,1024,128]{3,2,1,0:T(8,128)(2,1)}, bf16[4,4,1024,128]{3,2,1,0:T(8,128)(2,1)}) custom-call(bf16[1024,4096]{1,0:T(8,128)(2,1)} %get-tuple-element.44.g_ref.a_ref, bf16[1024,1024]{1,0:T(8,128)(2,1)} %get-tuple-element.47.b_ref.dz_ref), custom_call_target="tpu_custom_call" | custom-call | flops 8589934592 | bytes 16777216 | tf_op jit(solution)/shard_map/pallas_call | solution.py:418
  405.3 22.0 %shard_map.200 = (bf16[1024,4096]{1,0:T(8,128)(2,1)}, f32[8,4096]{1,0:T(8,128)}) custom-call(bf16[1024,1024]{1,0:T(8,128)(2,1)} %get-tuple-element.47.b_ref.dz_ref, bf16[4096,1024]{1,0:T(8,128)(2,1)} %bitcast.136, bf16[1024,4096]{1,0:T(8,128)(2,1)} %get-tuple-element.50.slope_ref), custom_call_target="tpu_custom_call" | custom-call | flops 8589934592 | bytes 25165824 | tf_op jit(solution)/shard_map/pallas_call | solution.py:279
  427.3 15.7 %shard_map.201 = (bf16[4,4,8,128,128]{4,3,2,1,0:T(8,128)(2,1)}, bf16[4,4,8,128,128]{4,3,2,1,0:T(8,128)(2,1)}) custom-call(bf16[1024,1024]{1,0:T(8,128)(2,1)} %get-tuple-element.43.h_ref.a_ref, bf16[1024,4096]{1,0:T(8,128)(2,1)} %get-tuple-element.51.b_ref.du_ref), custom_call_target="tpu_custom_call" | custom-call | flops 8589934592 | bytes 16777216 | tf_op jit(solution)/shard_map/pallas_call | solution.py:418
  443.3 17.8 %shard_map.202 = (f32[1024,1024]{1,0:T(8,128)}, bf16[1024,1024]{1,0:T(8,128)(2,1)}, f32[8,1024]{1,0:T(8,128)}) custom-call(bf16[1024,4096]{1,0:T(8,128)(2,1)} %get-tuple-element.51.b_ref.du_ref, bf16[1024,4096]{1,0:T(8,128)(2,1)} %bitcast.134, f32[1024,1024]{1,0:T(8,128)} %get-tuple-element.54.dr_ref, f32[1024,1024]{1,0:T(8,128)} %get-tuple-element.45.n_ref, ...), custom_call_target="tpu_custom_call" | custom-call | flops 8589934592 | bytes 16777216 | tf_op jit(solution)/shard_map/pallas_call | solution.py:279
  461.1 4.0 convolution_convert_fusion
  466.5 6.5 shard_map.203
  477.9 1.9 collective-permute-start.8
  480.8 2.6 collective-permute-start.7
  483.4 3.6 maximum_select_fusion.6.dc_ref
  488.6 3.4 add_convert_fusion.2
  492.0 4.1 add_convert_fusion.1
  497.2 13.6 %pad_maximum_fusion.2 = bf16[9216,128]{1,0:T(8,128)(2,1)} fusion(bf16[1024,128]{1,0:T(8,128)(2,1)S(1)} %bitcast.161, bf16[4096,128]{1,0:T(8,128)(2,1)S(1)} %bitcast.145, bf16[4096,128]{1,0:T(8,128)(2,1)S(1)} %bitcast.146), kind=kLoop, calls=%fused_computation.11 | loop fusion | flops 7077888 | bytes 4718592 | tf_op jit(solution)/shard_map/concatenate | solution.py:667
  511.1 13.8 %pad_maximum_fusion.1 = bf16[9216,128]{1,0:T(8,128)(2,1)} fusion(bf16[1024,128]{1,0:T(8,128)(2,1)S(1)} %bitcast.160, bf16[4096,128]{1,0:T(8,128)(2,1)S(1)} %bitcast.143, bf16[4096,128]{1,0:T(8,128)(2,1)S(1)} %bitcast.144), kind=kLoop, calls=%fused_computation.10 | loop fusion | flops 7077888 | bytes 4718592 | tf_op jit(solution)/shard_map/concatenate | solution.py:667
  526.1 13.5 %pad_maximum_fusion = bf16[9216,128]{1,0:T(8,128)(2,1)} fusion(bf16[1024,128]{1,0:T(8,128)(2,1)S(1)} %bitcast.159, bf16[4096,128]{1,0:T(8,128)(2,1)S(1)} %bitcast.141, bf16[4096,128]{1,0:T(8,128)(2,1)S(1)} %bitcast.142), kind=kLoop, calls=%fused_computation.9 | loop fusion | flops 7077888 | bytes 4718592 | tf_op jit(solution)/shard_map/concatenate | solution.py:667
  542.3 65.8 %shard_map.204 = (bf16[2048,512]{1,0:T(8,128)(2,1)}, bf16[2048,512]{1,0:T(8,128)(2,1)}, bf16[2048,512]{1,0:T(8,128)(2,1)}) custom-call(s32[4]{0:T(128)} %get-tuple-element.171.lo_ref, s32[4]{0:T(128)} %get-tuple-element.166.hi_ref, s32[4]{0:T(128)} %reduce_sum.29.pad_ref, bf16[2048,1536]{1,0:T(8,128)(2,1)} %add_convert_fusion.q_ref.k_ref.v_ref, ...), custom_call_target="tpu_custom_call" | custom-call | flops 21474836480 | bytes 50331648 | tf_op jit(solution)/shard_map/pallas_call | solution.py:186
  608.1 18.8 %shard_map.207 = (bf16[4,2,3,2,128,128]{5,4,3,2,1,0:T(8,128)(2,1)}, bf16[4,2,3,2,128,128]{5,4,3,2,1,0:T(8,128)(2,1)}, f32[8,512]{1,0:T(8,128)}) custom-call(bf16[2048,1024]{1,0:T(8,128)(2,1)} %maximum_select_fusion.x_ref, bf16[2048,512]{1,0:T(8,128)(2,1)} %get-tuple-element.61.dq_ref, bf16[2048,512]{1,0:T(8,128)(2,1)} %get-tuple-element.62.dk_ref, ...), custom_call_target="tpu_custom_call" | custom-call | flops 6442450944 | bytes 12582912 | tf_op jit(solution)/shard_map/pallas_call | solution.py:418
  627.0 7.2 collective-permute-start.16
  634.2 3.2 maximum_select_fusion.5
  637.4 7.4 shard_map.206
  646.2 40.2 %shard_map.208 = f32[96,128]{1,0:T(8,128)} custom-call(f32[96,128]{1,0:T(8,128)} %maximum_bitcast_fusion.in_ref), custom_call_target="tpu_custom_call" | custom-call | tf_op jit(solution)/shard_map/pallas_call | solution.py:547
  690.3 8.6 %shard_map.205 = f32[1024,1024]{1,0:T(8,128)} custom-call(s32[1]{0:T(128)} %bitcast.22.core_ref, bf16[2048,512]{1,0:T(8,128)(2,1)} %get-tuple-element.61.dq_ref, bf16[2048,512]{1,0:T(8,128)(2,1)} %get-tuple-element.62.dk_ref, bf16[2048,512]{1,0:T(8,128)(2,1)} %get-tuple-element.63.dv_ref, bf16[1024,1536]{1,0:T(8,128)(2,1)} %copy-done.1, ...), custom_call_target="tpu_custom_call" | custom-call | flops 3221225472 | bytes 16777216 | tf_op jit(solution)/shard_map/pallas_call | solution.py:492
  698.9 3.2 maximum_select_fusion.1
  702.7 2.0 collective-permute-start.18
  704.7 2.3 collective-permute-start.17
  707.0 14.7 %add_convert_fusion.3 = bf16[9216,128]{1,0:T(8,128)(2,1)S(1)} fusion(bf16[9216,128]{1,0:T(8,128)(2,1)} %collective-permute-done.25, bf16[9216,128]{1,0:T(8,128)(2,1)} %collective-permute-done.24, bf16[9216,128]{1,0:T(8,128)(2,1)} %collective-permute-done.23, bf16[1024,128]{1,0:T(8,128)(2,1)S(1)} %bitcast.157, bf16[4096,128]{1,0:T(8,128)(2,1)S(1)} %bitcast.139, ...), kind=kLoop, calls=%fused_computation.4 | loop fusion | flops 15335424 | bytes 11796480 | tf_op jit(solution)/shard_map/convert_element_type | solution.py:674
  723.0 2.5 collective-permute-start.28
  726.4 13.1 %collective-permute-done.18 = bf16[3072,128]{1,0:T(8,128)(2,1)S(1)} collective-permute-done((bf16[3072,128]{1,0:T(8,128)(2,1)S(1)}, bf16[3072,128]{1,0:T(8,128)(2,1)S(1)}, u32[]{:S(2)}, u32[]{:S(2)}) %collective-permute-start.18) | collective-permute-done | bytes 786464 | tf_op jit(solution)/shard_map/ppermute | solution.py:672
  740.0 2.5 collective-permute-start.22
  744.5 7.9 collective-permute-done.22
  752.4 34.2 %collective-permute-start.20 = (bf16[768,128]{1,0:T(8,128)(2,1)S(1)}, bf16[768,128]{1,0:T(8,128)(2,1)S(1)}, u32[]{:S(2)}, u32[]{:S(2)}) collective-permute-start(bf16[768,128]{1,0:T(8,128)(2,1)S(1)} %bitcast.170), channel_id=1, source_target_pairs={{0,1},{1,2},{2,3},{3,0},{4,5},{5,6},{6,7},{7,4},{8,9},{9,10},{10,1... | collective-permute-start | bytes 589832 | tf_op jit(solution)/shard_map/ppermute | solution.py:672
  786.6 2.5 add_convert_fusion.4
  790.5 3.3 collective-permute-start.15
  793.8 7.1 collective-permute-start.14
  806.2 10.8 %collective-permute-done.15 = bf16[512,1024]{1,0:T(8,128)(2,1)} collective-permute-done((bf16[512,1024]{1,0:T(8,128)(2,1)S(1)}, bf16[512,1024]{1,0:T(8,128)(2,1)}, u32[]{:S(2)}, u32[]{:S(2)}) %collective-permute-start.15) | collective-permute-done | bytes 1048608 | tf_op jit(solution)/shard_map/ppermute | solution.py:606
  817.0 23.6 %collective-permute-done.14 = bf16[512,1024]{1,0:T(8,128)(2,1)} collective-permute-done((bf16[512,1024]{1,0:T(8,128)(2,1)S(1)}, bf16[512,1024]{1,0:T(8,128)(2,1)}, u32[]{:S(2)}, u32[]{:S(2)}) %collective-permute-start.14) | collective-permute-done | bytes 1048608 | tf_op jit(solution)/shard_map/ppermute | solution.py:605
  840.6 4.7 fusion
  (143 shorter events, 42.6 us)
Async XLA Ops:
  7.2 142.2 %all-gather.11.cloned.1.call-start = ((), (), s32[]{:S(2)}) async-start(), calls=%async_computation | async-start | bytes 6488064 | tf_op jit(solution)/shard_map/all_gather | solution.py:610
  7.9 231.7 %all-gather.13.cloned.1.call-start = ((), (), s32[]{:S(2)}) async-start(), calls=%async_computation.1 | async-start | bytes 2162688 | tf_op jit(solution)/shard_map/all_gather | solution.py:610
  8.7 247.8 %all-gather.15.cloned.1.call-start = ((), (), s32[]{:S(2)}) async-start(), calls=%async_computation.2 | async-start | bytes 8650752 | tf_op jit(solution)/shard_map/all_gather | solution.py:610
  9.4 315.4 %all-gather.17.cloned.1.call-start = ((), (), s32[]{:S(2)}) async-start(), calls=%async_computation.3 | async-start | bytes 8650752 | tf_op jit(solution)/shard_map/all_gather | solution.py:610
  11.7 64.7 %copy-start.8 = (s32[2,1,2048]{2,1,0:T(1,128)S(1)}, s32[2,1,2048]{2,1,0:T(1,128)}, u32[]{:S(2)}) copy-start(s32[2,1,2048]{2,1,0:T(1,128)} %param.13) | copy-start | bytes 49156
  11.7 64.7 %copy-start.9 = (s32[2,1,2048]{2,1,0:T(1,128)S(1)}, s32[2,1,2048]{2,1,0:T(1,128)}, u32[]{:S(2)}) copy-start(s32[2,1,2048]{2,1,0:T(1,128)} %param.14) | copy-start | bytes 49156
  11.7 32.5 %collective-permute-start.1 = (bf16[512,1024]{1,0:T(8,128)(2,1)S(1)}, bf16[512,1024]{1,0:T(8,128)(2,1)S(1)}, u32[]{:S(2)}, u32[]{:S(2)}) collective-permute-start(bf16[512,1024]{1,0:T(8,128)(2,1)S(1)} %get-tuple-element.133), channel_id=1, source_target_pairs={{0,1},{1,0},{2,5},{3,4},{4,3},{5,2},{6,7},{7,6},{8,9},{9,8},{10,13... | collective-permute-start | bytes 3145736 | tf_op jit(solution)/shard_map/ppermute | solution.py:601
  15.7 58.0 %collective-permute-start = (bf16[512,1024]{1,0:T(8,128)(2,1)S(1)}, bf16[512,1024]{1,0:T(8,128)(2,1)}, u32[]{:S(2)}, u32[]{:S(2)}) collective-permute-start(bf16[512,1024]{1,0:T(8,128)(2,1)S(1)} %get-tuple-element.132), channel_id=1, source_target_pairs={{0,0},{1,1},{2,4},{3,5},{4,2},{5,3},{6,6},{7,7},{8,8},{9,9},{10,12... | collective-permute-start | bytes 3145736 | tf_op jit(solution)/shard_map/ppermute | solution.py:600
  76.3 73.1 %copy-start.2 = (bf16[1024,1024]{1,0:T(8,128)(2,1)}, bf16[1024,1024]{1,0:T(8,128)(2,1)S(1)}, u32[]{:S(2)}) copy-start(bf16[1024,1024]{1,0:T(8,128)(2,1)S(1)} %maximum_select_fusion.2.x_ref) | copy-start | bytes 6291460
  76.3 12.3 %copy-start.11 = (f32[2,256]{1,0:T(2,128)S(1)}, f32[2,256]{1,0:T(2,128)}, u32[]{:S(2)}) copy-start(f32[2,256]{1,0:T(2,128)} %param.16) | copy-start | bytes 6148
  76.3 12.3 %copy-start.10 = (f32[1024]{0:T(1024)S(1)}, f32[1024]{0:T(1024)}, u32[]{:S(2)}) copy-start(f32[1024]{0:T(1024)} %param.21) | copy-start | bytes 12292
  76.3 68.3 %collective-permute-start.3 = (bf16[1024,1024]{1,0:T(8,128)(2,1)S(1)}, bf16[1024,1024]{1,0:T(8,128)(2,1)}, u32[]{:S(2)}, u32[]{:S(2)}) collective-permute-start(bf16[1024,1024]{1,0:T(8,128)(2,1)S(1)} %maximum_select_fusion.2.x_ref), channel_id=1, source_target_pairs={{0,4},{4,0},{1,5},{5,1},{2,6},{6,2},{3,7},{7,3},{8,12},{12,8},{9,1... | collective-permute-start | bytes 6291464 | tf_op jit(solution)/shard_map/ppermute | solution.py:562
  76.5 65.7 %collective-permute-start.2 = (s32[2,2048]{1,0:T(2,128)S(1)}, s32[2,2048]{1,0:T(2,128)S(1)}, u32[]{:S(2)}, u32[]{:S(2)}) collective-permute-start(s32[2,2048]{1,0:T(2,128)S(1)} %fusion.7), channel_id=1, source_target_pairs={{0,4},{4,0},{1,5},{5,1},{2,6},{6,2},{3,7},{7,3},{8,12},{12,8},{9,1... | collective-permute-start | bytes 49160 | tf_op jit(solution)/shard_map/ppermute | solution.py:562
  80.1 154.7 %collective-permute-start.6 = (bf16[512,1024]{1,0:T(8,128)(2,1)}, bf16[512,1024]{1,0:T(8,128)(2,1)}, u32[]{:S(2)}, u32[]{:S(2)}) collective-permute-start(bf16[512,1024]{1,0:T(8,128)(2,1)} %get-tuple-element.129), channel_id=1, source_target_pairs={{0,1},{1,0},{2,5},{3,4},{4,3},{5,2},{6,7},{7,6},{8,9},{9,8},{10,13... | collective-permute-start | bytes 3145736 | tf_op jit(solution)/shard_map/ppermute | solution.py:601
  86.7 148.1 %collective-permute-start.5 = (bf16[512,1024]{1,0:T(8,128)(2,1)}, bf16[512,1024]{1,0:T(8,128)(2,1)}, u32[]{:S(2)}, u32[]{:S(2)}) collective-permute-start(bf16[512,1024]{1,0:T(8,128)(2,1)} %get-tuple-element.128), channel_id=1, source_target_pairs={{0,0},{1,1},{2,4},{3,5},{4,2},{5,3},{6,6},{7,7},{8,8},{9,9},{10,12... | collective-permute-start | bytes 3145736 | tf_op jit(solution)/shard_map/ppermute | solution.py:600
  142.8 330.5 %copy-start.7 = (s32[1,2048]{1,0:T(1,128)}, s32[1,2048]{1,0:T(1,128)S(1)}, u32[]{:S(2)}) copy-start(s32[1,2048]{1,0:T(1,128)S(1)} %get-tuple-element.161.qcode_ref) | copy-start | bytes 24580
  163.1 12.0 %copy-start.1 = (bf16[1024,1536]{1,0:T(8,128)(2,1)}, bf16[1024,1536]{1,0:T(8,128)(2,1)S(1)}, u32[]{:S(2)}) copy-start(bf16[1024,1536]{1,0:T(8,128)(2,1)S(1)} %reshape.227.w_ref) | copy-start | bytes 9437188
  233.0 11.6 %collective-permute-start.4 = (bf16[1024,512]{1,0:T(8,128)(2,1)}, bf16[1024,512]{1,0:T(8,128)(2,1)}, u32[]{:S(2)}, u32[]{:S(2)}) collective-permute-start(bf16[1024,512]{1,0:T(8,128)(2,1)} %get-tuple-element.131), channel_id=1, source_target_pairs={{0,4},{4,0},{1,5},{5,1},{2,6},{6,2},{3,7},{7,3},{8,12},{12,8},{9,1... | collective-permute-start | bytes 3145736 | tf_op jit(solution)/shard_map/ppermute | solution.py:562
  405.1 83.4 %collective-permute-start.9 = (bf16[4,4,1024,128]{3,2,1,0:T(8,128)(2,1)}, bf16[4,4,1024,128]{3,2,1,0:T(8,128)(2,1)}, u32[]{:S(2)}, u32[]{:S(2)}) collective-permute-start(bf16[4,4,1024,128]{3,2,1,0:T(8,128)(2,1)} %get-tuple-element.49), channel_id=1, source_target_pairs={{0,4},{4,0},{1,5},{5,1},{2,6},{6,2},{3,7},{7,3},{8,12},{12,8},{9,1... | collective-permute-start | bytes 12582920 | tf_op jit(solution)/shard_map/ppermute | solution.py:562
  443.0 49.0 %collective-permute-start.10 = (bf16[4,4,8,128,128]{4,3,2,1,0:T(8,128)(2,1)}, bf16[4,4,8,128,128]{4,3,2,1,0:T(8,128)(2,1)}, u32[]{:S(2)}, u32[]{:S(2)}) collective-permute-start(bf16[4,4,8,128,128]{4,3,2,1,0:T(8,128)(2,1)} %get-tuple-element.53), channel_id=1, source_target_pairs={{0,4},{4,0},{1,5},{5,1},{2,6},{6,2},{3,7},{7,3},{8,12},{12,8},{9,1... | collective-permute-start | bytes 12582920 | tf_op jit(solution)/shard_map/ppermute | solution.py:562
  466.3 10.1 %copy-start.5 = (bf16[1024,1024]{1,0:T(8,128)(2,1)S(1)}, bf16[1024,1024]{1,0:T(8,128)(2,1)}, u32[]{:S(2)}) copy-start(bf16[1024,1024]{1,0:T(8,128)(2,1)} %get-tuple-element.46) | copy-start | bytes 6291460
  466.3 14.5 %collective-permute-start.12 = (bf16[1024,512]{1,0:T(8,128)(2,1)}, bf16[1024,512]{1,0:T(8,128)(2,1)}, u32[]{:S(2)}, u32[]{:S(2)}) collective-permute-start(bf16[1024,512]{1,0:T(8,128)(2,1)} %get-tuple-element.125), channel_id=1, source_target_pairs={{0,4},{4,0},{1,5},{5,1},{2,6},{6,2},{3,7},{7,3},{8,12},{12,8},{9,1... | collective-permute-start | bytes 3145736 | tf_op jit(solution)/shard_map/ppermute | solution.py:562
  473.1 13.9 %collective-permute-start.11 = (bf16[4,4,256,128]{3,2,1,0:T(8,128)(2,1)}, bf16[4,4,256,128]{3,2,1,0:T(8,128)(2,1)}, u32[]{:S(2)}, u32[]{:S(2)}) collective-permute-start(bf16[4,4,256,128]{3,2,1,0:T(8,128)(2,1)} %get-tuple-element.58), channel_id=1, source_target_pairs={{0,4},{4,0},{1,5},{5,1},{2,6},{6,2},{3,7},{7,3},{8,12},{12,8},{9,1... | collective-permute-start | bytes 3145736 | tf_op jit(solution)/shard_map/ppermute | solution.py:562
  477.9 9.1 %copy-start.6 = (bf16[4,4,256,128]{3,2,1,0:T(8,128)(2,1)S(1)}, bf16[4,4,256,128]{3,2,1,0:T(8,128)(2,1)}, u32[]{:S(2)}) copy-start(bf16[4,4,256,128]{3,2,1,0:T(8,128)(2,1)} %get-tuple-element.57) | copy-start | bytes 3145732
  477.9 149.0 %collective-permute-start.8 = (bf16[512,1024]{1,0:T(8,128)(2,1)}, bf16[512,1024]{1,0:T(8,128)(2,1)S(1)}, u32[]{:S(2)}, u32[]{:S(2)}) collective-permute-start(bf16[512,1024]{1,0:T(8,128)(2,1)} %get-tuple-element.127), channel_id=1, source_target_pairs={{1,0},{0,1},{5,2},{4,3},{3,4},{2,5},{7,6},{6,7},{9,8},{8,9},{13,10... | collective-permute-start | bytes 3145736 | tf_op jit(solution)/shard_map/ppermute | solution.py:606
  480.8 153.3 %collective-permute-start.7 = (bf16[512,1024]{1,0:T(8,128)(2,1)}, bf16[512,1024]{1,0:T(8,128)(2,1)}, u32[]{:S(2)}, u32[]{:S(2)}) collective-permute-start(bf16[512,1024]{1,0:T(8,128)(2,1)} %get-tuple-element.126), channel_id=1, source_target_pairs={{0,0},{1,1},{4,2},{5,3},{2,4},{3,5},{6,6},{7,7},{8,8},{9,9},{12,10... | collective-permute-start | bytes 3145736 | tf_op jit(solution)/shard_map/ppermute | solution.py:605
  483.4 5.2 copy-start.3
  488.6 3.5 copy-start.4
  510.8 191.9 %collective-permute-start.25 = (bf16[9216,128]{1,0:T(8,128)(2,1)}, bf16[9216,128]{1,0:T(8,128)(2,1)}, u32[]{:S(2)}, u32[]{:S(2)}) collective-permute-start(bf16[9216,128]{1,0:T(8,128)(2,1)} %pad_maximum_fusion.2), channel_id=1, source_target_pairs={{0,24},{8,0},{16,8},{24,16},{1,25},{9,1},{17,9},{25,17},{2,26},{10... | collective-permute-start | bytes 7077896 | tf_op jit(solution)/shard_map/ppermute | solution.py:672
  524.9 179.8 %collective-permute-start.24 = (bf16[9216,128]{1,0:T(8,128)(2,1)}, bf16[9216,128]{1,0:T(8,128)(2,1)}, u32[]{:S(2)}, u32[]{:S(2)}) collective-permute-start(bf16[9216,128]{1,0:T(8,128)(2,1)} %pad_maximum_fusion.1), channel_id=1, source_target_pairs={{0,16},{8,24},{16,0},{24,8},{1,17},{9,25},{17,1},{25,9},{2,18},{10... | collective-permute-start | bytes 7077896 | tf_op jit(solution)/shard_map/ppermute | solution.py:672
  539.6 167.4 %collective-permute-start.23 = (bf16[9216,128]{1,0:T(8,128)(2,1)}, bf16[9216,128]{1,0:T(8,128)(2,1)}, u32[]{:S(2)}, u32[]{:S(2)}) collective-permute-start(bf16[9216,128]{1,0:T(8,128)(2,1)} %pad_maximum_fusion), channel_id=1, source_target_pairs={{0,8},{8,16},{16,24},{24,0},{1,9},{9,17},{17,25},{25,1},{2,10},{10... | collective-permute-start | bytes 7077896 | tf_op jit(solution)/shard_map/ppermute | solution.py:672
  627.0 71.9 %collective-permute-start.16 = (bf16[4,2,3,2,128,128]{5,4,3,2,1,0:T(8,128)(2,1)}, bf16[4,2,3,2,128,128]{5,4,3,2,1,0:T(8,128)(2,1)}, u32[]{:S(2)}, u32[]{:S(2)}) collective-permute-start(bf16[4,2,3,2,128,128]{5,4,3,2,1,0:T(8,128)(2,1)} %get-tuple-element.66), channel_id=1, source_target_pairs={{0,4},{4,0},{1,5},{5,1},{2,6},{6,2},{3,7},{7,3},{8,12},{12,8},{9,1... | collective-permute-start | bytes 4718600 | tf_op jit(solution)/shard_map/ppermute | solution.py:562
  644.8 98.6 %collective-permute-start.13 = (bf16[1024,1024]{1,0:T(8,128)(2,1)}, bf16[1024,1024]{1,0:T(8,128)(2,1)}, u32[]{:S(2)}, u32[]{:S(2)}) collective-permute-start(bf16[1024,1024]{1,0:T(8,128)(2,1)} %shard_map.206), channel_id=1, source_target_pairs={{0,4},{4,0},{1,5},{5,1},{2,6},{6,2},{3,7},{7,3},{8,12},{12,8},{9,1... | collective-permute-start | bytes 6291464 | tf_op jit(solution)/shard_map/ppermute | solution.py:562
  702.5 23.8 %collective-permute-start.19 = (bf16[3072,128]{1,0:T(8,128)(2,1)S(1)}, bf16[3072,128]{1,0:T(8,128)(2,1)S(1)}, u32[]{:S(2)}, u32[]{:S(2)}) collective-permute-start(bf16[3072,128]{1,0:T(8,128)(2,1)S(1)} %bitcast.168), channel_id=1, source_target_pairs={{0,24},{8,0},{16,8},{24,16},{1,25},{9,1},{17,9},{25,17},{2,26},{10... | collective-permute-start | bytes 2359304 | tf_op jit(solution)/shard_map/ppermute | solution.py:672
  702.7 36.8 %collective-permute-start.18 = (bf16[3072,128]{1,0:T(8,128)(2,1)S(1)}, bf16[3072,128]{1,0:T(8,128)(2,1)S(1)}, u32[]{:S(2)}, u32[]{:S(2)}) collective-permute-start(bf16[3072,128]{1,0:T(8,128)(2,1)S(1)} %bitcast.167), channel_id=1, source_target_pairs={{0,16},{8,24},{16,0},{24,8},{1,17},{9,25},{17,1},{25,9},{2,18},{10... | collective-permute-start | bytes 2359304 | tf_op jit(solution)/shard_map/ppermute | solution.py:672
  704.7 34.8 %collective-permute-start.17 = (bf16[3072,128]{1,0:T(8,128)(2,1)S(1)}, bf16[3072,128]{1,0:T(8,128)(2,1)S(1)}, u32[]{:S(2)}, u32[]{:S(2)}) collective-permute-start(bf16[3072,128]{1,0:T(8,128)(2,1)S(1)} %bitcast.166), channel_id=1, source_target_pairs={{0,8},{8,16},{16,24},{24,0},{1,9},{9,17},{17,25},{25,1},{2,10},{10... | collective-permute-start | bytes 2359304 | tf_op jit(solution)/shard_map/ppermute | solution.py:672
  723.0 79.2 %collective-permute-start.28 = (bf16[2304,128]{1,0:T(8,128)(2,1)}, bf16[2304,128]{1,0:T(8,128)(2,1)}, u32[]{:S(2)}, u32[]{:S(2)}) collective-permute-start(bf16[2304,128]{1,0:T(8,128)(2,1)} %pad_maximum_fusion.5), channel_id=1, source_target_pairs={{0,3},{1,0},{2,1},{3,2},{4,7},{5,4},{6,5},{7,6},{8,11},{9,8},{10,9... | collective-permute-start | bytes 1769480 | tf_op jit(solution)/shard_map/ppermute | solution.py:672
  726.3 75.8 %collective-permute-start.27 = (bf16[2304,128]{1,0:T(8,128)(2,1)}, bf16[2304,128]{1,0:T(8,128)(2,1)}, u32[]{:S(2)}, u32[]{:S(2)}) collective-permute-start(bf16[2304,128]{1,0:T(8,128)(2,1)} %pad_maximum_fusion.4), channel_id=1, source_target_pairs={{0,2},{1,3},{2,0},{3,1},{4,6},{5,7},{6,4},{7,5},{8,10},{9,11},{10,... | collective-permute-start | bytes 1769480 | tf_op jit(solution)/shard_map/ppermute | solution.py:672
  739.5 47.1 %copy-start = (f32[1024,1024]{1,0:T(8,128)S(1)}, f32[1024,1024]{1,0:T(8,128)}, u32[]{:S(2)}) copy-start(f32[1024,1024]{1,0:T(8,128)} %shard_map.205) | copy-start | bytes 12582916
  740.0 12.4 %collective-permute-start.22 = (bf16[768,128]{1,0:T(8,128)(2,1)S(1)}, bf16[768,128]{1,0:T(8,128)(2,1)S(1)}, u32[]{:S(2)}, u32[]{:S(2)}) collective-permute-start(bf16[768,128]{1,0:T(8,128)(2,1)S(1)} %bitcast.172), channel_id=1, source_target_pairs={{0,3},{1,0},{2,1},{3,2},{4,7},{5,4},{6,5},{7,6},{8,11},{9,8},{10,9... | collective-permute-start | bytes 589832 | tf_op jit(solution)/shard_map/ppermute | solution.py:672
  743.4 58.8 %collective-permute-start.26 = (bf16[2304,128]{1,0:T(8,128)(2,1)}, bf16[2304,128]{1,0:T(8,128)(2,1)}, u32[]{:S(2)}, u32[]{:S(2)}) collective-permute-start(bf16[2304,128]{1,0:T(8,128)(2,1)} %pad_maximum_fusion.3), channel_id=1, source_target_pairs={{0,1},{1,2},{2,3},{3,0},{4,5},{5,6},{6,7},{7,4},{8,9},{9,10},{10,1... | collective-permute-start | bytes 1769480 | tf_op jit(solution)/shard_map/ppermute | solution.py:672
  743.4 47.2 %collective-permute-start.21 = (bf16[768,128]{1,0:T(8,128)(2,1)S(1)}, bf16[768,128]{1,0:T(8,128)(2,1)S(1)}, u32[]{:S(2)}, u32[]{:S(2)}) collective-permute-start(bf16[768,128]{1,0:T(8,128)(2,1)S(1)} %bitcast.171), channel_id=1, source_target_pairs={{0,2},{1,3},{2,0},{3,1},{4,6},{5,7},{6,4},{7,5},{8,10},{9,11},{10,... | collective-permute-start | bytes 589832 | tf_op jit(solution)/shard_map/ppermute | solution.py:672
  752.4 41.5 %collective-permute-start.20 = (bf16[768,128]{1,0:T(8,128)(2,1)S(1)}, bf16[768,128]{1,0:T(8,128)(2,1)S(1)}, u32[]{:S(2)}, u32[]{:S(2)}) collective-permute-start(bf16[768,128]{1,0:T(8,128)(2,1)S(1)} %bitcast.170), channel_id=1, source_target_pairs={{0,1},{1,2},{2,3},{3,0},{4,5},{5,6},{6,7},{7,4},{8,9},{9,10},{10,1... | collective-permute-start | bytes 589832 | tf_op jit(solution)/shard_map/ppermute | solution.py:672
  790.5 26.4 %collective-permute-start.15 = (bf16[512,1024]{1,0:T(8,128)(2,1)S(1)}, bf16[512,1024]{1,0:T(8,128)(2,1)}, u32[]{:S(2)}, u32[]{:S(2)}) collective-permute-start(bf16[512,1024]{1,0:T(8,128)(2,1)S(1)} %get-tuple-element.123), channel_id=1, source_target_pairs={{1,0},{0,1},{5,2},{4,3},{3,4},{2,5},{7,6},{6,7},{9,8},{8,9},{13,10... | collective-permute-start | bytes 3145736 | tf_op jit(solution)/shard_map/ppermute | solution.py:606
  793.8 46.8 %collective-permute-start.14 = (bf16[512,1024]{1,0:T(8,128)(2,1)S(1)}, bf16[512,1024]{1,0:T(8,128)(2,1)}, u32[]{:S(2)}, u32[]{:S(2)}) collective-permute-start(bf16[512,1024]{1,0:T(8,128)(2,1)S(1)} %get-tuple-element.122), channel_id=1, source_target_pairs={{0,0},{1,1},{4,2},{5,3},{2,4},{3,5},{6,6},{7,7},{8,8},{9,9},{12,10... | collective-permute-start | bytes 3145736 | tf_op jit(solution)/shard_map/ppermute | solution.py:605
Sparse Core Ops, SparseCore 0:
  10.9 87.7 all-gather.10
  101.5 65.7 all-gather.12
  170.3 75.9 all-gather.14
  249.1 75.6 all-gather.16

commit v3 on v2

--- a/solution.py
+++ b/solution.py
@@ -144,6 +144,10 @@
     return qcode, kcode, wide(qcode), wide(kcode)
 
 
+def qkv_at(pair, which):
+    return pair // 2 * 6 + which * 2 + pair % 2
+
+
 def attend_fwd(qkv, segment, valid, bq=256, bk=256):
     length, width = qkv.shape
     pairs = width // 3 // PAIR
@@ -155,9 +159,9 @@
             num_scalar_prefetch=3,
             grid=(pairs, length // bq),
             in_specs=[
-                pl.BlockSpec((bq, PAIR), lambda h, i, *_: (i, h)),
-                pl.BlockSpec((length, PAIR), lambda h, i, *_: (0, pairs + h)),
-                pl.BlockSpec((length, PAIR), lambda h, i, *_: (0, 2 * pairs + h)),
+                pl.BlockSpec((bq, PAIR), lambda h, i, *_: (i, qkv_at(h, 0))),
+                pl.BlockSpec((length, PAIR), lambda h, i, *_: (0, qkv_at(h, 1))),
+                pl.BlockSpec((length, PAIR), lambda h, i, *_: (0, qkv_at(h, 2))),
                 pl.BlockSpec((bq, 128), lambda h, i, *_: (i, 0)),
                 pl.BlockSpec((1, length), lambda h, i, *_: (0, 0)),
             ],
@@ -180,8 +184,9 @@
     pairs = width // 3 // PAIR
     lo, hi, pad = block_bounds(segment, valid, bk, bq)
     qcode, kcode, qwide, kwide = attention_codes(segment, valid)
-    whole = lambda at: pl.BlockSpec((length, PAIR), lambda h, i, *_: (0, at * pairs + h))
-    part = lambda at: pl.BlockSpec((bk, PAIR), lambda h, i, *_: (i, at * pairs + h))
+    whole = pl.BlockSpec((length, PAIR), lambda h, i, *_: (0, h))
+    part = pl.BlockSpec((bk, PAIR), lambda h, i, *_: (i, h))
+    cols = lambda at: pl.BlockSpec((bk, PAIR), lambda h, i, *_: (i, qkv_at(h, at)))
     shape = jax.ShapeDtypeStruct((length, pairs * PAIR), BF16)
     return pl.pallas_call(
         functools.partial(attend_bwd_kernel, bq),
@@ -189,12 +194,12 @@
             num_scalar_prefetch=3,
             grid=(pairs, length // bk),
             in_specs=[
-                whole(0), part(1), part(2), whole(0), whole(0),
+                pl.BlockSpec((length, PAIR), lambda h, i, *_: (0, qkv_at(h, 0))), cols(1), cols(2), whole, whole,
                 pl.BlockSpec((8, length), lambda h, i, *_: (h, 0)),
                 pl.BlockSpec((1, length), lambda h, i, *_: (0, 0)),
                 pl.BlockSpec((bk, 128), lambda h, i, *_: (i, 0)),
             ],
-            out_specs=[whole(0), part(0), part(0)],
+            out_specs=[whole, part, part],
             scratch_shapes=[pltpu.VMEM((length, PAIR), F32), pltpu.VMEM((8, length), F32)],
         ),
         out_shape=[shape, shape, shape],
@@ -229,7 +234,7 @@
         ref[at : at + 1, :] += col_sum(part)
 
 
-def mix_kernel(x_ref, c_ref, w_ref, bias_ref, gain_ref, hl_ref, n_ref, r_ref):
+def mix_kernel(at_ref, x_ref, c_ref, w_ref, bias_ref, gain_ref, hl_ref, n_ref, r_ref):
     mixed = x_ref[...].astype(F32) + dot(c_ref[...], w_ref[...]) + bias_ref[0:1, :]
     normed, inverse = norm_stats(mixed)
     hl_ref[...] = (normed * gain_ref[0:1, :] + bias_ref[1:2, :]).astype(BF16)
@@ -303,15 +308,25 @@
     return jax.ShapeDtypeStruct(shape, dtype)
 
 
-def mix(x, c, w, biases, gains, block=256):
-    n, d = x.shape
-    r = functools.partial(rows, block)
-    return call(
-        mix_kernel, (n // block,),
-        [r(d), r(c.shape[1]), once(w.shape), held(biases.shape), held(gains.shape)],
-        ([r(d), r(d), r(128)], [sds((n, d)), sds((n, d), F32), sds((n, 128), F32)]),
-        2 * n * d * d, 12 * n * d, x, c, w, biases, gains,
-    )
+def mix(core_at, x, c, w, biases, gains, block=256):
+    n, d = c.shape
+    r = lambda width: pl.BlockSpec((block, width), lambda i, at: (i, 0))
+    fixed = lambda value: pl.BlockSpec(value.shape, lambda i, at: (0, 0), pipeline_mode=pl.Buffered(1))
+    steps = n // block
+    return pl.pallas_call(
+        mix_kernel,
+        grid_spec=pltpu.PrefetchScalarGridSpec(
+            num_scalar_prefetch=1,
+            grid=(steps,),
+            in_specs=[
+                pl.BlockSpec((block, d), lambda i, at: (at[0] * steps + i, 0)), r(d), fixed(w), fixed(biases), fixed(gains),
+            ],
+            out_specs=[r(d), r(d), r(128)],
+        ),
+        out_shape=[sds((n, d)), sds((n, d), F32), sds((n, 128), F32)],
+        compiler_params=pltpu.CompilerParams(dimension_semantics=("arbitrary",)),
+        cost_estimate=pl.CostEstimate(flops=2 * n * d * d, bytes_accessed=12 * n * d, transcendentals=0),
+    )(core_at, x, c, w, biases, gains)
 
 
 def up(h, w, bias, block=256, cols=1024):
@@ -472,36 +487,38 @@
     )
 
 
-def input_pull_kernel(core_ref, dq_ref, dk_ref, dv_ref, w_ref, *refs):
-    f = dq_ref.shape[1]
-    total = dot(dq_ref[...], w_ref[:, :f], NT)
-    total = total + dot(dk_ref[...], w_ref[:, f : 2 * f], NT)
-    total = total + dot(dv_ref[...], w_ref[:, 2 * f :], NT)
+def input_pull_kernel(at_ref, dq_ref, dk_ref, dv_ref, w_ref, *refs):
+    c = w_ref.shape[1] // 6
+    total = None
+    for j in range(6):
+        ref = (dq_ref, dk_ref, dv_ref)[j % 3]
+        part = dot(ref[:, j // 3 * c : (j // 3 + 1) * c], w_ref[:, j * c : (j + 1) * c], NT)
+        total = part if total is None else total + part
     if len(refs) == 2:
         total = total + refs[0][...]
     refs[-1][...] = total.astype(refs[-1].dtype)
 
 
-def input_pull(part, dq, dk, dv, w, dm=None, block=256):
+def input_pull(part, core, dq, dk, dv, w, dm=None, block=256):
     n, f = dq.shape
     d = w.shape[0]
     steps = n // 2 // block
     cols = pl.BlockSpec((block, f), lambda i, at: (at[0] * steps + i, 0))
     own = pl.BlockSpec((block, d), lambda i, at: (i, 0))
     extra = [] if dm is None else [dm]
+    held_w = pl.BlockSpec((d, w.shape[1] // 2), lambda i, at: (0, at[1]), pipeline_mode=pl.Buffered(1))
     return pl.pallas_call(
         input_pull_kernel,
         grid_spec=pltpu.PrefetchScalarGridSpec(
             num_scalar_prefetch=1,
             grid=(steps,),
-            in_specs=[cols, cols, cols, pl.BlockSpec(w.shape, lambda i, at: (0, 0), pipeline_mode=pl.Buffered(1))]
-            + [own] * len(extra),
+            in_specs=[cols, cols, cols, held_w] + [own] * len(extra),
             out_specs=own,
         ),
         out_shape=sds((n // 2, d), BF16 if dm is None else F32),
         compiler_params=pltpu.CompilerParams(dimension_semantics=("arbitrary",)),
         cost_estimate=pl.CostEstimate(flops=3 * n * f * d, bytes_accessed=8 * n * d, transcendentals=0),
-    )(jnp.reshape(part, (1,)).astype(jnp.int32), dq, dk, dv, w, *extra)
+    )(jnp.stack([part, core]).astype(jnp.int32), dq, dk, dv, w, *extra)
 
 
 def small_sum_kernel(n_p, n_t, in_ref, out_ref, pair, pair_sum, plane, plane_sum, column, send_sems, recv_sems):
@@ -558,6 +575,248 @@
     )(values)
 
 
+MESH_ID = pl.DeviceIdType.MESH
+
+
+def flip(value, bit):
+    return value + bit - 2 * bit * ((value // bit) % 2)
+
+
+def start_kernel(n_p, n_t, kinds, *refs):
+    n = len(kinds)
+    x_ref, bias_ref, *shards = refs[: n + 2]
+    x_out, bias_out, *fulls = refs[n + 2 : 2 * n + 4]
+    send_sems, recv_sems, own_sems = refs[2 * n + 4 :]
+    p, core, t = lax.axis_index("p"), lax.axis_index("core"), lax.axis_index("tensor")
+    me = 2 * p + core
+    bits = [1 << s for s in range(n_p.bit_length() - 1)]
+    column = [{"tensor": lax.rem(t + r, n_t)} for r in range(1, n_t)]
+    across = [{"core": 1 - core, "tensor": lax.rem(t + r, n_t)} for r in range(n_t)]
+    plane = [{"p": flip(p, bit)} for bit in bits]
+    barrier = pltpu.get_barrier_semaphore()
+    for peer in column + across + plane:
+        pl.semaphore_signal(barrier, inc=1, device_id=peer, device_id_type=MESH_ID)
+    pl.semaphore_wait(barrier, len(column + across + plane))
+
+    used = [0, 0]
+
+    def group():
+        used[0] += 1
+        return used[0] - 1
+
+    def send(source, target, at, peer):
+        pltpu.make_async_remote_copy(
+            src_ref=source, dst_ref=target, send_sem=send_sems.at[at], recv_sem=recv_sems.at[at],
+            device_id=peer, device_id_type=MESH_ID,
+        ).start()
+
+    def arrived(view, at):
+        pltpu.make_async_copy(view, view, recv_sems.at[at]).wait()
+
+    def left(view, at):
+        pltpu.make_async_copy(view, view, send_sems.at[at]).wait()
+
+    def keep(source, target):
+        used[1] += 1
+        copy = pltpu.make_async_copy(source, target, own_sems.at[used[1] - 1])
+        copy.start()
+        return copy
+
+    def slab(i, d, half):
+        full, kind = fulls[i], kinds[i]
+        if kind == "rows":
+            depth, wide = shards[i].shape[-2], full.shape[1] // 2
+            return full.at[pl.ds(pl.multiple_of(d * depth, depth), depth), pl.ds(half * wide, wide)]
+        depth, tall = shards[i].shape[-1], full.shape[0] // 2
+        return full.at[pl.ds(half * tall, tall), pl.ds(pl.multiple_of(d * depth, depth), depth)]
+
+    def slabs(i, count, half):
+        full, kind = fulls[i], kinds[i]
+        if kind == "rows":
+            wide = full.shape[1] // 2
+            return full.at[pl.ds(0, count * shards[i].shape[-2]), pl.ds(half * wide, wide)]
+        tall = full.shape[0] // 2
+        return full.at[pl.ds(half * tall, tall), pl.ds(0, count * shards[i].shape[-1])]
+
+    def places(i):
+        shard, full = shards[i], fulls[i]
+        if kinds[i] == "columns":
+            tall, depth = shard.shape
+            return [(shard, full.at[pl.ds(pl.multiple_of(t * tall, tall), tall), pl.ds(pl.multiple_of(me * depth, depth), depth)])]
+        depth, wide = shard.shape[-2:]
+        rows_at = pl.ds(pl.multiple_of(me * depth, depth), depth)
+        if len(shard.shape) == 2:
+            return [(shard, full.at[rows_at, pl.ds(pl.multiple_of(t * wide, wide), wide)])]
+        count = shard.shape[0]
+        return [
+            (shard.at[w], full.at[rows_at, pl.ds(pl.multiple_of((t * count + w) * wide, wide), wide)])
+            for w in range(count)
+        ]
+
+    def shares(i, count):
+        shard, full = shards[i], fulls[i]
+        if kinds[i] == "columns":
+            return full.at[pl.ds(0, count * shard.shape[0]), pl.ds(0, shard.shape[1])]
+        wide = math.prod(shard.shape) // shard.shape[-2]
+        return full.at[pl.ds(0, shard.shape[-2]), pl.ds(0, count * wide)]
+
+    own, line = [], []
+    for i in range(n):
+        at = group()
+        line.append(at)
+        own.append([keep(source, target) for source, target in places(i)])
+        for peer in column:
+            for source, target in places(i):
+                send(source, target, at, peer)
+    bias_at = group()
+    bias_own = keep(bias_ref, bias_out.at[t])
+    for peer in column:
+        send(bias_ref, bias_out.at[t], bias_at, peer)
+
+    held = x_ref.shape[1]
+    odd = t % 2
+    x_rows = x_out.at[pl.ds(pl.multiple_of(t * held, held), held), :]
+    x_at = [group(), group()]
+    stays = core == t // 2
+    peer_a = {"core": t // 2, "tensor": 2 * core + odd}
+    peer_b = {"core": t // 2, "tensor": 2 * core + 1 - odd}
+
+    pl.when(jnp.logical_not(stays))(lambda: send(x_ref.at[odd], x_rows, x_at[0], peer_a))
+    x_own = pltpu.make_async_copy(x_ref.at[odd], x_rows, own_sems.at[used[1]])
+    used[1] += 1
+    pl.when(stays)(x_own.start)
+    send(x_ref.at[1 - odd], x_rows, x_at[1], peer_b)
+
+    partner = {"core": 1 - core}
+    passes = []
+
+    def forward(i, masks, half):
+        at = group()
+        guard = i == 0
+
+        def go():
+            for mask in masks:
+                d = 2 * mask + core
+                send(slab(i, d, half), slab(i, d, half), at, partner)
+
+        if guard:
+            pl.when(core == 1 - half)(go)
+        else:
+            go()
+        passes.append((i, len(masks), half, at))
+
+    states = {}
+
+    def stage(i, s):
+        if s == 0:
+            for copy in own[i]:
+                copy.wait()
+            arrived(shares(i, n_t - 1), line[i])
+            states[i] = {}
+            for half in (0, 1):
+                states[i][half] = ([p], None)
+        else:
+            for half in (0, 1):
+                masks, at = states[i][half]
+                arrived(slabs(i, len(masks), half), at)
+                bit = bits[s - 1] if half == 0 else bits[-s]
+                states[i][half] = (masks + [flip(m, bit) for m in masks], None)
+        for half in (0, 1):
+            masks, _ = states[i][half]
+            if s < len(bits):
+                at = group()
+                bit = bits[s] if half == 0 else bits[-s - 1]
+                for m in masks:
+                    d = 2 * m + core
+                    send(slab(i, d, half), slab(i, d, half), at, {"p": flip(p, bit)})
+                states[i][half] = (masks, at)
+                finish.append((i, len(masks), half, at))
+            fresh = masks if s == 0 else masks[len(masks) // 2 :]
+            forward(i, fresh, half)
+
+    finish = []
+    for step in range(n + len(bits)):
+        for i in range(n):
+            if 0 <= step - i <= len(bits):
+                stage(i, step - i)
+
+    pl.when(jnp.logical_not(stays))(lambda: arrived(x_rows, x_at[0]))
+    pl.when(stays)(x_own.wait)
+    arrived(x_rows, x_at[1])
+    half_rows = x_out.at[pl.ds(pl.multiple_of(core * 2 * held, 2 * held), 2 * held), :]
+    x_pass = group()
+    send(half_rows, half_rows, x_pass, partner)
+    bias_own.wait()
+    arrived(bias_out.at[pl.ds(0, n_t - 1)], bias_at)
+    for i, count, half, at in passes:
+        if i == 0:
+            pl.when(core == half)(functools.partial(arrived, slabs(i, count, half), at))
+        else:
+            arrived(slabs(i, count, half), at)
+    arrived(half_rows, x_pass)
+    left(half_rows, x_pass)
+    for i, count, half, at in passes:
+        if i == 0:
+            pl.when(core == 1 - half)(functools.partial(left, slabs(i, count, half), at))
+        else:
+            left(slabs(i, count, half), at)
+    for i, count, half, at in finish:
+        left(slabs(i, count, half), at)
+    for i in range(n):
+        left(shares(i, n_t - 1), line[i])
+    left(bias_out.at[pl.ds(0, n_t - 1)], bias_at)
+    pl.when(jnp.logical_not(stays))(lambda: left(x_rows, x_at[0]))
+    left(x_rows, x_at[1])
+
+
+def start_gather(x, bias, shards, kinds, n_p, n_t):
+    n_dp = 2 * n_p
+    fulls = []
+    for shard, kind in zip(shards, kinds):
+        if kind == "columns":
+            fulls.append(sds((shard.shape[0] * n_t, shard.shape[1] * n_dp)))
+        else:
+            fulls.append(sds((shard.shape[-2] * n_dp, math.prod(shard.shape) // shard.shape[-2] * n_t)))
+    bits = n_p.bit_length() - 1
+    count = len(shards) * (1 + 2 * bits + 2 * (bits + 1)) + 4
+    vmem, away = pl.BlockSpec(memory_space=pltpu.VMEM), pl.BlockSpec(memory_space=pl.ANY)
+    return pl.pallas_call(
+        functools.partial(start_kernel, n_p, n_t, kinds),
+        out_shape=[sds((n_t * x.shape[1], x.shape[2])), sds((n_t,) + bias.shape, F32)] + fulls,
+        in_specs=[vmem] * (2 + len(shards)),
+        out_specs=[away] * (2 + len(shards)),
+        scratch_shapes=[
+            pltpu.SemaphoreType.DMA((count,)), pltpu.SemaphoreType.DMA((count,)), pltpu.SemaphoreType.DMA((10,)),
+        ],
+        compiler_params=pltpu.CompilerParams(collective_id=1, has_side_effects=True),
+    )(x, bias, *shards)
+
+
+def project_kernel(core_ref, x_ref, w_ref, bias_ref, out_ref):
+    out_ref[...] = (dot(x_ref[...], w_ref[...]) + bias_ref[...]).astype(BF16)
+
+
+def project(core_at, x, w, bias, block=256):
+    n, d = x.shape
+    f = w.shape[1] // 2
+    return pl.pallas_call(
+        project_kernel,
+        grid_spec=pltpu.PrefetchScalarGridSpec(
+            num_scalar_prefetch=1,
+            grid=(n // block,),
+            in_specs=[
+                pl.BlockSpec((block, d), lambda i, at: (i, 0)),
+                pl.BlockSpec((d, f), lambda i, at: (0, at[0]), pipeline_mode=pl.Buffered(1)),
+                pl.BlockSpec((1, f), lambda i, at: (0, 0)),
+            ],
+            out_specs=pl.BlockSpec((block, f), lambda i, at: (i, 0)),
+        ),
+        out_shape=sds((n, f)),
+        compiler_params=pltpu.CompilerParams(dimension_semantics=("arbitrary",)),
+        cost_estimate=pl.CostEstimate(flops=2 * n * d * f, bytes_accessed=4 * n * d + 2 * n * f, transcendentals=0),
+    )(core_at, x, w, bias)
+
+
 def swap_cores(value):
     return lax.ppermute(value, "core", [(0, 1), (1, 0)])
 
@@ -610,34 +869,37 @@
         got = lax.all_gather(weight, ALL, axis=0, tiled=False)
         return got.reshape((n_dp, n_t) + weight.shape)
 
-    x_own = bring(inputs)
-    rows = x_own.shape[0]
     labels = jnp.stack([segment_ids[:, 0], token_valid[:, 0]], axis=1)[odd]
     labels = jnp.where((tensor >> 1) == core, labels, swap_cores(labels))
     segment, valid = labels[0], labels[1]
 
-    bias_all = lax.all_gather(jnp.concatenate([qv_bias.reshape(-1), up_bias]), "tensor")
+    shards, kinds = [qkv_weight, up_weight], ["rows", "rows"]
+    wide = out_weight.shape[1] % 128 == 0
+    if wide:
+        shards, kinds = [qkv_weight, out_weight, up_weight, down_weight], ["rows", "columns", "rows", "columns"]
+    local_bias = jnp.concatenate([qv_bias.reshape(-1), up_bias]).reshape(-1, 128)
+    x_full, bias_all, *fulls = start_gather(inputs, local_bias, shards, kinds, n_p, n_t)
+    if wide:
+        w_qkv, w_out, w_up, w_down = fulls
+    else:
+        w_qkv, w_up = fulls
+        w_out = gathered(out_weight).transpose(1, 2, 0, 3).reshape(-1, width)
+        w_down = gathered(down_weight).transpose(1, 2, 0, 3).reshape(-1, width)
+    out_grad, x_full = lax.optimization_barrier((out_grad, x_full))
+    rows = x_full.shape[0] // 2
+    own = w_qkv.shape[1] // 6
+    bias_all = bias_all.reshape(n_t, -1)
     n_qv = qv_bias.size
-    qv_all = bias_all[:, :n_qv].reshape(n_t, 2, -1).transpose(1, 0, 2).reshape(2, -1)
     up_bias_all = bias_all[:, n_qv:].reshape(1, -1)
-
-    w_qkv = gathered(qkv_weight)
-    w_qkv = lax.dynamic_slice_in_dim(w_qkv, 2 * core, 2, 1)
-    w_qkv = w_qkv.transpose(0, 3, 2, 1, 4).reshape(width, -1)
-    own = w_qkv.shape[1] // 3
-    w_out = gathered(out_weight).transpose(1, 2, 0, 3).reshape(-1, width)
-    w_up = gathered(up_weight).transpose(0, 2, 1, 3).reshape(width, -1)
-    w_down = gathered(down_weight).transpose(1, 2, 0, 3).reshape(-1, width)
-
-    x_full = by_core(core, x_own, swap_cores(x_own), 0)
-    qv_own = lax.dynamic_slice_in_dim(qv_all, core * own, own, 1)
-    bias = jnp.concatenate([qv_own[0], jnp.zeros_like(qv_own[0]), qv_own[1]])
-    qkv = (jnp.dot(x_full, w_qkv, preferred_element_type=F32) + bias).astype(BF16)
+    qv_own = lax.dynamic_slice_in_dim(bias_all[:, :n_qv], 2 * core, 2).reshape(2, 2, -1)
+    bias = jnp.stack([qv_own[:, 0], jnp.zeros_like(qv_own[:, 0]), qv_own[:, 1]], axis=1).reshape(1, -1)
+    core_at = jnp.reshape(core, (1,)).astype(jnp.int32)
+    qkv = project(core_at, x_full, w_qkv, bias)
     context, lse = attend_fwd(qkv, segment, valid, 512, 512)
     mine = lax.dynamic_slice_in_dim(context, core * rows, rows)
     other = lax.dynamic_slice_in_dim(context, (1 - core) * rows, rows)
     c_own = by_core(core, mine, swap_cores(other), 1)
-    hl, normed, inverse = mix(x_own, c_own, w_out, row_biases, norm_gains)
+    hl, normed, inverse = mix(core_at, x_full, c_own, w_out, row_biases, norm_gains)
     active, slope = up(hl, w_up, up_bias_all)
     grad_own = bring(out_grad)
     layer, dr, dz, sums_two = down(active, w_down, normed, grad_own, row_biases, norm_gains)
@@ -656,45 +918,40 @@
     other = lax.dynamic_slice_in_dim(dc, (1 - core) * own, own, 1)
     dc_full = by_core(core, mine, swap_cores(other), 0)
 
-    def flat(values):
-        return values.reshape(-1, values.shape[-1])
-
-    def totals(axis, size, at, parts, dtype):
-        widths = sorted({part.shape[-1] for part in parts})
-        done = [None] * len(parts)
-        for lanes in widths:
-            index = [j for j, part in enumerate(parts) if part.shape[-1] == lanes]
-            pick = lambda to: jnp.concatenate(
-                [flat(lax.dynamic_index_in_dim(parts[j], to, 0, keepdims=False)) for j in index]
-            )
-            total = pick(at).astype(F32)
-            for r in range(1, size):
-                moved = lax.ppermute(pick((at + r) % size), axis, [(i, (i + r) % size) for i in range(size)])
-                total = total + moved.astype(F32)
-            total = total.astype(dtype)
-            first = 0
-            for j in index:
-                shape = parts[j].shape[1:]
-                count = math.prod(shape) // lanes
-                done[j] = total[first : first + count].reshape(shape)
-                first += count
-        return done
+    def pieces(size, at, *parts):
+        pick = lambda part, to: lax.dynamic_index_in_dim(part, to, 0, keepdims=False)
+        out = []
+        for r in range(size):
+            to = (at + r) % size
+            total = pick(parts[0], to)
+            for part in parts[1:]:
+                total = (total.astype(F32) + pick(part, to).astype(F32)).astype(BF16)
+            out.append(total)
+        return out
+
+    def collect(axis, size, own_piece, *others):
+        total = own_piece.astype(F32)
+        for r, piece in enumerate(others, 1):
+            total = total + lax.ppermute(piece, axis, [(i, (i + r) % size) for i in range(size)]).astype(F32)
+        return total
 
     p_at = lax.axis_index("p")
-    plus = lambda a, b: (a.astype(F32) + b.astype(F32)).astype(BF16)
-    ffn_parts = [plus(down_keep, down_recv), plus(up_keep, up_recv), plus(out_keep, out_recv)]
-    *ffn_parts, dc_full = lax.optimization_barrier((*ffn_parts, dc_full))
-    ffn_parts = totals("p", n_p, p_at, ffn_parts, BF16)
+    ffn_parts = [
+        pieces(n_p, p_at, down_keep, down_recv), pieces(n_p, p_at, up_keep, up_recv), pieces(n_p, p_at, out_keep, out_recv),
+    ]
+    ffn_parts, dc_full = lax.optimization_barrier((ffn_parts, dc_full))
+    ffn_sums = [collect("p", n_p, *part).astype(BF16) for part in ffn_parts]
 
     dq, dk, dv = attend_bwd(qkv, context, dc_full, lse, segment, valid, 256, 512)
-    dx_other = swap_cores(input_pull(1 - core, dq, dk, dv, w_qkv))
+    dx_other = swap_cores(input_pull(1 - core, core, dq, dk, dv, w_qkv))
     qkv_keep, qkv_send, qv_sum = qkv_grad(x_full, dq, dk, dv, n_p, n_t)
     qkv_recv = swap_cores(qkv_send)
-    dx_mine = input_pull(core, dq, dk, dv, w_qkv, dm)
+    dx_mine = input_pull(core, core, dq, dk, dv, w_qkv, dm)
     input_grad = give((dx_mine + dx_other.astype(F32)).astype(BF16)).astype(F32)
-    qkv_parts = totals("p", n_p, p_at, [by_core(core, qkv_keep, qkv_recv, 1)], BF16)
-    down_total, up_total, out_total = totals("tensor", n_t, tensor, ffn_parts, F32)
-    (qkv_total,) = totals("tensor", n_t, tensor, qkv_parts, F32)
+    qkv_sum = collect("p", n_p, *pieces(n_p, p_at, by_core(core, qkv_keep, qkv_recv, 1))).astype(BF16)
+    down_total, up_total, out_total, qkv_total = [
+        collect("tensor", n_t, *pieces(n_t, tensor, part)) for part in (*ffn_sums, qkv_sum)
+    ]
     up_total = up_total.transpose(1, 0, 2).reshape(up_weight.shape)
     qkv_total = qkv_total.transpose(0, 2, 1, 3).reshape(qkv_weight.shape)
 

time: 859 us -> 818 us (0.952)
  the two profiles are of different devices: /device:TPU:3 before, /device:TPU:0 now
where the time goes in v3:
time: 818 us; the launch traced here: 807 us
  Pallas kernels  506 us (62%)
  starting transfers between devices  111 us (14%)
  waiting for transfers between devices  101 us (12%)
  other arithmetic  55.1 us (7%)
  local copies, waits for them, and re-layouts  30.6 us (4%)
    pallas_call x1, Pallas kernels, start_gather(): pl.pallas_call(functools.partial(start_kernel, n_p, n_t, kinds), out_shap...  139 us
    ppermute x24, waiting for transfers between devices, collect(): lax.ppermute(piece, axis, [(i, (i + r) % size) for i in range(size)])  94.7 us
    pallas_call x4, Pallas kernels, call(): pl.pallas_call(kernel, grid=grid, in_specs=ins, out_specs=outs[0], out_sh...  83.8 us
    pallas_call x1, Pallas kernels, small_sum(): pl.pallas_call(functools.partial(small_sum_kernel, n_p, n_t), out_shape=s...  69 us
    pallas_call x1, Pallas kernels, attend_bwd(): pl.pallas_call(functools.partial(attend_bwd_kernel, bq), grid_spec=pltpu....  65.8 us
    ppermute x24, starting transfers between devices, collect(): lax.ppermute(piece, axis, [(i, (i + r) % size) for i in range(size)])  58.9 us
    pallas_call x4, Pallas kernels, grad_call(): pl.pallas_call(kernel, grid=grid, in_specs=ins, out_specs=outs[0], out_sh...  56.4 us
    pallas_call x1, Pallas kernels, attend_fwd(): pl.pallas_call(functools.partial(attend_fwd_kernel, bk), grid_spec=pltpu....  54.1 us
  transfers between devices with their start and end apart: 38, of which 12 were waited for; matrix products, arithmetic and copies ran while one was open for 9% of the time, Pallas kernels for 54%

profile of v3, /device:TPU:0, one launch (start us, length us, event | category | flops | bytes accessed | tf_op | source)
XLA Modules:
  0.0 807.3 jit_solution(11742730973987509268)
XLA Ops:
  4.1 139.3 %shard_map.195 = (bf16[2048,1024]{1,0:T(8,128)(2,1)}, f32[4,12,128]{2,1,0:T(8,128)}, bf16[1024,3072]{1,0:T(8,128)(2,1)}, bf16[1024,1024]{1,0:T(8,128)(2,1)}, bf1...) custom-call(bf16[2,512,1024]{2,1,0:T(8,128)(2,1)} %refs_0_.1, f32[12,128]{1,0:T(8,128)} %maximum_bitcast_fusion.1.refs_1_, ...), custom_call_target="tpu_custom_call" | custom-call | tf_op jit(solution)/shard_map/pallas_call | solution.py:783
  144.6 15.3 %collective-permute-start.3 = (bf16[512,1024]{1,0:T(8,128)(2,1)}, bf16[512,1024]{1,0:T(8,128)(2,1)S(1)}, u32[]{:S(2)}, u32[]{:S(2)}) collective-permute-start(bf16[512,1024]{1,0:T(8,128)(2,1)} %get-tuple-element.154), channel_id=1, source_target_pairs={{0,1},{1,0},{2,5},{3,4},{4,3},{5,2},{6,7},{7,6},{8,9},{9,8},{10,13... | collective-permute-start | bytes 3145736 | tf_op jit(solution)/shard_map/ppermute | solution.py:860
  159.9 1.7 collective-permute-start.2
  162.4 12.0 %shard_map.196.q_ref.k_ref.v_ref = bf16[2048,1536]{1,0:T(8,128)(2,1)} custom-call(s32[1]{0:T(128)} %bitcast.core_ref.at_ref, bf16[2048,1024]{1,0:T(8,128)(2,1)} %get-tuple-element.60.x_ref, bf16[1024,3072]{1,0:T(8,128)(2,1)} %get-tuple-element.61.w_ref, f32[1,1536]{1,0:T(1,128)} %reshape.153.bias_ref), custom_call_target="tpu_custom_call" | custom-call | flops 6442450944 | bytes 14680064 | tf_op jit(solution)/shard_map/pallas_call | solution.py:802
  178.1 54.1 %shard_map.197 = (bf16[2048,512]{1,0:T(8,128)(2,1)}, f32[32,2048]{1,0:T(8,128)}) custom-call(s32[4]{0:T(128)} %get-tuple-element.183.lo_ref, s32[4]{0:T(128)} %get-tuple-element.180.hi_ref, s32[4]{0:T(128)} %reduce_sum.29.pad_ref, bf16[2048,1536]{1,0:T(8,128)(2,1)} %shard_map.196.q_ref.k_ref.v_ref, bf16[2048,1536]{1,0:T(8,128)(2,1)} %shard_map.196.q_ref.k_ref.v_ref, ...), custom_call_target="tpu_custom_call" | custom-call | flops 8589934592 | bytes 25165824 | tf_op jit(solution)/shard_map/pallas_call | solution.py:156
  232.2 2.6 constant_dynamic-slice_fusion.8
  234.8 1.8 collective-permute-start.1
  237.3 3.8 maximum_select_fusion.2.e_ref
  241.1 3.6 maximum_select_fusion.1.c_ref.a_ref
  244.7 8.2 %shard_map.198 = (bf16[1024,1024]{1,0:T(8,128)(2,1)}, f32[1024,1024]{1,0:T(8,128)}, f32[1024,128]{1,0:T(8,128)}) custom-call(s32[1]{0:T(128)} %bitcast.core_ref.at_ref, bf16[2048,1024]{1,0:T(8,128)(2,1)} %get-tuple-element.60.x_ref, bf16[1024,1024]{1,0:T(8,128)(2,1)} %maximum_select_fusion.1.c_ref.a_ref, bf16[1024,1024]{1,0:T(8,128)(2,1)} %get-tuple-element.64.w_ref, ...), custom_call_target="tpu_custom_call" | custom-call | flops 2147483648 | bytes 12582912 | tf_op jit(solution)/shard_map/pallas_call | solution.py:316
  252.9 24.7 %shard_map.199 = (bf16[1024,4096]{1,0:T(8,128)(2,1)}, bf16[1024,4096]{1,0:T(8,128)(2,1)}) custom-call(bf16[1024,1024]{1,0:T(8,128)(2,1)} %get-tuple-element.65.h_ref.a_ref, bf16[1024,4096]{1,0:T(8,128)(2,1)} %get-tuple-element.66.w_ref, f32[1,4096]{1,0:T(1,128)} %bitcast.126), custom_call_target="tpu_custom_call" | custom-call | flops 8589934592 | bytes 25165824 | tf_op jit(solution)/shard_map/pallas_call | solution.py:284
  277.6 19.3 %shard_map.200 = (bf16[1024,1024]{1,0:T(8,128)(2,1)}, f32[1024,1024]{1,0:T(8,128)}, bf16[1024,1024]{1,0:T(8,128)(2,1)}, f32[8,1024]{1,0:T(8,128)}) custom-call(bf16[1024,4096]{1,0:T(8,128)(2,1)} %get-tuple-element.67.g_ref.a_ref, bf16[4096,1024]{1,0:T(8,128)(2,1)} %get-tuple-element.68.w_ref, f32[1024,1024]{1,0:T(8,128)} %get-tuple-element.69.n_ref, ...), custom_call_target="tpu_custom_call" | custom-call | flops 8589934592 | bytes 16777216 | tf_op jit(solution)/shard_map/pallas_call | solution.py:284
  296.9 15.5 %shard_map.201 = (bf16[4,4,1024,128]{3,2,1,0:T(8,128)(2,1)}, bf16[4,4,1024,128]{3,2,1,0:T(8,128)(2,1)}) custom-call(bf16[1024,4096]{1,0:T(8,128)(2,1)} %get-tuple-element.67.g_ref.a_ref, bf16[1024,1024]{1,0:T(8,128)(2,1)} %get-tuple-element.72.b_ref.dz_ref), custom_call_target="tpu_custom_call" | custom-call | flops 8589934592 | bytes 16777216 | tf_op jit(solution)/shard_map/pallas_call | solution.py:433
  312.6 22.0 %shard_map.202 = (bf16[1024,4096]{1,0:T(8,128)(2,1)}, f32[8,4096]{1,0:T(8,128)}) custom-call(bf16[1024,1024]{1,0:T(8,128)(2,1)} %get-tuple-element.72.b_ref.dz_ref, bf16[4096,1024]{1,0:T(8,128)(2,1)} %get-tuple-element.68.w_ref, bf16[1024,4096]{1,0:T(8,128)(2,1)} %get-tuple-element.75.slope_ref), custom_call_target="tpu_custom_call" | custom-call | flops 8589934592 | bytes 25165824 | tf_op jit(solution)/shard_map/pallas_call | solution.py:284
  334.6 15.7 %shard_map.203 = (bf16[4,4,8,128,128]{4,3,2,1,0:T(8,128)(2,1)}, bf16[4,4,8,128,128]{4,3,2,1,0:T(8,128)(2,1)}) custom-call(bf16[1024,1024]{1,0:T(8,128)(2,1)} %get-tuple-element.65.h_ref.a_ref, bf16[1024,4096]{1,0:T(8,128)(2,1)} %get-tuple-element.76.b_ref.du_ref), custom_call_target="tpu_custom_call" | custom-call | flops 8589934592 | bytes 16777216 | tf_op jit(solution)/shard_map/pallas_call | solution.py:433
  350.7 17.8 %shard_map.204 = (f32[1024,1024]{1,0:T(8,128)}, bf16[1024,1024]{1,0:T(8,128)(2,1)}, f32[8,1024]{1,0:T(8,128)}) custom-call(bf16[1024,4096]{1,0:T(8,128)(2,1)} %get-tuple-element.76.b_ref.du_ref, bf16[1024,4096]{1,0:T(8,128)(2,1)} %get-tuple-element.66.w_ref, f32[1024,1024]{1,0:T(8,128)} %get-tuple-element.79.dr_ref, f32[1024,1024]{1,0:T(8,128)} %get-tuple-element.69.n_ref, ...), custom_call_target="tpu_custom_call" | custom-call | flops 8589934592 | bytes 16777216 | tf_op jit(solution)/shard_map/pallas_call | solution.py:284
  368.4 6.5 shard_map.205
  376.2 18.5 %collective-permute-start.5 = (bf16[512,1024]{1,0:T(8,128)(2,1)}, bf16[512,1024]{1,0:T(8,128)(2,1)S(1)}, u32[]{:S(2)}, u32[]{:S(2)}) collective-permute-start(bf16[512,1024]{1,0:T(8,128)(2,1)} %get-tuple-element.152), channel_id=1, source_target_pairs={{1,0},{0,1},{5,2},{4,3},{3,4},{2,5},{7,6},{6,7},{9,8},{8,9},{13,10... | collective-permute-start | bytes 3145736 | tf_op jit(solution)/shard_map/ppermute | solution.py:865
  394.7 1.6 collective-permute-start.4
  396.3 2.4 convolution_convert_fusion
  400.0 2.9 collective-permute-start.9
  408.1 2.7 fusion.23
  410.8 5.9 collective-permute-done.5
  416.7 3.2 maximum_select_fusion.3
  419.9 3.6 maximum_select_fusion.4.dc_ref
  423.5 4.8 fusion.7
  428.4 5.1 fusion.11
  433.5 1.6 collective-permute-start.22
  436.5 65.8 %shard_map.206 = (bf16[2048,512]{1,0:T(8,128)(2,1)}, bf16[2048,512]{1,0:T(8,128)(2,1)}, bf16[2048,512]{1,0:T(8,128)(2,1)}) custom-call(s32[4]{0:T(128)} %get-tuple-element.184.lo_ref, s32[4]{0:T(128)} %get-tuple-element.179.hi_ref, s32[4]{0:T(128)} %reduce_sum.29.pad_ref, bf16[2048,1536]{1,0:T(8,128)(2,1)} %shard_map.196.q_ref.k_ref.v_ref, ...), custom_call_target="tpu_custom_call" | custom-call | flops 21474836480 | bytes 50331648 | tf_op jit(solution)/shard_map/pallas_call | solution.py:191
  502.3 18.7 %shard_map.209 = (bf16[4,2,3,2,128,128]{5,4,3,2,1,0:T(8,128)(2,1)}, bf16[4,2,3,2,128,128]{5,4,3,2,1,0:T(8,128)(2,1)}, f32[8,512]{1,0:T(8,128)}) custom-call(bf16[2048,1024]{1,0:T(8,128)(2,1)} %get-tuple-element.60.x_ref, bf16[2048,512]{1,0:T(8,128)(2,1)} %get-tuple-element.86.dq_ref, bf16[2048,512]{1,0:T(8,128)(2,1)} %get-tuple-element.87.dk_ref, ...), custom_call_target="tpu_custom_call" | custom-call | flops 6442450944 | bytes 12582912 | tf_op jit(solution)/shard_map/pallas_call | solution.py:433
  522.4 69.0 %shard_map.210 = f32[96,128]{1,0:T(8,128)} custom-call(f32[96,128]{1,0:T(8,128)} %maximum_bitcast_fusion.in_ref), custom_call_target="tpu_custom_call" | custom-call | tf_op jit(solution)/shard_map/pallas_call | solution.py:564
  592.4 2.1 collective-permute-start.28
  594.5 1.8 collective-permute-start.27
  596.4 8.2 %shard_map.208 = bf16[1024,1024]{1,0:T(8,128)(2,1)} custom-call(s32[2]{0:T(128)} %pad_add_fusion.1.at_ref, bf16[2048,512]{1,0:T(8,128)(2,1)} %get-tuple-element.86.dq_ref, bf16[2048,512]{1,0:T(8,128)(2,1)} %get-tuple-element.87.dk_ref, bf16[2048,512]{1,0:T(8,128)(2,1)} %get-tuple-element.88.dv_ref, bf16[1024,3072]{1,0:T(8,128)(2,1)} %get-tuple-element.61.w_ref), custom_call_target="tpu_custom_call" | custom-call | flops 3221225472 | bytes 16777216 | tf_op jit(solution)/shard_map/pallas_call | solution.py:510
  606.6 3.9 collective-permute-start.25
  612.4 4.2 collective-permute-done.24
  616.6 2.7 collective-permute-done.23
  619.2 5.5 collective-permute-done.28
  624.8 11.1 %collective-permute-start.34 = (bf16[4,1024,128]{2,1,0:T(8,128)(2,1)}, bf16[4,1024,128]{2,1,0:T(8,128)(2,1)}, u32[]{:S(2)}, u32[]{:S(2)}) collective-permute-start(bf16[4,1024,128]{2,1,0:T(8,128)(2,1)} %get-tuple-element.107), channel_id=1, source_target_pairs={{0,24},{8,0},{16,8},{24,16},{1,25},{9,1},{17,9},{25,17},{2,26},{10... | collective-permute-start | bytes 3145736 | tf_op jit(solution)/shard_map/ppermute | solution.py:935
  635.9 12.5 %collective-permute-done.27 = bf16[4,8,128,128]{3,2,1,0:T(8,128)(2,1)} collective-permute-done((bf16[4,8,128,128]{3,2,1,0:T(8,128)(2,1)}, bf16[4,8,128,128]{3,2,1,0:T(8,128)(2,1)}, u32[]{:S(2)}, u32[]{:S(2)}) %collective-permute-start.27) | collective-permute-done | bytes 1048608 | tf_op jit(solution)/shard_map/ppermute | solution.py:935
  648.5 15.5 %collective-permute-start.32 = (bf16[4,1024,128]{2,1,0:T(8,128)(2,1)}, bf16[4,1024,128]{2,1,0:T(8,128)(2,1)}, u32[]{:S(2)}, u32[]{:S(2)}) collective-permute-start(bf16[4,1024,128]{2,1,0:T(8,128)(2,1)} %get-tuple-element.105), channel_id=1, source_target_pairs={{0,8},{8,16},{16,24},{24,0},{1,9},{9,17},{17,25},{25,1},{2,10},{10... | collective-permute-start | bytes 3145736 | tf_op jit(solution)/shard_map/ppermute | solution.py:935
  667.1 9.3 %shard_map.207 = f32[1024,1024]{1,0:T(8,128)} custom-call(s32[2]{0:T(128)} %pad_add_fusion.at_ref, bf16[2048,512]{1,0:T(8,128)(2,1)} %get-tuple-element.86.dq_ref, bf16[2048,512]{1,0:T(8,128)(2,1)} %get-tuple-element.87.dk_ref, bf16[2048,512]{1,0:T(8,128)(2,1)} %get-tuple-element.88.dv_ref, bf16[1024,3072]{1,0:T(8,128)(2,1)} %get-tuple-element.61.w_ref, ...), custom_call_target="tpu_custom_call" | custom-call | flops 3221225472 | bytes 16777216 | tf_op jit(solution)/shard_map/pallas_call | solution.py:510
  676.4 1.6 fusion.25
  678.0 2.2 add_convert_fusion.2
  680.3 14.9 %collective-permute-done.33 = bf16[4,1024,128]{2,1,0:T(8,128)(2,1)} collective-permute-done((bf16[4,1024,128]{2,1,0:T(8,128)(2,1)}, bf16[4,1024,128]{2,1,0:T(8,128)(2,1)}, u32[]{:S(2)}, u32[]{:S(2)}) %collective-permute-start.33) | collective-permute-done | bytes 1048608 | tf_op jit(solution)/shard_map/ppermute | solution.py:935
  695.2 2.0 collective-permute-start.30
  697.3 2.5 collective-permute-start.29
  699.8 2.4 add_convert_fusion.1
  704.2 2.4 maximum_select_fusion
  706.6 1.5 dynamic-slice_bitcast_fusion.4
  708.4 2.0 collective-permute-start.14
  710.4 2.4 add_convert_fusion
  712.8 1.6 constant_dynamic-slice_fusion.2
  714.4 9.5 %collective-permute-start.11 = (bf16[512,1024]{1,0:T(8,128)(2,1)}, bf16[512,1024]{1,0:T(8,128)(2,1)}, u32[]{:S(2)}, u32[]{:S(2)}) collective-permute-start(bf16[512,1024]{1,0:T(8,128)(2,1)} %get-tuple-element.143), channel_id=1, source_target_pairs={{0,0},{1,1},{4,2},{5,3},{2,4},{3,5},{6,6},{7,7},{8,8},{9,9},{12,10... | collective-permute-start | bytes 3145736 | tf_op jit(solution)/shard_map/ppermute | solution.py:864
  724.8 2.0 copy.33
  726.8 2.0 copy.35
  730.1 12.2 %collective-permute-done.15 = bf16[4,3,2,128,128]{4,3,2,1,0:T(8,128)(2,1)} collective-permute-done((bf16[4,3,2,128,128]{4,3,2,1,0:T(8,128)(2,1)}, bf16[4,3,2,128,128]{4,3,2,1,0:T(8,128)(2,1)}, u32[]{:S(2)}, u32[]{:S(2)}) %collective-permute-start.15) | collective-permute-done | bytes 786464 | tf_op jit(solution)/shard_map/ppermute | solution.py:935
  742.6 1.6 collective-permute-start.35
  744.2 2.1 fusion.3
  747.3 11.6 %collective-permute-start.19 = (bf16[3,2,128,128]{3,2,1,0:T(8,128)(2,1)S(1)}, bf16[3,2,128,128]{3,2,1,0:T(8,128)(2,1)S(1)}, u32[]{:S(2)}, u32[]{:S(2)}) collective-permute-start(bf16[3,2,128,128]{3,2,1,0:T(8,128)(2,1)S(1)} %get-tuple-element.164), channel_id=1, source_target_pairs={{0,3},{1,0},{2,1},{3,2},{4,7},{5,4},{6,5},{7,6},{8,11},{9,8},{10,9... | collective-permute-start | bytes 589832 | tf_op jit(solution)/shard_map/ppermute | solution.py:935
  758.9 29.0 %collective-permute-done.36 = bf16[1024,128]{1,0:T(8,128)(2,1)S(1)} collective-permute-done((bf16[1024,128]{1,0:T(8,128)(2,1)}, bf16[1024,128]{1,0:T(8,128)(2,1)S(1)}, u32[]{:S(2)}, u32[]{:S(2)}) %collective-permute-start.36) | collective-permute-done | bytes 262176 | tf_op jit(solution)/shard_map/ppermute | solution.py:935
  787.9 1.9 fusion.13
  789.9 11.3 %collective-permute-done.18 = bf16[3,2,128,128]{3,2,1,0:T(8,128)(2,1)S(1)} collective-permute-done((bf16[3,2,128,128]{3,2,1,0:T(8,128)(2,1)S(1)}, bf16[3,2,128,128]{3,2,1,0:T(8,128)(2,1)S(1)}, u32[]{:S(2)}, u32[]{:S(2)}) %collective-permute-start.18) | collective-permute-done | bytes 196640 | tf_op jit(solution)/shard_map/ppermute | solution.py:935
  802.4 4.6 fusion
  (134 shorter events, 36.3 us)
Async XLA Ops:
  0.6 142.8 %copy-start.5 = (bf16[2,512,1024]{2,1,0:T(8,128)(2,1)S(1)}, bf16[2,512,1024]{2,1,0:T(8,128)(2,1)}, u32[]{:S(2)}) copy-start(bf16[2,512,1024]{2,1,0:T(8,128)(2,1)} %param.23) | copy-start | bytes 6291460
  1.5 172.9 %collective-permute-start = (s32[2,2048]{1,0:T(2,128)S(1)}, s32[2,2048]{1,0:T(2,128)S(1)}, u32[]{:S(2)}, u32[]{:S(2)}) collective-permute-start(s32[2,2048]{1,0:T(2,128)S(1)} %fusion.27), channel_id=1, source_target_pairs={{0,4},{4,0},{1,5},{5,1},{2,6},{6,2},{3,7},{7,3},{8,12},{12,8},{9,1... | collective-permute-start | bytes 49160 | tf_op jit(solution)/shard_map/ppermute | solution.py:821
  143.4 18.2 %copy-start.11 = (f32[4,12,128]{2,1,0:T(8,128)S(1)}, f32[4,12,128]{2,1,0:T(8,128)}, u32[]{:S(2)}) copy-start(f32[4,12,128]{2,1,0:T(8,128)} %get-tuple-element.62) | copy-start | bytes 73732
  144.6 92.7 %collective-permute-start.3 = (bf16[512,1024]{1,0:T(8,128)(2,1)}, bf16[512,1024]{1,0:T(8,128)(2,1)S(1)}, u32[]{:S(2)}, u32[]{:S(2)}) collective-permute-start(bf16[512,1024]{1,0:T(8,128)(2,1)} %get-tuple-element.154), channel_id=1, source_target_pairs={{0,1},{1,0},{2,5},{3,4},{4,3},{5,2},{6,7},{7,6},{8,9},{9,8},{10,13... | collective-permute-start | bytes 3145736 | tf_op jit(solution)/shard_map/ppermute | solution.py:860
  159.9 77.4 %collective-permute-start.2 = (bf16[512,1024]{1,0:T(8,128)(2,1)S(1)}, bf16[512,1024]{1,0:T(8,128)(2,1)}, u32[]{:S(2)}, u32[]{:S(2)}) collective-permute-start(bf16[512,1024]{1,0:T(8,128)(2,1)S(1)} %get-tuple-element.153), channel_id=1, source_target_pairs={{0,0},{1,1},{2,4},{3,5},{4,2},{5,3},{6,6},{7,7},{8,8},{9,9},{10,12... | collective-permute-start | bytes 3145736 | tf_op jit(solution)/shard_map/ppermute | solution.py:859
  175.1 229.0 %copy-start.10 = (s32[1,2048]{1,0:T(1,128)}, s32[1,2048]{1,0:T(1,128)S(1)}, u32[]{:S(2)}) copy-start(s32[1,2048]{1,0:T(1,128)S(1)} %get-tuple-element.174.qcode_ref) | copy-start | bytes 24580
  234.8 6.3 collective-permute-start.1
  312.4 111.1 %collective-permute-start.6 = (bf16[4,4,1024,128]{3,2,1,0:T(8,128)(2,1)}, bf16[4,4,1024,128]{3,2,1,0:T(8,128)(2,1)}, u32[]{:S(2)}, u32[]{:S(2)}) collective-permute-start(bf16[4,4,1024,128]{3,2,1,0:T(8,128)(2,1)} %get-tuple-element.74), channel_id=1, source_target_pairs={{0,4},{4,0},{1,5},{5,1},{2,6},{6,2},{3,7},{7,3},{8,12},{12,8},{9,1... | collective-permute-start | bytes 12582920 | tf_op jit(solution)/shard_map/ppermute | solution.py:821
  350.3 78.1 %collective-permute-start.7 = (bf16[4,4,8,128,128]{4,3,2,1,0:T(8,128)(2,1)}, bf16[4,4,8,128,128]{4,3,2,1,0:T(8,128)(2,1)}, u32[]{:S(2)}, u32[]{:S(2)}) collective-permute-start(bf16[4,4,8,128,128]{4,3,2,1,0:T(8,128)(2,1)} %get-tuple-element.78), channel_id=1, source_target_pairs={{0,4},{4,0},{1,5},{5,1},{2,6},{6,2},{3,7},{7,3},{8,12},{12,8},{9,1... | collective-permute-start | bytes 12582920 | tf_op jit(solution)/shard_map/ppermute | solution.py:821
  368.4 6.7 copy-start.6
  374.9 25.0 %collective-permute-start.8 = (bf16[4,4,256,128]{3,2,1,0:T(8,128)(2,1)}, bf16[4,4,256,128]{3,2,1,0:T(8,128)(2,1)}, u32[]{:S(2)}, u32[]{:S(2)}) collective-permute-start(bf16[4,4,256,128]{3,2,1,0:T(8,128)(2,1)} %get-tuple-element.83), channel_id=1, source_target_pairs={{0,4},{4,0},{1,5},{5,1},{2,6},{6,2},{3,7},{7,3},{8,12},{12,8},{9,1... | collective-permute-start | bytes 3145736 | tf_op jit(solution)/shard_map/ppermute | solution.py:821
  375.1 21.3 %copy-start.4 = (bf16[1024,1024]{1,0:T(8,128)(2,1)S(1)}, bf16[1024,1024]{1,0:T(8,128)(2,1)}, u32[]{:S(2)}) copy-start(bf16[1024,1024]{1,0:T(8,128)(2,1)} %get-tuple-element.64.w_ref) | copy-start | bytes 6291460
  375.1 21.3 %copy-start.12 = (bf16[1024,1024]{1,0:T(8,128)(2,1)S(1)}, bf16[1024,1024]{1,0:T(8,128)(2,1)}, u32[]{:S(2)}) copy-start(bf16[1024,1024]{1,0:T(8,128)(2,1)} %get-tuple-element.81.b_ref) | copy-start | bytes 6291460
  376.2 40.5 %collective-permute-start.5 = (bf16[512,1024]{1,0:T(8,128)(2,1)}, bf16[512,1024]{1,0:T(8,128)(2,1)S(1)}, u32[]{:S(2)}, u32[]{:S(2)}) collective-permute-start(bf16[512,1024]{1,0:T(8,128)(2,1)} %get-tuple-element.152), channel_id=1, source_target_pairs={{1,0},{0,1},{5,2},{4,3},{3,4},{2,5},{7,6},{6,7},{9,8},{8,9},{13,10... | collective-permute-start | bytes 3145736 | tf_op jit(solution)/shard_map/ppermute | solution.py:865
  394.7 22.0 %collective-permute-start.4 = (bf16[512,1024]{1,0:T(8,128)(2,1)S(1)}, bf16[512,1024]{1,0:T(8,128)(2,1)}, u32[]{:S(2)}, u32[]{:S(2)}) collective-permute-start(bf16[512,1024]{1,0:T(8,128)(2,1)S(1)} %get-tuple-element.151), channel_id=1, source_target_pairs={{0,0},{1,1},{4,2},{5,3},{2,4},{3,5},{6,6},{7,7},{8,8},{9,9},{12,10... | collective-permute-start | bytes 3145736 | tf_op jit(solution)/shard_map/ppermute | solution.py:864
  400.0 19.9 %collective-permute-start.9 = (bf16[1024,512]{1,0:T(8,128)(2,1)}, bf16[1024,512]{1,0:T(8,128)(2,1)}, u32[]{:S(2)}, u32[]{:S(2)}) collective-permute-start(bf16[1024,512]{1,0:T(8,128)(2,1)} %get-tuple-element.146), channel_id=1, source_target_pairs={{0,4},{4,0},{1,5},{5,1},{2,6},{6,2},{3,7},{7,3},{8,12},{12,8},{9,1... | collective-permute-start | bytes 3145736 | tf_op jit(solution)/shard_map/ppermute | solution.py:821
  419.9 3.6 copy-start.2
  423.5 4.9 copy-start.3
  433.5 162.9 %collective-permute-start.22 = (bf16[4,256,128]{2,1,0:T(8,128)(2,1)}, bf16[4,256,128]{2,1,0:T(8,128)(2,1)S(1)}, u32[]{:S(2)}, u32[]{:S(2)}) collective-permute-start(bf16[4,256,128]{2,1,0:T(8,128)(2,1)} %get-tuple-element.99), channel_id=1, source_target_pairs={{0,24},{8,0},{16,8},{24,16},{1,25},{9,1},{17,9},{25,17},{2,26},{10... | collective-permute-start | bytes 786440 | tf_op jit(solution)/shard_map/ppermute | solution.py:935
  591.4 19.1 %copy-start.9 = (f32[96,128]{1,0:T(8,128)S(1)}, f32[96,128]{1,0:T(8,128)}, u32[]{:S(2)}) copy-start(f32[96,128]{1,0:T(8,128)} %shard_map.210) | copy-start | bytes 147460
  591.4 13.2 %collective-permute-start.21 = (bf16[4,256,128]{2,1,0:T(8,128)(2,1)}, bf16[4,256,128]{2,1,0:T(8,128)(2,1)}, u32[]{:S(2)}, u32[]{:S(2)}) collective-permute-start(bf16[4,256,128]{2,1,0:T(8,128)(2,1)} %get-tuple-element.98), channel_id=1, source_target_pairs={{0,16},{8,24},{16,0},{24,8},{1,17},{9,25},{17,1},{25,9},{2,18},{10... | collective-permute-start | bytes 786440 | tf_op jit(solution)/shard_map/ppermute | solution.py:935
  591.6 13.0 %collective-permute-start.20 = (bf16[4,256,128]{2,1,0:T(8,128)(2,1)}, bf16[4,256,128]{2,1,0:T(8,128)(2,1)}, u32[]{:S(2)}, u32[]{:S(2)}) collective-permute-start(bf16[4,256,128]{2,1,0:T(8,128)(2,1)} %get-tuple-element.97), channel_id=1, source_target_pairs={{0,8},{8,16},{16,24},{24,0},{1,9},{9,17},{17,25},{25,1},{2,10},{10... | collective-permute-start | bytes 786440 | tf_op jit(solution)/shard_map/ppermute | solution.py:935
  592.4 32.3 %collective-permute-start.28 = (bf16[4,8,128,128]{3,2,1,0:T(8,128)(2,1)}, bf16[4,8,128,128]{3,2,1,0:T(8,128)(2,1)S(1)}, u32[]{:S(2)}, u32[]{:S(2)}) collective-permute-start(bf16[4,8,128,128]{3,2,1,0:T(8,128)(2,1)} %get-tuple-element.103), channel_id=1, source_target_pairs={{0,24},{8,0},{16,8},{24,16},{1,25},{9,1},{17,9},{25,17},{2,26},{10... | collective-permute-start | bytes 3145736 | tf_op jit(solution)/shard_map/ppermute | solution.py:935
  594.5 53.8 %collective-permute-start.27 = (bf16[4,8,128,128]{3,2,1,0:T(8,128)(2,1)}, bf16[4,8,128,128]{3,2,1,0:T(8,128)(2,1)}, u32[]{:S(2)}, u32[]{:S(2)}) collective-permute-start(bf16[4,8,128,128]{3,2,1,0:T(8,128)(2,1)} %get-tuple-element.102), channel_id=1, source_target_pairs={{0,16},{8,24},{16,0},{24,8},{1,17},{9,25},{17,1},{25,9},{2,18},{10... | collective-permute-start | bytes 3145736 | tf_op jit(solution)/shard_map/ppermute | solution.py:935
  596.4 8.2 %copy-start.8 = (bf16[4,256,128]{2,1,0:T(8,128)(2,1)}, bf16[4,256,128]{2,1,0:T(8,128)(2,1)S(1)}, u32[]{:S(2)}) copy-start(bf16[4,256,128]{2,1,0:T(8,128)(2,1)S(1)} %collective-permute-done.22) | copy-start | bytes 786436
  596.4 52.1 %collective-permute-start.26 = (bf16[4,8,128,128]{3,2,1,0:T(8,128)(2,1)}, bf16[4,8,128,128]{3,2,1,0:T(8,128)(2,1)}, u32[]{:S(2)}, u32[]{:S(2)}) collective-permute-start(bf16[4,8,128,128]{3,2,1,0:T(8,128)(2,1)} %get-tuple-element.101), channel_id=1, source_target_pairs={{0,8},{8,16},{16,24},{24,0},{1,9},{9,17},{17,25},{25,1},{2,10},{10... | collective-permute-start | bytes 3145736 | tf_op jit(solution)/shard_map/ppermute | solution.py:935
  606.6 5.8 collective-permute-start.25
  611.1 5.5 collective-permute-start.24
  612.4 6.9 collective-permute-start.23
  616.5 91.8 %collective-permute-start.10 = (bf16[1024,1024]{1,0:T(8,128)(2,1)}, bf16[1024,1024]{1,0:T(8,128)(2,1)}, u32[]{:S(2)}, u32[]{:S(2)}) collective-permute-start(bf16[1024,1024]{1,0:T(8,128)(2,1)} %shard_map.208), channel_id=1, source_target_pairs={{0,4},{4,0},{1,5},{5,1},{2,6},{6,2},{3,7},{7,3},{8,12},{12,8},{9,1... | collective-permute-start | bytes 6291464 | tf_op jit(solution)/shard_map/ppermute | solution.py:821
  619.2 83.9 %collective-permute-start.13 = (bf16[4,2,3,2,128,128]{5,4,3,2,1,0:T(8,128)(2,1)}, bf16[4,2,3,2,128,128]{5,4,3,2,1,0:T(8,128)(2,1)}, u32[]{:S(2)}, u32[]{:S(2)}) collective-permute-start(bf16[4,2,3,2,128,128]{5,4,3,2,1,0:T(8,128)(2,1)} %get-tuple-element.91), channel_id=1, source_target_pairs={{0,4},{4,0},{1,5},{5,1},{2,6},{6,2},{3,7},{7,3},{8,12},{12,8},{9,1... | collective-permute-start | bytes 4718600 | tf_op jit(solution)/shard_map/ppermute | solution.py:821
  624.8 55.5 %collective-permute-start.34 = (bf16[4,1024,128]{2,1,0:T(8,128)(2,1)}, bf16[4,1024,128]{2,1,0:T(8,128)(2,1)}, u32[]{:S(2)}, u32[]{:S(2)}) collective-permute-start(bf16[4,1024,128]{2,1,0:T(8,128)(2,1)} %get-tuple-element.107), channel_id=1, source_target_pairs={{0,24},{8,0},{16,8},{24,16},{1,25},{9,1},{17,9},{25,17},{2,26},{10... | collective-permute-start | bytes 3145736 | tf_op jit(solution)/shard_map/ppermute | solution.py:935
  648.3 46.9 %collective-permute-start.33 = (bf16[4,1024,128]{2,1,0:T(8,128)(2,1)}, bf16[4,1024,128]{2,1,0:T(8,128)(2,1)}, u32[]{:S(2)}, u32[]{:S(2)}) collective-permute-start(bf16[4,1024,128]{2,1,0:T(8,128)(2,1)} %get-tuple-element.106), channel_id=1, source_target_pairs={{0,16},{8,24},{16,0},{24,8},{1,17},{9,25},{17,1},{25,9},{2,18},{10... | collective-permute-start | bytes 3145736 | tf_op jit(solution)/shard_map/ppermute | solution.py:935
  648.5 48.8 %collective-permute-start.32 = (bf16[4,1024,128]{2,1,0:T(8,128)(2,1)}, bf16[4,1024,128]{2,1,0:T(8,128)(2,1)}, u32[]{:S(2)}, u32[]{:S(2)}) collective-permute-start(bf16[4,1024,128]{2,1,0:T(8,128)(2,1)} %get-tuple-element.105), channel_id=1, source_target_pairs={{0,8},{8,16},{16,24},{24,0},{1,9},{9,17},{17,25},{25,1},{2,10},{10... | collective-permute-start | bytes 3145736 | tf_op jit(solution)/shard_map/ppermute | solution.py:935
  680.3 27.8 %collective-permute-start.31 = (bf16[8,128,128]{2,1,0:T(8,128)(2,1)S(1)}, bf16[8,128,128]{2,1,0:T(8,128)(2,1)S(1)}, u32[]{:S(2)}, u32[]{:S(2)}) collective-permute-start(bf16[8,128,128]{2,1,0:T(8,128)(2,1)S(1)} %get-tuple-element.161), channel_id=1, source_target_pairs={{0,3},{1,0},{2,1},{3,2},{4,7},{5,4},{6,5},{7,6},{8,11},{9,8},{10,9... | collective-permute-start | bytes 786440 | tf_op jit(solution)/shard_map/ppermute | solution.py:935
  695.2 19.2 %collective-permute-start.30 = (bf16[8,128,128]{2,1,0:T(8,128)(2,1)S(1)}, bf16[8,128,128]{2,1,0:T(8,128)(2,1)S(1)}, u32[]{:S(2)}, u32[]{:S(2)}) collective-permute-start(bf16[8,128,128]{2,1,0:T(8,128)(2,1)S(1)} %get-tuple-element.162), channel_id=1, source_target_pairs={{0,2},{1,3},{2,0},{3,1},{4,6},{5,7},{6,4},{7,5},{8,10},{9,11},{10,... | collective-permute-start | bytes 786440 | tf_op jit(solution)/shard_map/ppermute | solution.py:935
  697.3 17.1 %collective-permute-start.29 = (bf16[8,128,128]{2,1,0:T(8,128)(2,1)S(1)}, bf16[8,128,128]{2,1,0:T(8,128)(2,1)S(1)}, u32[]{:S(2)}, u32[]{:S(2)}) collective-permute-start(bf16[8,128,128]{2,1,0:T(8,128)(2,1)S(1)} %get-tuple-element.160), channel_id=1, source_target_pairs={{0,1},{1,2},{2,3},{3,0},{4,5},{5,6},{6,7},{7,4},{8,9},{9,10},{10,1... | collective-permute-start | bytes 786440 | tf_op jit(solution)/shard_map/ppermute | solution.py:935
  702.2 1.2 copy-start.1
  702.2 2.0 copy-start.7
  706.6 3.8 copy-start
  708.1 20.8 %collective-permute-start.16 = (bf16[4,3,2,128,128]{4,3,2,1,0:T(8,128)(2,1)}, bf16[4,3,2,128,128]{4,3,2,1,0:T(8,128)(2,1)}, u32[]{:S(2)}, u32[]{:S(2)}) collective-permute-start(bf16[4,3,2,128,128]{4,3,2,1,0:T(8,128)(2,1)} %get-tuple-element.141), channel_id=1, source_target_pairs={{0,24},{8,0},{16,8},{24,16},{1,25},{9,1},{17,9},{25,17},{2,26},{10... | collective-permute-start | bytes 2359304 | tf_op jit(solution)/shard_map/ppermute | solution.py:935
  708.1 34.2 %collective-permute-start.15 = (bf16[4,3,2,128,128]{4,3,2,1,0:T(8,128)(2,1)}, bf16[4,3,2,128,128]{4,3,2,1,0:T(8,128)(2,1)}, u32[]{:S(2)}, u32[]{:S(2)}) collective-permute-start(bf16[4,3,2,128,128]{4,3,2,1,0:T(8,128)(2,1)} %get-tuple-element.142), channel_id=1, source_target_pairs={{0,16},{8,24},{16,0},{24,8},{1,17},{9,25},{17,1},{25,9},{2,18},{10... | collective-permute-start | bytes 2359304 | tf_op jit(solution)/shard_map/ppermute | solution.py:935
  708.4 34.2 %collective-permute-start.14 = (bf16[4,3,2,128,128]{4,3,2,1,0:T(8,128)(2,1)}, bf16[4,3,2,128,128]{4,3,2,1,0:T(8,128)(2,1)}, u32[]{:S(2)}, u32[]{:S(2)}) collective-permute-start(bf16[4,3,2,128,128]{4,3,2,1,0:T(8,128)(2,1)} %get-tuple-element.140), channel_id=1, source_target_pairs={{0,8},{8,16},{16,24},{24,0},{1,9},{9,17},{17,25},{25,1},{2,10},{10... | collective-permute-start | bytes 2359304 | tf_op jit(solution)/shard_map/ppermute | solution.py:935
  714.4 88.0 %collective-permute-start.12 = (bf16[512,1024]{1,0:T(8,128)(2,1)}, bf16[512,1024]{1,0:T(8,128)(2,1)}, u32[]{:S(2)}, u32[]{:S(2)}) collective-permute-start(bf16[512,1024]{1,0:T(8,128)(2,1)} %get-tuple-element.144), channel_id=1, source_target_pairs={{1,0},{0,1},{5,2},{4,3},{3,4},{2,5},{7,6},{6,7},{9,8},{8,9},{13,10... | collective-permute-start | bytes 3145736 | tf_op jit(solution)/shard_map/ppermute | solution.py:865
  714.4 88.0 %collective-permute-start.11 = (bf16[512,1024]{1,0:T(8,128)(2,1)}, bf16[512,1024]{1,0:T(8,128)(2,1)}, u32[]{:S(2)}, u32[]{:S(2)}) collective-permute-start(bf16[512,1024]{1,0:T(8,128)(2,1)} %get-tuple-element.143), channel_id=1, source_target_pairs={{0,0},{1,1},{4,2},{5,3},{2,4},{3,5},{6,6},{7,7},{8,8},{9,9},{12,10... | collective-permute-start | bytes 3145736 | tf_op jit(solution)/shard_map/ppermute | solution.py:864
  728.8 18.5 %collective-permute-start.37 = (bf16[1024,128]{1,0:T(8,128)(2,1)}, bf16[1024,128]{1,0:T(8,128)(2,1)S(1)}, u32[]{:S(2)}, u32[]{:S(2)}) collective-permute-start(bf16[1024,128]{1,0:T(8,128)(2,1)} %get-tuple-element.158), channel_id=1, source_target_pairs={{0,3},{1,0},{2,1},{3,2},{4,7},{5,4},{6,5},{7,6},{8,11},{9,8},{10,9... | collective-permute-start | bytes 786440 | tf_op jit(solution)/shard_map/ppermute | solution.py:935
  742.3 45.6 %collective-permute-start.36 = (bf16[1024,128]{1,0:T(8,128)(2,1)}, bf16[1024,128]{1,0:T(8,128)(2,1)S(1)}, u32[]{:S(2)}, u32[]{:S(2)}) collective-permute-start(bf16[1024,128]{1,0:T(8,128)(2,1)} %get-tuple-element.159), channel_id=1, source_target_pairs={{0,2},{1,3},{2,0},{3,1},{4,6},{5,7},{6,4},{7,5},{8,10},{9,11},{10,... | collective-permute-start | bytes 786440 | tf_op jit(solution)/shard_map/ppermute | solution.py:935
  742.6 45.3 %collective-permute-start.35 = (bf16[1024,128]{1,0:T(8,128)(2,1)S(1)}, bf16[1024,128]{1,0:T(8,128)(2,1)S(1)}, u32[]{:S(2)}, u32[]{:S(2)}) collective-permute-start(bf16[1024,128]{1,0:T(8,128)(2,1)S(1)} %get-tuple-element.157), channel_id=1, source_target_pairs={{0,1},{1,2},{2,3},{3,0},{4,5},{5,6},{6,7},{7,4},{8,9},{9,10},{10,1... | collective-permute-start | bytes 786440 | tf_op jit(solution)/shard_map/ppermute | solution.py:935
  747.3 42.6 %collective-permute-start.19 = (bf16[3,2,128,128]{3,2,1,0:T(8,128)(2,1)S(1)}, bf16[3,2,128,128]{3,2,1,0:T(8,128)(2,1)S(1)}, u32[]{:S(2)}, u32[]{:S(2)}) collective-permute-start(bf16[3,2,128,128]{3,2,1,0:T(8,128)(2,1)S(1)} %get-tuple-element.164), channel_id=1, source_target_pairs={{0,3},{1,0},{2,1},{3,2},{4,7},{5,4},{6,5},{7,6},{8,11},{9,8},{10,9... | collective-permute-start | bytes 589832 | tf_op jit(solution)/shard_map/ppermute | solution.py:935
  787.9 13.3 %collective-permute-start.18 = (bf16[3,2,128,128]{3,2,1,0:T(8,128)(2,1)S(1)}, bf16[3,2,128,128]{3,2,1,0:T(8,128)(2,1)S(1)}, u32[]{:S(2)}, u32[]{:S(2)}) collective-permute-start(bf16[3,2,128,128]{3,2,1,0:T(8,128)(2,1)S(1)} %get-tuple-element.165), channel_id=1, source_target_pairs={{0,2},{1,3},{2,0},{3,1},{4,6},{5,7},{6,4},{7,5},{8,10},{9,11},{10,... | collective-permute-start | bytes 589832 | tf_op jit(solution)/shard_map/ppermute | solution.py:935
  787.9 13.3 %collective-permute-start.17 = (bf16[3,2,128,128]{3,2,1,0:T(8,128)(2,1)S(1)}, bf16[3,2,128,128]{3,2,1,0:T(8,128)(2,1)S(1)}, u32[]{:S(2)}, u32[]{:S(2)}) collective-permute-start(bf16[3,2,128,128]{3,2,1,0:T(8,128)(2,1)S(1)} %get-tuple-element.163), channel_id=1, source_target_pairs={{0,1},{1,2},{2,3},{3,0},{4,5},{5,6},{6,7},{7,4},{8,9},{9,10},{10,1... | collective-permute-start | bytes 589832 | tf_op jit(solution)/shard_map/ppermute | solution.py:935

commit v4 on v3

--- a/solution.py
+++ b/solution.py
@@ -26,43 +26,48 @@
     return (lane < HEAD) if which == 0 else (lane >= HEAD)
 
 
-def attend_fwd_kernel(bk, lo_ref, hi_ref, pad_ref, q_ref, k_ref, v_ref, qcode_ref, kcode_ref, o_ref, lse_ref):
+def attend_fwd_kernel(bk, lo_ref, hi_ref, pad_ref, q_ref, k_ref, v_ref, qcode_ref, kcode_ref, o_ref, lse_ref, v_turned):
     i = pl.program_id(1)
     bq = q_ref.shape[0]
+
+    @pl.when(i == 0)
+    def _():
+        v_turned[...] = v_ref[...].T
+
     q = q_ref[...] * jnp.asarray(0.125, BF16)
     heads = [jnp.where(head_lanes(bq, w), q, jnp.zeros_like(q)) for w in (0, 1)]
-    qcode = jnp.tile(qcode_ref[...], (1, bk // 128))
+    qcode = qcode_ref[...]
     first = i * bq
 
     def run(diagonal):
         def step(t, carry):
             at = pl.multiple_of(t * bk, bk)
-            k = k_ref[pl.ds(at, bk), :]
-            v = v_ref[pl.ds(at, bk), :]
-            mask = qcode == kcode_ref[:, pl.ds(at, bk)]
+            keys = pl.ds(at, bk)
+            k = k_ref[keys, :]
+            mask = jnp.tile(kcode_ref[keys, :], (1, bq // 128)) == qcode
             if diagonal:
-                gap = lax.broadcasted_iota(jnp.int32, (bq, bk), 1) - lax.broadcasted_iota(jnp.int32, (bq, bk), 0)
+                gap = lax.broadcasted_iota(jnp.int32, (bk, bq), 0) - lax.broadcasted_iota(jnp.int32, (bk, bq), 1)
                 mask = mask | (gap == first - at)
             out = []
             for h in (0, 1):
                 top, total, acc = carry[3 * h : 3 * h + 3]
-                s = jnp.where(mask, dot(heads[h], k, NT), NEG_FILL)
-                new = jnp.maximum(top, jnp.max(s, axis=1, keepdims=True))
+                s = jnp.where(mask, dot(k, heads[h], NT), NEG_FILL)
+                new = jnp.maximum(top, jnp.max(s, axis=0, keepdims=True))
                 p = jnp.exp(s - new)
                 old = jnp.exp(top - new)
+                v = v_turned[h * HEAD : (h + 1) * HEAD, keys]
                 out += [
                     new,
-                    total * old + jnp.sum(p, axis=1, keepdims=True),
-                    acc * old + dot(p.astype(BF16), v),
+                    total * old + jnp.sum(p, axis=0, keepdims=True),
+                    acc * old + dot(v, p.astype(BF16)),
                 ]
             return tuple(out)
 
-        one = (jnp.full((bq, 1), NEG_FILL, F32), jnp.zeros((bq, 1), F32), jnp.zeros((bq, PAIR), F32))
+        one = (jnp.full((1, bq), NEG_FILL, F32), jnp.zeros((1, bq), F32), jnp.zeros((HEAD, bq), F32))
         ma, la, aa, mb, lb, ab = lax.fori_loop(lo_ref[i], hi_ref[i], step, one + one)
-        o_ref[...] = jnp.where(head_lanes(bq, 0), aa / la, ab / lb).astype(BF16)
-        lane = lax.broadcasted_iota(jnp.int32, (bq, PAIR), 1)
-        wide = jnp.where(lane == 0, ma + jnp.log(la), mb + jnp.log(lb))
-        lse_ref[...] = wide.T[0:8, :]
+        o_ref[...] = jnp.concatenate([aa / la, ab / lb], axis=0).T.astype(BF16)
+        lse_ref[0:1, :] = ma + jnp.log(la)
+        lse_ref[1:2, :] = mb + jnp.log(lb)
 
     pl.when(pad_ref[i] > 0)(lambda: run(True))
     pl.when(pad_ref[i] == 0)(lambda: run(False))
@@ -87,6 +92,7 @@
 
     k = k_ref[...] * jnp.asarray(0.125, BF16)
     v = v_ref[...]
+    k_turned = k.T
     kh = [jnp.where(head_lanes(bk, w), k, jnp.zeros_like(k)) for w in (0, 1)]
     vh = [jnp.where(head_lanes(bk, w), v, jnp.zeros_like(v)) for w in (0, 1)]
     kcode = jnp.tile(kcode_ref[...], (1, bq // 128))
@@ -102,7 +108,6 @@
             if diagonal:
                 gap = lax.broadcasted_iota(jnp.int32, (bk, bq), 1) - lax.broadcasted_iota(jnp.int32, (bk, bq), 0)
                 mask = mask | (gap == first - at)
-            dq = jnp.zeros((bq, PAIR), F32)
             for h in (0, 1):
                 s = dot(kh[h], q, NT)
                 p = jnp.exp(jnp.where(mask, s - lse_ref[h : h + 1, rows], NEG_FILL))
@@ -111,8 +116,7 @@
                 own = head_lanes(bq, h)
                 dv = dv + dot(p.astype(BF16), jnp.where(own, dc, jnp.zeros_like(dc)))
                 dk = dk + dot(ds, jnp.where(own, q, jnp.zeros_like(q)))
-                dq = dq + dot(ds, kh[h], TN)
-            dq_acc[rows, :] += dq
+                dq_acc[h * HEAD : (h + 1) * HEAD, rows] += dot(k_turned[h * HEAD : (h + 1) * HEAD, :], ds)
             return dk, dv
 
         zero = jnp.zeros((bk, PAIR), F32)
@@ -125,7 +129,7 @@
 
     @pl.when(i == pl.num_programs(1) - 1)
     def _():
-        dq_ref[...] = dq_acc[...].astype(BF16)
+        dq_ref[...] = dq_acc[...].T.astype(BF16)
 
 
 def block_bounds(segment, valid, block, other):
@@ -162,13 +166,14 @@
                 pl.BlockSpec((bq, PAIR), lambda h, i, *_: (i, qkv_at(h, 0))),
                 pl.BlockSpec((length, PAIR), lambda h, i, *_: (0, qkv_at(h, 1))),
                 pl.BlockSpec((length, PAIR), lambda h, i, *_: (0, qkv_at(h, 2))),
-                pl.BlockSpec((bq, 128), lambda h, i, *_: (i, 0)),
-                pl.BlockSpec((1, length), lambda h, i, *_: (0, 0)),
+                pl.BlockSpec((1, bq), lambda h, i, *_: (0, i)),
+                pl.BlockSpec((length, 128), lambda h, i, *_: (0, 0)),
             ],
             out_specs=[
                 pl.BlockSpec((bq, PAIR), lambda h, i, *_: (i, h)),
                 pl.BlockSpec((8, bq), lambda h, i, *_: (h, i)),
             ],
+            scratch_shapes=[pltpu.VMEM((PAIR, length), BF16)],
         ),
         out_shape=[
             jax.ShapeDtypeStruct((length, pairs * PAIR), BF16),
@@ -176,17 +181,19 @@
         ],
         compiler_params=pltpu.CompilerParams(dimension_semantics=("arbitrary", "arbitrary")),
         cost_estimate=pl.CostEstimate(flops=8 * 2 * length * length * PAIR, bytes_accessed=8 * length * width, transcendentals=4 * length * length),
-    )(lo, hi, pad, qkv, qkv, qkv, qwide, kcode[None, :])
-
-
-def attend_bwd(qkv, context, context_grad, lse, segment, valid, bq=256, bk=256):
+    )(lo, hi, pad, qkv, qkv, qkv, qcode[None, :], kwide)
+
+
+def attend_bwd(part, qkv, context, context_grad, lse, segment, valid, bq=256, bk=256):
     length, width = qkv.shape
-    pairs = width // 3 // PAIR
+    pairs = width // 6 // PAIR
+    base = part * pairs
     lo, hi, pad = block_bounds(segment, valid, bk, bq)
     qcode, kcode, qwide, kwide = attention_codes(segment, valid)
     whole = pl.BlockSpec((length, PAIR), lambda h, i, *_: (0, h))
-    part = pl.BlockSpec((bk, PAIR), lambda h, i, *_: (i, h))
-    cols = lambda at: pl.BlockSpec((bk, PAIR), lambda h, i, *_: (i, qkv_at(h, at)))
+    piece = pl.BlockSpec((bk, PAIR), lambda h, i, *_: (i, h))
+    source = pl.BlockSpec((length, PAIR), lambda h, i, *_: (0, base + h))
+    cols = lambda at: pl.BlockSpec((bk, PAIR), lambda h, i, *_: (i, qkv_at(base + h, at)))
     shape = jax.ShapeDtypeStruct((length, pairs * PAIR), BF16)
     return pl.pallas_call(
         functools.partial(attend_bwd_kernel, bq),
@@ -194,13 +201,13 @@
             num_scalar_prefetch=3,
             grid=(pairs, length // bk),
             in_specs=[
-                pl.BlockSpec((length, PAIR), lambda h, i, *_: (0, qkv_at(h, 0))), cols(1), cols(2), whole, whole,
-                pl.BlockSpec((8, length), lambda h, i, *_: (h, 0)),
+                pl.BlockSpec((length, PAIR), lambda h, i, *_: (0, qkv_at(base + h, 0))), cols(1), cols(2), source, source,
+                pl.BlockSpec((8, length), lambda h, i, *_: (base + h, 0)),
                 pl.BlockSpec((1, length), lambda h, i, *_: (0, 0)),
                 pl.BlockSpec((bk, 128), lambda h, i, *_: (i, 0)),
             ],
-            out_specs=[whole, part, part],
-            scratch_shapes=[pltpu.VMEM((length, PAIR), F32), pltpu.VMEM((8, length), F32)],
+            out_specs=[whole, piece, piece],
+            scratch_shapes=[pltpu.VMEM((PAIR, length), F32), pltpu.VMEM((8, length), F32)],
         ),
         out_shape=[shape, shape, shape],
         compiler_params=pltpu.CompilerParams(dimension_semantics=("arbitrary", "arbitrary")),
@@ -234,10 +241,12 @@
         ref[at : at + 1, :] += col_sum(part)
 
 
-def mix_kernel(at_ref, x_ref, c_ref, w_ref, bias_ref, gain_ref, hl_ref, n_ref, r_ref):
+def mix_kernel(at_ref, x_ref, c_ref, w_ref, bias_ref, gain_ref, hl_ref, turned_ref, n_ref, r_ref):
     mixed = x_ref[...].astype(F32) + dot(c_ref[...], w_ref[...]) + bias_ref[0:1, :]
     normed, inverse = norm_stats(mixed)
-    hl_ref[...] = (normed * gain_ref[0:1, :] + bias_ref[1:2, :]).astype(BF16)
+    hl = (normed * gain_ref[0:1, :] + bias_ref[1:2, :]).astype(BF16)
+    hl_ref[...] = hl
+    turned_ref[...] = hl.T
     n_ref[...] = normed
     r_ref[...] = jnp.broadcast_to(inverse, r_ref.shape)
 
@@ -321,9 +330,9 @@
             in_specs=[
                 pl.BlockSpec((block, d), lambda i, at: (at[0] * steps + i, 0)), r(d), fixed(w), fixed(biases), fixed(gains),
             ],
-            out_specs=[r(d), r(d), r(128)],
+            out_specs=[r(d), pl.BlockSpec((d, block), lambda i, at: (0, i)), r(d), r(128)],
         ),
-        out_shape=[sds((n, d)), sds((n, d), F32), sds((n, 128), F32)],
+        out_shape=[sds((n, d)), sds((d, n)), sds((n, d), F32), sds((n, 128), F32)],
         compiler_params=pltpu.CompilerParams(dimension_semantics=("arbitrary",)),
         cost_estimate=pl.CostEstimate(flops=2 * n * d * d, bytes_accessed=12 * n * d, transcendentals=0),
     )(core_at, x, c, w, biases, gains)
@@ -408,22 +417,14 @@
     split_columns(acc, keep_ref, send_ref)
 
 
-def row_grad_kernel(a_ref, b_ref, keep_ref, send_ref, turned, acc):
-    @pl.when(pl.program_id(0) == 0)
-    def _():
-        turned[...] = a_ref[...].T
-
-    acc[...] = dot(turned[...], b_ref[...]).astype(BF16)
+def row_grad_kernel(a_ref, b_ref, keep_ref, send_ref, acc):
+    acc[...] = dot(a_ref[...], b_ref[...]).astype(BF16)
     split_rows(acc, (), keep_ref, send_ref)
 
 
-def qkv_grad_kernel(x_ref, dq_ref, dk_ref, dv_ref, keep_ref, send_ref, sum_ref, turned, acc):
-    @pl.when(pl.program_id(0) == 0)
-    def _():
-        turned[...] = x_ref[...].T
-
+def qkv_grad_kernel(x_ref, dq_ref, dk_ref, dv_ref, keep_ref, send_ref, sum_ref, acc):
     for at, ref in enumerate((dq_ref, dk_ref, dv_ref)):
-        acc[...] = dot(turned[...], ref[...]).astype(BF16)
+        acc[...] = dot(x_ref[...], ref[...]).astype(BF16)
         split_rows(acc, (at,), keep_ref, send_ref)
     sum_ref[0:1, :] = col_sum(dq_ref[...].astype(F32))
     sum_ref[1:2, :] = col_sum(dv_ref[...].astype(F32))
@@ -458,7 +459,7 @@
 
 
 def row_grad(a, b, n_p, n_t, block=512):
-    n, d = a.shape
+    d, n = a.shape
     f = b.shape[1]
     per_t, r = f // n_t, d // (2 * n_p)
     steps = per_t // block
@@ -466,41 +467,38 @@
     shape = sds((n_p, n_t, per_t // 128, r, 128))
     return grad_call(
         row_grad_kernel, (f // block,),
-        [once((n, d)), pl.BlockSpec((n, block), lambda i: (0, i))],
-        ([spec, spec], [shape, shape]),
-        [pltpu.VMEM((d, n), BF16), pltpu.VMEM((d, block), BF16)], 2 * n * f * d, a, b,
-    )
-
-
-def qkv_grad(x, dq, dk, dv, n_p, n_t):
-    n, d = x.shape
+        [once((d, n)), pl.BlockSpec((n, block), lambda i: (0, i))],
+        ([spec, spec], [shape, shape]), [pltpu.VMEM((d, block), BF16)], 2 * n * f * d, a, b,
+    )
+
+
+def qkv_grad(x, dq, dk, dv, n_p):
+    d, n = x.shape
     f = dq.shape[1]
-    half, r = f // (n_t // 2), d // (2 * n_p)
-    spec = pl.BlockSpec((n_p, 1, 3, half // 128, r, 128), lambda i: (0, i, 0, 0, 0, 0))
-    shape = sds((n_p, n_t // 2, 3, half // 128, r, 128))
-    cols = pl.BlockSpec((n, half), lambda i: (0, i))
+    r = d // (2 * n_p)
+    spec = pl.BlockSpec((n_p, 1, 3, f // 128, r, 128), lambda i: (0, 0, 0, 0, 0, 0))
+    shape = sds((n_p, 1, 3, f // 128, r, 128))
     return grad_call(
-        qkv_grad_kernel, (n_t // 2,),
-        [once((n, d)), cols, cols, cols],
-        ([spec, spec, pl.BlockSpec((8, half), lambda i: (0, i))], [shape, shape, sds((8, f), F32)]),
-        [pltpu.VMEM((d, n), BF16), pltpu.VMEM((d, half), BF16)], 6 * n * f * d, x, dq, dk, dv,
-    )
-
-
-def input_pull_kernel(at_ref, dq_ref, dk_ref, dv_ref, w_ref, *refs):
+        qkv_grad_kernel, (1,),
+        [held((d, n)), held((n, f)), held((n, f)), held((n, f))],
+        ([spec, spec, held((8, f))], [shape, shape, sds((8, f), F32)]),
+        [pltpu.VMEM((d, f), BF16)], 6 * n * f * d, x, dq, dk, dv,
+    )
+
+
+def input_pull_kernel(extra, at_ref, *refs):
+    parts, w_ref = refs[:6], refs[6]
     c = w_ref.shape[1] // 6
-    total = None
-    for j in range(6):
-        ref = (dq_ref, dk_ref, dv_ref)[j % 3]
-        part = dot(ref[:, j // 3 * c : (j // 3 + 1) * c], w_ref[:, j * c : (j + 1) * c], NT)
-        total = part if total is None else total + part
-    if len(refs) == 2:
-        total = total + refs[0][...]
+    total = dot(parts[0][...], w_ref[:, :c], NT)
+    for j in range(1, 6):
+        total = total + dot(parts[j][...], w_ref[:, j * c : (j + 1) * c], NT)
+    if extra:
+        total = total + refs[7][...]
     refs[-1][...] = total.astype(refs[-1].dtype)
 
 
-def input_pull(part, core, dq, dk, dv, w, dm=None, block=256):
-    n, f = dq.shape
+def input_pull(half, core, parts, w, dm=None, block=256):
+    n, f = parts[0].shape
     d = w.shape[0]
     steps = n // 2 // block
     cols = pl.BlockSpec((block, f), lambda i, at: (at[0] * steps + i, 0))
@@ -508,17 +506,17 @@
     extra = [] if dm is None else [dm]
     held_w = pl.BlockSpec((d, w.shape[1] // 2), lambda i, at: (0, at[1]), pipeline_mode=pl.Buffered(1))
     return pl.pallas_call(
-        input_pull_kernel,
+        functools.partial(input_pull_kernel, len(extra)),
         grid_spec=pltpu.PrefetchScalarGridSpec(
             num_scalar_prefetch=1,
             grid=(steps,),
-            in_specs=[cols, cols, cols, held_w] + [own] * len(extra),
+            in_specs=[cols] * 6 + [held_w] + [own] * len(extra),
             out_specs=own,
         ),
         out_shape=sds((n // 2, d), BF16 if dm is None else F32),
         compiler_params=pltpu.CompilerParams(dimension_semantics=("arbitrary",)),
-        cost_estimate=pl.CostEstimate(flops=3 * n * f * d, bytes_accessed=8 * n * d, transcendentals=0),
-    )(jnp.stack([part, core]).astype(jnp.int32), dq, dk, dv, w, *extra)
+        cost_estimate=pl.CostEstimate(flops=6 * n * f * d, bytes_accessed=8 * n * d, transcendentals=0),
+    )(jnp.stack([half, core]).astype(jnp.int32), *parts, w, *extra)
 
 
 def small_sum_kernel(n_p, n_t, in_ref, out_ref, pair, pair_sum, plane, plane_sum, column, send_sems, recv_sems):
@@ -792,7 +790,8 @@
     )(x, bias, *shards)
 
 
-def project_kernel(core_ref, x_ref, w_ref, bias_ref, out_ref):
+def project_kernel(core_ref, x_ref, w_ref, bias_ref, out_ref, turned_ref):
+    turned_ref[...] = x_ref[...].T
     out_ref[...] = (dot(x_ref[...], w_ref[...]) + bias_ref[...]).astype(BF16)
 
 
@@ -809,9 +808,9 @@
                 pl.BlockSpec((d, f), lambda i, at: (0, at[0]), pipeline_mode=pl.Buffered(1)),
                 pl.BlockSpec((1, f), lambda i, at: (0, 0)),
             ],
-            out_specs=pl.BlockSpec((block, f), lambda i, at: (i, 0)),
+            out_specs=[pl.BlockSpec((block, f), lambda i, at: (i, 0)), pl.BlockSpec((d, block), lambda i, at: (0, i))],
         ),
-        out_shape=sds((n, f)),
+        out_shape=[sds((n, f)), sds((d, n))],
         compiler_params=pltpu.CompilerParams(dimension_semantics=("arbitrary",)),
         cost_estimate=pl.CostEstimate(flops=2 * n * d * f, bytes_accessed=4 * n * d + 2 * n * f, transcendentals=0),
     )(core_at, x, w, bias)
@@ -860,9 +859,11 @@
         b = lax.ppermute(value[1 - odd], COL, route_b)
         return jnp.where(odd == 0, jnp.concatenate([a, b]), jnp.concatenate([b, a]))
 
-    def give(value):
-        a = lax.ppermute(lax.dynamic_slice_in_dim(value, odd * held_rows, held_rows), COL, back(route_a))
-        b = lax.ppermute(lax.dynamic_slice_in_dim(value, (1 - odd) * held_rows, held_rows), COL, back(route_b))
+    def blocks(value):
+        return [lax.dynamic_slice_in_dim(value, at * held_rows, held_rows) for at in (odd, 1 - odd)]
+
+    def give(a, b):
+        a, b = lax.ppermute(a, COL, back(route_a)), lax.ppermute(b, COL, back(route_b))
         return jnp.where(odd == 0, jnp.stack([a, b]), jnp.stack([b, a]))
 
     def gathered(weight):
@@ -894,64 +895,110 @@
     qv_own = lax.dynamic_slice_in_dim(bias_all[:, :n_qv], 2 * core, 2).reshape(2, 2, -1)
     bias = jnp.stack([qv_own[:, 0], jnp.zeros_like(qv_own[:, 0]), qv_own[:, 1]], axis=1).reshape(1, -1)
     core_at = jnp.reshape(core, (1,)).astype(jnp.int32)
-    qkv = project(core_at, x_full, w_qkv, bias)
+    qkv, x_turned = project(core_at, x_full, w_qkv, bias)
     context, lse = attend_fwd(qkv, segment, valid, 512, 512)
     mine = lax.dynamic_slice_in_dim(context, core * rows, rows)
     other = lax.dynamic_slice_in_dim(context, (1 - core) * rows, rows)
     c_own = by_core(core, mine, swap_cores(other), 1)
-    hl, normed, inverse = mix(core_at, x_full, c_own, w_out, row_biases, norm_gains)
+    hl, hl_turned, normed, inverse = mix(core_at, x_full, c_own, w_out, row_biases, norm_gains)
     active, slope = up(hl, w_up, up_bias_all)
     grad_own = bring(out_grad)
     layer, dr, dz, sums_two = down(active, w_down, normed, grad_own, row_biases, norm_gains)
-    layer_out = give(layer)
+    layer_out = give(*blocks(layer))
+
+    p_bits = [1 << s for s in range(n_p.bit_length() - 1)]
+    t_bits = [2, 1]
+
+    class Total:
+        def __init__(self, parts, downward):
+            lead = [("p", n_p, bit) for bit in reversed(p_bits)] + [("tensor", n_t, bit) for bit in t_bits]
+            lead = lead[: len(lead) - (parts[0].shape[1] == 2)]
+            self.rest = parts[0].shape[2:]
+            self.dims = lead
+            self.parts = [part.reshape((2,) * len(lead) + self.rest) for part in parts]
+            order = list(reversed(p_bits)) if downward else p_bits
+            self.groups = [order[:1], order[1:], t_bits[:1], t_bits[1:]]
+
+        def sum_of(self, pick):
+            total = pick(self.parts[0]).astype(F32)
+            for part in self.parts[1:]:
+                total = total + pick(part).astype(F32)
+            return total
+
+        def cut_one(self, axis, bit):
+            at = [d[0] + str(d[2]) for d in self.dims].index(axis + str(bit))
+            size = self.dims[at][1]
+            self.dims = self.dims[:at] + self.dims[at + 1 :]
+            mine = (lax.axis_index(axis) // bit) % 2
+            side = lambda which: self.sum_of(lambda part: lax.dynamic_index_in_dim(part, which, at, keepdims=False)).astype(BF16)
+            self.live = [side(mine), side(1 - mine)]
+            self.route = (axis, [(i, i ^ bit) for i in range(size)])
+
+        def move(self):
+            self.parts = [self.live[0], lax.ppermute(self.live[1], *self.route)]
+            return self
+
+        def cut(self, group):
+            axis = "p" if group < 2 else "tensor"
+            for j, bit in enumerate(self.groups[group]):
+                if j:
+                    self.move()
+                self.cut_one(axis, bit)
+            return self
+
+    def together(sums, *others):
+        lives, others = lax.optimization_barrier(([s.live for s in sums], others))
+        for s, live in zip(sums, lives):
+            s.live = live
+            s.move()
+        return others
 
     du, up_sum = slope_pull(dz, w_down, slope)
+    active, du = lax.optimization_barrier((active, du))
+    down_keep, down_send = col_grad(active, dz, n_p, n_t)
+    down_send, du = lax.optimization_barrier((down_send, du))
+    down_recv = swap_cores(down_send)
+    up_keep, up_send = row_grad(hl_turned, du, n_p, n_t)
+    up_recv = swap_cores(up_send)
+    down_sum = Total([down_keep, down_recv], False).cut(0)
+    (du,) = together([down_sum], du)
     dm, da, sums_one = mix_pull(du, w_up, dr, normed, inverse, norm_gains)
-    down_keep, down_send = col_grad(active, dz, n_p, n_t)
-    down_recv = swap_cores(down_send)
-    up_keep, up_send = row_grad(hl, du, n_p, n_t)
-    up_recv = swap_cores(up_send)
-    out_keep, out_send = col_grad(c_own, da, n_p, n_t)
-    out_recv = swap_cores(out_send)
     dc = dot(da, w_out, NT).astype(BF16)
     mine = lax.dynamic_slice_in_dim(dc, core * own, own, 1)
     other = lax.dynamic_slice_in_dim(dc, (1 - core) * own, own, 1)
-    dc_full = by_core(core, mine, swap_cores(other), 0)
-
-    def pieces(size, at, *parts):
-        pick = lambda part, to: lax.dynamic_index_in_dim(part, to, 0, keepdims=False)
-        out = []
-        for r in range(size):
-            to = (at + r) % size
-            total = pick(parts[0], to)
-            for part in parts[1:]:
-                total = (total.astype(F32) + pick(part, to).astype(F32)).astype(BF16)
-            out.append(total)
-        return out
-
-    def collect(axis, size, own_piece, *others):
-        total = own_piece.astype(F32)
-        for r, piece in enumerate(others, 1):
-            total = total + lax.ppermute(piece, axis, [(i, (i + r) % size) for i in range(size)]).astype(F32)
-        return total
-
-    p_at = lax.axis_index("p")
-    ffn_parts = [
-        pieces(n_p, p_at, down_keep, down_recv), pieces(n_p, p_at, up_keep, up_recv), pieces(n_p, p_at, out_keep, out_recv),
-    ]
-    ffn_parts, dc_full = lax.optimization_barrier((ffn_parts, dc_full))
-    ffn_sums = [collect("p", n_p, *part).astype(BF16) for part in ffn_parts]
-
-    dq, dk, dv = attend_bwd(qkv, context, dc_full, lse, segment, valid, 256, 512)
-    dx_other = swap_cores(input_pull(1 - core, core, dq, dk, dv, w_qkv))
-    qkv_keep, qkv_send, qv_sum = qkv_grad(x_full, dq, dk, dv, n_p, n_t)
-    qkv_recv = swap_cores(qkv_send)
-    dx_mine = input_pull(core, core, dq, dk, dv, w_qkv, dm)
-    input_grad = give((dx_mine + dx_other.astype(F32)).astype(BF16)).astype(F32)
-    qkv_sum = collect("p", n_p, *pieces(n_p, p_at, by_core(core, qkv_keep, qkv_recv, 1))).astype(BF16)
-    down_total, up_total, out_total, qkv_total = [
-        collect("tensor", n_t, *pieces(n_t, tensor, part)) for part in (*ffn_sums, qkv_sum)
-    ]
+    dc_recv = swap_cores(other)
+    up_sums = Total([up_keep, up_recv], True).cut(0)
+    out_keep, out_send = col_grad(c_own, da, n_p, n_t)
+    out_recv = swap_cores(out_send)
+    dc_full = by_core(core, mine, dc_recv, 0)
+    down_sum.cut(1)
+    dc_full, layer_out = together([down_sum, up_sums], dc_full, layer_out)
+
+    first = attend_bwd(0, qkv, context, dc_full, lse, segment, valid, 512, 256)
+    out_sum = Total([out_keep, out_recv], False)
+    keep, send, sum_first = qkv_grad(x_turned, *first, n_p)
+    first_sum = Total([by_core(core, keep, swap_cores(send), 1)], True)
+    (dc_full,) = together([down_sum.cut(2), up_sums.cut(1), out_sum.cut(0), first_sum.cut(0)], dc_full)
+    second = attend_bwd(1, qkv, context, dc_full, lse, segment, valid, 512, 256)
+    (second,) = together([down_sum.cut(3), up_sums.cut(2), out_sum.cut(1), first_sum.cut(1)], second)
+
+    dx_other = swap_cores(input_pull(1 - core, core, (*first, *second), w_qkv))
+    dx_mine = input_pull(core, core, (*first, *second), w_qkv, dm)
+    dx = (dx_mine + dx_other.astype(F32)).astype(BF16)
+    dx, second = lax.optimization_barrier((blocks(dx), second))
+    input_grad = give(*dx).astype(F32)
+    keep, send, sum_second = qkv_grad(x_turned, *second, n_p)
+    second_sum = Total([by_core(core, keep, swap_cores(send), 1)], True).cut(0).move()
+    first_sum.cut(2).move()
+    up_sums.cut(3).move()
+    out_sum.cut(2).move().cut(3).move()
+    second_sum.cut(1).move().cut(2).move()
+    qv_sum = jnp.concatenate([sum_first, sum_second], axis=1)
+    same = lambda part: part
+    down_total, up_total, out_total = down_sum.sum_of(same), up_sums.sum_of(same), out_sum.sum_of(same)
+    pair = [first_sum.sum_of(same), second_sum.sum_of(same)]
+    moved = lax.ppermute(jnp.where(odd == 0, pair[1], pair[0]).astype(BF16), "tensor", [(i, i ^ 1) for i in range(n_t)])
+    qkv_total = jnp.where(odd == 0, pair[0], pair[1]) + moved.astype(F32)
     up_total = up_total.transpose(1, 0, 2).reshape(up_weight.shape)
     qkv_total = qkv_total.transpose(0, 2, 1, 3).reshape(qkv_weight.shape)
 

time: 818 us -> 763 us (0.933)
  waiting for transfers between devices: 101 us -> 55.6 us
  other arithmetic: 55.1 us -> 75.8 us
  Pallas kernels: 506 us -> 488 us
  local copies, waits for them, and re-layouts: 30.6 us -> 20.6 us
    ppermute x28 -> x23, waiting for transfers between devices: 101 us -> 55.5 us  [the longest x18 54.3 us: move(): self.parts = [self.live[0], lax.ppermute(self.live[1], *self.route)]]
    pallas_call x1, Pallas kernels: 69 us -> 47.2 us  [small_sum(): pl.pallas_call(functools.partial(small_sum_kernel, n_p, n_t), out_shape=s...]
    convert_element_type x9 -> x19, other arithmetic: 27.8 us -> 45 us  [the longest x16 36.1 us: cut_one(): self.sum_of(lambda part: lax.dynamic_index_in_dim(part, which, at, keepdi...]
    pallas_call x1 -> x2, Pallas kernels: 65.8 us -> 72.3 us  [attend_bwd(): pl.pallas_call(functools.partial(attend_bwd_kernel, bq), grid_spec=pltpu....]
    ppermute x28 -> x23, starting transfers between devices: 88.5 us -> 82.7 us  [the longest x18 71.4 us: move(): self.parts = [self.live[0], lax.ppermute(self.live[1], *self.route)]]
    pallas_call x4 -> x5, Pallas kernels: 56.4 us -> 58 us  [grad_call(): pl.pallas_call(kernel, grid=grid, in_specs=ins, out_specs=outs[0], out_sh...]
  transfers between devices with their start and end apart: 38 -> 34, of which waited for: 12 -> 6; matrix products, arithmetic and copies ran while one was open for 9% -> 11% of each run, Pallas kernels for 54% -> 51%
where the time goes in v4:
time: 763 us; the launch traced here: 750 us
  Pallas kernels  488 us (64%)
  starting transfers between devices  105 us (14%)
  other arithmetic  75.8 us (10%)
  waiting for transfers between devices  55.6 us (7%)
  local copies, waits for them, and re-layouts  20.6 us (3%)
    pallas_call x1, Pallas kernels, start_gather(): pl.pallas_call(functools.partial(start_kernel, n_p, n_t, kinds), out_shap...  139 us
    pallas_call x4, Pallas kernels, call(): pl.pallas_call(kernel, grid=grid, in_specs=ins, out_specs=outs[0], out_sh...  83.7 us
    pallas_call x2, Pallas kernels, attend_bwd(): pl.pallas_call(functools.partial(attend_bwd_kernel, bq), grid_spec=pltpu....  72.3 us
    ppermute x18, starting transfers between devices, move(): self.parts = [self.live[0], lax.ppermute(self.live[1], *self.route)]  71.4 us
    pallas_call x5, Pallas kernels, grad_call(): pl.pallas_call(kernel, grid=grid, in_specs=ins, out_specs=outs[0], out_sh...  58 us
    ppermute x18, waiting for transfers between devices, move(): self.parts = [self.live[0], lax.ppermute(self.live[1], *self.route)]  54.3 us
    pallas_call x1, Pallas kernels, attend_fwd(): pl.pallas_call(functools.partial(attend_fwd_kernel, bk), grid_spec=pltpu....  48.7 us
    pallas_call x1, Pallas kernels, small_sum(): pl.pallas_call(functools.partial(small_sum_kernel, n_p, n_t), out_shape=s...  47.2 us
  transfers between devices with their start and end apart: 34, of which 6 were waited for; matrix products, arithmetic and copies ran while one was open for 11% of the time, Pallas kernels for 51%

profile of v4, /device:TPU:0, one launch (start us, length us, event | category | flops | bytes accessed | tf_op | source)
XLA Modules:
  0.0 750.4 jit_solution(16923443064612557178)
XLA Ops:
  4.1 139.3 %shard_map.195 = (bf16[2048,1024]{1,0:T(8,128)(2,1)}, f32[4,12,128]{2,1,0:T(8,128)}, bf16[1024,3072]{1,0:T(8,128)(2,1)}, bf16[1024,1024]{1,0:T(8,128)(2,1)}, bf1...) custom-call(bf16[2,512,1024]{2,1,0:T(8,128)(2,1)} %refs_0_.1, f32[12,128]{1,0:T(8,128)} %maximum_bitcast_fusion.1.refs_1_, ...), custom_call_target="tpu_custom_call" | custom-call | tf_op jit(solution)/shard_map/pallas_call | solution.py:781
  144.6 1.9 collective-permute-start.2
  146.5 15.3 %collective-permute-start.3 = (bf16[512,1024]{1,0:T(8,128)(2,1)S(1)}, bf16[512,1024]{1,0:T(8,128)(2,1)}, u32[]{:S(2)}, u32[]{:S(2)}) collective-permute-start(bf16[512,1024]{1,0:T(8,128)(2,1)S(1)} %get-tuple-element.205), channel_id=1, source_target_pairs={{0,1},{1,0},{2,5},{3,4},{4,3},{5,2},{6,7},{7,6},{8,9},{9,8},{10,13... | collective-permute-start | bytes 3145736 | tf_op jit(solution)/shard_map/ppermute | solution.py:859
  162.6 12.3 %shard_map.196 = (bf16[2048,1536]{1,0:T(8,128)(2,1)}, bf16[1024,2048]{1,0:T(8,128)(2,1)}) custom-call(s32[1]{0:T(128)} %bitcast.core_ref.at_ref, bf16[2048,1024]{1,0:T(8,128)(2,1)} %get-tuple-element.94.x_ref, bf16[1024,3072]{1,0:T(8,128)(2,1)} %get-tuple-element.95.w_ref.refs_6_, f32[1,1536]{1,0:T(1,128)} %reshape.272.bias_ref), custom_call_target="tpu_custom_call" | custom-call | flops 6442450944 | bytes 14680064 | tf_op jit(solution)/shard_map/pallas_call | solution.py:801
  176.8 1.3 broadcast_in_dim.11.kcode_ref
  178.1 48.7 %shard_map.197 = (bf16[2048,512]{1,0:T(8,128)(2,1)}, f32[32,2048]{1,0:T(8,128)}) custom-call(s32[4]{0:T(128)} %get-tuple-element.234.lo_ref, s32[4]{0:T(128)} %get-tuple-element.233.hi_ref, s32[4]{0:T(128)} %reduce_sum.56.pad_ref, bf16[2048,1536]{1,0:T(8,128)(2,1)} %get-tuple-element.97.q_ref.k_ref.v_ref, ...), custom_call_target="tpu_custom_call" | custom-call | flops 8589934592 | bytes 25165824 | tf_op jit(solution)/shard_map/pallas_call | solution.py:160
  226.8 2.6 constant_dynamic-slice_fusion.11
  229.5 2.6 collective-permute-start.1
  232.7 3.8 maximum_select_fusion.1.e_ref
  236.5 3.6 maximum_select_fusion.c_ref.a_ref
  240.2 8.6 %shard_map.198 = (bf16[1024,1024]{1,0:T(8,128)(2,1)}, bf16[1024,1024]{1,0:T(8,128)(2,1)}, f32[1024,1024]{1,0:T(8,128)}, f32[1024,128]{1,0:T(8,128)}) custom-call(s32[1]{0:T(128)} %bitcast.core_ref.at_ref, bf16[2048,1024]{1,0:T(8,128)(2,1)} %get-tuple-element.94.x_ref, bf16[1024,1024]{1,0:T(8,128)(2,1)} %maximum_select_fusion.c_ref.a_ref, ...), custom_call_target="tpu_custom_call" | custom-call | flops 2147483648 | bytes 12582912 | tf_op jit(solution)/shard_map/pallas_call | solution.py:325
  248.8 24.7 %shard_map.199 = (bf16[1024,4096]{1,0:T(8,128)(2,1)}, bf16[1024,4096]{1,0:T(8,128)(2,1)}) custom-call(bf16[1024,1024]{1,0:T(8,128)(2,1)} %get-tuple-element.100.h_ref, bf16[1024,4096]{1,0:T(8,128)(2,1)} %get-tuple-element.101.w_ref, f32[1,4096]{1,0:T(1,128)} %bitcast.203), custom_call_target="tpu_custom_call" | custom-call | flops 8589934592 | bytes 25165824 | tf_op jit(solution)/shard_map/pallas_call | solution.py:293
  273.5 19.2 %shard_map.200 = (bf16[1024,1024]{1,0:T(8,128)(2,1)}, f32[1024,1024]{1,0:T(8,128)}, bf16[1024,1024]{1,0:T(8,128)(2,1)}, f32[8,1024]{1,0:T(8,128)}) custom-call(bf16[1024,4096]{1,0:T(8,128)(2,1)} %get-tuple-element.109.g_ref.a_ref, bf16[4096,1024]{1,0:T(8,128)(2,1)} %get-tuple-element.103.w_ref, f32[1024,1024]{1,0:T(8,128)} %get-tuple-element.104.n_ref, ...), custom_call_target="tpu_custom_call" | custom-call | flops 8589934592 | bytes 16777216 | tf_op jit(solution)/shard_map/pallas_call | solution.py:293
  292.8 22.0 %shard_map.201 = (bf16[1024,4096]{1,0:T(8,128)(2,1)}, f32[8,4096]{1,0:T(8,128)}) custom-call(bf16[1024,1024]{1,0:T(8,128)(2,1)} %get-tuple-element.106.dz_ref.b_ref, bf16[4096,1024]{1,0:T(8,128)(2,1)} %get-tuple-element.103.w_ref, bf16[1024,4096]{1,0:T(8,128)(2,1)} %get-tuple-element.107.slope_ref), custom_call_target="tpu_custom_call" | custom-call | flops 8589934592 | bytes 25165824 | tf_op jit(solution)/shard_map/pallas_call | solution.py:293
  314.7 15.5 %shard_map.202 = (bf16[4,4,1024,128]{3,2,1,0:T(8,128)(2,1)}, bf16[4,4,1024,128]{3,2,1,0:T(8,128)(2,1)}) custom-call(bf16[1024,4096]{1,0:T(8,128)(2,1)} %get-tuple-element.109.g_ref.a_ref, bf16[1024,1024]{1,0:T(8,128)(2,1)} %get-tuple-element.106.dz_ref.b_ref), custom_call_target="tpu_custom_call" | custom-call | flops 8589934592 | bytes 16777216 | tf_op jit(solution)/shard_map/pallas_call | solution.py:434
  330.5 15.2 %shard_map.203 = (bf16[4,4,8,128,128]{4,3,2,1,0:T(8,128)(2,1)}, bf16[4,4,8,128,128]{4,3,2,1,0:T(8,128)(2,1)}) custom-call(bf16[1024,1024]{1,0:T(8,128)(2,1)} %get-tuple-element.117.a_ref, bf16[1024,4096]{1,0:T(8,128)(2,1)} %get-tuple-element.120.b_ref.du_ref), custom_call_target="tpu_custom_call" | custom-call | flops 8589934592 | bytes 16777216 | tf_op jit(solution)/shard_map/pallas_call | solution.py:434
  346.0 1.5 constant_dynamic-slice_fusion.7
  347.5 9.6 %collective-permute-start.8 = (bf16[512,1024]{1,0:T(8,128)(2,1)}, bf16[512,1024]{1,0:T(8,128)(2,1)}, u32[]{:S(2)}, u32[]{:S(2)}) collective-permute-start(bf16[512,1024]{1,0:T(8,128)(2,1)} %get-tuple-element.200), channel_id=1, source_target_pairs={{0,0},{1,1},{4,2},{5,3},{2,4},{3,5},{6,6},{7,7},{8,8},{9,9},{12,10... | collective-permute-start | bytes 3145736 | tf_op jit(solution)/shard_map/ppermute | solution.py:866
  357.2 5.4 fusion.1
  362.6 21.0 %collective-permute-start.5 = (bf16[2,2,2,1024,128]{4,3,2,1,0:T(8,128)(2,1)}, bf16[2,2,2,1024,128]{4,3,2,1,0:T(8,128)(2,1)}, u32[]{:S(2)}, u32[]{:S(2)}) collective-permute-start(bf16[2,2,2,1024,128]{4,3,2,1,0:T(8,128)(2,1)} %get-tuple-element.116), channel_id=1, source_target_pairs={{0,8},{8,0},{16,24},{24,16},{1,9},{9,1},{17,25},{25,17},{2,10},{10... | collective-permute-start | bytes 6291464 | tf_op jit(solution)/shard_map/ppermute | solution.py:938
  383.5 17.7 %shard_map.204 = (f32[1024,1024]{1,0:T(8,128)}, bf16[1024,1024]{1,0:T(8,128)(2,1)}, f32[8,1024]{1,0:T(8,128)}) custom-call(bf16[1024,4096]{1,0:T(8,128)(2,1)} %get-tuple-element.120.b_ref.du_ref, bf16[1024,4096]{1,0:T(8,128)(2,1)} %get-tuple-element.101.w_ref, f32[1024,1024]{1,0:T(8,128)} %get-tuple-element.121.dr_ref, ...), custom_call_target="tpu_custom_call" | custom-call | flops 8589934592 | bytes 16777216 | tf_op jit(solution)/shard_map/pallas_call | solution.py:293
  401.3 4.0 convolution_convert_fusion
  408.2 3.9 maximum_select_fusion.3
  412.1 6.4 shard_map.206
  419.1 7.0 fusion.3
  426.1 3.6 maximum_select_fusion.2.dc_ref
  429.7 3.0 fusion.6
  432.7 5.8 collective-permute-start.11
  438.5 36.1 %shard_map.205 = (bf16[2048,256]{1,0:T(8,128)(2,1)}, bf16[2048,256]{1,0:T(8,128)(2,1)}, bf16[2048,256]{1,0:T(8,128)(2,1)}) custom-call(s32[8]{0:T(128)} %get-tuple-element.232.lo_ref, s32[8]{0:T(128)} %get-tuple-element.231.hi_ref, s32[8]{0:T(128)} %reduce_sum.62.pad_ref, bf16[2048,1536]{1,0:T(8,128)(2,1)} %get-tuple-element.97.q_ref.k_ref.v_ref, ...), custom_call_target="tpu_custom_call" | custom-call | flops 21474836480 | bytes 50331648 | tf_op jit(solution)/shard_map/pallas_call | solution.py:198
  474.6 10.3 %shard_map.207 = (bf16[4,1,3,2,128,128]{5,4,3,2,1,0:T(8,128)(2,1)}, bf16[4,1,3,2,128,128]{5,4,3,2,1,0:T(8,128)(2,1)}, f32[8,256]{1,0:T(8,128)}) custom-call(bf16[1024,2048]{1,0:T(8,128)(2,1)} %get-tuple-element.137.x_ref, bf16[2048,256]{1,0:T(8,128)(2,1)} %get-tuple-element.128.dq_ref.refs_0_, bf16[2048,256]{1,0:T(8,128)(2,1)} %get-tuple-element.129.dk_ref.refs_1_, ...), custom_call_target="tpu_custom_call" | custom-call | flops 3221225472 | bytes 6291456 | tf_op jit(solution)/shard_map/pallas_call | solution.py:434
  485.2 12.6 %collective-permute-start.10 = (bf16[2,2,1024,128]{3,2,1,0:T(8,128)(2,1)}, bf16[2,2,1024,128]{3,2,1,0:T(8,128)(2,1)}, u32[]{:S(2)}, u32[]{:S(2)}) collective-permute-start(bf16[2,2,1024,128]{3,2,1,0:T(8,128)(2,1)} %get-tuple-element.132), channel_id=1, source_target_pairs={{0,16},{8,24},{16,0},{24,8},{1,17},{9,25},{17,1},{25,9},{2,18},{10... | collective-permute-start | bytes 3145736 | tf_op jit(solution)/shard_map/ppermute | solution.py:938
  498.4 2.8 fusion.14
  501.2 1.6 maximum_select_fusion.5
  504.9 16.5 %collective-permute-done.10 = bf16[2,2,1024,128]{3,2,1,0:T(8,128)(2,1)} collective-permute-done((bf16[2,2,1024,128]{3,2,1,0:T(8,128)(2,1)}, bf16[2,2,1024,128]{3,2,1,0:T(8,128)(2,1)}, u32[]{:S(2)}, u32[]{:S(2)}) %collective-permute-start.10) | collective-permute-done | bytes 1048608 | tf_op jit(solution)/shard_map/ppermute | solution.py:938
  521.4 2.5 fusion.12
  523.9 3.4 fusion.8
  527.3 1.7 collective-permute-start.17
  529.7 1.3 collective-permute-start.15
  531.0 2.5 collective-permute-start.14
  533.5 36.2 %shard_map.208 = (bf16[2048,256]{1,0:T(8,128)(2,1)}, bf16[2048,256]{1,0:T(8,128)(2,1)}, bf16[2048,256]{1,0:T(8,128)(2,1)}) custom-call(s32[8]{0:T(128)} %get-tuple-element.232.lo_ref, s32[8]{0:T(128)} %get-tuple-element.231.hi_ref, s32[8]{0:T(128)} %reduce_sum.62.pad_ref, bf16[2048,1536]{1,0:T(8,128)(2,1)} %get-tuple-element.97.q_ref.k_ref.v_ref, ...), custom_call_target="tpu_custom_call" | custom-call | flops 21474836480 | bytes 50331648 | tf_op jit(solution)/shard_map/pallas_call | solution.py:198
  569.8 1.9 fusion.23
  571.7 2.0 fusion.21
  573.7 2.1 fusion.19
  575.8 2.4 fusion.16
  578.2 8.4 %shard_map.210 = bf16[1024,1024]{1,0:T(8,128)(2,1)} custom-call(s32[2]{0:T(128)} %pad_add_fusion.1.at_ref, bf16[2048,256]{1,0:T(8,128)(2,1)} %get-tuple-element.128.dq_ref.refs_0_, bf16[2048,256]{1,0:T(8,128)(2,1)} %get-tuple-element.129.dk_ref.refs_1_, bf16[2048,256]{1,0:T(8,128)(2,1)} %get-tuple-element.130.dv_ref.refs_2_, ...), custom_call_target="tpu_custom_call" | custom-call | flops 3221225472 | bytes 16777216 | tf_op jit(solution)/shard_map/pallas_call | solution.py:508
  587.2 9.5 %shard_map.209 = f32[1024,1024]{1,0:T(8,128)} custom-call(s32[2]{0:T(128)} %pad_add_fusion.at_ref, bf16[2048,256]{1,0:T(8,128)(2,1)} %get-tuple-element.128.dq_ref.refs_0_, bf16[2048,256]{1,0:T(8,128)(2,1)} %get-tuple-element.129.dk_ref.refs_1_, bf16[2048,256]{1,0:T(8,128)(2,1)} %get-tuple-element.130.dv_ref.refs_2_, ...), custom_call_target="tpu_custom_call" | custom-call | flops 3221225472 | bytes 16777216 | tf_op jit(solution)/shard_map/pallas_call | solution.py:508
  596.7 3.0 add_convert_fusion
  599.8 10.6 %shard_map.211 = (bf16[4,1,3,2,128,128]{5,4,3,2,1,0:T(8,128)(2,1)}, bf16[4,1,3,2,128,128]{5,4,3,2,1,0:T(8,128)(2,1)}, f32[8,256]{1,0:T(8,128)}) custom-call(bf16[1024,2048]{1,0:T(8,128)(2,1)} %get-tuple-element.137.x_ref, bf16[2048,256]{1,0:T(8,128)(2,1)} %get-tuple-element.160.refs_3_.dq_ref, bf16[2048,256]{1,0:T(8,128)(2,1)} %get-tuple-element.161.refs_4_.dk_ref, ...), custom_call_target="tpu_custom_call" | custom-call | flops 3221225472 | bytes 6291456 | tf_op jit(solution)/shard_map/pallas_call | solution.py:434
  611.0 14.0 %collective-permute-start.28 = (bf16[2,2,256,128]{3,2,1,0:T(8,128)(2,1)}, bf16[2,2,256,128]{3,2,1,0:T(8,128)(2,1)}, u32[]{:S(2)}, u32[]{:S(2)}) collective-permute-start(bf16[2,2,256,128]{3,2,1,0:T(8,128)(2,1)} %get-tuple-element.171), channel_id=1, source_target_pairs={{0,16},{8,24},{16,0},{24,8},{1,17},{9,25},{17,1},{25,9},{2,18},{10... | collective-permute-start | bytes 786440 | tf_op jit(solution)/shard_map/ppermute | solution.py:938
  629.0 1.3 collective-permute-start.31
  630.3 3.4 collective-permute-start.21
  635.4 1.9 convert_add_fusion.3
  637.3 1.6 maximum_select_fusion.6
  639.0 1.6 collective-permute-start.24
  640.6 20.0 %collective-permute-done.29 = bf16[2,256,128]{2,1,0:T(8,128)(2,1)S(1)} collective-permute-done((bf16[2,256,128]{2,1,0:T(8,128)(2,1)S(1)}, bf16[2,256,128]{2,1,0:T(8,128)(2,1)S(1)}, u32[]{:S(2)}, u32[]{:S(2)}) %collective-permute-start.29) | collective-permute-done | bytes 131104 | tf_op jit(solution)/shard_map/ppermute | solution.py:938
  660.8 2.1 collective-permute-start.32
  663.7 2.0 collective-permute-done.30
  666.4 6.7 collective-permute-done.32
  674.0 1.6 collective-permute-start.19
  676.6 2.6 collective-permute-start.25
  679.9 47.2 %shard_map.212 = f32[96,128]{1,0:T(8,128)} custom-call(f32[96,128]{1,0:T(8,128)} %maximum_bitcast_fusion.in_ref), custom_call_target="tpu_custom_call" | custom-call | tf_op jit(solution)/shard_map/pallas_call | solution.py:562
  731.7 9.0 %collective-permute-done.26 = bf16[3,2,128,128]{3,2,1,0:T(8,128)(2,1)} collective-permute-done((bf16[3,2,128,128]{3,2,1,0:T(8,128)(2,1)}, bf16[3,2,128,128]{3,2,1,0:T(8,128)(2,1)}, u32[]{:S(2)}, u32[]{:S(2)}) %collective-permute-start.26) | collective-permute-done | bytes 196640 | tf_op jit(solution)/shard_map/ppermute | solution.py:938
  742.1 4.7 fusion.4
  748.0 1.9 copy_bitcast_fusion.4
  (149 shorter events, 34.1 us)
Async XLA Ops:
  0.6 142.8 %copy-start.4 = (bf16[2,512,1024]{2,1,0:T(8,128)(2,1)S(1)}, bf16[2,512,1024]{2,1,0:T(8,128)(2,1)}, u32[]{:S(2)}) copy-start(bf16[2,512,1024]{2,1,0:T(8,128)(2,1)} %param.23) | copy-start | bytes 6291460
  1.5 173.4 %collective-permute-start = (s32[2,2048]{1,0:T(2,128)S(1)}, s32[2,2048]{1,0:T(2,128)S(1)}, u32[]{:S(2)}, u32[]{:S(2)}) collective-permute-start(s32[2,2048]{1,0:T(2,128)S(1)} %fusion.36), channel_id=1, source_target_pairs={{0,4},{4,0},{1,5},{5,1},{2,6},{6,2},{3,7},{7,3},{8,12},{12,8},{9,1... | collective-permute-start | bytes 49160 | tf_op jit(solution)/shard_map/ppermute | solution.py:820
  143.4 18.4 %copy-start.14 = (f32[4,12,128]{2,1,0:T(8,128)S(1)}, f32[4,12,128]{2,1,0:T(8,128)}, u32[]{:S(2)}) copy-start(f32[4,12,128]{2,1,0:T(8,128)} %get-tuple-element.96) | copy-start | bytes 73732
  144.6 88.1 %collective-permute-start.2 = (bf16[512,1024]{1,0:T(8,128)(2,1)}, bf16[512,1024]{1,0:T(8,128)(2,1)S(1)}, u32[]{:S(2)}, u32[]{:S(2)}) collective-permute-start(bf16[512,1024]{1,0:T(8,128)(2,1)} %get-tuple-element.204), channel_id=1, source_target_pairs={{0,0},{1,1},{2,4},{3,5},{4,2},{5,3},{6,6},{7,7},{8,8},{9,9},{10,12... | collective-permute-start | bytes 3145736 | tf_op jit(solution)/shard_map/ppermute | solution.py:858
  146.5 86.2 %collective-permute-start.3 = (bf16[512,1024]{1,0:T(8,128)(2,1)S(1)}, bf16[512,1024]{1,0:T(8,128)(2,1)}, u32[]{:S(2)}, u32[]{:S(2)}) collective-permute-start(bf16[512,1024]{1,0:T(8,128)(2,1)S(1)} %get-tuple-element.205), channel_id=1, source_target_pairs={{0,1},{1,0},{2,5},{3,4},{4,3},{5,2},{6,7},{7,6},{8,9},{9,8},{10,13... | collective-permute-start | bytes 3145736 | tf_op jit(solution)/shard_map/ppermute | solution.py:859
  175.1 3.1 copy-start.12
  229.5 7.0 collective-permute-start.1
  330.3 26.9 %collective-permute-start.4 = (bf16[4,4,1024,128]{3,2,1,0:T(8,128)(2,1)}, bf16[4,4,1024,128]{3,2,1,0:T(8,128)(2,1)}, u32[]{:S(2)}, u32[]{:S(2)}) collective-permute-start(bf16[4,4,1024,128]{3,2,1,0:T(8,128)(2,1)} %get-tuple-element.113), channel_id=1, source_target_pairs={{0,4},{4,0},{1,5},{5,1},{2,6},{6,2},{3,7},{7,3},{8,12},{12,8},{9,1... | collective-permute-start | bytes 12582920 | tf_op jit(solution)/shard_map/ppermute | solution.py:820
  330.5 15.6 %copy-start.13 = (s32[1,2048]{1,0:T(1,128)S(1)}, s32[1,2048]{1,0:T(1,128)}, u32[]{:S(2)}) copy-start(s32[1,2048]{1,0:T(1,128)} %copy-done.12) | copy-start | bytes 24580
  330.5 15.6 %copy-start.5 = (bf16[1024,1024]{1,0:T(8,128)(2,1)S(1)}, bf16[1024,1024]{1,0:T(8,128)(2,1)}, u32[]{:S(2)}) copy-start(bf16[1024,1024]{1,0:T(8,128)(2,1)} %get-tuple-element.124) | copy-start | bytes 6291460
  345.6 73.5 %collective-permute-start.6 = (bf16[4,4,8,128,128]{4,3,2,1,0:T(8,128)(2,1)}, bf16[4,4,8,128,128]{4,3,2,1,0:T(8,128)(2,1)}, u32[]{:S(2)}, u32[]{:S(2)}) collective-permute-start(bf16[4,4,8,128,128]{4,3,2,1,0:T(8,128)(2,1)} %get-tuple-element.119), channel_id=1, source_target_pairs={{0,4},{4,0},{1,5},{5,1},{2,6},{6,2},{3,7},{7,3},{8,12},{12,8},{9,1... | collective-permute-start | bytes 12582920 | tf_op jit(solution)/shard_map/ppermute | solution.py:820
  346.0 11.1 %copy-start.1 = (bf16[4,4,1024,128]{3,2,1,0:T(8,128)(2,1)S(1)}, bf16[4,4,1024,128]{3,2,1,0:T(8,128)(2,1)}, u32[]{:S(2)}) copy-start(bf16[4,4,1024,128]{3,2,1,0:T(8,128)(2,1)} %get-tuple-element.110) | copy-start | bytes 12582916
  347.5 60.7 %collective-permute-start.8 = (bf16[512,1024]{1,0:T(8,128)(2,1)}, bf16[512,1024]{1,0:T(8,128)(2,1)}, u32[]{:S(2)}, u32[]{:S(2)}) collective-permute-start(bf16[512,1024]{1,0:T(8,128)(2,1)} %get-tuple-element.200), channel_id=1, source_target_pairs={{0,0},{1,1},{4,2},{5,3},{2,4},{3,5},{6,6},{7,7},{8,8},{9,9},{12,10... | collective-permute-start | bytes 3145736 | tf_op jit(solution)/shard_map/ppermute | solution.py:866
  357.1 51.1 %collective-permute-start.9 = (bf16[512,1024]{1,0:T(8,128)(2,1)}, bf16[512,1024]{1,0:T(8,128)(2,1)}, u32[]{:S(2)}, u32[]{:S(2)}) collective-permute-start(bf16[512,1024]{1,0:T(8,128)(2,1)} %get-tuple-element.201), channel_id=1, source_target_pairs={{1,0},{0,1},{5,2},{4,3},{3,4},{2,5},{7,6},{6,7},{9,8},{8,9},{13,10... | collective-permute-start | bytes 3145736 | tf_op jit(solution)/shard_map/ppermute | solution.py:866
  362.6 67.1 %collective-permute-start.5 = (bf16[2,2,2,1024,128]{4,3,2,1,0:T(8,128)(2,1)}, bf16[2,2,2,1024,128]{4,3,2,1,0:T(8,128)(2,1)}, u32[]{:S(2)}, u32[]{:S(2)}) collective-permute-start(bf16[2,2,2,1024,128]{4,3,2,1,0:T(8,128)(2,1)} %get-tuple-element.116), channel_id=1, source_target_pairs={{0,8},{8,0},{16,24},{24,16},{1,9},{9,1},{17,25},{25,17},{2,10},{10... | collective-permute-start | bytes 6291464 | tf_op jit(solution)/shard_map/ppermute | solution.py:938
  383.5 17.8 %copy-start.3 = (bf16[1024,1024]{1,0:T(8,128)(2,1)S(1)}, bf16[1024,1024]{1,0:T(8,128)(2,1)}, u32[]{:S(2)}) copy-start(bf16[1024,1024]{1,0:T(8,128)(2,1)} %get-tuple-element.99.w_ref) | copy-start | bytes 6291460
  406.5 19.6 %collective-permute-start.7 = (bf16[1024,512]{1,0:T(8,128)(2,1)}, bf16[1024,512]{1,0:T(8,128)(2,1)}, u32[]{:S(2)}, u32[]{:S(2)}) collective-permute-start(bf16[1024,512]{1,0:T(8,128)(2,1)} %get-tuple-element.203), channel_id=1, source_target_pairs={{0,4},{4,0},{1,5},{5,1},{2,6},{6,2},{3,7},{7,3},{8,12},{12,8},{9,1... | collective-permute-start | bytes 3145736 | tf_op jit(solution)/shard_map/ppermute | solution.py:820
  418.5 79.9 %collective-permute-start.12 = (bf16[4,4,256,128]{3,2,1,0:T(8,128)(2,1)}, bf16[4,4,256,128]{3,2,1,0:T(8,128)(2,1)}, u32[]{:S(2)}, u32[]{:S(2)}) collective-permute-start(bf16[4,4,256,128]{3,2,1,0:T(8,128)(2,1)} %get-tuple-element.136), channel_id=1, source_target_pairs={{0,4},{4,0},{1,5},{5,1},{2,6},{6,2},{3,7},{7,3},{8,12},{12,8},{9,1... | collective-permute-start | bytes 3145736 | tf_op jit(solution)/shard_map/ppermute | solution.py:820
  426.1 3.6 copy-start
  432.7 91.2 %collective-permute-start.11 = (bf16[2,2,2,8,128,128]{5,4,3,2,1,0:T(8,128)(2,1)}, bf16[2,2,2,8,128,128]{5,4,3,2,1,0:T(8,128)(2,1)}, u32[]{:S(2)}, u32[]{:S(2)}) collective-permute-start(bf16[2,2,2,8,128,128]{5,4,3,2,1,0:T(8,128)(2,1)} %get-tuple-element.134), channel_id=1, source_target_pairs={{0,16},{8,24},{16,0},{24,8},{1,17},{9,25},{17,1},{25,9},{2,18},{10... | collective-permute-start | bytes 6291464 | tf_op jit(solution)/shard_map/ppermute | solution.py:938
  484.9 16.2 %collective-permute-start.13 = (bf16[4,1,3,2,128,128]{5,4,3,2,1,0:T(8,128)(2,1)}, bf16[4,1,3,2,128,128]{5,4,3,2,1,0:T(8,128)(2,1)}, u32[]{:S(2)}, u32[]{:S(2)}) collective-permute-start(bf16[4,1,3,2,128,128]{5,4,3,2,1,0:T(8,128)(2,1)} %get-tuple-element.139), channel_id=1, source_target_pairs={{0,4},{4,0},{1,5},{5,1},{2,6},{6,2},{3,7},{7,3},{8,12},{12,8},{9,1... | collective-permute-start | bytes 2359304 | tf_op jit(solution)/shard_map/ppermute | solution.py:820
  485.2 36.2 %collective-permute-start.10 = (bf16[2,2,1024,128]{3,2,1,0:T(8,128)(2,1)}, bf16[2,2,1024,128]{3,2,1,0:T(8,128)(2,1)}, u32[]{:S(2)}, u32[]{:S(2)}) collective-permute-start(bf16[2,2,1024,128]{3,2,1,0:T(8,128)(2,1)} %get-tuple-element.132), channel_id=1, source_target_pairs={{0,16},{8,24},{16,0},{24,8},{1,17},{9,25},{17,1},{25,9},{2,18},{10... | collective-permute-start | bytes 3145736 | tf_op jit(solution)/shard_map/ppermute | solution.py:938
  497.8 3.4 copy-start.10
  527.3 42.5 %copy-start.6 = (bf16[2,2,2,256,128]{4,3,2,1,0:T(8,128)(2,1)S(1)}, bf16[2,2,2,256,128]{4,3,2,1,0:T(8,128)(2,1)}, u32[]{:S(2)}) copy-start(bf16[2,2,2,256,128]{4,3,2,1,0:T(8,128)(2,1)} %get-tuple-element.144) | copy-start | bytes 1572868
  527.3 44.5 %copy-start.7 = (bf16[2,1024,128]{2,1,0:T(8,128)(2,1)S(1)}, bf16[2,1024,128]{2,1,0:T(8,128)(2,1)}, u32[]{:S(2)}) copy-start(bf16[2,1024,128]{2,1,0:T(8,128)(2,1)} %get-tuple-element.140) | copy-start | bytes 1572868
  527.3 46.4 %collective-permute-start.17 = (bf16[2,2,3,2,128,128]{5,4,3,2,1,0:T(8,128)(2,1)}, bf16[2,2,3,2,128,128]{5,4,3,2,1,0:T(8,128)(2,1)}, u32[]{:S(2)}, u32[]{:S(2)}) collective-permute-start(bf16[2,2,3,2,128,128]{5,4,3,2,1,0:T(8,128)(2,1)} %bitcast.182), channel_id=1, source_target_pairs={{0,16},{8,24},{16,0},{24,8},{1,17},{9,25},{17,1},{25,9},{2,18},{10... | collective-permute-start | bytes 2359304 | tf_op jit(solution)/shard_map/ppermute | solution.py:938
  529.0 40.8 %collective-permute-start.16 = (bf16[2,2,2,256,128]{4,3,2,1,0:T(8,128)(2,1)}, bf16[2,2,2,256,128]{4,3,2,1,0:T(8,128)(2,1)}, u32[]{:S(2)}, u32[]{:S(2)}) collective-permute-start(bf16[2,2,2,256,128]{4,3,2,1,0:T(8,128)(2,1)} %get-tuple-element.145), channel_id=1, source_target_pairs={{0,8},{8,0},{16,24},{24,16},{1,9},{9,1},{17,25},{25,17},{2,10},{10... | collective-permute-start | bytes 1572872 | tf_op jit(solution)/shard_map/ppermute | solution.py:938
  529.7 46.1 %collective-permute-start.15 = (bf16[2,2,8,128,128]{4,3,2,1,0:T(8,128)(2,1)}, bf16[2,2,8,128,128]{4,3,2,1,0:T(8,128)(2,1)}, u32[]{:S(2)}, u32[]{:S(2)}) collective-permute-start(bf16[2,2,8,128,128]{4,3,2,1,0:T(8,128)(2,1)} %get-tuple-element.143), channel_id=1, source_target_pairs={{0,8},{8,0},{16,24},{24,16},{1,9},{9,1},{17,25},{25,17},{2,10},{10... | collective-permute-start | bytes 3145736 | tf_op jit(solution)/shard_map/ppermute | solution.py:938
  531.0 40.7 %collective-permute-start.14 = (bf16[2,1024,128]{2,1,0:T(8,128)(2,1)}, bf16[2,1024,128]{2,1,0:T(8,128)(2,1)}, u32[]{:S(2)}, u32[]{:S(2)}) collective-permute-start(bf16[2,1024,128]{2,1,0:T(8,128)(2,1)} %get-tuple-element.141), channel_id=1, source_target_pairs={{0,2},{1,3},{2,0},{3,1},{4,6},{5,7},{6,4},{7,5},{8,10},{9,11},{10,... | collective-permute-start | bytes 1572872 | tf_op jit(solution)/shard_map/ppermute | solution.py:938
  569.8 4.0 copy-start.2
  586.6 10.1 %collective-permute-start.18 = (bf16[1024,1024]{1,0:T(8,128)(2,1)}, bf16[1024,1024]{1,0:T(8,128)(2,1)S(1)}, u32[]{:S(2)}, u32[]{:S(2)}) collective-permute-start(bf16[1024,1024]{1,0:T(8,128)(2,1)} %shard_map.210), channel_id=1, source_target_pairs={{0,4},{4,0},{1,5},{5,1},{2,6},{6,2},{3,7},{7,3},{8,12},{12,8},{9,1... | collective-permute-start | bytes 6291464 | tf_op jit(solution)/shard_map/ppermute | solution.py:820
  610.4 26.9 %collective-permute-start.23 = (bf16[4,1,3,2,128,128]{5,4,3,2,1,0:T(8,128)(2,1)}, bf16[4,1,3,2,128,128]{5,4,3,2,1,0:T(8,128)(2,1)}, u32[]{:S(2)}, u32[]{:S(2)}) collective-permute-start(bf16[4,1,3,2,128,128]{5,4,3,2,1,0:T(8,128)(2,1)} %get-tuple-element.164), channel_id=1, source_target_pairs={{0,4},{4,0},{1,5},{5,1},{2,6},{6,2},{3,7},{7,3},{8,12},{12,8},{9,1... | collective-permute-start | bytes 2359304 | tf_op jit(solution)/shard_map/ppermute | solution.py:820
  611.0 22.8 %collective-permute-start.28 = (bf16[2,2,256,128]{3,2,1,0:T(8,128)(2,1)}, bf16[2,2,256,128]{3,2,1,0:T(8,128)(2,1)}, u32[]{:S(2)}, u32[]{:S(2)}) collective-permute-start(bf16[2,2,256,128]{3,2,1,0:T(8,128)(2,1)} %get-tuple-element.171), channel_id=1, source_target_pairs={{0,16},{8,24},{16,0},{24,8},{1,17},{9,25},{17,1},{25,9},{2,18},{10... | collective-permute-start | bytes 786440 | tf_op jit(solution)/shard_map/ppermute | solution.py:938
  625.0 10.4 %collective-permute-start.33 = (bf16[1024,128]{1,0:T(8,128)(2,1)}, bf16[1024,128]{1,0:T(8,128)(2,1)}, u32[]{:S(2)}, u32[]{:S(2)}) collective-permute-start(bf16[1024,128]{1,0:T(8,128)(2,1)} %get-tuple-element.175), channel_id=1, source_target_pairs={{0,1},{1,0},{2,3},{3,2},{4,5},{5,4},{6,7},{7,6},{8,9},{9,8},{10,11... | collective-permute-start | bytes 786440 | tf_op jit(solution)/shard_map/ppermute | solution.py:938
  629.0 8.3 %copy-start.11 = (bf16[4,1,3,2,128,128]{5,4,3,2,1,0:T(8,128)(2,1)S(1)}, bf16[4,1,3,2,128,128]{5,4,3,2,1,0:T(8,128)(2,1)}, u32[]{:S(2)}) copy-start(bf16[4,1,3,2,128,128]{5,4,3,2,1,0:T(8,128)(2,1)} %get-tuple-element.163) | copy-start | bytes 2359300
  629.0 31.7 %collective-permute-start.31 = (bf16[2,8,128,128]{3,2,1,0:T(8,128)(2,1)}, bf16[2,8,128,128]{3,2,1,0:T(8,128)(2,1)S(1)}, u32[]{:S(2)}, u32[]{:S(2)}) collective-permute-start(bf16[2,8,128,128]{3,2,1,0:T(8,128)(2,1)} %get-tuple-element.173), channel_id=1, source_target_pairs={{0,2},{1,3},{2,0},{3,1},{4,6},{5,7},{6,4},{7,5},{8,10},{9,11},{10,... | collective-permute-start | bytes 1572872 | tf_op jit(solution)/shard_map/ppermute | solution.py:938
  630.3 32.6 %collective-permute-start.21 = (bf16[2,3,2,128,128]{4,3,2,1,0:T(8,128)(2,1)}, bf16[2,3,2,128,128]{4,3,2,1,0:T(8,128)(2,1)S(1)}, u32[]{:S(2)}, u32[]{:S(2)}) collective-permute-start(bf16[2,3,2,128,128]{4,3,2,1,0:T(8,128)(2,1)} %get-tuple-element.159), channel_id=1, source_target_pairs={{0,8},{8,0},{16,24},{24,16},{1,9},{9,1},{17,25},{25,17},{2,10},{10... | collective-permute-start | bytes 1179656 | tf_op jit(solution)/shard_map/ppermute | solution.py:938
  634.8 25.9 %collective-permute-start.29 = (bf16[2,256,128]{2,1,0:T(8,128)(2,1)S(1)}, bf16[2,256,128]{2,1,0:T(8,128)(2,1)S(1)}, u32[]{:S(2)}, u32[]{:S(2)}) collective-permute-start(bf16[2,256,128]{2,1,0:T(8,128)(2,1)S(1)} %get-tuple-element.217), channel_id=1, source_target_pairs={{0,2},{1,3},{2,0},{3,1},{4,6},{5,7},{6,4},{7,5},{8,10},{9,11},{10,... | collective-permute-start | bytes 393224 | tf_op jit(solution)/shard_map/ppermute | solution.py:938
  639.0 36.6 %collective-permute-start.24 = (bf16[2,2,3,2,128,128]{5,4,3,2,1,0:T(8,128)(2,1)S(1)}, bf16[2,2,3,2,128,128]{5,4,3,2,1,0:T(8,128)(2,1)S(1)}, u32[]{:S(2)}, u32[]{:S(2)}) collective-permute-start(bf16[2,2,3,2,128,128]{5,4,3,2,1,0:T(8,128)(2,1)S(1)} %copy_bitcast_fusion), channel_id=1, source_target_pairs={{0,16},{8,24},{16,0},{24,8},{1,17},{9,25},{17,1},{25,9},{2,18},{10... | collective-permute-start | bytes 2359304 | tf_op jit(solution)/shard_map/ppermute | solution.py:938
  660.7 5.0 collective-permute-start.30
  660.8 12.3 %collective-permute-start.32 = (bf16[8,128,128]{2,1,0:T(8,128)(2,1)S(1)}, bf16[8,128,128]{2,1,0:T(8,128)(2,1)S(1)}, u32[]{:S(2)}, u32[]{:S(2)}) collective-permute-start(bf16[8,128,128]{2,1,0:T(8,128)(2,1)S(1)} %fusion.25), channel_id=1, source_target_pairs={{0,1},{1,0},{2,3},{3,2},{4,5},{5,4},{6,7},{7,6},{8,9},{9,8},{10,11... | collective-permute-start | bytes 786440 | tf_op jit(solution)/shard_map/ppermute | solution.py:938
  662.9 13.7 %copy-start.8 = (bf16[2,3,2,128,128]{4,3,2,1,0:T(8,128)(2,1)}, bf16[2,3,2,128,128]{4,3,2,1,0:T(8,128)(2,1)S(1)}, u32[]{:S(2)}) copy-start(bf16[2,3,2,128,128]{4,3,2,1,0:T(8,128)(2,1)S(1)} %collective-permute-done.21) | copy-start | bytes 1179652
  663.7 15.5 %copy-start.15 = (f32[8,256]{1,0:T(8,128)S(1)}, f32[8,256]{1,0:T(8,128)}, u32[]{:S(2)}) copy-start(f32[8,256]{1,0:T(8,128)} %get-tuple-element.167) | copy-start | bytes 24580
  663.7 15.5 %copy-start.16 = (f32[8,256]{1,0:T(8,128)S(1)}, f32[8,256]{1,0:T(8,128)}, u32[]{:S(2)}) copy-start(f32[8,256]{1,0:T(8,128)} %get-tuple-element.168) | copy-start | bytes 24580
  663.7 68.0 %collective-permute-start.22 = (bf16[3,2,128,128]{3,2,1,0:T(8,128)(2,1)}, bf16[3,2,128,128]{3,2,1,0:T(8,128)(2,1)}, u32[]{:S(2)}, u32[]{:S(2)}) collective-permute-start(bf16[3,2,128,128]{3,2,1,0:T(8,128)(2,1)} %fusion.27), channel_id=1, source_target_pairs={{0,2},{1,3},{2,0},{3,1},{4,6},{5,7},{6,4},{7,5},{8,10},{9,11},{10,... | collective-permute-start | bytes 589832 | tf_op jit(solution)/shard_map/ppermute | solution.py:938
  674.0 68.1 %collective-permute-start.19 = (bf16[512,1024]{1,0:T(8,128)(2,1)S(1)}, bf16[512,1024]{1,0:T(8,128)(2,1)}, u32[]{:S(2)}, u32[]{:S(2)}) collective-permute-start(bf16[512,1024]{1,0:T(8,128)(2,1)S(1)} %get-tuple-element.156), channel_id=1, source_target_pairs={{0,0},{1,1},{4,2},{5,3},{2,4},{3,5},{6,6},{7,7},{8,8},{9,9},{12,10... | collective-permute-start | bytes 3145736 | tf_op jit(solution)/shard_map/ppermute | solution.py:866
  675.6 66.5 %collective-permute-start.20 = (bf16[512,1024]{1,0:T(8,128)(2,1)S(1)}, bf16[512,1024]{1,0:T(8,128)(2,1)}, u32[]{:S(2)}, u32[]{:S(2)}) collective-permute-start(bf16[512,1024]{1,0:T(8,128)(2,1)S(1)} %get-tuple-element.157), channel_id=1, source_target_pairs={{1,0},{0,1},{5,2},{4,3},{3,4},{2,5},{7,6},{6,7},{9,8},{8,9},{13,10... | collective-permute-start | bytes 3145736 | tf_op jit(solution)/shard_map/ppermute | solution.py:866
  676.6 51.2 %collective-permute-start.25 = (bf16[2,3,2,128,128]{4,3,2,1,0:T(8,128)(2,1)}, bf16[2,3,2,128,128]{4,3,2,1,0:T(8,128)(2,1)S(1)}, u32[]{:S(2)}, u32[]{:S(2)}) collective-permute-start(bf16[2,3,2,128,128]{4,3,2,1,0:T(8,128)(2,1)} %get-tuple-element.191), channel_id=1, source_target_pairs={{0,8},{8,0},{16,24},{24,16},{1,9},{9,1},{17,25},{25,17},{2,10},{10... | collective-permute-start | bytes 1179656 | tf_op jit(solution)/shard_map/ppermute | solution.py:938
  728.5 12.2 %collective-permute-start.26 = (bf16[3,2,128,128]{3,2,1,0:T(8,128)(2,1)}, bf16[3,2,128,128]{3,2,1,0:T(8,128)(2,1)}, u32[]{:S(2)}, u32[]{:S(2)}) collective-permute-start(bf16[3,2,128,128]{3,2,1,0:T(8,128)(2,1)} %fusion.29), channel_id=1, source_target_pairs={{0,2},{1,3},{2,0},{3,1},{4,6},{5,7},{6,4},{7,5},{8,10},{9,11},{10,... | collective-permute-start | bytes 589832 | tf_op jit(solution)/shard_map/ppermute | solution.py:938
  742.0 6.0 collective-permute-start.27
  742.1 5.9 copy-start.9

commit v5 on v4

--- a/solution.py
+++ b/solution.py
@@ -519,60 +519,6 @@
     )(jnp.stack([half, core]).astype(jnp.int32), *parts, w, *extra)
 
 
-def small_sum_kernel(n_p, n_t, in_ref, out_ref, pair, pair_sum, plane, plane_sum, column, send_sems, recv_sems):
-    p, core, t = lax.axis_index("p"), lax.axis_index("core"), lax.axis_index("tensor")
-    peers = [{"core": 1 - core}] + [{"p": lax.rem(p + r, n_p)} for r in range(1, n_p)]
-    peers += [{"tensor": lax.rem(t + r, n_t)} for r in range(1, n_t)]
-    barrier = pltpu.get_barrier_semaphore()
-    for peer in peers:
-        pl.semaphore_signal(barrier, inc=1, device_id=peer, device_id_type=pl.DeviceIdType.MESH)
-    pl.semaphore_wait(barrier, len(peers))
-
-    def exchange(first, count, source, slots, at):
-        copies = []
-        for j in range(count):
-            copy = pltpu.make_async_remote_copy(
-                src_ref=source, dst_ref=slots.at[at], send_sem=send_sems.at[first + j], recv_sem=recv_sems.at[first + j],
-                device_id=peers[first + j], device_id_type=pl.DeviceIdType.MESH,
-            )
-            copy.start()
-            copies.append(copy)
-        for copy in copies:
-            copy.wait()
-
-    exchange(0, 1, in_ref, pair, 0)
-    pair_sum[...] = in_ref[...] + pair[0]
-    exchange(1, n_p - 1, pair_sum, plane, p)
-    plane[p] = pair_sum[...]
-    total = plane[0]
-    for j in range(1, n_p):
-        total = total + plane[j]
-    plane_sum[...] = total
-    exchange(n_p, n_t - 1, plane_sum, column, t)
-    column[t] = plane_sum[...]
-    total = column[0]
-    for j in range(1, n_t):
-        total = total + column[j]
-    out_ref[...] = total
-
-
-def small_sum(values, n_p, n_t):
-    rows_ = values.shape[0]
-    count = n_p + n_t - 1
-    return pl.pallas_call(
-        functools.partial(small_sum_kernel, n_p, n_t),
-        out_shape=sds(values.shape, F32),
-        in_specs=[pl.BlockSpec(memory_space=pltpu.VMEM)],
-        out_specs=pl.BlockSpec(memory_space=pltpu.VMEM),
-        scratch_shapes=[
-            pltpu.VMEM((1, rows_, 128), F32), pltpu.VMEM((rows_, 128), F32), pltpu.VMEM((n_p, rows_, 128), F32),
-            pltpu.VMEM((rows_, 128), F32), pltpu.VMEM((n_t, rows_, 128), F32),
-            pltpu.SemaphoreType.DMA((count,)), pltpu.SemaphoreType.DMA((count,)),
-        ],
-        compiler_params=pltpu.CompilerParams(collective_id=0, has_side_effects=True),
-    )(values)
-
-
 MESH_ID = pl.DeviceIdType.MESH
 
 
@@ -636,7 +582,7 @@
         tall = full.shape[0] // 2
         return full.at[pl.ds(half * tall, tall), pl.ds(0, count * shards[i].shape[-1])]
 
-    def places(i):
+    def places(i, t):
         shard, full = shards[i], fulls[i]
         if kinds[i] == "columns":
             tall, depth = shard.shape
@@ -658,14 +604,36 @@
         wide = math.prod(shard.shape) // shard.shape[-2]
         return full.at[pl.ds(0, shard.shape[-2]), pl.ds(0, count * wide)]
 
-    own, line = [], []
+    hops = n_t - 1
+    own = [[keep(source, target) for source, target in places(i, t)] for i in range(n)]
+    right, left_to = {"tensor": lax.rem(t + 1, n_t)}, {"tensor": lax.rem(t + n_t - 1, n_t)}
+    line = [[(group(), group()) for _ in range(hops)] for _ in range(n)]
+
+    def hop(i, s):
+        to_right, to_left = line[i][s]
+
+        @pl.when(jnp.logical_and(t + 1 < n_t, t >= s))
+        def _():
+            for source, target in places(i, t - s):
+                send(source if s == 0 else target, target, to_right, right)
+
+        @pl.when(jnp.logical_and(t >= 1, t + s < n_t))
+        def _():
+            for source, target in places(i, t + s):
+                send(source if s == 0 else target, target, to_left, left_to)
+
+    def hop_arrived(i, s):
+        to_right, to_left = line[i][s]
+        pl.when(t >= s + 1)(lambda: arrived(shares(i, 1), to_right))
+        pl.when(t + s + 1 < n_t)(lambda: arrived(shares(i, 1), to_left))
+
+    def hop_left(i, s):
+        to_right, to_left = line[i][s]
+        pl.when(jnp.logical_and(t + 1 < n_t, t >= s))(lambda: left(shares(i, 1), to_right))
+        pl.when(jnp.logical_and(t >= 1, t + s < n_t))(lambda: left(shares(i, 1), to_left))
+
     for i in range(n):
-        at = group()
-        line.append(at)
-        own.append([keep(source, target) for source, target in places(i)])
-        for peer in column:
-            for source, target in places(i):
-                send(source, target, at, peer)
+        hop(i, 0)
     bias_at = group()
     bias_own = keep(bias_ref, bias_out.at[t])
     for peer in column:
@@ -707,9 +675,7 @@
 
     def stage(i, s):
         if s == 0:
-            for copy in own[i]:
-                copy.wait()
-            arrived(shares(i, n_t - 1), line[i])
+            hop_arrived(i, hops - 1)
             states[i] = {}
             for half in (0, 1):
                 states[i][half] = ([p], None)
@@ -733,10 +699,17 @@
             forward(i, fresh, half)
 
     finish = []
-    for step in range(n + len(bits)):
+    for step in range(n + hops - 1 + len(bits)):
         for i in range(n):
-            if 0 <= step - i <= len(bits):
-                stage(i, step - i)
+            at = step - i
+            if 0 <= at < hops - 1:
+                if at == 0:
+                    for copy in own[i]:
+                        copy.wait()
+                hop_arrived(i, at)
+                hop(i, at + 1)
+            elif 0 <= at - (hops - 1) <= len(bits):
+                stage(i, at - (hops - 1))
 
     pl.when(jnp.logical_not(stays))(lambda: arrived(x_rows, x_at[0]))
     pl.when(stays)(x_own.wait)
@@ -761,7 +734,8 @@
     for i, count, half, at in finish:
         left(slabs(i, count, half), at)
     for i in range(n):
-        left(shares(i, n_t - 1), line[i])
+        for s in range(hops):
+            hop_left(i, s)
     left(bias_out.at[pl.ds(0, n_t - 1)], bias_at)
     pl.when(jnp.logical_not(stays))(lambda: left(x_rows, x_at[0]))
     left(x_rows, x_at[1])
@@ -776,7 +750,7 @@
         else:
             fulls.append(sds((shard.shape[-2] * n_dp, math.prod(shard.shape) // shard.shape[-2] * n_t)))
     bits = n_p.bit_length() - 1
-    count = len(shards) * (1 + 2 * bits + 2 * (bits + 1)) + 4
+    count = len(shards) * (2 * (n_t - 1) + 2 * bits + 2 * (bits + 1)) + 4
     vmem, away = pl.BlockSpec(memory_space=pltpu.VMEM), pl.BlockSpec(memory_space=pl.ANY)
     return pl.pallas_call(
         functools.partial(start_kernel, n_p, n_t, kinds),
@@ -814,6 +788,150 @@
         compiler_params=pltpu.CompilerParams(dimension_semantics=("arbitrary",)),
         cost_estimate=pl.CostEstimate(flops=2 * n * d * f, bytes_accessed=4 * n * d + 2 * n * f, transcendentals=0),
     )(core_at, x, w, bias)
+
+
+def finish_kernel(n_p, n_t, *refs):
+    dx, keep2, send2, first_a, first_b, up_a, up_b, out_a, out_b, small = refs[:10]
+    given, qkv_out, up_out, out_out, small_out = refs[10:15]
+    recv2, pair1, pair2, slot1, slot2, last, last_slot, up_cur, up_slot, out_cur, out_slot = refs[15:26]
+    out_next, out_last, small_cur, small_slot = refs[26:30]
+    bits = [n_p >> (s + 1) for s in range(n_p.bit_length() - 1)]
+    curs, slots = refs[30 : 30 + len(bits)], refs[30 + len(bits) : 30 + 2 * len(bits)]
+    send_sems, recv_sems = refs[-2:]
+    p, core, t = lax.axis_index("p"), lax.axis_index("core"), lax.axis_index("tensor")
+    partner = {"core": 1 - core}
+    column = [{"tensor": lax.rem(t + r, n_t)} for r in range(1, n_t)]
+    column += [{"core": 1 - core, "tensor": lax.rem(t + r, n_t)} for r in range(n_t)]
+    plane = [{"p": flip(p, bit)} for bit in bits]
+    line = {bit: {"tensor": flip(t, bit)} for bit in (2, 1)}
+    barrier = pltpu.get_barrier_semaphore()
+    for peer in column + plane:
+        pl.semaphore_signal(barrier, inc=1, device_id=peer, device_id_type=MESH_ID)
+    pl.semaphore_wait(barrier, len(column + plane))
+
+    used = [0]
+
+    def send(source, target, peer):
+        at = used[0]
+        used[0] += 1
+        copy = pltpu.make_async_remote_copy(
+            src_ref=source, dst_ref=target, send_sem=send_sems.at[at], recv_sem=recv_sems.at[at],
+            device_id=peer, device_id_type=MESH_ID,
+        )
+        return copy
+
+    def go(source, target, peer):
+        copy = send(source, target, peer)
+        copy.start()
+        return copy
+
+    def plus(a, b):
+        return (a.astype(F32) + b.astype(F32)).astype(BF16)
+
+    u, odd = t // 2, t % 2
+    swap = go(send2, recv2, partner)
+    for at in (0, 1):
+        pair1[at] = plus(first_a[at], first_b[at])
+    first_move = go(pair1.at[1 - u], slot1, line[2])
+    for at in range(4):
+        out_cur[at] = plus(out_a[at], out_b[at])
+    out_move = go(out_cur.at[pl.ds(2 * (1 - u), 2)], out_slot, line[2])
+    for at in (0, 1):
+        up_cur[at] = plus(up_a[at], up_b[at])
+    up_move = go(up_cur.at[1 - odd], up_slot, line[1])
+
+    held = given.shape[1]
+    stays = core == u
+    rows_a = dx.at[pl.ds(pl.multiple_of(odd * held, held), held), :]
+    rows_b = dx.at[pl.ds(pl.multiple_of((1 - odd) * held, held), held), :]
+    give_a = send(rows_a, given.at[odd], {"core": u, "tensor": 2 * core + odd})
+    pl.when(jnp.logical_not(stays))(give_a.start)
+
+    @pl.when(stays)
+    def _():
+        given[odd] = dx[pl.ds(pl.multiple_of(odd * held, held), held), :]
+
+    moves = []
+    small_cur[0] = small[...]
+    peers = [partner] + plane
+    for at, peer in enumerate(peers):
+        copy = go(small_cur.at[at], small_slot.at[at], peer)
+        copy.wait()
+        small_cur[at + 1] = small_cur[at] + small_slot[at]
+
+    swap.wait()
+    source = [keep2, recv2]
+    for s, bit in enumerate(bits):
+        mine = (p // bit) % 2
+        copies = [
+            go(source[j].at[pl.ds((1 - mine) * bit, bit)], slots[s].at[j], plane[s]) for j in (0, 1)
+        ]
+        for j, copy in enumerate(copies):
+            copy.wait()
+            if bit == 1:
+                pair2[core if j == 0 else 1 - core] = plus(source[j][mine], slots[s][j, 0])
+            else:
+                for at in range(bit):
+                    curs[s][j, at] = plus(source[j][mine * bit + at], slots[s][j, at])
+        source = [curs[s].at[0], curs[s].at[1]]
+    second_move = go(pair2.at[1 - u], slot2, line[2])
+    give_b = go(rows_b, given.at[odd], {"core": u, "tensor": 2 * core + 1 - odd})
+
+    up_move.wait()
+    up_out[...] = up_cur[odd].astype(F32) + up_slot[...].astype(F32)
+    out_move.wait()
+    for at in (0, 1):
+        out_next[at] = plus(out_cur[2 * u + at], out_slot[at])
+    out_move = go(out_next.at[1 - odd], out_last, line[1])
+    first_move.wait()
+    last[0] = plus(pair1[u], slot1[...])
+    second_move.wait()
+    last[1] = plus(pair2[u], slot2[...])
+    last_move = go(last.at[1 - odd], last_slot, line[1])
+    for bit in (2, 1):
+        at = len(peers)
+        copy = go(small_cur.at[at], small_slot.at[at], line[bit])
+        copy.wait()
+        peers.append(None)
+        if bit == 1:
+            small_out[...] = small_cur[at] + small_slot[at]
+        else:
+            small_cur[at + 1] = small_cur[at] + small_slot[at]
+    out_move.wait()
+    out_out[...] = out_next[odd].astype(F32) + out_last[...].astype(F32)
+    last_move.wait()
+    qkv_out[...] = last[odd].astype(F32) + last_slot[...].astype(F32)
+    pl.when(jnp.logical_not(stays))(give_a.wait)
+    give_b.wait()
+
+
+def finish(n_p, n_t, dx, keep2, send2, first, up_, out_, small):
+    rows_, lanes = keep2.shape[1:]
+    bits = n_p.bit_length() - 1
+    steps = 1 + bits + 2
+    block = lambda count, like: pltpu.VMEM((count,) + like.shape[1:], BF16)
+    one = lambda like: pltpu.VMEM(like.shape[1:], BF16)
+    sizes = [n_p >> (s + 1) for s in range(bits)]
+    halves = [pltpu.VMEM((2, size, rows_, lanes), BF16) for size in sizes]
+    vmem = pl.BlockSpec(memory_space=pltpu.VMEM)
+    count = 9 + steps + 2 * bits
+    return pl.pallas_call(
+        functools.partial(finish_kernel, n_p, n_t),
+        out_shape=[
+            sds((2, dx.shape[0] // 2, dx.shape[1])), sds((rows_, lanes), F32), sds(up_[0].shape[1:], F32),
+            sds(out_[0].shape[1:], F32), sds(small.shape, F32),
+        ],
+        in_specs=[vmem] * 10,
+        out_specs=[vmem] * 5,
+        scratch_shapes=[
+            block(n_p, keep2), block(2, keep2), block(2, keep2), one(keep2), one(keep2), block(2, keep2), one(keep2),
+            block(2, up_[0]), one(up_[0]), block(4, out_[0]), block(2, out_[0]), block(2, out_[0]), one(out_[0]),
+            pltpu.VMEM((steps,) + small.shape, F32), pltpu.VMEM((steps,) + small.shape, F32),
+            *halves, *halves,
+            pltpu.SemaphoreType.DMA((count,)), pltpu.SemaphoreType.DMA((count,)),
+        ],
+        compiler_params=pltpu.CompilerParams(collective_id=0, has_side_effects=True),
+    )(dx, keep2, send2, *first, *up_, *out_, small)
 
 
 def swap_cores(value):
@@ -985,23 +1103,9 @@
     dx_other = swap_cores(input_pull(1 - core, core, (*first, *second), w_qkv))
     dx_mine = input_pull(core, core, (*first, *second), w_qkv, dm)
     dx = (dx_mine + dx_other.astype(F32)).astype(BF16)
-    dx, second = lax.optimization_barrier((blocks(dx), second))
-    input_grad = give(*dx).astype(F32)
     keep, send, sum_second = qkv_grad(x_turned, *second, n_p)
-    second_sum = Total([by_core(core, keep, swap_cores(send), 1)], True).cut(0).move()
-    first_sum.cut(2).move()
-    up_sums.cut(3).move()
-    out_sum.cut(2).move().cut(3).move()
-    second_sum.cut(1).move().cut(2).move()
     qv_sum = jnp.concatenate([sum_first, sum_second], axis=1)
-    same = lambda part: part
-    down_total, up_total, out_total = down_sum.sum_of(same), up_sums.sum_of(same), out_sum.sum_of(same)
-    pair = [first_sum.sum_of(same), second_sum.sum_of(same)]
-    moved = lax.ppermute(jnp.where(odd == 0, pair[1], pair[0]).astype(BF16), "tensor", [(i, i ^ 1) for i in range(n_t)])
-    qkv_total = jnp.where(odd == 0, pair[0], pair[1]) + moved.astype(F32)
-    up_total = up_total.transpose(1, 0, 2).reshape(up_weight.shape)
-    qkv_total = qkv_total.transpose(0, 2, 1, 3).reshape(qkv_weight.shape)
-
+    down_total = down_sum.sum_of(lambda part: part)
     qv_pad = lax.dynamic_update_slice(jnp.zeros((2, width), F32), qv_sum[0:2], (0, core * own))
     small = jnp.concatenate(
         [
@@ -1010,7 +1114,15 @@
             up_sum[0],
         ]
     )
-    small = small_sum(small.reshape(-1, 128), n_p, n_t).reshape(-1)
+    rows_of = lambda part, count: part.reshape(count, -1, part.shape[-1])
+    given, qkv_total, up_total, out_total, small = finish(
+        n_p, n_t, dx, rows_of(keep, n_p), rows_of(send, n_p), [rows_of(part, 2) for part in first_sum.parts],
+        [rows_of(part, 2) for part in up_sums.parts], [rows_of(part, 4) for part in out_sum.parts], small.reshape(-1, 128),
+    )
+    input_grad = given.astype(F32)
+    small = small.reshape(-1)
+    up_total = up_total.reshape(up_sums.rest).transpose(1, 0, 2).reshape(up_weight.shape)
+    qkv_total = qkv_total.reshape(first_sum.rest).transpose(0, 2, 1, 3).reshape(qkv_weight.shape)
     gain_sum = small[: 2 * width].reshape(2, width)
     bias_sum = small[2 * width : 6 * width].reshape(4, width)
     qv_total = lax.dynamic_slice_in_dim(small[6 * width : 8 * width].reshape(2, width), tensor * qv_bias.shape[1], qv_bias.shape[1], 1)

time: 763 us -> 779 us (1.021)
  Pallas kernels: 488 us -> 606 us
  starting transfers between devices: 105 us -> 32.9 us
  waiting for transfers between devices: 55.6 us -> 30.8 us
  other arithmetic: 75.8 us -> 67.6 us
    ppermute x18 -> x11, starting transfers between devices: 71.4 us -> 14.4 us  [move(): self.parts = [self.live[0], lax.ppermute(self.live[1], *self.route)]]
    pallas_call x1, Pallas kernels: 139 us -> 183 us  [start_gather(): pl.pallas_call(functools.partial(start_kernel, n_p, n_t, kinds), out_shap...]
    pallas_call x1, Pallas kernels: 47.2 us -> 80.2 us  [finish(): pl.pallas_call(functools.partial(finish_kernel, n_p, n_t), out_shape=[sds...]
    ppermute x18 -> x11, waiting for transfers between devices: 54.3 us -> 25.7 us  [move(): self.parts = [self.live[0], lax.ppermute(self.live[1], *self.route)]]
    pallas_call x2, Pallas kernels: 72.3 us -> 93.7 us  [attend_bwd(): pl.pallas_call(functools.partial(attend_bwd_kernel, bq), grid_spec=pltpu....]
    pallas_call x1, Pallas kernels: 48.7 us -> 68.1 us  [attend_fwd(): pl.pallas_call(functools.partial(attend_fwd_kernel, bk), grid_spec=pltpu....]
    ppermute x1, starting transfers between devices: 15.3 us -> 0.72 us  [bring(): b = lax.ppermute(value[1 - odd], COL, route_b)]
    convert_element_type x16 -> x10, other arithmetic: 36.1 us -> 32.8 us  [cut_one(): self.sum_of(lambda part: lax.dynamic_index_in_dim(part, which, at, keepdi...]
  transfers between devices with their start and end apart: 34 -> 23, of which waited for: 6 -> 3; matrix products, arithmetic and copies ran while one was open for 11% -> 10% of each run, Pallas kernels for 51% -> 56%
where the time goes in v5:
time: 779 us; the launch traced here: 766 us
  Pallas kernels  606 us (78%)
  other arithmetic  67.6 us (9%)
  starting transfers between devices  32.9 us (4%)
  waiting for transfers between devices  30.8 us (4%)
  local copies, waits for them, and re-layouts  23.4 us (3%)
    pallas_call x1, Pallas kernels, start_gather(): pl.pallas_call(functools.partial(start_kernel, n_p, n_t, kinds), out_shap...  183 us
    pallas_call x2, Pallas kernels, attend_bwd(): pl.pallas_call(functools.partial(attend_bwd_kernel, bq), grid_spec=pltpu....  93.7 us
    pallas_call x4, Pallas kernels, call(): pl.pallas_call(kernel, grid=grid, in_specs=ins, out_specs=outs[0], out_sh...  83.8 us
    pallas_call x1, Pallas kernels, finish(): pl.pallas_call(functools.partial(finish_kernel, n_p, n_t), out_shape=[sds...  80.2 us
    pallas_call x1, Pallas kernels, attend_fwd(): pl.pallas_call(functools.partial(attend_fwd_kernel, bk), grid_spec=pltpu....  68.1 us
    pallas_call x5, Pallas kernels, grad_call(): pl.pallas_call(kernel, grid=grid, in_specs=ins, out_specs=outs[0], out_sh...  57.8 us
    convert_element_type x10, other arithmetic, cut_one(): self.sum_of(lambda part: lax.dynamic_index_in_dim(part, which, at, keepdi...  32.8 us
    ppermute x11, waiting for transfers between devices, move(): self.parts = [self.live[0], lax.ppermute(self.live[1], *self.route)]  25.7 us
  transfers between devices with their start and end apart: 23, of which 3 were waited for; matrix products, arithmetic and copies ran while one was open for 10% of the time, Pallas kernels for 56%

profile of v5, /device:TPU:0, one launch (start us, length us, event | category | flops | bytes accessed | tf_op | source)
XLA Modules:
  0.0 765.6 jit_solution(11942476514403976941)
XLA Ops:
  0.7 0.9 fusion.21
  2.8 1.3 maximum_bitcast_fusion.1.refs_1_
  4.1 183.4 %shard_map.195 = (bf16[2048,1024]{1,0:T(8,128)(2,1)}, f32[4,12,128]{2,1,0:T(8,128)}, bf16[1024,3072]{1,0:T(8,128)(2,1)}, bf16[1024,1024]{1,0:T(8,128)(2,1)}, bf1...) custom-call(bf16[2,512,1024]{2,1,0:T(8,128)(2,1)} %refs_0_.1, f32[12,128]{1,0:T(8,128)} %maximum_bitcast_fusion.1.refs_1_, ...), custom_call_target="tpu_custom_call" | custom-call | tf_op jit(solution)/shard_map/pallas_call | solution.py:755
  187.5 1.2 dynamic-slice_bitcast_fusion.1
  188.6 1.9 collective-permute-start.2
  192.1 12.3 %shard_map.196 = (bf16[2048,1536]{1,0:T(8,128)(2,1)}, bf16[1024,2048]{1,0:T(8,128)(2,1)}) custom-call(s32[1]{0:T(128)} %bitcast.core_ref.at_ref, bf16[2048,1024]{1,0:T(8,128)(2,1)} %get-tuple-element.94.x_ref, bf16[1024,3072]{1,0:T(8,128)(2,1)} %get-tuple-element.95.w_ref.refs_6_, f32[1,1536]{1,0:T(1,128)} %reshape.231.bias_ref), custom_call_target="tpu_custom_call" | custom-call | flops 6442450944 | bytes 14680064 | tf_op jit(solution)/shard_map/pallas_call | solution.py:775
  206.2 1.3 broadcast_in_dim.11.kcode_ref
  207.5 68.1 %shard_map.197 = (bf16[2048,512]{1,0:T(8,128)(2,1)}, f32[32,2048]{1,0:T(8,128)}) custom-call(s32[4]{0:T(128)} %get-tuple-element.228.lo_ref, s32[4]{0:T(128)} %get-tuple-element.227.hi_ref, s32[4]{0:T(128)} %reduce_sum.56.pad_ref, bf16[2048,1536]{1,0:T(8,128)(2,1)} %get-tuple-element.97.q_ref.k_ref.v_ref, ...), custom_call_target="tpu_custom_call" | custom-call | flops 8589934592 | bytes 25165824 | tf_op jit(solution)/shard_map/pallas_call | solution.py:160
  275.6 2.6 constant_dynamic-slice_fusion.8
  278.3 3.7 collective-permute-start.1
  282.6 3.8 maximum_select_fusion.1.e_ref
  286.5 3.7 maximum_select_fusion.c_ref.a_ref
  290.1 8.7 %shard_map.198 = (bf16[1024,1024]{1,0:T(8,128)(2,1)}, bf16[1024,1024]{1,0:T(8,128)(2,1)}, f32[1024,1024]{1,0:T(8,128)}, f32[1024,128]{1,0:T(8,128)}) custom-call(s32[1]{0:T(128)} %bitcast.core_ref.at_ref, bf16[2048,1024]{1,0:T(8,128)(2,1)} %get-tuple-element.94.x_ref, bf16[1024,1024]{1,0:T(8,128)(2,1)} %maximum_select_fusion.c_ref.a_ref, ...), custom_call_target="tpu_custom_call" | custom-call | flops 2147483648 | bytes 12582912 | tf_op jit(solution)/shard_map/pallas_call | solution.py:325
  298.8 24.8 %shard_map.199 = (bf16[1024,4096]{1,0:T(8,128)(2,1)}, bf16[1024,4096]{1,0:T(8,128)(2,1)}) custom-call(bf16[1024,1024]{1,0:T(8,128)(2,1)} %get-tuple-element.100.h_ref, bf16[1024,4096]{1,0:T(8,128)(2,1)} %get-tuple-element.101.w_ref, f32[1,4096]{1,0:T(1,128)} %bitcast.159), custom_call_target="tpu_custom_call" | custom-call | flops 8589934592 | bytes 25165824 | tf_op jit(solution)/shard_map/pallas_call | solution.py:293
  323.6 19.2 %shard_map.200 = (bf16[1024,1024]{1,0:T(8,128)(2,1)}, f32[1024,1024]{1,0:T(8,128)}, bf16[1024,1024]{1,0:T(8,128)(2,1)}, f32[8,1024]{1,0:T(8,128)}) custom-call(bf16[1024,4096]{1,0:T(8,128)(2,1)} %get-tuple-element.109.g_ref.a_ref, bf16[4096,1024]{1,0:T(8,128)(2,1)} %get-tuple-element.103.w_ref, f32[1024,1024]{1,0:T(8,128)} %get-tuple-element.104.n_ref, ...), custom_call_target="tpu_custom_call" | custom-call | flops 8589934592 | bytes 16777216 | tf_op jit(solution)/shard_map/pallas_call | solution.py:293
  342.8 22.0 %shard_map.201 = (bf16[1024,4096]{1,0:T(8,128)(2,1)}, f32[8,4096]{1,0:T(8,128)}) custom-call(bf16[1024,1024]{1,0:T(8,128)(2,1)} %get-tuple-element.106.dz_ref.b_ref, bf16[4096,1024]{1,0:T(8,128)(2,1)} %get-tuple-element.103.w_ref, bf16[1024,4096]{1,0:T(8,128)(2,1)} %get-tuple-element.107.slope_ref), custom_call_target="tpu_custom_call" | custom-call | flops 8589934592 | bytes 25165824 | tf_op jit(solution)/shard_map/pallas_call | solution.py:293
  364.8 15.6 %shard_map.202 = (bf16[4,4,1024,128]{3,2,1,0:T(8,128)(2,1)}, bf16[4,4,1024,128]{3,2,1,0:T(8,128)(2,1)}) custom-call(bf16[1024,4096]{1,0:T(8,128)(2,1)} %get-tuple-element.109.g_ref.a_ref, bf16[1024,1024]{1,0:T(8,128)(2,1)} %get-tuple-element.106.dz_ref.b_ref), custom_call_target="tpu_custom_call" | custom-call | flops 8589934592 | bytes 16777216 | tf_op jit(solution)/shard_map/pallas_call | solution.py:434
  380.5 15.2 %shard_map.203 = (bf16[4,4,8,128,128]{4,3,2,1,0:T(8,128)(2,1)}, bf16[4,4,8,128,128]{4,3,2,1,0:T(8,128)(2,1)}) custom-call(bf16[1024,1024]{1,0:T(8,128)(2,1)} %get-tuple-element.117.a_ref, bf16[1024,4096]{1,0:T(8,128)(2,1)} %get-tuple-element.120.b_ref.du_ref), custom_call_target="tpu_custom_call" | custom-call | flops 8589934592 | bytes 16777216 | tf_op jit(solution)/shard_map/pallas_call | solution.py:434
  396.2 1.5 constant_dynamic-slice_fusion.4
  397.7 9.6 %collective-permute-start.8 = (bf16[512,1024]{1,0:T(8,128)(2,1)}, bf16[512,1024]{1,0:T(8,128)(2,1)}, u32[]{:S(2)}, u32[]{:S(2)}) collective-permute-start(bf16[512,1024]{1,0:T(8,128)(2,1)} %get-tuple-element.196), channel_id=1, source_target_pairs={{0,0},{1,1},{4,2},{5,3},{2,4},{3,5},{6,6},{7,7},{8,8},{9,9},{12,10... | collective-permute-start | bytes 3145736 | tf_op jit(solution)/shard_map/ppermute | solution.py:984
  407.3 0.9 collective-permute-start.9
  408.2 5.4 fusion.1
  413.6 17.7 %shard_map.204 = (f32[1024,1024]{1,0:T(8,128)}, bf16[1024,1024]{1,0:T(8,128)(2,1)}, f32[8,1024]{1,0:T(8,128)}) custom-call(bf16[1024,4096]{1,0:T(8,128)(2,1)} %get-tuple-element.120.b_ref.du_ref, bf16[1024,4096]{1,0:T(8,128)(2,1)} %get-tuple-element.101.w_ref, f32[1024,1024]{1,0:T(8,128)} %get-tuple-element.121.dr_ref, ...), custom_call_target="tpu_custom_call" | custom-call | flops 8589934592 | bytes 16777216 | tf_op jit(solution)/shard_map/pallas_call | solution.py:293
  431.4 4.0 convolution_convert_fusion
  435.3 1.2 constant_dynamic-slice_fusion.6
  438.3 5.1 collective-permute-done.9
  443.4 4.0 maximum_select_fusion.3
  447.4 6.4 shard_map.206
  453.8 7.0 fusion.3
  460.8 3.6 maximum_select_fusion.2.dc_ref
  464.4 3.1 fusion.5
  467.5 46.7 %shard_map.205 = (bf16[2048,256]{1,0:T(8,128)(2,1)}, bf16[2048,256]{1,0:T(8,128)(2,1)}, bf16[2048,256]{1,0:T(8,128)(2,1)}) custom-call(s32[8]{0:T(128)} %get-tuple-element.226.lo_ref, s32[8]{0:T(128)} %get-tuple-element.225.hi_ref, s32[8]{0:T(128)} %reduce_sum.62.pad_ref, bf16[2048,1536]{1,0:T(8,128)(2,1)} %get-tuple-element.97.q_ref.k_ref.v_ref, ...), custom_call_target="tpu_custom_call" | custom-call | flops 21474836480 | bytes 50331648 | tf_op jit(solution)/shard_map/pallas_call | solution.py:198
  514.3 10.4 %shard_map.207 = (bf16[4,1,3,2,128,128]{5,4,3,2,1,0:T(8,128)(2,1)}, bf16[4,1,3,2,128,128]{5,4,3,2,1,0:T(8,128)(2,1)}, f32[8,256]{1,0:T(8,128)}) custom-call(bf16[1024,2048]{1,0:T(8,128)(2,1)} %get-tuple-element.137.x_ref, bf16[2048,256]{1,0:T(8,128)(2,1)} %get-tuple-element.128.dq_ref.refs_0_, bf16[2048,256]{1,0:T(8,128)(2,1)} %get-tuple-element.129.dk_ref.refs_1_, ...), custom_call_target="tpu_custom_call" | custom-call | flops 3221225472 | bytes 6291456 | tf_op jit(solution)/shard_map/pallas_call | solution.py:434
  525.2 1.5 collective-permute-start.10
  527.3 2.8 fusion.11
  530.1 1.6 maximum_select_fusion.4
  531.9 0.9 copy.94
  532.8 1.0 copy.95
  533.8 16.8 %collective-permute-done.10 = bf16[2,2,1024,128]{3,2,1,0:T(8,128)(2,1)} collective-permute-done((bf16[2,2,1024,128]{3,2,1,0:T(8,128)(2,1)}, bf16[2,2,1024,128]{3,2,1,0:T(8,128)(2,1)}, u32[]{:S(2)}, u32[]{:S(2)}) %collective-permute-start.10) | collective-permute-done | bytes 1048608 | tf_op jit(solution)/shard_map/ppermute | solution.py:1056
  550.6 2.5 fusion.9
  553.0 3.3 fusion.7
  556.4 1.7 collective-permute-start.17
  558.1 2.0 collective-permute-start.15
  560.1 46.9 %shard_map.208 = (bf16[2048,256]{1,0:T(8,128)(2,1)}, bf16[2048,256]{1,0:T(8,128)(2,1)}, bf16[2048,256]{1,0:T(8,128)(2,1)}) custom-call(s32[8]{0:T(128)} %get-tuple-element.226.lo_ref, s32[8]{0:T(128)} %get-tuple-element.225.hi_ref, s32[8]{0:T(128)} %reduce_sum.62.pad_ref, bf16[2048,1536]{1,0:T(8,128)(2,1)} %get-tuple-element.97.q_ref.k_ref.v_ref, ...), custom_call_target="tpu_custom_call" | custom-call | flops 21474836480 | bytes 50331648 | tf_op jit(solution)/shard_map/pallas_call | solution.py:198
  607.0 2.1 fusion.19
  609.1 1.9 fusion.17
  611.0 2.2 fusion.15
  613.2 2.5 fusion.13
  615.8 8.4 %shard_map.210 = bf16[1024,1024]{1,0:T(8,128)(2,1)} custom-call(s32[2]{0:T(128)} %pad_add_fusion.1.at_ref, bf16[2048,256]{1,0:T(8,128)(2,1)} %get-tuple-element.128.dq_ref.refs_0_, bf16[2048,256]{1,0:T(8,128)(2,1)} %get-tuple-element.129.dk_ref.refs_1_, bf16[2048,256]{1,0:T(8,128)(2,1)} %get-tuple-element.130.dv_ref.refs_2_, ...), custom_call_target="tpu_custom_call" | custom-call | flops 3221225472 | bytes 16777216 | tf_op jit(solution)/shard_map/pallas_call | solution.py:508
  624.7 0.8 slice.85
  626.2 0.9 slice.87
  627.2 0.8 slice.84
  628.7 8.2 %collective-permute-start.22 = (bf16[1024,128]{1,0:T(8,128)(2,1)}, bf16[1024,128]{1,0:T(8,128)(2,1)}, u32[]{:S(2)}, u32[]{:S(2)}) collective-permute-start(bf16[1024,128]{1,0:T(8,128)(2,1)} %get-tuple-element.175), channel_id=1, source_target_pairs={{0,1},{1,0},{2,3},{3,2},{4,5},{5,4},{6,7},{7,6},{8,9},{9,8},{10,11... | collective-permute-start | bytes 786440 | tf_op jit(solution)/shard_map/ppermute | solution.py:1056
  637.0 10.3 %shard_map.211 = (bf16[4,1,3,2,128,128]{5,4,3,2,1,0:T(8,128)(2,1)}, bf16[4,1,3,2,128,128]{5,4,3,2,1,0:T(8,128)(2,1)}, f32[8,256]{1,0:T(8,128)}) custom-call(bf16[1024,2048]{1,0:T(8,128)(2,1)} %get-tuple-element.137.x_ref, bf16[2048,256]{1,0:T(8,128)(2,1)} %get-tuple-element.152.refs_3_.dq_ref, bf16[2048,256]{1,0:T(8,128)(2,1)} %get-tuple-element.153.refs_4_.dk_ref, ...), custom_call_target="tpu_custom_call" | custom-call | flops 3221225472 | bytes 6291456 | tf_op jit(solution)/shard_map/pallas_call | solution.py:434
  648.0 1.0 collective-permute-start.20
  649.6 9.5 %shard_map.209 = f32[1024,1024]{1,0:T(8,128)} custom-call(s32[2]{0:T(128)} %pad_add_fusion.at_ref, bf16[2048,256]{1,0:T(8,128)(2,1)} %get-tuple-element.128.dq_ref.refs_0_, bf16[2048,256]{1,0:T(8,128)(2,1)} %get-tuple-element.129.dk_ref.refs_1_, bf16[2048,256]{1,0:T(8,128)(2,1)} %get-tuple-element.130.dv_ref.refs_2_, ...), custom_call_target="tpu_custom_call" | custom-call | flops 3221225472 | bytes 16777216 | tf_op jit(solution)/shard_map/pallas_call | solution.py:508
  659.1 1.8 convert_add_fusion
  660.9 4.3 add_convert_fusion.refs_0_
  665.2 8.8 %collective-permute-done.20 = bf16[2,8,128,128]{3,2,1,0:T(8,128)(2,1)S(1)} collective-permute-done((bf16[2,8,128,128]{3,2,1,0:T(8,128)(2,1)S(1)}, bf16[2,8,128,128]{3,2,1,0:T(8,128)(2,1)S(1)}, u32[]{:S(2)}, u32[]{:S(2)}) %collective-permute-start.20) | collective-permute-done | bytes 524320 | tf_op jit(solution)/shard_map/ppermute | solution.py:1056
  674.1 0.8 copy-done.9
  674.9 80.2 %shard_map.212 = (bf16[2,512,1024]{2,1,0:T(8,128)(2,1)}, f32[768,128]{1,0:T(8,128)}, f32[1024,128]{1,0:T(8,128)}, f32[256,128]{1,0:T(8,128)}, f32[96,128]{1,0:T(8,128)}) custom-call(bf16[1024,1024]{1,0:T(8,128)(2,1)} %add_convert_fusion.refs_0_, bf16[4,768,128]{2,1,0:T(8,128)(2,1)} %bitcast.141, bf16[4,768,128]{2,1,0:T(8,128)(2,1)} %bitcast.142, ...), custom_call_target="tpu_custom_call" | custom-call | tf_op jit(solution)/shard_map/pallas_call | solution.py:918
  756.5 4.2 convert_element_type.428
  760.7 0.8 copy.96
  761.5 0.8 copy.97
  (119 shorter events, 17.0 us)
Async XLA Ops:
  0.6 186.8 %copy-start.4 = (bf16[2,512,1024]{2,1,0:T(8,128)(2,1)S(1)}, bf16[2,512,1024]{2,1,0:T(8,128)(2,1)}, u32[]{:S(2)}) copy-start(bf16[2,512,1024]{2,1,0:T(8,128)(2,1)} %param.23) | copy-start | bytes 6291460
  1.5 202.9 %collective-permute-start = (s32[2,2048]{1,0:T(2,128)S(1)}, s32[2,2048]{1,0:T(2,128)S(1)}, u32[]{:S(2)}, u32[]{:S(2)}) collective-permute-start(s32[2,2048]{1,0:T(2,128)S(1)} %fusion.21), channel_id=1, source_target_pairs={{0,4},{4,0},{1,5},{5,1},{2,6},{6,2},{3,7},{7,3},{8,12},{12,8},{9,1... | collective-permute-start | bytes 49160 | tf_op jit(solution)/shard_map/ppermute | solution.py:938
  187.5 3.8 copy-start.16
  188.6 94.0 %collective-permute-start.2 = (bf16[512,1024]{1,0:T(8,128)(2,1)}, bf16[512,1024]{1,0:T(8,128)(2,1)S(1)}, u32[]{:S(2)}, u32[]{:S(2)}) collective-permute-start(bf16[512,1024]{1,0:T(8,128)(2,1)} %get-tuple-element.200), channel_id=1, source_target_pairs={{0,0},{1,1},{2,4},{3,5},{4,2},{5,3},{6,6},{7,7},{8,8},{9,9},{10,12... | collective-permute-start | bytes 3145736 | tf_op jit(solution)/shard_map/ppermute | solution.py:976
  190.5 92.1 %collective-permute-start.3 = (bf16[512,1024]{1,0:T(8,128)(2,1)S(1)}, bf16[512,1024]{1,0:T(8,128)(2,1)}, u32[]{:S(2)}, u32[]{:S(2)}) collective-permute-start(bf16[512,1024]{1,0:T(8,128)(2,1)S(1)} %get-tuple-element.201), channel_id=1, source_target_pairs={{0,1},{1,0},{2,5},{3,4},{4,3},{5,2},{6,7},{7,6},{8,9},{9,8},{10,13... | collective-permute-start | bytes 3145736 | tf_op jit(solution)/shard_map/ppermute | solution.py:977
  204.5 3.1 copy-start.13
  278.3 8.2 %collective-permute-start.1 = (bf16[1024,512]{1,0:T(8,128)(2,1)}, bf16[1024,512]{1,0:T(8,128)(2,1)}, u32[]{:S(2)}, u32[]{:S(2)}) collective-permute-start(bf16[1024,512]{1,0:T(8,128)(2,1)} %get-tuple-element.203), channel_id=1, source_target_pairs={{0,4},{4,0},{1,5},{5,1},{2,6},{6,2},{3,7},{7,3},{8,12},{12,8},{9,1... | collective-permute-start | bytes 3145736 | tf_op jit(solution)/shard_map/ppermute | solution.py:938
  380.4 27.8 %collective-permute-start.4 = (bf16[4,4,1024,128]{3,2,1,0:T(8,128)(2,1)}, bf16[4,4,1024,128]{3,2,1,0:T(8,128)(2,1)}, u32[]{:S(2)}, u32[]{:S(2)}) collective-permute-start(bf16[4,4,1024,128]{3,2,1,0:T(8,128)(2,1)} %get-tuple-element.113), channel_id=1, source_target_pairs={{0,4},{4,0},{1,5},{5,1},{2,6},{6,2},{3,7},{7,3},{8,12},{12,8},{9,1... | collective-permute-start | bytes 12582920 | tf_op jit(solution)/shard_map/ppermute | solution.py:938
  380.5 15.7 %copy-start.14 = (s32[1,2048]{1,0:T(1,128)S(1)}, s32[1,2048]{1,0:T(1,128)}, u32[]{:S(2)}) copy-start(s32[1,2048]{1,0:T(1,128)} %copy-done.13) | copy-start | bytes 24580
  380.5 15.7 %copy-start.5 = (bf16[1024,1024]{1,0:T(8,128)(2,1)S(1)}, bf16[1024,1024]{1,0:T(8,128)(2,1)}, u32[]{:S(2)}) copy-start(bf16[1024,1024]{1,0:T(8,128)(2,1)} %get-tuple-element.124) | copy-start | bytes 6291460
  395.7 58.1 %collective-permute-start.6 = (bf16[4,4,8,128,128]{4,3,2,1,0:T(8,128)(2,1)}, bf16[4,4,8,128,128]{4,3,2,1,0:T(8,128)(2,1)}, u32[]{:S(2)}, u32[]{:S(2)}) collective-permute-start(bf16[4,4,8,128,128]{4,3,2,1,0:T(8,128)(2,1)} %get-tuple-element.119), channel_id=1, source_target_pairs={{0,4},{4,0},{1,5},{5,1},{2,6},{6,2},{3,7},{7,3},{8,12},{12,8},{9,1... | collective-permute-start | bytes 12582920 | tf_op jit(solution)/shard_map/ppermute | solution.py:938
  396.2 12.0 %copy-start.1 = (bf16[4,4,1024,128]{3,2,1,0:T(8,128)(2,1)S(1)}, bf16[4,4,1024,128]{3,2,1,0:T(8,128)(2,1)}, u32[]{:S(2)}) copy-start(bf16[4,4,1024,128]{3,2,1,0:T(8,128)(2,1)} %get-tuple-element.110) | copy-start | bytes 12582916
  397.7 40.6 %collective-permute-start.8 = (bf16[512,1024]{1,0:T(8,128)(2,1)}, bf16[512,1024]{1,0:T(8,128)(2,1)}, u32[]{:S(2)}, u32[]{:S(2)}) collective-permute-start(bf16[512,1024]{1,0:T(8,128)(2,1)} %get-tuple-element.196), channel_id=1, source_target_pairs={{0,0},{1,1},{4,2},{5,3},{2,4},{3,5},{6,6},{7,7},{8,8},{9,9},{12,10... | collective-permute-start | bytes 3145736 | tf_op jit(solution)/shard_map/ppermute | solution.py:984
  407.3 36.1 %collective-permute-start.9 = (bf16[512,1024]{1,0:T(8,128)(2,1)}, bf16[512,1024]{1,0:T(8,128)(2,1)}, u32[]{:S(2)}, u32[]{:S(2)}) collective-permute-start(bf16[512,1024]{1,0:T(8,128)(2,1)} %get-tuple-element.197), channel_id=1, source_target_pairs={{1,0},{0,1},{5,2},{4,3},{3,4},{2,5},{7,6},{6,7},{9,8},{8,9},{13,10... | collective-permute-start | bytes 3145736 | tf_op jit(solution)/shard_map/ppermute | solution.py:984
  413.6 50.8 %collective-permute-start.5 = (bf16[2,2,2,1024,128]{4,3,2,1,0:T(8,128)(2,1)}, bf16[2,2,2,1024,128]{4,3,2,1,0:T(8,128)(2,1)}, u32[]{:S(2)}, u32[]{:S(2)}) collective-permute-start(bf16[2,2,2,1024,128]{4,3,2,1,0:T(8,128)(2,1)} %get-tuple-element.116), channel_id=1, source_target_pairs={{0,8},{8,0},{16,24},{24,16},{1,9},{9,1},{17,25},{25,17},{2,10},{10... | collective-permute-start | bytes 6291464 | tf_op jit(solution)/shard_map/ppermute | solution.py:1056
  413.6 17.7 %copy-start.3 = (bf16[1024,1024]{1,0:T(8,128)(2,1)S(1)}, bf16[1024,1024]{1,0:T(8,128)(2,1)}, u32[]{:S(2)}) copy-start(bf16[1024,1024]{1,0:T(8,128)(2,1)} %get-tuple-element.99.w_ref) | copy-start | bytes 6291460
  436.6 24.3 %collective-permute-start.7 = (bf16[1024,512]{1,0:T(8,128)(2,1)}, bf16[1024,512]{1,0:T(8,128)(2,1)}, u32[]{:S(2)}, u32[]{:S(2)}) collective-permute-start(bf16[1024,512]{1,0:T(8,128)(2,1)} %get-tuple-element.199), channel_id=1, source_target_pairs={{0,4},{4,0},{1,5},{5,1},{2,6},{6,2},{3,7},{7,3},{8,12},{12,8},{9,1... | collective-permute-start | bytes 3145736 | tf_op jit(solution)/shard_map/ppermute | solution.py:938
  453.8 73.5 %collective-permute-start.12 = (bf16[4,4,256,128]{3,2,1,0:T(8,128)(2,1)}, bf16[4,4,256,128]{3,2,1,0:T(8,128)(2,1)}, u32[]{:S(2)}, u32[]{:S(2)}) collective-permute-start(bf16[4,4,256,128]{3,2,1,0:T(8,128)(2,1)} %get-tuple-element.136), channel_id=1, source_target_pairs={{0,4},{4,0},{1,5},{5,1},{2,6},{6,2},{3,7},{7,3},{8,12},{12,8},{9,1... | collective-permute-start | bytes 3145736 | tf_op jit(solution)/shard_map/ppermute | solution.py:938
  460.8 3.6 copy-start
  467.5 85.5 %collective-permute-start.11 = (bf16[2,2,2,8,128,128]{5,4,3,2,1,0:T(8,128)(2,1)}, bf16[2,2,2,8,128,128]{5,4,3,2,1,0:T(8,128)(2,1)}, u32[]{:S(2)}, u32[]{:S(2)}) collective-permute-start(bf16[2,2,2,8,128,128]{5,4,3,2,1,0:T(8,128)(2,1)} %get-tuple-element.134), channel_id=1, source_target_pairs={{0,16},{8,24},{16,0},{24,8},{1,17},{9,25},{17,1},{25,9},{2,18},{10... | collective-permute-start | bytes 6291464 | tf_op jit(solution)/shard_map/ppermute | solution.py:1056
  524.6 5.5 collective-permute-start.13
  525.2 25.4 %collective-permute-start.10 = (bf16[2,2,1024,128]{3,2,1,0:T(8,128)(2,1)}, bf16[2,2,1024,128]{3,2,1,0:T(8,128)(2,1)}, u32[]{:S(2)}, u32[]{:S(2)}) collective-permute-start(bf16[2,2,1024,128]{3,2,1,0:T(8,128)(2,1)} %get-tuple-element.132), channel_id=1, source_target_pairs={{0,16},{8,24},{16,0},{24,8},{1,17},{9,25},{17,1},{25,9},{2,18},{10... | collective-permute-start | bytes 3145736 | tf_op jit(solution)/shard_map/ppermute | solution.py:1056
  526.7 3.4 copy-start.8
  556.4 50.7 %copy-start.6 = (bf16[2,2,2,256,128]{4,3,2,1,0:T(8,128)(2,1)S(1)}, bf16[2,2,2,256,128]{4,3,2,1,0:T(8,128)(2,1)}, u32[]{:S(2)}) copy-start(bf16[2,2,2,256,128]{4,3,2,1,0:T(8,128)(2,1)} %get-tuple-element.144) | copy-start | bytes 1572868
  556.4 52.7 %copy-start.7 = (bf16[2,1024,128]{2,1,0:T(8,128)(2,1)S(1)}, bf16[2,1024,128]{2,1,0:T(8,128)(2,1)}, u32[]{:S(2)}) copy-start(bf16[2,1024,128]{2,1,0:T(8,128)(2,1)} %get-tuple-element.140) | copy-start | bytes 1572868
  556.4 54.6 %collective-permute-start.17 = (bf16[2,2,3,2,128,128]{5,4,3,2,1,0:T(8,128)(2,1)}, bf16[2,2,3,2,128,128]{5,4,3,2,1,0:T(8,128)(2,1)}, u32[]{:S(2)}, u32[]{:S(2)}) collective-permute-start(bf16[2,2,3,2,128,128]{5,4,3,2,1,0:T(8,128)(2,1)} %bitcast.127), channel_id=1, source_target_pairs={{0,16},{8,24},{16,0},{24,8},{1,17},{9,25},{17,1},{25,9},{2,18},{10... | collective-permute-start | bytes 2359304 | tf_op jit(solution)/shard_map/ppermute | solution.py:1056
  558.1 49.0 %collective-permute-start.16 = (bf16[2,2,2,256,128]{4,3,2,1,0:T(8,128)(2,1)}, bf16[2,2,2,256,128]{4,3,2,1,0:T(8,128)(2,1)}, u32[]{:S(2)}, u32[]{:S(2)}) collective-permute-start(bf16[2,2,2,256,128]{4,3,2,1,0:T(8,128)(2,1)} %get-tuple-element.145), channel_id=1, source_target_pairs={{0,8},{8,0},{16,24},{24,16},{1,9},{9,1},{17,25},{25,17},{2,10},{10... | collective-permute-start | bytes 1572872 | tf_op jit(solution)/shard_map/ppermute | solution.py:1056
  558.1 55.2 %collective-permute-start.15 = (bf16[2,2,8,128,128]{4,3,2,1,0:T(8,128)(2,1)}, bf16[2,2,8,128,128]{4,3,2,1,0:T(8,128)(2,1)}, u32[]{:S(2)}, u32[]{:S(2)}) collective-permute-start(bf16[2,2,8,128,128]{4,3,2,1,0:T(8,128)(2,1)} %get-tuple-element.143), channel_id=1, source_target_pairs={{0,8},{8,0},{16,24},{24,16},{1,9},{9,1},{17,25},{25,17},{2,10},{10... | collective-permute-start | bytes 3145736 | tf_op jit(solution)/shard_map/ppermute | solution.py:1056
  560.1 49.0 %collective-permute-start.14 = (bf16[2,1024,128]{2,1,0:T(8,128)(2,1)}, bf16[2,1024,128]{2,1,0:T(8,128)(2,1)}, u32[]{:S(2)}, u32[]{:S(2)}) collective-permute-start(bf16[2,1024,128]{2,1,0:T(8,128)(2,1)} %get-tuple-element.141), channel_id=1, source_target_pairs={{0,2},{1,3},{2,0},{3,1},{4,6},{5,7},{6,4},{7,5},{8,10},{9,11},{10,... | collective-permute-start | bytes 1572872 | tf_op jit(solution)/shard_map/ppermute | solution.py:1056
  607.0 4.0 copy-start.2
  624.1 36.8 %collective-permute-start.18 = (bf16[1024,1024]{1,0:T(8,128)(2,1)}, bf16[1024,1024]{1,0:T(8,128)(2,1)S(1)}, u32[]{:S(2)}, u32[]{:S(2)}) collective-permute-start(bf16[1024,1024]{1,0:T(8,128)(2,1)} %shard_map.210), channel_id=1, source_target_pairs={{0,4},{4,0},{1,5},{5,1},{2,6},{6,2},{3,7},{7,3},{8,12},{12,8},{9,1... | collective-permute-start | bytes 6291464 | tf_op jit(solution)/shard_map/ppermute | solution.py:938
  628.7 18.6 %copy-start.17 = (f32[8,256]{1,0:T(8,128)S(1)}, f32[8,256]{1,0:T(8,128)}, u32[]{:S(2)}) copy-start(f32[8,256]{1,0:T(8,128)} %get-tuple-element.166) | copy-start | bytes 24580
  628.7 19.3 %copy-start.11 = (bf16[2,8,128,128]{3,2,1,0:T(8,128)(2,1)S(1)}, bf16[2,8,128,128]{3,2,1,0:T(8,128)(2,1)}, u32[]{:S(2)}) copy-start(bf16[2,8,128,128]{3,2,1,0:T(8,128)(2,1)} %get-tuple-element.161) | copy-start | bytes 1572868
  628.7 30.4 %collective-permute-start.22 = (bf16[1024,128]{1,0:T(8,128)(2,1)}, bf16[1024,128]{1,0:T(8,128)(2,1)}, u32[]{:S(2)}, u32[]{:S(2)}) collective-permute-start(bf16[1024,128]{1,0:T(8,128)(2,1)} %get-tuple-element.175), channel_id=1, source_target_pairs={{0,1},{1,0},{2,3},{3,2},{4,5},{5,4},{6,7},{7,6},{8,9},{9,8},{10,11... | collective-permute-start | bytes 786440 | tf_op jit(solution)/shard_map/ppermute | solution.py:1056
  648.0 26.0 %collective-permute-start.20 = (bf16[2,8,128,128]{3,2,1,0:T(8,128)(2,1)S(1)}, bf16[2,8,128,128]{3,2,1,0:T(8,128)(2,1)S(1)}, u32[]{:S(2)}, u32[]{:S(2)}) collective-permute-start(bf16[2,8,128,128]{3,2,1,0:T(8,128)(2,1)S(1)} %copy-done.11), channel_id=1, source_target_pairs={{0,2},{1,3},{2,0},{3,1},{4,6},{5,7},{6,4},{7,5},{8,10},{9,11},{10,... | collective-permute-start | bytes 1572872 | tf_op jit(solution)/shard_map/ppermute | solution.py:1056
  649.0 16.2 %collective-permute-start.19 = (bf16[2,3,2,128,128]{4,3,2,1,0:T(8,128)(2,1)}, bf16[2,3,2,128,128]{4,3,2,1,0:T(8,128)(2,1)}, u32[]{:S(2)}, u32[]{:S(2)}) collective-permute-start(bf16[2,3,2,128,128]{4,3,2,1,0:T(8,128)(2,1)} %get-tuple-element.159), channel_id=1, source_target_pairs={{0,8},{8,0},{16,24},{24,16},{1,9},{9,1},{17,25},{25,17},{2,10},{10... | collective-permute-start | bytes 1179656 | tf_op jit(solution)/shard_map/ppermute | solution.py:1056
  649.0 16.2 %collective-permute-start.21 = (bf16[2,2,256,128]{3,2,1,0:T(8,128)(2,1)}, bf16[2,2,256,128]{3,2,1,0:T(8,128)(2,1)}, u32[]{:S(2)}, u32[]{:S(2)}) collective-permute-start(bf16[2,2,256,128]{3,2,1,0:T(8,128)(2,1)} %get-tuple-element.163), channel_id=1, source_target_pairs={{0,16},{8,24},{16,0},{24,8},{1,17},{9,25},{17,1},{25,9},{2,18},{10... | collective-permute-start | bytes 786440 | tf_op jit(solution)/shard_map/ppermute | solution.py:1056
  674.1 0.8 copy-start.9
  756.5 4.2 copy-start.10
  756.5 5.0 copy-start.12
  756.5 8.2 %copy-start.15 = (f32[256,128]{1,0:T(8,128)S(1)}, f32[256,128]{1,0:T(8,128)}, u32[]{:S(2)}) copy-start(f32[256,128]{1,0:T(8,128)} %get-tuple-element.243) | copy-start | bytes 393220

commit v6 on v5

--- a/solution.py
+++ b/solution.py
@@ -482,7 +482,7 @@
         qkv_grad_kernel, (1,),
         [held((d, n)), held((n, f)), held((n, f)), held((n, f))],
         ([spec, spec, held((8, f))], [shape, shape, sds((8, f), F32)]),
-        [pltpu.VMEM((d, f), BF16)], 6 * n * f * d, x, dq, dk, dv,
+        [pltpu.VMEM((d, f), BF16)], n * f * d // 64, x, dq, dk, dv,
     )
 
 
@@ -647,11 +647,13 @@
     peer_a = {"core": t // 2, "tensor": 2 * core + odd}
     peer_b = {"core": t // 2, "tensor": 2 * core + 1 - odd}
 
-    pl.when(jnp.logical_not(stays))(lambda: send(x_ref.at[odd], x_rows, x_at[0], peer_a))
     x_own = pltpu.make_async_copy(x_ref.at[odd], x_rows, own_sems.at[used[1]])
     used[1] += 1
     pl.when(stays)(x_own.start)
-    send(x_ref.at[1 - odd], x_rows, x_at[1], peer_b)
+
+    def send_tokens():
+        pl.when(jnp.logical_not(stays))(lambda: send(x_ref.at[odd], x_rows, x_at[0], peer_a))
+        send(x_ref.at[1 - odd], x_rows, x_at[1], peer_b)
 
     partner = {"core": 1 - core}
     passes = []
@@ -708,6 +710,8 @@
                         copy.wait()
                 hop_arrived(i, at)
                 hop(i, at + 1)
+                if i == n - 1 and at == hops - 2:
+                    send_tokens()
             elif 0 <= at - (hops - 1) <= len(bits):
                 stage(i, at - (hops - 1))
 

time: 779 us -> 740 us (0.950)
  Pallas kernels: 606 us -> 572 us
    pallas_call x1, Pallas kernels: 183 us -> 147 us  [start_gather(): pl.pallas_call(functools.partial(start_kernel, n_p, n_t, kinds), out_shap...]
  transfers between devices with their start and end apart: 23 -> 23, of which waited for: 3 -> 3; matrix products, arithmetic and copies ran while one was open for 10% -> 10% of each run, Pallas kernels for 56% -> 54%
where the time goes in v6:
time: 740 us; the launch traced here: 726 us
  Pallas kernels  572 us (77%)
  other arithmetic  67.6 us (9%)
  starting transfers between devices  29 us (4%)
  waiting for transfers between devices  28.5 us (4%)
  local copies, waits for them, and re-layouts  23.4 us (3%)
    pallas_call x1, Pallas kernels, start_gather(): pl.pallas_call(functools.partial(start_kernel, n_p, n_t, kinds), out_shap...  147 us
    pallas_call x2, Pallas kernels, attend_bwd(): pl.pallas_call(functools.partial(attend_bwd_kernel, bq), grid_spec=pltpu....  96.6 us
    pallas_call x4, Pallas kernels, call(): pl.pallas_call(kernel, grid=grid, in_specs=ins, out_specs=outs[0], out_sh...  83.8 us
    pallas_call x1, Pallas kernels, finish(): pl.pallas_call(functools.partial(finish_kernel, n_p, n_t), out_shape=[sds...  80.2 us
    pallas_call x1, Pallas kernels, attend_fwd(): pl.pallas_call(functools.partial(attend_fwd_kernel, bk), grid_spec=pltpu....  68.1 us
    pallas_call x5, Pallas kernels, grad_call(): pl.pallas_call(kernel, grid=grid, in_specs=ins, out_specs=outs[0], out_sh...  57.9 us
    convert_element_type x10, other arithmetic, cut_one(): self.sum_of(lambda part: lax.dynamic_index_in_dim(part, which, at, keepdi...  32.8 us
    ppermute x11, waiting for transfers between devices, move(): self.parts = [self.live[0], lax.ppermute(self.live[1], *self.route)]  28.1 us
  transfers between devices with their start and end apart: 23, of which 3 were waited for; matrix products, arithmetic and copies ran while one was open for 10% of the time, Pallas kernels for 54%

profile of v6, /device:TPU:0, one launch (start us, length us, event | category | flops | bytes accessed | tf_op | source)
XLA Modules:
  0.0 725.8 jit_solution(5280049361969771765)
XLA Ops:
  0.7 0.9 fusion.21
  2.8 1.3 maximum_bitcast_fusion.1.refs_1_
  4.1 146.7 %shard_map.195 = (bf16[2048,1024]{1,0:T(8,128)(2,1)}, f32[4,12,128]{2,1,0:T(8,128)}, bf16[1024,3072]{1,0:T(8,128)(2,1)}, bf16[1024,1024]{1,0:T(8,128)(2,1)}, bf1...) custom-call(bf16[2,512,1024]{2,1,0:T(8,128)(2,1)} %refs_0_.1, f32[12,128]{1,0:T(8,128)} %maximum_bitcast_fusion.1.refs_1_, ...), custom_call_target="tpu_custom_call" | custom-call | tf_op jit(solution)/shard_map/pallas_call | solution.py:759
  150.8 1.2 dynamic-slice_bitcast_fusion.1
  152.0 1.9 collective-permute-start.2
  154.7 12.3 %shard_map.196 = (bf16[2048,1536]{1,0:T(8,128)(2,1)}, bf16[1024,2048]{1,0:T(8,128)(2,1)}) custom-call(s32[1]{0:T(128)} %bitcast.core_ref.at_ref, bf16[2048,1024]{1,0:T(8,128)(2,1)} %get-tuple-element.94.x_ref, bf16[1024,3072]{1,0:T(8,128)(2,1)} %get-tuple-element.95.w_ref.refs_6_, f32[1,1536]{1,0:T(1,128)} %reshape.231.bias_ref), custom_call_target="tpu_custom_call" | custom-call | flops 6442450944 | bytes 14680064 | tf_op jit(solution)/shard_map/pallas_call | solution.py:779
  168.8 1.3 broadcast_in_dim.11.kcode_ref
  170.2 68.1 %shard_map.197 = (bf16[2048,512]{1,0:T(8,128)(2,1)}, f32[32,2048]{1,0:T(8,128)}) custom-call(s32[4]{0:T(128)} %get-tuple-element.228.lo_ref, s32[4]{0:T(128)} %get-tuple-element.227.hi_ref, s32[4]{0:T(128)} %reduce_sum.56.pad_ref, bf16[2048,1536]{1,0:T(8,128)(2,1)} %get-tuple-element.97.q_ref.k_ref.v_ref, ...), custom_call_target="tpu_custom_call" | custom-call | flops 8589934592 | bytes 25165824 | tf_op jit(solution)/shard_map/pallas_call | solution.py:160
  238.3 2.6 constant_dynamic-slice_fusion.8
  240.9 2.6 collective-permute-start.1
  244.1 3.8 maximum_select_fusion.1.e_ref
  248.0 3.7 maximum_select_fusion.c_ref.a_ref
  251.6 8.7 %shard_map.198 = (bf16[1024,1024]{1,0:T(8,128)(2,1)}, bf16[1024,1024]{1,0:T(8,128)(2,1)}, f32[1024,1024]{1,0:T(8,128)}, f32[1024,128]{1,0:T(8,128)}) custom-call(s32[1]{0:T(128)} %bitcast.core_ref.at_ref, bf16[2048,1024]{1,0:T(8,128)(2,1)} %get-tuple-element.94.x_ref, bf16[1024,1024]{1,0:T(8,128)(2,1)} %maximum_select_fusion.c_ref.a_ref, ...), custom_call_target="tpu_custom_call" | custom-call | flops 2147483648 | bytes 12582912 | tf_op jit(solution)/shard_map/pallas_call | solution.py:325
  260.3 24.8 %shard_map.199 = (bf16[1024,4096]{1,0:T(8,128)(2,1)}, bf16[1024,4096]{1,0:T(8,128)(2,1)}) custom-call(bf16[1024,1024]{1,0:T(8,128)(2,1)} %get-tuple-element.100.h_ref, bf16[1024,4096]{1,0:T(8,128)(2,1)} %get-tuple-element.101.w_ref, f32[1,4096]{1,0:T(1,128)} %bitcast.159), custom_call_target="tpu_custom_call" | custom-call | flops 8589934592 | bytes 25165824 | tf_op jit(solution)/shard_map/pallas_call | solution.py:293
  285.1 19.2 %shard_map.200 = (bf16[1024,1024]{1,0:T(8,128)(2,1)}, f32[1024,1024]{1,0:T(8,128)}, bf16[1024,1024]{1,0:T(8,128)(2,1)}, f32[8,1024]{1,0:T(8,128)}) custom-call(bf16[1024,4096]{1,0:T(8,128)(2,1)} %get-tuple-element.109.g_ref.a_ref, bf16[4096,1024]{1,0:T(8,128)(2,1)} %get-tuple-element.103.w_ref, f32[1024,1024]{1,0:T(8,128)} %get-tuple-element.104.n_ref, ...), custom_call_target="tpu_custom_call" | custom-call | flops 8589934592 | bytes 16777216 | tf_op jit(solution)/shard_map/pallas_call | solution.py:293
  304.3 22.0 %shard_map.201 = (bf16[1024,4096]{1,0:T(8,128)(2,1)}, f32[8,4096]{1,0:T(8,128)}) custom-call(bf16[1024,1024]{1,0:T(8,128)(2,1)} %get-tuple-element.106.dz_ref.b_ref, bf16[4096,1024]{1,0:T(8,128)(2,1)} %get-tuple-element.103.w_ref, bf16[1024,4096]{1,0:T(8,128)(2,1)} %get-tuple-element.107.slope_ref), custom_call_target="tpu_custom_call" | custom-call | flops 8589934592 | bytes 25165824 | tf_op jit(solution)/shard_map/pallas_call | solution.py:293
  326.3 15.6 %shard_map.202 = (bf16[4,4,1024,128]{3,2,1,0:T(8,128)(2,1)}, bf16[4,4,1024,128]{3,2,1,0:T(8,128)(2,1)}) custom-call(bf16[1024,4096]{1,0:T(8,128)(2,1)} %get-tuple-element.109.g_ref.a_ref, bf16[1024,1024]{1,0:T(8,128)(2,1)} %get-tuple-element.106.dz_ref.b_ref), custom_call_target="tpu_custom_call" | custom-call | flops 8589934592 | bytes 16777216 | tf_op jit(solution)/shard_map/pallas_call | solution.py:434
  342.0 15.2 %shard_map.203 = (bf16[4,4,8,128,128]{4,3,2,1,0:T(8,128)(2,1)}, bf16[4,4,8,128,128]{4,3,2,1,0:T(8,128)(2,1)}) custom-call(bf16[1024,1024]{1,0:T(8,128)(2,1)} %get-tuple-element.117.a_ref, bf16[1024,4096]{1,0:T(8,128)(2,1)} %get-tuple-element.120.b_ref.du_ref), custom_call_target="tpu_custom_call" | custom-call | flops 8589934592 | bytes 16777216 | tf_op jit(solution)/shard_map/pallas_call | solution.py:434
  357.7 1.5 constant_dynamic-slice_fusion.4
  359.2 9.6 %collective-permute-start.8 = (bf16[512,1024]{1,0:T(8,128)(2,1)}, bf16[512,1024]{1,0:T(8,128)(2,1)}, u32[]{:S(2)}, u32[]{:S(2)}) collective-permute-start(bf16[512,1024]{1,0:T(8,128)(2,1)} %get-tuple-element.196), channel_id=1, source_target_pairs={{0,0},{1,1},{4,2},{5,3},{2,4},{3,5},{6,6},{7,7},{8,8},{9,9},{12,10... | collective-permute-start | bytes 3145736 | tf_op jit(solution)/shard_map/ppermute | solution.py:988
  368.8 5.4 fusion.1
  374.2 17.7 %shard_map.204 = (f32[1024,1024]{1,0:T(8,128)}, bf16[1024,1024]{1,0:T(8,128)(2,1)}, f32[8,1024]{1,0:T(8,128)}) custom-call(bf16[1024,4096]{1,0:T(8,128)(2,1)} %get-tuple-element.120.b_ref.du_ref, bf16[1024,4096]{1,0:T(8,128)(2,1)} %get-tuple-element.101.w_ref, f32[1024,1024]{1,0:T(8,128)} %get-tuple-element.121.dr_ref, ...), custom_call_target="tpu_custom_call" | custom-call | flops 8589934592 | bytes 16777216 | tf_op jit(solution)/shard_map/pallas_call | solution.py:293
  392.0 4.0 convolution_convert_fusion
  396.0 1.2 constant_dynamic-slice_fusion.6
  399.3 4.0 maximum_select_fusion.3
  403.3 6.4 shard_map.206
  409.9 7.0 fusion.3
  416.9 3.6 maximum_select_fusion.2.dc_ref
  420.5 3.1 fusion.5
  423.6 7.0 collective-permute-start.11
  430.6 48.2 %shard_map.205 = (bf16[2048,256]{1,0:T(8,128)(2,1)}, bf16[2048,256]{1,0:T(8,128)(2,1)}, bf16[2048,256]{1,0:T(8,128)(2,1)}) custom-call(s32[8]{0:T(128)} %get-tuple-element.226.lo_ref, s32[8]{0:T(128)} %get-tuple-element.225.hi_ref, s32[8]{0:T(128)} %reduce_sum.62.pad_ref, bf16[2048,1536]{1,0:T(8,128)(2,1)} %get-tuple-element.97.q_ref.k_ref.v_ref, ...), custom_call_target="tpu_custom_call" | custom-call | flops 21474836480 | bytes 50331648 | tf_op jit(solution)/shard_map/pallas_call | solution.py:198
  478.8 10.4 %shard_map.207 = (bf16[4,1,3,2,128,128]{5,4,3,2,1,0:T(8,128)(2,1)}, bf16[4,1,3,2,128,128]{5,4,3,2,1,0:T(8,128)(2,1)}, f32[8,256]{1,0:T(8,128)}) custom-call(bf16[1024,2048]{1,0:T(8,128)(2,1)} %get-tuple-element.137.x_ref, bf16[2048,256]{1,0:T(8,128)(2,1)} %get-tuple-element.128.dq_ref.refs_0_, bf16[2048,256]{1,0:T(8,128)(2,1)} %get-tuple-element.129.dk_ref.refs_1_, ...), custom_call_target="tpu_custom_call" | custom-call | flops 8388608 | bytes 16384 | tf_op jit(solution)/shard_map/pallas_call | solution.py:434
  490.4 2.8 fusion.11
  493.2 1.6 maximum_select_fusion.4
  494.9 0.9 copy.94
  495.9 1.0 copy.95
  496.9 18.2 %collective-permute-done.10 = bf16[2,2,1024,128]{3,2,1,0:T(8,128)(2,1)} collective-permute-done((bf16[2,2,1024,128]{3,2,1,0:T(8,128)(2,1)}, bf16[2,2,1024,128]{3,2,1,0:T(8,128)(2,1)}, u32[]{:S(2)}, u32[]{:S(2)}) %collective-permute-start.10) | collective-permute-done | bytes 1048608 | tf_op jit(solution)/shard_map/ppermute | solution.py:1060
  515.1 2.5 fusion.9
  517.5 3.3 fusion.7
  521.2 2.0 collective-permute-start.15
  523.2 3.2 collective-permute-start.14
  526.4 48.4 %shard_map.208 = (bf16[2048,256]{1,0:T(8,128)(2,1)}, bf16[2048,256]{1,0:T(8,128)(2,1)}, bf16[2048,256]{1,0:T(8,128)(2,1)}) custom-call(s32[8]{0:T(128)} %get-tuple-element.226.lo_ref, s32[8]{0:T(128)} %get-tuple-element.225.hi_ref, s32[8]{0:T(128)} %reduce_sum.62.pad_ref, bf16[2048,1536]{1,0:T(8,128)(2,1)} %get-tuple-element.97.q_ref.k_ref.v_ref, ...), custom_call_target="tpu_custom_call" | custom-call | flops 21474836480 | bytes 50331648 | tf_op jit(solution)/shard_map/pallas_call | solution.py:198
  574.8 2.1 fusion.19
  576.9 1.9 fusion.17
  578.8 2.2 fusion.15
  581.0 2.5 fusion.13
  583.5 8.4 %shard_map.210 = bf16[1024,1024]{1,0:T(8,128)(2,1)} custom-call(s32[2]{0:T(128)} %pad_add_fusion.1.at_ref, bf16[2048,256]{1,0:T(8,128)(2,1)} %get-tuple-element.128.dq_ref.refs_0_, bf16[2048,256]{1,0:T(8,128)(2,1)} %get-tuple-element.129.dk_ref.refs_1_, bf16[2048,256]{1,0:T(8,128)(2,1)} %get-tuple-element.130.dv_ref.refs_2_, ...), custom_call_target="tpu_custom_call" | custom-call | flops 3221225472 | bytes 16777216 | tf_op jit(solution)/shard_map/pallas_call | solution.py:508
  592.5 0.8 slice.85
  593.3 0.8 slice.83
  594.0 0.9 slice.87
  594.9 0.8 slice.84
  595.7 0.8 slice.82
  596.6 10.3 %shard_map.211 = (bf16[4,1,3,2,128,128]{5,4,3,2,1,0:T(8,128)(2,1)}, bf16[4,1,3,2,128,128]{5,4,3,2,1,0:T(8,128)(2,1)}, f32[8,256]{1,0:T(8,128)}) custom-call(bf16[1024,2048]{1,0:T(8,128)(2,1)} %get-tuple-element.137.x_ref, bf16[2048,256]{1,0:T(8,128)(2,1)} %get-tuple-element.152.refs_3_.dq_ref, bf16[2048,256]{1,0:T(8,128)(2,1)} %get-tuple-element.153.refs_4_.dk_ref, ...), custom_call_target="tpu_custom_call" | custom-call | flops 8388608 | bytes 16384 | tf_op jit(solution)/shard_map/pallas_call | solution.py:434
  608.7 9.5 %shard_map.209 = f32[1024,1024]{1,0:T(8,128)} custom-call(s32[2]{0:T(128)} %pad_add_fusion.at_ref, bf16[2048,256]{1,0:T(8,128)(2,1)} %get-tuple-element.128.dq_ref.refs_0_, bf16[2048,256]{1,0:T(8,128)(2,1)} %get-tuple-element.129.dk_ref.refs_1_, bf16[2048,256]{1,0:T(8,128)(2,1)} %get-tuple-element.130.dv_ref.refs_2_, ...), custom_call_target="tpu_custom_call" | custom-call | flops 3221225472 | bytes 16777216 | tf_op jit(solution)/shard_map/pallas_call | solution.py:508
  618.2 1.8 convert_add_fusion
  620.0 4.3 add_convert_fusion.refs_0_
  624.4 9.9 %collective-permute-done.20 = bf16[2,8,128,128]{3,2,1,0:T(8,128)(2,1)S(1)} collective-permute-done((bf16[2,8,128,128]{3,2,1,0:T(8,128)(2,1)S(1)}, bf16[2,8,128,128]{3,2,1,0:T(8,128)(2,1)S(1)}, u32[]{:S(2)}, u32[]{:S(2)}) %collective-permute-start.20) | collective-permute-done | bytes 524320 | tf_op jit(solution)/shard_map/ppermute | solution.py:1060
  634.2 0.8 copy-done.9
  635.0 80.2 %shard_map.212 = (bf16[2,512,1024]{2,1,0:T(8,128)(2,1)}, f32[768,128]{1,0:T(8,128)}, f32[1024,128]{1,0:T(8,128)}, f32[256,128]{1,0:T(8,128)}, f32[96,128]{1,0:T(8,128)}) custom-call(bf16[1024,1024]{1,0:T(8,128)(2,1)} %add_convert_fusion.refs_0_, bf16[4,768,128]{2,1,0:T(8,128)(2,1)} %bitcast.141, bf16[4,768,128]{2,1,0:T(8,128)(2,1)} %bitcast.142, ...), custom_call_target="tpu_custom_call" | custom-call | tf_op jit(solution)/shard_map/pallas_call | solution.py:922
  715.2 0.7 slice_bitcast_fusion.1
  716.0 0.7 fusion.23
  716.7 4.2 convert_element_type.428
  720.8 0.8 copy.96
  721.7 0.8 copy.97
  (119 shorter events, 14.6 us)
Async XLA Ops:
  0.6 150.2 %copy-start.4 = (bf16[2,512,1024]{2,1,0:T(8,128)(2,1)S(1)}, bf16[2,512,1024]{2,1,0:T(8,128)(2,1)}, u32[]{:S(2)}) copy-start(bf16[2,512,1024]{2,1,0:T(8,128)(2,1)} %param.23) | copy-start | bytes 6291460
  1.5 165.5 %collective-permute-start = (s32[2,2048]{1,0:T(2,128)S(1)}, s32[2,2048]{1,0:T(2,128)S(1)}, u32[]{:S(2)}, u32[]{:S(2)}) collective-permute-start(s32[2,2048]{1,0:T(2,128)S(1)} %fusion.21), channel_id=1, source_target_pairs={{0,4},{4,0},{1,5},{5,1},{2,6},{6,2},{3,7},{7,3},{8,12},{12,8},{9,1... | collective-permute-start | bytes 49160 | tf_op jit(solution)/shard_map/ppermute | solution.py:942
  150.8 3.0 copy-start.16
  152.0 92.1 %collective-permute-start.2 = (bf16[512,1024]{1,0:T(8,128)(2,1)}, bf16[512,1024]{1,0:T(8,128)(2,1)S(1)}, u32[]{:S(2)}, u32[]{:S(2)}) collective-permute-start(bf16[512,1024]{1,0:T(8,128)(2,1)} %get-tuple-element.200), channel_id=1, source_target_pairs={{0,0},{1,1},{2,4},{3,5},{4,2},{5,3},{6,6},{7,7},{8,8},{9,9},{10,12... | collective-permute-start | bytes 3145736 | tf_op jit(solution)/shard_map/ppermute | solution.py:980
  153.9 90.3 %collective-permute-start.3 = (bf16[512,1024]{1,0:T(8,128)(2,1)S(1)}, bf16[512,1024]{1,0:T(8,128)(2,1)}, u32[]{:S(2)}, u32[]{:S(2)}) collective-permute-start(bf16[512,1024]{1,0:T(8,128)(2,1)S(1)} %get-tuple-element.201), channel_id=1, source_target_pairs={{0,1},{1,0},{2,5},{3,4},{4,3},{5,2},{6,7},{7,6},{8,9},{9,8},{10,13... | collective-permute-start | bytes 3145736 | tf_op jit(solution)/shard_map/ppermute | solution.py:981
  167.1 3.1 copy-start.13
  240.9 7.0 collective-permute-start.1
  341.9 26.9 %collective-permute-start.4 = (bf16[4,4,1024,128]{3,2,1,0:T(8,128)(2,1)}, bf16[4,4,1024,128]{3,2,1,0:T(8,128)(2,1)}, u32[]{:S(2)}, u32[]{:S(2)}) collective-permute-start(bf16[4,4,1024,128]{3,2,1,0:T(8,128)(2,1)} %get-tuple-element.113), channel_id=1, source_target_pairs={{0,4},{4,0},{1,5},{5,1},{2,6},{6,2},{3,7},{7,3},{8,12},{12,8},{9,1... | collective-permute-start | bytes 12582920 | tf_op jit(solution)/shard_map/ppermute | solution.py:942
  342.0 15.7 %copy-start.14 = (s32[1,2048]{1,0:T(1,128)S(1)}, s32[1,2048]{1,0:T(1,128)}, u32[]{:S(2)}) copy-start(s32[1,2048]{1,0:T(1,128)} %copy-done.13) | copy-start | bytes 24580
  342.0 15.7 %copy-start.5 = (bf16[1024,1024]{1,0:T(8,128)(2,1)S(1)}, bf16[1024,1024]{1,0:T(8,128)(2,1)}, u32[]{:S(2)}) copy-start(bf16[1024,1024]{1,0:T(8,128)(2,1)} %get-tuple-element.124) | copy-start | bytes 6291460
  357.2 52.7 %collective-permute-start.6 = (bf16[4,4,8,128,128]{4,3,2,1,0:T(8,128)(2,1)}, bf16[4,4,8,128,128]{4,3,2,1,0:T(8,128)(2,1)}, u32[]{:S(2)}, u32[]{:S(2)}) collective-permute-start(bf16[4,4,8,128,128]{4,3,2,1,0:T(8,128)(2,1)} %get-tuple-element.119), channel_id=1, source_target_pairs={{0,4},{4,0},{1,5},{5,1},{2,6},{6,2},{3,7},{7,3},{8,12},{12,8},{9,1... | collective-permute-start | bytes 12582920 | tf_op jit(solution)/shard_map/ppermute | solution.py:942
  357.7 11.1 %copy-start.1 = (bf16[4,4,1024,128]{3,2,1,0:T(8,128)(2,1)S(1)}, bf16[4,4,1024,128]{3,2,1,0:T(8,128)(2,1)}, u32[]{:S(2)}) copy-start(bf16[4,4,1024,128]{3,2,1,0:T(8,128)(2,1)} %get-tuple-element.110) | copy-start | bytes 12582916
  359.2 39.7 %collective-permute-start.8 = (bf16[512,1024]{1,0:T(8,128)(2,1)}, bf16[512,1024]{1,0:T(8,128)(2,1)}, u32[]{:S(2)}, u32[]{:S(2)}) collective-permute-start(bf16[512,1024]{1,0:T(8,128)(2,1)} %get-tuple-element.196), channel_id=1, source_target_pairs={{0,0},{1,1},{4,2},{5,3},{2,4},{3,5},{6,6},{7,7},{8,8},{9,9},{12,10... | collective-permute-start | bytes 3145736 | tf_op jit(solution)/shard_map/ppermute | solution.py:988
  368.8 30.5 %collective-permute-start.9 = (bf16[512,1024]{1,0:T(8,128)(2,1)}, bf16[512,1024]{1,0:T(8,128)(2,1)}, u32[]{:S(2)}, u32[]{:S(2)}) collective-permute-start(bf16[512,1024]{1,0:T(8,128)(2,1)} %get-tuple-element.197), channel_id=1, source_target_pairs={{1,0},{0,1},{5,2},{4,3},{3,4},{2,5},{7,6},{6,7},{9,8},{8,9},{13,10... | collective-permute-start | bytes 3145736 | tf_op jit(solution)/shard_map/ppermute | solution.py:988
  374.2 46.3 %collective-permute-start.5 = (bf16[2,2,2,1024,128]{4,3,2,1,0:T(8,128)(2,1)}, bf16[2,2,2,1024,128]{4,3,2,1,0:T(8,128)(2,1)}, u32[]{:S(2)}, u32[]{:S(2)}) collective-permute-start(bf16[2,2,2,1024,128]{4,3,2,1,0:T(8,128)(2,1)} %get-tuple-element.116), channel_id=1, source_target_pairs={{0,8},{8,0},{16,24},{24,16},{1,9},{9,1},{17,25},{25,17},{2,10},{10... | collective-permute-start | bytes 6291464 | tf_op jit(solution)/shard_map/ppermute | solution.py:1060
  374.2 17.7 %copy-start.3 = (bf16[1024,1024]{1,0:T(8,128)(2,1)S(1)}, bf16[1024,1024]{1,0:T(8,128)(2,1)}, u32[]{:S(2)}) copy-start(bf16[1024,1024]{1,0:T(8,128)(2,1)} %get-tuple-element.99.w_ref) | copy-start | bytes 6291460
  397.2 19.7 %collective-permute-start.7 = (bf16[1024,512]{1,0:T(8,128)(2,1)}, bf16[1024,512]{1,0:T(8,128)(2,1)}, u32[]{:S(2)}, u32[]{:S(2)}) collective-permute-start(bf16[1024,512]{1,0:T(8,128)(2,1)} %get-tuple-element.199), channel_id=1, source_target_pairs={{0,4},{4,0},{1,5},{5,1},{2,6},{6,2},{3,7},{7,3},{8,12},{12,8},{9,1... | collective-permute-start | bytes 3145736 | tf_op jit(solution)/shard_map/ppermute | solution.py:942
  409.7 80.7 %collective-permute-start.12 = (bf16[4,4,256,128]{3,2,1,0:T(8,128)(2,1)}, bf16[4,4,256,128]{3,2,1,0:T(8,128)(2,1)}, u32[]{:S(2)}, u32[]{:S(2)}) collective-permute-start(bf16[4,4,256,128]{3,2,1,0:T(8,128)(2,1)} %get-tuple-element.136), channel_id=1, source_target_pairs={{0,4},{4,0},{1,5},{5,1},{2,6},{6,2},{3,7},{7,3},{8,12},{12,8},{9,1... | collective-permute-start | bytes 3145736 | tf_op jit(solution)/shard_map/ppermute | solution.py:942
  416.9 3.6 copy-start
  423.6 94.0 %collective-permute-start.11 = (bf16[2,2,2,8,128,128]{5,4,3,2,1,0:T(8,128)(2,1)}, bf16[2,2,2,8,128,128]{5,4,3,2,1,0:T(8,128)(2,1)}, u32[]{:S(2)}, u32[]{:S(2)}) collective-permute-start(bf16[2,2,2,8,128,128]{5,4,3,2,1,0:T(8,128)(2,1)} %get-tuple-element.134), channel_id=1, source_target_pairs={{0,16},{8,24},{16,0},{24,8},{1,17},{9,25},{17,1},{25,9},{2,18},{10... | collective-permute-start | bytes 6291464 | tf_op jit(solution)/shard_map/ppermute | solution.py:1060
  489.2 4.0 collective-permute-start.13
  489.5 25.6 %collective-permute-start.10 = (bf16[2,2,1024,128]{3,2,1,0:T(8,128)(2,1)}, bf16[2,2,1024,128]{3,2,1,0:T(8,128)(2,1)}, u32[]{:S(2)}, u32[]{:S(2)}) collective-permute-start(bf16[2,2,1024,128]{3,2,1,0:T(8,128)(2,1)} %get-tuple-element.132), channel_id=1, source_target_pairs={{0,16},{8,24},{16,0},{24,8},{1,17},{9,25},{17,1},{25,9},{2,18},{10... | collective-permute-start | bytes 3145736 | tf_op jit(solution)/shard_map/ppermute | solution.py:1060
  489.8 3.4 copy-start.8
  520.9 53.9 %copy-start.6 = (bf16[2,2,2,256,128]{4,3,2,1,0:T(8,128)(2,1)S(1)}, bf16[2,2,2,256,128]{4,3,2,1,0:T(8,128)(2,1)}, u32[]{:S(2)}) copy-start(bf16[2,2,2,256,128]{4,3,2,1,0:T(8,128)(2,1)} %get-tuple-element.144) | copy-start | bytes 1572868
  520.9 56.0 %copy-start.7 = (bf16[2,1024,128]{2,1,0:T(8,128)(2,1)S(1)}, bf16[2,1024,128]{2,1,0:T(8,128)(2,1)}, u32[]{:S(2)}) copy-start(bf16[2,1024,128]{2,1,0:T(8,128)(2,1)} %get-tuple-element.140) | copy-start | bytes 1572868
  520.9 57.9 %collective-permute-start.17 = (bf16[2,2,3,2,128,128]{5,4,3,2,1,0:T(8,128)(2,1)}, bf16[2,2,3,2,128,128]{5,4,3,2,1,0:T(8,128)(2,1)}, u32[]{:S(2)}, u32[]{:S(2)}) collective-permute-start(bf16[2,2,3,2,128,128]{5,4,3,2,1,0:T(8,128)(2,1)} %bitcast.127), channel_id=1, source_target_pairs={{0,16},{8,24},{16,0},{24,8},{1,17},{9,25},{17,1},{25,9},{2,18},{10... | collective-permute-start | bytes 2359304 | tf_op jit(solution)/shard_map/ppermute | solution.py:1060
  521.2 53.6 %collective-permute-start.16 = (bf16[2,2,2,256,128]{4,3,2,1,0:T(8,128)(2,1)}, bf16[2,2,2,256,128]{4,3,2,1,0:T(8,128)(2,1)}, u32[]{:S(2)}, u32[]{:S(2)}) collective-permute-start(bf16[2,2,2,256,128]{4,3,2,1,0:T(8,128)(2,1)} %get-tuple-element.145), channel_id=1, source_target_pairs={{0,8},{8,0},{16,24},{24,16},{1,9},{9,1},{17,25},{25,17},{2,10},{10... | collective-permute-start | bytes 1572872 | tf_op jit(solution)/shard_map/ppermute | solution.py:1060
  521.2 59.8 %collective-permute-start.15 = (bf16[2,2,8,128,128]{4,3,2,1,0:T(8,128)(2,1)}, bf16[2,2,8,128,128]{4,3,2,1,0:T(8,128)(2,1)}, u32[]{:S(2)}, u32[]{:S(2)}) collective-permute-start(bf16[2,2,8,128,128]{4,3,2,1,0:T(8,128)(2,1)} %get-tuple-element.143), channel_id=1, source_target_pairs={{0,8},{8,0},{16,24},{24,16},{1,9},{9,1},{17,25},{25,17},{2,10},{10... | collective-permute-start | bytes 3145736 | tf_op jit(solution)/shard_map/ppermute | solution.py:1060
  523.2 53.7 %collective-permute-start.14 = (bf16[2,1024,128]{2,1,0:T(8,128)(2,1)}, bf16[2,1024,128]{2,1,0:T(8,128)(2,1)}, u32[]{:S(2)}, u32[]{:S(2)}) collective-permute-start(bf16[2,1024,128]{2,1,0:T(8,128)(2,1)} %get-tuple-element.141), channel_id=1, source_target_pairs={{0,2},{1,3},{2,0},{3,1},{4,6},{5,7},{6,4},{7,5},{8,10},{9,11},{10,... | collective-permute-start | bytes 1572872 | tf_op jit(solution)/shard_map/ppermute | solution.py:1060
  574.8 4.0 copy-start.2
  591.9 28.1 %collective-permute-start.18 = (bf16[1024,1024]{1,0:T(8,128)(2,1)}, bf16[1024,1024]{1,0:T(8,128)(2,1)S(1)}, u32[]{:S(2)}, u32[]{:S(2)}) collective-permute-start(bf16[1024,1024]{1,0:T(8,128)(2,1)} %shard_map.210), channel_id=1, source_target_pairs={{0,4},{4,0},{1,5},{5,1},{2,6},{6,2},{3,7},{7,3},{8,12},{12,8},{9,1... | collective-permute-start | bytes 6291464 | tf_op jit(solution)/shard_map/ppermute | solution.py:942
  596.5 10.5 %copy-start.17 = (f32[8,256]{1,0:T(8,128)S(1)}, f32[8,256]{1,0:T(8,128)}, u32[]{:S(2)}) copy-start(f32[8,256]{1,0:T(8,128)} %get-tuple-element.166) | copy-start | bytes 24580
  596.5 11.2 %copy-start.11 = (bf16[2,8,128,128]{3,2,1,0:T(8,128)(2,1)S(1)}, bf16[2,8,128,128]{3,2,1,0:T(8,128)(2,1)}, u32[]{:S(2)}) copy-start(bf16[2,8,128,128]{3,2,1,0:T(8,128)(2,1)} %get-tuple-element.161) | copy-start | bytes 1572868
  596.5 21.7 %collective-permute-start.22 = (bf16[1024,128]{1,0:T(8,128)(2,1)}, bf16[1024,128]{1,0:T(8,128)(2,1)}, u32[]{:S(2)}, u32[]{:S(2)}) collective-permute-start(bf16[1024,128]{1,0:T(8,128)(2,1)} %get-tuple-element.175), channel_id=1, source_target_pairs={{0,1},{1,0},{2,3},{3,2},{4,5},{5,4},{6,7},{7,6},{8,9},{9,8},{10,11... | collective-permute-start | bytes 786440 | tf_op jit(solution)/shard_map/ppermute | solution.py:1060
  607.7 26.5 %collective-permute-start.20 = (bf16[2,8,128,128]{3,2,1,0:T(8,128)(2,1)S(1)}, bf16[2,8,128,128]{3,2,1,0:T(8,128)(2,1)S(1)}, u32[]{:S(2)}, u32[]{:S(2)}) collective-permute-start(bf16[2,8,128,128]{3,2,1,0:T(8,128)(2,1)S(1)} %copy-done.11), channel_id=1, source_target_pairs={{0,2},{1,3},{2,0},{3,1},{4,6},{5,7},{6,4},{7,5},{8,10},{9,11},{10,... | collective-permute-start | bytes 1572872 | tf_op jit(solution)/shard_map/ppermute | solution.py:1060
  607.7 16.7 %collective-permute-start.19 = (bf16[2,3,2,128,128]{4,3,2,1,0:T(8,128)(2,1)}, bf16[2,3,2,128,128]{4,3,2,1,0:T(8,128)(2,1)}, u32[]{:S(2)}, u32[]{:S(2)}) collective-permute-start(bf16[2,3,2,128,128]{4,3,2,1,0:T(8,128)(2,1)} %get-tuple-element.159), channel_id=1, source_target_pairs={{0,8},{8,0},{16,24},{24,16},{1,9},{9,1},{17,25},{25,17},{2,10},{10... | collective-permute-start | bytes 1179656 | tf_op jit(solution)/shard_map/ppermute | solution.py:1060
  607.8 16.6 %collective-permute-start.21 = (bf16[2,2,256,128]{3,2,1,0:T(8,128)(2,1)}, bf16[2,2,256,128]{3,2,1,0:T(8,128)(2,1)}, u32[]{:S(2)}, u32[]{:S(2)}) collective-permute-start(bf16[2,2,256,128]{3,2,1,0:T(8,128)(2,1)} %get-tuple-element.163), channel_id=1, source_target_pairs={{0,16},{8,24},{16,0},{24,8},{1,17},{9,25},{17,1},{25,9},{2,18},{10... | collective-permute-start | bytes 786440 | tf_op jit(solution)/shard_map/ppermute | solution.py:1060
  634.2 0.8 copy-start.9
  716.7 4.2 copy-start.10
  716.7 5.0 copy-start.12
  716.7 8.2 %copy-start.15 = (f32[256,128]{1,0:T(8,128)S(1)}, f32[256,128]{1,0:T(8,128)}, u32[]{:S(2)}) copy-start(f32[256,128]{1,0:T(8,128)} %get-tuple-element.243) | copy-start | bytes 393220

commit v7 on v6

--- a/solution.py
+++ b/solution.py
@@ -422,14 +422,6 @@
     split_rows(acc, (), keep_ref, send_ref)
 
 
-def qkv_grad_kernel(x_ref, dq_ref, dk_ref, dv_ref, keep_ref, send_ref, sum_ref, acc):
-    for at, ref in enumerate((dq_ref, dk_ref, dv_ref)):
-        acc[...] = dot(x_ref[...], ref[...]).astype(BF16)
-        split_rows(acc, (at,), keep_ref, send_ref)
-    sum_ref[0:1, :] = col_sum(dq_ref[...].astype(F32))
-    sum_ref[1:2, :] = col_sum(dv_ref[...].astype(F32))
-
-
 def grad_call(kernel, grid, ins, outs, scratch, flops, *args):
     return pl.pallas_call(
         kernel,
@@ -469,20 +461,6 @@
         row_grad_kernel, (f // block,),
         [once((d, n)), pl.BlockSpec((n, block), lambda i: (0, i))],
         ([spec, spec], [shape, shape]), [pltpu.VMEM((d, block), BF16)], 2 * n * f * d, a, b,
-    )
-
-
-def qkv_grad(x, dq, dk, dv, n_p):
-    d, n = x.shape
-    f = dq.shape[1]
-    r = d // (2 * n_p)
-    spec = pl.BlockSpec((n_p, 1, 3, f // 128, r, 128), lambda i: (0, 0, 0, 0, 0, 0))
-    shape = sds((n_p, 1, 3, f // 128, r, 128))
-    return grad_call(
-        qkv_grad_kernel, (1,),
-        [held((d, n)), held((n, f)), held((n, f)), held((n, f))],
-        ([spec, spec, held((8, f))], [shape, shape, sds((8, f), F32)]),
-        [pltpu.VMEM((d, f), BF16)], n * f * d // 64, x, dq, dk, dv,
     )
 
 
@@ -795,12 +773,12 @@
 
 
 def finish_kernel(n_p, n_t, *refs):
-    dx, keep2, send2, first_a, first_b, up_a, up_b, out_a, out_b, small = refs[:10]
-    given, qkv_out, up_out, out_out, small_out = refs[10:15]
-    recv2, pair1, pair2, slot1, slot2, last, last_slot, up_cur, up_slot, out_cur, out_slot = refs[15:26]
-    out_next, out_last, small_cur, small_slot = refs[26:30]
+    dx, x_turned, *grads, up_a, up_b, out_a, out_b, small = refs[:13]
+    given, qkv_out, up_out, out_out, small_out = refs[13:18]
+    keep2, send2, acc, recv2, pairs, slots1, last, last_slot, up_cur, up_slot, out_cur, out_slot = refs[18:30]
+    out_next, out_last, small_cur, small_slot = refs[30:34]
     bits = [n_p >> (s + 1) for s in range(n_p.bit_length() - 1)]
-    curs, slots = refs[30 : 30 + len(bits)], refs[30 + len(bits) : 30 + 2 * len(bits)]
+    curs, slots = refs[34 : 34 + len(bits)], refs[34 + len(bits) : 34 + 2 * len(bits)]
     send_sems, recv_sems = refs[-2:]
     p, core, t = lax.axis_index("p"), lax.axis_index("core"), lax.axis_index("tensor")
     partner = {"core": 1 - core}
@@ -833,16 +811,12 @@
         return (a.astype(F32) + b.astype(F32)).astype(BF16)
 
     u, odd = t // 2, t % 2
-    swap = go(send2, recv2, partner)
-    for at in (0, 1):
-        pair1[at] = plus(first_a[at], first_b[at])
-    first_move = go(pair1.at[1 - u], slot1, line[2])
     for at in range(4):
-        out_cur[at] = plus(out_a[at], out_b[at])
-    out_move = go(out_cur.at[pl.ds(2 * (1 - u), 2)], out_slot, line[2])
+        out_cur[at % 2, at // 2] = plus(out_a[at], out_b[at])
+    out_move = go(out_cur.at[1 - odd], out_slot, line[1])
     for at in (0, 1):
         up_cur[at] = plus(up_a[at], up_b[at])
-    up_move = go(up_cur.at[1 - odd], up_slot, line[1])
+    up_move = go(up_cur.at[1 - u], up_slot, line[2])
 
     held = given.shape[1]
     stays = core == u
@@ -850,92 +824,131 @@
     rows_b = dx.at[pl.ds(pl.multiple_of((1 - odd) * held, held), held), :]
     give_a = send(rows_a, given.at[odd], {"core": u, "tensor": 2 * core + odd})
     pl.when(jnp.logical_not(stays))(give_a.start)
+    give_b = go(rows_b, given.at[odd], {"core": u, "tensor": 2 * core + 1 - odd})
 
     @pl.when(stays)
     def _():
         given[odd] = dx[pl.ds(pl.multiple_of(odd * held, held), held), :]
 
-    moves = []
+    orders = [bits, bits[::-1]]
+
+    def spot(part, j):
+        return sum(n_p >> (s + 1) for s, bit in enumerate(orders[part]) if j // bit % 2)
+
+    r = keep2.shape[2] // 6
+    swaps = []
+    for part in (0, 1):
+        for which in range(3):
+            acc[...] = dot(x_turned[...], grads[3 * part + which][...]).astype(BF16)
+            for bit in (0, 1):
+
+                @pl.when(core == bit)
+                def _():
+                    for j in range(n_p):
+                        at, to = (2 * j + bit) * r, (2 * j + 1 - bit) * r
+                        for cb in (0, 1):
+                            place = pl.ds((2 * which + cb) * r, r)
+                            keep2[part, spot(part, j), place, :] = acc[at : at + r, cb * 128 : cb * 128 + 128]
+                            send2[part, spot(part, j), place, :] = acc[to : to + r, cb * 128 : cb * 128 + 128]
+        swaps.append(go(send2.at[part], recv2.at[part], partner))
     small_cur[0] = small[...]
+    per_row = dx.shape[1] // 128
+    for part in (0, 1):
+        for which in (0, 1):
+            total = jnp.sum(grads[3 * part + 2 * which][...].astype(F32), axis=0, keepdims=True)
+            for bit in (0, 1):
+
+                @pl.when(core == bit)
+                def _():
+                    at = (6 + which) * per_row + bit * (per_row // 2) + part * (per_row // 4)
+                    for cb in (0, 1):
+                        small_cur[0, at + cb : at + cb + 1, :] = total[:, cb * 128 : cb * 128 + 128]
+
     peers = [partner] + plane
     for at, peer in enumerate(peers):
         copy = go(small_cur.at[at], small_slot.at[at], peer)
         copy.wait()
         small_cur[at + 1] = small_cur[at] + small_slot[at]
 
-    swap.wait()
-    source = [keep2, recv2]
-    for s, bit in enumerate(bits):
-        mine = (p // bit) % 2
-        copies = [
-            go(source[j].at[pl.ds((1 - mine) * bit, bit)], slots[s].at[j], plane[s]) for j in (0, 1)
-        ]
-        for j, copy in enumerate(copies):
-            copy.wait()
-            if bit == 1:
-                pair2[core if j == 0 else 1 - core] = plus(source[j][mine], slots[s][j, 0])
-            else:
-                for at in range(bit):
-                    curs[s][j, at] = plus(source[j][mine * bit + at], slots[s][j, at])
-        source = [curs[s].at[0], curs[s].at[1]]
-    second_move = go(pair2.at[1 - u], slot2, line[2])
-    give_b = go(rows_b, given.at[odd], {"core": u, "tensor": 2 * core + 1 - odd})
-
-    up_move.wait()
-    up_out[...] = up_cur[odd].astype(F32) + up_slot[...].astype(F32)
+    sources = []
+    for part in (0, 1):
+        swaps[part].wait()
+        sources.append([keep2.at[part], recv2.at[part]])
+    for s in range(len(bits)):
+        size = n_p >> (s + 1)
+        copies = []
+        for part in (0, 1):
+            bit = orders[part][s]
+            mine = (p // bit) % 2
+            peer = {"p": flip(p, bit)}
+            copies.append(
+                [go(sources[part][j].at[pl.ds((1 - mine) * size, size)], slots[s].at[part, j], peer) for j in (0, 1)]
+            )
+        for part in (0, 1):
+            mine = (p // orders[part][s]) % 2
+            for j in (0, 1):
+                copies[part][j].wait()
+                if size == 1:
+                    pairs[part, core if j == 0 else 1 - core] = plus(sources[part][j][mine], slots[s][part, j, 0])
+                else:
+                    for at in range(size):
+                        curs[s][part, j, at] = plus(sources[part][j][mine * size + at], slots[s][part, j, at])
+            sources[part] = [curs[s].at[part, 0], curs[s].at[part, 1]]
+    pair_move = go(pairs.at[1 - odd], slots1, line[1])
     out_move.wait()
     for at in (0, 1):
-        out_next[at] = plus(out_cur[2 * u + at], out_slot[at])
-    out_move = go(out_next.at[1 - odd], out_last, line[1])
-    first_move.wait()
-    last[0] = plus(pair1[u], slot1[...])
-    second_move.wait()
-    last[1] = plus(pair2[u], slot2[...])
-    last_move = go(last.at[1 - odd], last_slot, line[1])
-    for bit in (2, 1):
+        out_next[at] = plus(out_cur[odd, at], out_slot[at])
+    out_move = go(out_next.at[1 - u], out_last, line[2])
+    pair_move.wait()
+    for at in (0, 1):
+        last[at] = plus(pairs[odd, at], slots1[at])
+    last_move = go(last.at[1 - u], last_slot, line[2])
+    for bit in (1, 2):
         at = len(peers)
         copy = go(small_cur.at[at], small_slot.at[at], line[bit])
         copy.wait()
         peers.append(None)
-        if bit == 1:
+        if bit == 2:
             small_out[...] = small_cur[at] + small_slot[at]
         else:
             small_cur[at + 1] = small_cur[at] + small_slot[at]
+    up_move.wait()
+    up_out[...] = up_cur[u].astype(F32) + up_slot[...].astype(F32)
     out_move.wait()
-    out_out[...] = out_next[odd].astype(F32) + out_last[...].astype(F32)
+    out_out[...] = out_next[u].astype(F32) + out_last[...].astype(F32)
     last_move.wait()
-    qkv_out[...] = last[odd].astype(F32) + last_slot[...].astype(F32)
+    qkv_out[...] = last[u].astype(F32) + last_slot[...].astype(F32)
     pl.when(jnp.logical_not(stays))(give_a.wait)
     give_b.wait()
 
 
-def finish(n_p, n_t, dx, keep2, send2, first, up_, out_, small):
-    rows_, lanes = keep2.shape[1:]
+def finish(n_p, n_t, dx, x_turned, first, second, up_, out_, small):
+    d, wide = x_turned.shape[0], first[0].shape[1]
+    rows_ = 3 * wide * d // (2 * n_p) // 128
     bits = n_p.bit_length() - 1
     steps = 1 + bits + 2
-    block = lambda count, like: pltpu.VMEM((count,) + like.shape[1:], BF16)
-    one = lambda like: pltpu.VMEM(like.shape[1:], BF16)
-    sizes = [n_p >> (s + 1) for s in range(bits)]
-    halves = [pltpu.VMEM((2, size, rows_, lanes), BF16) for size in sizes]
+    box = lambda *lead: pltpu.VMEM(lead + (rows_, 128), BF16)
+    like = lambda lead, value: pltpu.VMEM(lead + value.shape[1:], BF16)
+    halves = [box(2, 2, n_p >> (s + 1)) for s in range(bits)]
     vmem = pl.BlockSpec(memory_space=pltpu.VMEM)
-    count = 9 + steps + 2 * bits
+    count = 9 + steps + 4 * bits
     return pl.pallas_call(
         functools.partial(finish_kernel, n_p, n_t),
         out_shape=[
-            sds((2, dx.shape[0] // 2, dx.shape[1])), sds((rows_, lanes), F32), sds(up_[0].shape[1:], F32),
+            sds((2, dx.shape[0] // 2, dx.shape[1])), sds((rows_, 128), F32), sds(up_[0].shape[1:], F32),
             sds(out_[0].shape[1:], F32), sds(small.shape, F32),
         ],
-        in_specs=[vmem] * 10,
+        in_specs=[vmem] * 13,
         out_specs=[vmem] * 5,
         scratch_shapes=[
-            block(n_p, keep2), block(2, keep2), block(2, keep2), one(keep2), one(keep2), block(2, keep2), one(keep2),
-            block(2, up_[0]), one(up_[0]), block(4, out_[0]), block(2, out_[0]), block(2, out_[0]), one(out_[0]),
-            pltpu.VMEM((steps,) + small.shape, F32), pltpu.VMEM((steps,) + small.shape, F32),
+            box(2, n_p), box(2, n_p), pltpu.VMEM((d, wide), BF16), box(2, n_p), box(2, 2), box(2), box(2), box(),
+            like((2,), up_[0]), like((), up_[0]), like((2, 2), out_[0]), like((2,), out_[0]), like((2,), out_[0]),
+            like((), out_[0]), pltpu.VMEM((steps,) + small.shape, F32), pltpu.VMEM((steps,) + small.shape, F32),
             *halves, *halves,
             pltpu.SemaphoreType.DMA((count,)), pltpu.SemaphoreType.DMA((count,)),
         ],
         compiler_params=pltpu.CompilerParams(collective_id=0, has_side_effects=True),
-    )(dx, keep2, send2, *first, *up_, *out_, small)
+    )(dx, x_turned, *first, *second, *up_, *out_, small)
 
 
 def swap_cores(value):
@@ -1029,12 +1042,11 @@
     layer_out = give(*blocks(layer))
 
     p_bits = [1 << s for s in range(n_p.bit_length() - 1)]
-    t_bits = [2, 1]
+    t_bits = [1, 2]
 
     class Total:
         def __init__(self, parts, downward):
-            lead = [("p", n_p, bit) for bit in reversed(p_bits)] + [("tensor", n_t, bit) for bit in t_bits]
-            lead = lead[: len(lead) - (parts[0].shape[1] == 2)]
+            lead = [("p", n_p, bit) for bit in reversed(p_bits)] + [("tensor", n_t, bit) for bit in (2, 1)]
             self.rest = parts[0].shape[2:]
             self.dims = lead
             self.parts = [part.reshape((2,) * len(lead) + self.rest) for part in parts]
@@ -1098,35 +1110,30 @@
 
     first = attend_bwd(0, qkv, context, dc_full, lse, segment, valid, 512, 256)
     out_sum = Total([out_keep, out_recv], False)
-    keep, send, sum_first = qkv_grad(x_turned, *first, n_p)
-    first_sum = Total([by_core(core, keep, swap_cores(send), 1)], True)
-    (dc_full,) = together([down_sum.cut(2), up_sums.cut(1), out_sum.cut(0), first_sum.cut(0)], dc_full)
+    (dc_full,) = together([down_sum.cut(2), up_sums.cut(1), out_sum.cut(0)], dc_full)
     second = attend_bwd(1, qkv, context, dc_full, lse, segment, valid, 512, 256)
-    (second,) = together([down_sum.cut(3), up_sums.cut(2), out_sum.cut(1), first_sum.cut(1)], second)
+    (second,) = together([down_sum.cut(3), up_sums.cut(2), out_sum.cut(1)], second)
 
     dx_other = swap_cores(input_pull(1 - core, core, (*first, *second), w_qkv))
     dx_mine = input_pull(core, core, (*first, *second), w_qkv, dm)
     dx = (dx_mine + dx_other.astype(F32)).astype(BF16)
-    keep, send, sum_second = qkv_grad(x_turned, *second, n_p)
-    qv_sum = jnp.concatenate([sum_first, sum_second], axis=1)
     down_total = down_sum.sum_of(lambda part: part)
-    qv_pad = lax.dynamic_update_slice(jnp.zeros((2, width), F32), qv_sum[0:2], (0, core * own))
     small = jnp.concatenate(
         [
             jnp.stack([sums_one[0], sums_two[0], sums_one[1], sums_one[2], sums_two[1], sums_two[2]]).reshape(-1),
-            qv_pad.reshape(-1),
+            jnp.zeros((2 * width,), F32),
             up_sum[0],
         ]
     )
     rows_of = lambda part, count: part.reshape(count, -1, part.shape[-1])
     given, qkv_total, up_total, out_total, small = finish(
-        n_p, n_t, dx, rows_of(keep, n_p), rows_of(send, n_p), [rows_of(part, 2) for part in first_sum.parts],
-        [rows_of(part, 2) for part in up_sums.parts], [rows_of(part, 4) for part in out_sum.parts], small.reshape(-1, 128),
+        n_p, n_t, dx, x_turned, first, second, [rows_of(part, 2) for part in up_sums.parts],
+        [rows_of(part, 4) for part in out_sum.parts], small.reshape(-1, 128),
     )
     input_grad = given.astype(F32)
     small = small.reshape(-1)
     up_total = up_total.reshape(up_sums.rest).transpose(1, 0, 2).reshape(up_weight.shape)
-    qkv_total = qkv_total.reshape(first_sum.rest).transpose(0, 2, 1, 3).reshape(qkv_weight.shape)
+    qkv_total = qkv_total.reshape(3, own // 256, -1, 128).transpose(0, 2, 1, 3).reshape(qkv_weight.shape)
     gain_sum = small[: 2 * width].reshape(2, width)
     bias_sum = small[2 * width : 6 * width].reshape(4, width)
     qv_total = lax.dynamic_slice_in_dim(small[6 * width : 8 * width].reshape(2, width), tensor * qv_bias.shape[1], qv_bias.shape[1], 1)

time: 740 us -> 766 us (1.035)
  Pallas kernels: 572 us -> 523 us
  starting transfers between devices: 29 us -> 75 us
  waiting for transfers between devices: 28.5 us -> 73.4 us
  other arithmetic: 67.6 us -> 51 us
    ppermute x11 -> x9, waiting for transfers between devices: 28.1 us -> 63.3 us  [move(): self.parts = [self.live[0], lax.ppermute(self.live[1], *self.route)]]
    pallas_call x2, Pallas kernels: 96.6 us -> 72.9 us  [attend_bwd(): pl.pallas_call(functools.partial(attend_bwd_kernel, bq), grid_spec=pltpu....]
    ppermute x1, starting transfers between devices: 0.01 us -> 21 us  [give(): lax.ppermute(b, COL, back(route_b))]
    pallas_call x1, Pallas kernels: 68.1 us -> 48.7 us  [attend_fwd(): pl.pallas_call(functools.partial(attend_fwd_kernel, bk), grid_spec=pltpu....]
    ppermute x11 -> x9, starting transfers between devices: 13.3 us -> 26.4 us  [move(): self.parts = [self.live[0], lax.ppermute(self.live[1], *self.route)]]
    convert_element_type x10 -> x11, other arithmetic: 32.8 us -> 20.3 us  [cut_one(): self.sum_of(lambda part: lax.dynamic_index_in_dim(part, which, at, keepdi...]
    ppermute x8 -> x7, starting transfers between devices: 4.17 us -> 16.3 us  [swap_cores(): return lax.ppermute(value, 'core', [(0, 1), (1, 0)])]
    ppermute x1, waiting for transfers between devices: 0.37 us -> 10 us  [give(): lax.ppermute(b, COL, back(route_b))]
  transfers between devices with their start and end apart: 23 -> 20, of which waited for: 3 -> 3; matrix products, arithmetic and copies ran while one was open for 10% -> 9% of each run, Pallas kernels for 54% -> 43%
where the time goes in v7:
time: 766 us; the launch traced here: 759 us
  Pallas kernels  523 us (68%)
  starting transfers between devices  75 us (10%)
  waiting for transfers between devices  73.4 us (10%)
  other arithmetic  51 us (7%)
  local copies, waits for them, and re-layouts  30.7 us (4%)
    pallas_call x1, Pallas kernels, start_gather(): pl.pallas_call(functools.partial(start_kernel, n_p, n_t, kinds), out_shap...  147 us
    pallas_call x4, Pallas kernels, call(): pl.pallas_call(kernel, grid=grid, in_specs=ins, out_specs=outs[0], out_sh...  83.5 us
    pallas_call x1, Pallas kernels, finish(): pl.pallas_call(functools.partial(finish_kernel, n_p, n_t), out_shape=[sds...  83 us
    pallas_call x2, Pallas kernels, attend_bwd(): pl.pallas_call(functools.partial(attend_bwd_kernel, bq), grid_spec=pltpu....  72.9 us
    ppermute x9, waiting for transfers between devices, move(): self.parts = [self.live[0], lax.ppermute(self.live[1], *self.route)]  63.3 us
    pallas_call x3, Pallas kernels, grad_call(): pl.pallas_call(kernel, grid=grid, in_specs=ins, out_specs=outs[0], out_sh...  49.3 us
    pallas_call x1, Pallas kernels, attend_fwd(): pl.pallas_call(functools.partial(attend_fwd_kernel, bk), grid_spec=pltpu....  48.7 us
    ppermute x9, starting transfers between devices, move(): self.parts = [self.live[0], lax.ppermute(self.live[1], *self.route)]  26.4 us
  transfers between devices with their start and end apart: 20, of which 3 were waited for; matrix products, arithmetic and copies ran while one was open for 9% of the time, Pallas kernels for 43%

profile of v7, /device:TPU:0, one launch (start us, length us, event | category | flops | bytes accessed | tf_op | source)
XLA Modules:
  0.0 758.9 jit_solution(2276445039172202587)
XLA Ops:
  0.7 0.9 fusion.19
  2.8 1.3 maximum_bitcast_fusion.1.refs_1_
  4.1 146.7 %shard_map.195 = (bf16[2048,1024]{1,0:T(8,128)(2,1)}, f32[4,12,128]{2,1,0:T(8,128)}, bf16[1024,3072]{1,0:T(8,128)(2,1)}, bf16[1024,1024]{1,0:T(8,128)(2,1)}, bf1...) custom-call(bf16[2,512,1024]{2,1,0:T(8,128)(2,1)} %refs_0_.1, f32[12,128]{1,0:T(8,128)} %maximum_bitcast_fusion.1.refs_1_, ...), custom_call_target="tpu_custom_call" | custom-call | tf_op jit(solution)/shard_map/pallas_call | solution.py:737
  150.8 1.2 dynamic-slice_bitcast_fusion.1
  152.0 1.9 collective-permute-start.2
  154.7 12.3 %shard_map.196 = (bf16[2048,1536]{1,0:T(8,128)(2,1)}, bf16[1024,2048]{1,0:T(8,128)(2,1)}) custom-call(s32[1]{0:T(128)} %bitcast.core_ref.at_ref, bf16[2048,1024]{1,0:T(8,128)(2,1)} %get-tuple-element.84.x_ref, bf16[1024,3072]{1,0:T(8,128)(2,1)} %get-tuple-element.85.w_ref.refs_6_, f32[1,1536]{1,0:T(1,128)} %reshape.203.bias_ref), custom_call_target="tpu_custom_call" | custom-call | flops 6442450944 | bytes 14680064 | tf_op jit(solution)/shard_map/pallas_call | solution.py:757
  168.9 1.3 broadcast_in_dim.11.kcode_ref
  170.2 48.7 %shard_map.197 = (bf16[2048,512]{1,0:T(8,128)(2,1)}, f32[32,2048]{1,0:T(8,128)}) custom-call(s32[4]{0:T(128)} %get-tuple-element.208.lo_ref, s32[4]{0:T(128)} %get-tuple-element.207.hi_ref, s32[4]{0:T(128)} %reduce_sum.56.pad_ref, bf16[2048,1536]{1,0:T(8,128)(2,1)} %get-tuple-element.87.q_ref.k_ref.v_ref, ...), custom_call_target="tpu_custom_call" | custom-call | flops 8589934592 | bytes 25165824 | tf_op jit(solution)/shard_map/pallas_call | solution.py:160
  218.9 2.6 constant_dynamic-slice_fusion.14
  221.5 2.6 collective-permute-start.1
  224.8 3.8 maximum_select_fusion.1.e_ref
  228.6 3.7 maximum_select_fusion.c_ref.a_ref
  232.3 8.7 %shard_map.198 = (bf16[1024,1024]{1,0:T(8,128)(2,1)}, bf16[1024,1024]{1,0:T(8,128)(2,1)}, f32[1024,1024]{1,0:T(8,128)}, f32[1024,128]{1,0:T(8,128)}) custom-call(s32[1]{0:T(128)} %bitcast.core_ref.at_ref, bf16[2048,1024]{1,0:T(8,128)(2,1)} %get-tuple-element.84.x_ref, bf16[1024,1024]{1,0:T(8,128)(2,1)} %maximum_select_fusion.c_ref.a_ref, ...), custom_call_target="tpu_custom_call" | custom-call | flops 2147483648 | bytes 12582912 | tf_op jit(solution)/shard_map/pallas_call | solution.py:325
  241.0 24.7 %shard_map.199 = (bf16[1024,4096]{1,0:T(8,128)(2,1)}, bf16[1024,4096]{1,0:T(8,128)(2,1)}) custom-call(bf16[1024,1024]{1,0:T(8,128)(2,1)} %get-tuple-element.90.h_ref, bf16[1024,4096]{1,0:T(8,128)(2,1)} %get-tuple-element.91.w_ref, f32[1,4096]{1,0:T(1,128)} %bitcast.125), custom_call_target="tpu_custom_call" | custom-call | flops 8589934592 | bytes 25165824 | tf_op jit(solution)/shard_map/pallas_call | solution.py:293
  265.6 19.2 %shard_map.200 = (bf16[1024,1024]{1,0:T(8,128)(2,1)}, f32[1024,1024]{1,0:T(8,128)}, bf16[1024,1024]{1,0:T(8,128)(2,1)}, f32[8,1024]{1,0:T(8,128)}) custom-call(bf16[1024,4096]{1,0:T(8,128)(2,1)} %get-tuple-element.99.g_ref.a_ref, bf16[4096,1024]{1,0:T(8,128)(2,1)} %get-tuple-element.93.w_ref, f32[1024,1024]{1,0:T(8,128)} %get-tuple-element.94.n_ref, ...), custom_call_target="tpu_custom_call" | custom-call | flops 8589934592 | bytes 16777216 | tf_op jit(solution)/shard_map/pallas_call | solution.py:293
  284.9 22.0 %shard_map.201 = (bf16[1024,4096]{1,0:T(8,128)(2,1)}, f32[8,4096]{1,0:T(8,128)}) custom-call(bf16[1024,1024]{1,0:T(8,128)(2,1)} %get-tuple-element.96.dz_ref.b_ref, bf16[4096,1024]{1,0:T(8,128)(2,1)} %get-tuple-element.93.w_ref, bf16[1024,4096]{1,0:T(8,128)(2,1)} %get-tuple-element.97.slope_ref), custom_call_target="tpu_custom_call" | custom-call | flops 8589934592 | bytes 25165824 | tf_op jit(solution)/shard_map/pallas_call | solution.py:293
  306.8 27.7 %shard_map.202 = (bf16[4,4,1024,128]{3,2,1,0:T(8,128)(2,1)}, bf16[4,4,1024,128]{3,2,1,0:T(8,128)(2,1)}) custom-call(bf16[1024,4096]{1,0:T(8,128)(2,1)} %get-tuple-element.99.g_ref.a_ref, bf16[1024,1024]{1,0:T(8,128)(2,1)} %get-tuple-element.96.dz_ref.b_ref), custom_call_target="tpu_custom_call" | custom-call | flops 8589934592 | bytes 16777216 | tf_op jit(solution)/shard_map/pallas_call | solution.py:426
  334.6 15.2 %shard_map.203 = (bf16[4,4,8,128,128]{4,3,2,1,0:T(8,128)(2,1)}, bf16[4,4,8,128,128]{4,3,2,1,0:T(8,128)(2,1)}) custom-call(bf16[1024,1024]{1,0:T(8,128)(2,1)} %get-tuple-element.107.a_ref, bf16[1024,4096]{1,0:T(8,128)(2,1)} %get-tuple-element.110.b_ref.du_ref), custom_call_target="tpu_custom_call" | custom-call | flops 8589934592 | bytes 16777216 | tf_op jit(solution)/shard_map/pallas_call | solution.py:426
  350.3 1.1 constant_dynamic-slice_fusion.2
  351.5 9.5 %collective-permute-start.8 = (bf16[512,1024]{1,0:T(8,128)(2,1)}, bf16[512,1024]{1,0:T(8,128)(2,1)}, u32[]{:S(2)}, u32[]{:S(2)}) collective-permute-start(bf16[512,1024]{1,0:T(8,128)(2,1)} %get-tuple-element.180), channel_id=1, source_target_pairs={{0,0},{1,1},{4,2},{5,3},{2,4},{3,5},{6,6},{7,7},{8,8},{9,9},{12,10... | collective-permute-start | bytes 3145736 | tf_op jit(solution)/shard_map/ppermute | solution.py:1001
  360.9 21.0 %collective-permute-start.9 = (bf16[512,1024]{1,0:T(8,128)(2,1)S(1)}, bf16[512,1024]{1,0:T(8,128)(2,1)}, u32[]{:S(2)}, u32[]{:S(2)}) collective-permute-start(bf16[512,1024]{1,0:T(8,128)(2,1)S(1)} %get-tuple-element.181), channel_id=1, source_target_pairs={{1,0},{0,1},{5,2},{4,3},{3,4},{2,5},{7,6},{6,7},{9,8},{8,9},{13,10... | collective-permute-start | bytes 3145736 | tf_op jit(solution)/shard_map/ppermute | solution.py:1001
  384.2 2.7 constant_dynamic-slice_fusion.10
  387.7 1.7 constant_dynamic-slice_fusion.6
  389.4 10.0 %collective-permute-done.9 = bf16[512,1024]{1,0:T(8,128)(2,1)} collective-permute-done((bf16[512,1024]{1,0:T(8,128)(2,1)S(1)}, bf16[512,1024]{1,0:T(8,128)(2,1)}, u32[]{:S(2)}, u32[]{:S(2)}) %collective-permute-start.9) | collective-permute-done | bytes 1048608 | tf_op jit(solution)/shard_map/ppermute | solution.py:1001
  399.4 4.0 maximum_select_fusion.3
  403.4 2.5 constant_dynamic-slice_fusion.9
  405.9 1.9 fusion.1
  407.8 1.9 fusion
  409.7 17.6 %shard_map.204 = (f32[1024,1024]{1,0:T(8,128)}, bf16[1024,1024]{1,0:T(8,128)(2,1)}, f32[8,1024]{1,0:T(8,128)}) custom-call(bf16[1024,4096]{1,0:T(8,128)(2,1)} %get-tuple-element.110.b_ref.du_ref, bf16[1024,4096]{1,0:T(8,128)(2,1)} %get-tuple-element.91.w_ref, f32[1024,1024]{1,0:T(8,128)} %get-tuple-element.111.dr_ref, f32[1024,1024]{1,0:T(8,128)} %get-tuple-element.94.n_ref, ...), custom_call_target="tpu_custom_call" | custom-call | flops 8589934592 | bytes 16777216 | tf_op jit(solution)/shard_map/pallas_call | solution.py:293
  427.3 6.4 shard_map.206
  433.7 12.4 %collective-permute-start.12 = (bf16[4,4,256,128]{3,2,1,0:T(8,128)(2,1)}, bf16[4,4,256,128]{3,2,1,0:T(8,128)(2,1)S(1)}, u32[]{:S(2)}, u32[]{:S(2)}) collective-permute-start(bf16[4,4,256,128]{3,2,1,0:T(8,128)(2,1)} %get-tuple-element.126), channel_id=1, source_target_pairs={{0,4},{4,0},{1,5},{5,1},{2,6},{6,2},{3,7},{7,3},{8,12},{12,8},{9,1... | collective-permute-start | bytes 3145736 | tf_op jit(solution)/shard_map/ppermute | solution.py:955
  446.1 0.8 collective-permute-start.5
  446.8 4.6 convolution_convert_fusion
  452.0 2.9 constant_dynamic-slice_fusion.5
  454.9 2.1 fusion.3
  457.0 2.1 fusion.2
  459.2 1.3 fusion.11
  460.4 2.0 maximum_select_fusion.2.dc_ref
  462.4 31.4 %collective-permute-done.5 = bf16[2,2,2,1024,128]{4,3,1,2,0:T(8,128)(2,1)S(1)} collective-permute-done((bf16[2,2,2,1024,128]{4,3,1,2,0:T(8,128)(2,1)}, bf16[2,2,2,1024,128]{4,3,1,2,0:T(8,128)(2,1)S(1)}, u32[]{:S(2)}, u32[]{:S(2)}) %collective-permute-start.5) | collective-permute-done | bytes 2097184 | tf_op jit(solution)/shard_map/ppermute | solution.py:1072
  493.8 1.6 fusion.5
  495.4 7.1 collective-permute-start.11
  502.5 36.5 %shard_map.205 = (bf16[2048,256]{1,0:T(8,128)(2,1)}, bf16[2048,256]{1,0:T(8,128)(2,1)}, bf16[2048,256]{1,0:T(8,128)(2,1)}) custom-call(s32[8]{0:T(128)} %get-tuple-element.206.lo_ref, s32[8]{0:T(128)} %get-tuple-element.205.hi_ref, s32[8]{0:T(128)} %reduce_sum.62.pad_ref, bf16[2048,1536]{1,0:T(8,128)(2,1)} %get-tuple-element.87.q_ref.k_ref.v_ref, ...), custom_call_target="tpu_custom_call" | custom-call | flops 21474836480 | bytes 50331648 | tf_op jit(solution)/shard_map/pallas_call | solution.py:198
  539.0 31.9 %collective-permute-done.10 = bf16[2,2,1024,128]{3,2,0,1:T(8,128)(2,1)} collective-permute-done((bf16[2,2,1024,128]{3,2,0,1:T(8,128)(2,1)}, bf16[2,2,1024,128]{3,2,0,1:T(8,128)(2,1)}, u32[]{:S(2)}, u32[]{:S(2)}) %collective-permute-start.10) | collective-permute-done | bytes 1048608 | tf_op jit(solution)/shard_map/ppermute | solution.py:1072
  570.9 2.5 fusion.9
  573.4 1.8 fusion.7
  575.2 1.5 collective-permute-start.15
  577.2 4.0 collective-permute-start.13
  581.2 36.3 %shard_map.207 = (bf16[2048,256]{1,0:T(8,128)(2,1)}, bf16[2048,256]{1,0:T(8,128)(2,1)}, bf16[2048,256]{1,0:T(8,128)(2,1)}) custom-call(s32[8]{0:T(128)} %get-tuple-element.206.lo_ref, s32[8]{0:T(128)} %get-tuple-element.205.hi_ref, s32[8]{0:T(128)} %reduce_sum.62.pad_ref, bf16[2048,1536]{1,0:T(8,128)(2,1)} %get-tuple-element.87.q_ref.k_ref.v_ref, ...), custom_call_target="tpu_custom_call" | custom-call | flops 21474836480 | bytes 50331648 | tf_op jit(solution)/shard_map/pallas_call | solution.py:198
  617.5 2.0 fusion.17
  619.5 1.9 fusion.15
  621.4 1.3 fusion.13
  622.7 8.5 %shard_map.209 = bf16[1024,1024]{1,0:T(8,128)(2,1)} custom-call(s32[2]{0:T(128)} %pad_add_fusion.1.at_ref, bf16[2048,256]{1,0:T(8,128)(2,1)} %get-tuple-element.118.refs_0_.refs_2_, bf16[2048,256]{1,0:T(8,128)(2,1)} %get-tuple-element.119.refs_1_.refs_3_, bf16[2048,256]{1,0:T(8,128)(2,1)} %get-tuple-element.120.refs_2_.refs_4_, ...), custom_call_target="tpu_custom_call" | custom-call | flops 3221225472 | bytes 16777216 | tf_op jit(solution)/shard_map/pallas_call | solution.py:486
  631.8 0.8 slice.82
  633.3 0.9 slice.83
  634.3 0.8 slice.81
  636.5 12.5 %collective-permute-start.17 = (bf16[2,8,128,128]{3,2,1,0:T(8,128)(2,1)S(1)}, bf16[2,8,128,128]{3,2,1,0:T(8,128)(2,1)S(1)}, u32[]{:S(2)}, u32[]{:S(2)}) collective-permute-start(bf16[2,8,128,128]{3,2,1,0:T(8,128)(2,1)S(1)} %copy-done.11), channel_id=1, source_target_pairs={{0,1},{1,0},{2,3},{3,2},{4,5},{5,4},{6,7},{7,6},{8,9},{9,8},{10,11... | collective-permute-start | bytes 1572872 | tf_op jit(solution)/shard_map/ppermute | solution.py:1072
  648.9 9.5 %shard_map.208 = f32[1024,1024]{1,0:T(8,128)} custom-call(s32[2]{0:T(128)} %pad_add_fusion.at_ref, bf16[2048,256]{1,0:T(8,128)(2,1)} %get-tuple-element.118.refs_0_.refs_2_, bf16[2048,256]{1,0:T(8,128)(2,1)} %get-tuple-element.119.refs_1_.refs_3_, bf16[2048,256]{1,0:T(8,128)(2,1)} %get-tuple-element.120.refs_2_.refs_4_, ...), custom_call_target="tpu_custom_call" | custom-call | flops 3221225472 | bytes 16777216 | tf_op jit(solution)/shard_map/pallas_call | solution.py:486
  658.4 1.8 convert_add_fusion
  660.2 4.3 add_convert_fusion.refs_0_
  664.6 0.8 copy-done.9
  665.4 83.0 %shard_map.210 = (bf16[2,512,1024]{2,1,0:T(8,128)(2,1)}, f32[768,128]{1,0:T(8,128)}, f32[1024,128]{1,0:T(8,128)}, f32[256,128]{1,0:T(8,128)}, f32[96,128]{1,0:T(8,128)}) custom-call(bf16[1024,1024]{1,0:T(8,128)(2,1)} %add_convert_fusion.refs_0_, bf16[1024,2048]{1,0:T(8,128)(2,1)} %get-tuple-element.141.refs_1_, ...), custom_call_target="tpu_custom_call" | custom-call | tf_op jit(solution)/shard_map/pallas_call | solution.py:935
  749.9 4.2 convert_element_type.388
  754.1 0.8 copy.108
  754.9 0.8 copy.109
  (108 shorter events, 16.6 us)
Async XLA Ops:
  0.6 150.2 %copy-start.4 = (bf16[2,512,1024]{2,1,0:T(8,128)(2,1)S(1)}, bf16[2,512,1024]{2,1,0:T(8,128)(2,1)}, u32[]{:S(2)}) copy-start(bf16[2,512,1024]{2,1,0:T(8,128)(2,1)} %param.23) | copy-start | bytes 6291460
  1.5 165.5 %collective-permute-start = (s32[2,2048]{1,0:T(2,128)S(1)}, s32[2,2048]{1,0:T(2,128)S(1)}, u32[]{:S(2)}, u32[]{:S(2)}) collective-permute-start(s32[2,2048]{1,0:T(2,128)S(1)} %fusion.19), channel_id=1, source_target_pairs={{0,4},{4,0},{1,5},{5,1},{2,6},{6,2},{3,7},{7,3},{8,12},{12,8},{9,1... | collective-permute-start | bytes 49160 | tf_op jit(solution)/shard_map/ppermute | solution.py:955
  150.8 3.0 copy-start.16
  152.0 72.8 %collective-permute-start.2 = (bf16[512,1024]{1,0:T(8,128)(2,1)}, bf16[512,1024]{1,0:T(8,128)(2,1)S(1)}, u32[]{:S(2)}, u32[]{:S(2)}) collective-permute-start(bf16[512,1024]{1,0:T(8,128)(2,1)} %get-tuple-element.184), channel_id=1, source_target_pairs={{0,0},{1,1},{2,4},{3,5},{4,2},{5,3},{6,6},{7,7},{8,8},{9,9},{10,12... | collective-permute-start | bytes 3145736 | tf_op jit(solution)/shard_map/ppermute | solution.py:993
  153.9 70.9 %collective-permute-start.3 = (bf16[512,1024]{1,0:T(8,128)(2,1)S(1)}, bf16[512,1024]{1,0:T(8,128)(2,1)}, u32[]{:S(2)}, u32[]{:S(2)}) collective-permute-start(bf16[512,1024]{1,0:T(8,128)(2,1)S(1)} %get-tuple-element.185), channel_id=1, source_target_pairs={{0,1},{1,0},{2,5},{3,4},{4,3},{5,2},{6,7},{7,6},{8,9},{9,8},{10,13... | collective-permute-start | bytes 3145736 | tf_op jit(solution)/shard_map/ppermute | solution.py:994
  167.1 3.0 copy-start.13
  221.5 7.0 collective-permute-start.1
  334.6 68.8 %collective-permute-start.4 = (bf16[4,4,1024,128]{3,2,1,0:T(8,128)(2,1)}, bf16[4,4,1024,128]{3,2,1,0:T(8,128)(2,1)}, u32[]{:S(2)}, u32[]{:S(2)}) collective-permute-start(bf16[4,4,1024,128]{3,2,1,0:T(8,128)(2,1)} %get-tuple-element.103), channel_id=1, source_target_pairs={{0,4},{4,0},{1,5},{5,1},{2,6},{6,2},{3,7},{7,3},{8,12},{12,8},{9,1... | collective-permute-start | bytes 12582920 | tf_op jit(solution)/shard_map/ppermute | solution.py:955
  334.6 15.7 %copy-start.5 = (bf16[1024,1024]{1,0:T(8,128)(2,1)S(1)}, bf16[1024,1024]{1,0:T(8,128)(2,1)}, u32[]{:S(2)}) copy-start(bf16[1024,1024]{1,0:T(8,128)(2,1)} %get-tuple-element.114) | copy-start | bytes 6291460
  349.8 102.2 %collective-permute-start.6 = (bf16[4,4,8,128,128]{4,3,2,1,0:T(8,128)(2,1)}, bf16[4,4,8,128,128]{4,3,2,1,0:T(8,128)(2,1)}, u32[]{:S(2)}, u32[]{:S(2)}) collective-permute-start(bf16[4,4,8,128,128]{4,3,2,1,0:T(8,128)(2,1)} %get-tuple-element.109), channel_id=1, source_target_pairs={{0,4},{4,0},{1,5},{5,1},{2,6},{6,2},{3,7},{7,3},{8,12},{12,8},{9,1... | collective-permute-start | bytes 12582920 | tf_op jit(solution)/shard_map/ppermute | solution.py:955
  350.3 32.2 %copy-start.14 = (s32[1,2048]{1,0:T(1,128)S(1)}, s32[1,2048]{1,0:T(1,128)}, u32[]{:S(2)}) copy-start(s32[1,2048]{1,0:T(1,128)} %copy-done.13) | copy-start | bytes 24580
  351.5 37.9 %collective-permute-start.8 = (bf16[512,1024]{1,0:T(8,128)(2,1)}, bf16[512,1024]{1,0:T(8,128)(2,1)}, u32[]{:S(2)}, u32[]{:S(2)}) collective-permute-start(bf16[512,1024]{1,0:T(8,128)(2,1)} %get-tuple-element.180), channel_id=1, source_target_pairs={{0,0},{1,1},{4,2},{5,3},{2,4},{3,5},{6,6},{7,7},{8,8},{9,9},{12,10... | collective-permute-start | bytes 3145736 | tf_op jit(solution)/shard_map/ppermute | solution.py:1001
  360.9 38.5 %collective-permute-start.9 = (bf16[512,1024]{1,0:T(8,128)(2,1)S(1)}, bf16[512,1024]{1,0:T(8,128)(2,1)}, u32[]{:S(2)}, u32[]{:S(2)}) collective-permute-start(bf16[512,1024]{1,0:T(8,128)(2,1)S(1)} %get-tuple-element.181), channel_id=1, source_target_pairs={{1,0},{0,1},{5,2},{4,3},{3,4},{2,5},{7,6},{6,7},{9,8},{8,9},{13,10... | collective-permute-start | bytes 3145736 | tf_op jit(solution)/shard_map/ppermute | solution.py:1001
  384.2 3.5 copy-start.3
  433.7 25.4 %collective-permute-start.12 = (bf16[4,4,256,128]{3,2,1,0:T(8,128)(2,1)}, bf16[4,4,256,128]{3,2,1,0:T(8,128)(2,1)S(1)}, u32[]{:S(2)}, u32[]{:S(2)}) collective-permute-start(bf16[4,4,256,128]{3,2,1,0:T(8,128)(2,1)} %get-tuple-element.126), channel_id=1, source_target_pairs={{0,4},{4,0},{1,5},{5,1},{2,6},{6,2},{3,7},{7,3},{8,12},{12,8},{9,1... | collective-permute-start | bytes 3145736 | tf_op jit(solution)/shard_map/ppermute | solution.py:955
  446.1 47.7 %collective-permute-start.5 = (bf16[2,2,2,1024,128]{4,3,1,2,0:T(8,128)(2,1)}, bf16[2,2,2,1024,128]{4,3,1,2,0:T(8,128)(2,1)S(1)}, u32[]{:S(2)}, u32[]{:S(2)}) collective-permute-start(bf16[2,2,2,1024,128]{4,3,1,2,0:T(8,128)(2,1)} %fusion.1), channel_id=1, source_target_pairs={{0,8},{8,0},{16,24},{24,16},{1,9},{9,1},{17,25},{25,17},{2,10},{10... | collective-permute-start | bytes 6291464 | tf_op jit(solution)/shard_map/ppermute | solution.py:1072
  451.7 8.7 %collective-permute-start.7 = (bf16[1024,512]{1,0:T(8,128)(2,1)S(1)}, bf16[1024,512]{1,0:T(8,128)(2,1)S(1)}, u32[]{:S(2)}, u32[]{:S(2)}) collective-permute-start(bf16[1024,512]{1,0:T(8,128)(2,1)S(1)} %get-tuple-element.183), channel_id=1, source_target_pairs={{0,4},{4,0},{1,5},{5,1},{2,6},{6,2},{3,7},{7,3},{8,12},{12,8},{9,1... | collective-permute-start | bytes 3145736 | tf_op jit(solution)/shard_map/ppermute | solution.py:955
  452.0 2.9 copy-start
  457.0 2.1 copy-start.8
  460.4 33.4 %copy-start.1 = (bf16[2,2,2,1024,128]{4,3,1,2,0:T(8,128)(2,1)S(1)}, bf16[2,2,2,1024,128]{4,3,1,2,0:T(8,128)(2,1)}, u32[]{:S(2)}) copy-start(bf16[2,2,2,1024,128]{4,3,1,2,0:T(8,128)(2,1)} %fusion) | copy-start | bytes 6291460
  495.4 78.0 %collective-permute-start.11 = (bf16[2,2,2,8,128,128]{5,4,3,1,2,0:T(8,128)(2,1)}, bf16[2,2,2,8,128,128]{5,4,3,1,2,0:T(8,128)(2,1)S(1)}, u32[]{:S(2)}, u32[]{:S(2)}) collective-permute-start(bf16[2,2,2,8,128,128]{5,4,3,1,2,0:T(8,128)(2,1)} %fusion.3), channel_id=1, source_target_pairs={{0,16},{8,24},{16,0},{24,8},{1,17},{9,25},{17,1},{25,9},{2,18},{10... | collective-permute-start | bytes 6291464 | tf_op jit(solution)/shard_map/ppermute | solution.py:1072
  502.4 68.5 %collective-permute-start.10 = (bf16[2,2,1024,128]{3,2,0,1:T(8,128)(2,1)}, bf16[2,2,1024,128]{3,2,0,1:T(8,128)(2,1)}, u32[]{:S(2)}, u32[]{:S(2)}) collective-permute-start(bf16[2,2,1024,128]{3,2,0,1:T(8,128)(2,1)} %get-tuple-element.122), channel_id=1, source_target_pairs={{0,16},{8,24},{16,0},{24,8},{1,17},{9,25},{17,1},{25,9},{2,18},{10... | collective-permute-start | bytes 3145736 | tf_op jit(solution)/shard_map/ppermute | solution.py:1072
  539.0 34.4 %copy-start.2 = (bf16[2,2,2,8,128,128]{5,4,3,1,2,0:T(8,128)(2,1)S(1)}, bf16[2,2,2,8,128,128]{5,4,3,1,2,0:T(8,128)(2,1)}, u32[]{:S(2)}) copy-start(bf16[2,2,2,8,128,128]{5,4,3,1,2,0:T(8,128)(2,1)} %fusion.2) | copy-start | bytes 6291460
  575.2 42.4 %copy-start.6 = (bf16[2,2,2,256,128]{4,3,2,1,0:T(8,128)(2,1)S(1)}, bf16[2,2,2,256,128]{4,3,2,1,0:T(8,128)(2,1)}, u32[]{:S(2)}) copy-start(bf16[2,2,2,256,128]{4,3,2,1,0:T(8,128)(2,1)} %get-tuple-element.131) | copy-start | bytes 1572868
  575.2 44.3 %copy-start.7 = (bf16[2,1024,128]{2,1,0:T(8,128)(2,1)S(1)}, bf16[2,1024,128]{2,1,0:T(8,128)(2,1)}, u32[]{:S(2)}) copy-start(bf16[2,1024,128]{2,1,0:T(8,128)(2,1)} %get-tuple-element.127) | copy-start | bytes 1572868
  575.2 42.4 %collective-permute-start.15 = (bf16[2,2,2,256,128]{4,3,2,1,0:T(8,128)(2,1)}, bf16[2,2,2,256,128]{4,3,2,1,0:T(8,128)(2,1)}, u32[]{:S(2)}, u32[]{:S(2)}) collective-permute-start(bf16[2,2,2,256,128]{4,3,2,1,0:T(8,128)(2,1)} %get-tuple-element.132), channel_id=1, source_target_pairs={{0,8},{8,0},{16,24},{24,16},{1,9},{9,1},{17,25},{25,17},{2,10},{10... | collective-permute-start | bytes 1572872 | tf_op jit(solution)/shard_map/ppermute | solution.py:1072
  576.6 44.8 %collective-permute-start.14 = (bf16[2,2,8,128,128]{4,3,2,0,1:T(8,128)(2,1)}, bf16[2,2,8,128,128]{4,3,2,0,1:T(8,128)(2,1)S(1)}, u32[]{:S(2)}, u32[]{:S(2)}) collective-permute-start(bf16[2,2,8,128,128]{4,3,2,0,1:T(8,128)(2,1)} %get-tuple-element.130), channel_id=1, source_target_pairs={{0,8},{8,0},{16,24},{24,16},{1,9},{9,1},{17,25},{25,17},{2,10},{10... | collective-permute-start | bytes 3145736 | tf_op jit(solution)/shard_map/ppermute | solution.py:1072
  577.2 42.3 %collective-permute-start.13 = (bf16[2,1024,128]{2,1,0:T(8,128)(2,1)}, bf16[2,1024,128]{2,1,0:T(8,128)(2,1)}, u32[]{:S(2)}, u32[]{:S(2)}) collective-permute-start(bf16[2,1024,128]{2,1,0:T(8,128)(2,1)} %get-tuple-element.128), channel_id=1, source_target_pairs={{0,1},{1,0},{2,3},{3,2},{4,5},{5,4},{6,7},{7,6},{8,9},{9,8},{10,11... | collective-permute-start | bytes 1572872 | tf_op jit(solution)/shard_map/ppermute | solution.py:1072
  622.7 13.7 %copy-start.11 = (bf16[2,8,128,128]{3,2,1,0:T(8,128)(2,1)S(1)}, bf16[2,8,128,128]{3,2,1,0:T(8,128)(2,1)}, u32[]{:S(2)}) copy-start(bf16[2,8,128,128]{3,2,1,0:T(8,128)(2,1)} %get-tuple-element.143) | copy-start | bytes 1572868
  631.2 29.0 %collective-permute-start.16 = (bf16[1024,1024]{1,0:T(8,128)(2,1)}, bf16[1024,1024]{1,0:T(8,128)(2,1)S(1)}, u32[]{:S(2)}, u32[]{:S(2)}) collective-permute-start(bf16[1024,1024]{1,0:T(8,128)(2,1)} %shard_map.209), channel_id=1, source_target_pairs={{0,4},{4,0},{1,5},{5,1},{2,6},{6,2},{3,7},{7,3},{8,12},{12,8},{9,1... | collective-permute-start | bytes 6291464 | tf_op jit(solution)/shard_map/ppermute | solution.py:955
  636.5 22.0 %collective-permute-start.19 = (bf16[1024,128]{1,0:T(8,128)(2,1)}, bf16[1024,128]{1,0:T(8,128)(2,1)}, u32[]{:S(2)}, u32[]{:S(2)}) collective-permute-start(bf16[1024,128]{1,0:T(8,128)(2,1)} %get-tuple-element.155), channel_id=1, source_target_pairs={{0,2},{1,3},{2,0},{3,1},{4,6},{5,7},{6,4},{7,5},{8,10},{9,11},{10,... | collective-permute-start | bytes 786440 | tf_op jit(solution)/shard_map/ppermute | solution.py:1072
  636.5 28.1 %collective-permute-start.17 = (bf16[2,8,128,128]{3,2,1,0:T(8,128)(2,1)S(1)}, bf16[2,8,128,128]{3,2,1,0:T(8,128)(2,1)S(1)}, u32[]{:S(2)}, u32[]{:S(2)}) collective-permute-start(bf16[2,8,128,128]{3,2,1,0:T(8,128)(2,1)S(1)} %copy-done.11), channel_id=1, source_target_pairs={{0,1},{1,0},{2,3},{3,2},{4,5},{5,4},{6,7},{7,6},{8,9},{9,8},{10,11... | collective-permute-start | bytes 1572872 | tf_op jit(solution)/shard_map/ppermute | solution.py:1072
  648.9 15.6 %collective-permute-start.18 = (bf16[2,2,256,128]{3,2,1,0:T(8,128)(2,1)}, bf16[2,2,256,128]{3,2,1,0:T(8,128)(2,1)}, u32[]{:S(2)}, u32[]{:S(2)}) collective-permute-start(bf16[2,2,256,128]{3,2,1,0:T(8,128)(2,1)} %get-tuple-element.145), channel_id=1, source_target_pairs={{0,16},{8,24},{16,0},{24,8},{1,17},{9,25},{17,1},{25,9},{2,18},{10... | collective-permute-start | bytes 786440 | tf_op jit(solution)/shard_map/ppermute | solution.py:1072
  664.6 0.8 copy-start.9
  749.9 4.2 copy-start.10
  749.9 5.0 copy-start.12
  749.9 8.2 %copy-start.15 = (f32[256,128]{1,0:T(8,128)S(1)}, f32[256,128]{1,0:T(8,128)}, u32[]{:S(2)}) copy-start(f32[256,128]{1,0:T(8,128)} %get-tuple-element.223) | copy-start | bytes 393220

commit v8 on v7

--- a/solution.py
+++ b/solution.py
@@ -948,6 +948,7 @@
             pltpu.SemaphoreType.DMA((count,)), pltpu.SemaphoreType.DMA((count,)),
         ],
         compiler_params=pltpu.CompilerParams(collective_id=0, has_side_effects=True),
+        cost_estimate=pl.CostEstimate(flops=32 * d * d * 1024, bytes_accessed=64 * d * d, transcendentals=0),
     )(dx, x_turned, *first, *second, *up_, *out_, small)
 
 
@@ -1039,7 +1040,6 @@
     active, slope = up(hl, w_up, up_bias_all)
     grad_own = bring(out_grad)
     layer, dr, dz, sums_two = down(active, w_down, normed, grad_own, row_biases, norm_gains)
-    layer_out = give(*blocks(layer))
 
     p_bits = [1 << s for s in range(n_p.bit_length() - 1)]
     t_bits = [1, 2]
@@ -1105,18 +1105,19 @@
     out_keep, out_send = col_grad(c_own, da, n_p, n_t)
     out_recv = swap_cores(out_send)
     dc_full = by_core(core, mine, dc_recv, 0)
-    down_sum.cut(1)
-    dc_full, layer_out = together([down_sum, up_sums], dc_full, layer_out)
+    dc_full, layer = together([up_sums], dc_full, blocks(layer))
+    layer_out = give(*layer)
 
     first = attend_bwd(0, qkv, context, dc_full, lse, segment, valid, 512, 256)
     out_sum = Total([out_keep, out_recv], False)
-    (dc_full,) = together([down_sum.cut(2), up_sums.cut(1), out_sum.cut(0)], dc_full)
+    dc_full, layer_out = together([down_sum.cut(1), up_sums.cut(1), out_sum.cut(0)], dc_full, layer_out)
     second = attend_bwd(1, qkv, context, dc_full, lse, segment, valid, 512, 256)
-    (second,) = together([down_sum.cut(3), up_sums.cut(2), out_sum.cut(1)], second)
+    (second,) = together([down_sum.cut(2), up_sums.cut(2), out_sum.cut(1)], second)
 
     dx_other = swap_cores(input_pull(1 - core, core, (*first, *second), w_qkv))
     dx_mine = input_pull(core, core, (*first, *second), w_qkv, dm)
     dx = (dx_mine + dx_other.astype(F32)).astype(BF16)
+    (dx,) = together([down_sum.cut(3)], dx)
     down_total = down_sum.sum_of(lambda part: part)
     small = jnp.concatenate(
         [

time: 766 us -> 687 us (0.90)
  waiting for transfers between devices: 73.4 us -> 7.42 us
  starting transfers between devices: 75 us -> 21.7 us
  Pallas kernels: 523 us -> 554 us
    ppermute x9, waiting for transfers between devices: 63.3 us -> 7.39 us  [move(): self.parts = [self.live[0], lax.ppermute(self.live[1], *self.route)]]
    pallas_call x2, Pallas kernels: 72.9 us -> 97.5 us  [attend_bwd(): pl.pallas_call(functools.partial(attend_bwd_kernel, bq), grid_spec=pltpu....]
    ppermute x1, starting transfers between devices: 21 us -> 0.01 us  [give(): lax.ppermute(b, COL, back(route_b))]
    ppermute x9, starting transfers between devices: 26.4 us -> 6.08 us  [move(): self.parts = [self.live[0], lax.ppermute(self.live[1], *self.route)]]
    pallas_call x1, Pallas kernels: 48.7 us -> 68.6 us  [attend_fwd(): pl.pallas_call(functools.partial(attend_fwd_kernel, bk), grid_spec=pltpu....]
    pallas_call x3, Pallas kernels: 49.3 us -> 37.1 us  [grad_call(): pl.pallas_call(kernel, grid=grid, in_specs=ins, out_specs=outs[0], out_sh...]
    ppermute x7, starting transfers between devices: 16.3 us -> 4.25 us  [swap_cores(): return lax.ppermute(value, 'core', [(0, 1), (1, 0)])]
    ppermute x1, waiting for transfers between devices: 10 us -> 0.01 us  [give(): lax.ppermute(b, COL, back(route_b))]
  transfers between devices with their start and end apart: 20 -> 20, of which waited for: 3 -> 2; matrix products, arithmetic and copies ran while one was open for 9% -> 11% of each run, Pallas kernels for 43% -> 67%
where the time goes in v8:
time: 687 us; the launch traced here: 675 us
  Pallas kernels  554 us (81%)
  other arithmetic  55.7 us (8%)
  local copies, waits for them, and re-layouts  30.1 us (4%)
  starting transfers between devices  21.7 us (3%)
  waiting for transfers between devices  7.42 us (1%)
    pallas_call x1, Pallas kernels, start_gather(): pl.pallas_call(functools.partial(start_kernel, n_p, n_t, kinds), out_shap...  147 us
    pallas_call x2, Pallas kernels, attend_bwd(): pl.pallas_call(functools.partial(attend_bwd_kernel, bq), grid_spec=pltpu....  97.5 us
    pallas_call x4, Pallas kernels, call(): pl.pallas_call(kernel, grid=grid, in_specs=ins, out_specs=outs[0], out_sh...  83.5 us
    pallas_call x1, Pallas kernels, finish(): pl.pallas_call(functools.partial(finish_kernel, n_p, n_t), out_shape=[sds...  81.1 us
    pallas_call x1, Pallas kernels, attend_fwd(): pl.pallas_call(functools.partial(attend_fwd_kernel, bk), grid_spec=pltpu....  68.6 us
    pallas_call x3, Pallas kernels, grad_call(): pl.pallas_call(kernel, grid=grid, in_specs=ins, out_specs=outs[0], out_sh...  37.1 us
    convert_element_type x11, other arithmetic, cut_one(): self.sum_of(lambda part: lax.dynamic_index_in_dim(part, which, at, keepdi...  24.5 us
    pallas_call x2, Pallas kernels, input_pull(): pl.pallas_call(functools.partial(input_pull_kernel, len(extra)), grid_spe...  18 us
  transfers between devices with their start and end apart: 20, of which 2 were waited for; matrix products, arithmetic and copies ran while one was open for 11% of the time, Pallas kernels for 67%

profile of v8, /device:TPU:0, one launch (start us, length us, event | category | flops | bytes accessed | tf_op | source)
XLA Modules:
  0.0 674.6 jit_solution(17037299035862815809)
XLA Ops:
  0.7 0.9 fusion.19
  2.1 0.7 copy.94
  2.8 1.3 maximum_bitcast_fusion.1.refs_1_
  4.1 146.7 %shard_map.195 = (bf16[2048,1024]{1,0:T(8,128)(2,1)}, f32[4,12,128]{2,1,0:T(8,128)}, bf16[1024,3072]{1,0:T(8,128)(2,1)}, bf16[1024,1024]{1,0:T(8,128)(2,1)}, bf1...) custom-call(bf16[2,512,1024]{2,1,0:T(8,128)(2,1)} %refs_0_.1, f32[12,128]{1,0:T(8,128)} %maximum_bitcast_fusion.1.refs_1_, ...), custom_call_target="tpu_custom_call" | custom-call | tf_op jit(solution)/shard_map/pallas_call | solution.py:737
  150.8 1.2 dynamic-slice_bitcast_fusion.1
  152.0 1.9 collective-permute-start.2
  154.7 12.3 %shard_map.196 = (bf16[2048,1536]{1,0:T(8,128)(2,1)}, bf16[1024,2048]{1,0:T(8,128)(2,1)}) custom-call(s32[1]{0:T(128)} %bitcast.core_ref.at_ref, bf16[2048,1024]{1,0:T(8,128)(2,1)} %get-tuple-element.87.x_ref, bf16[1024,3072]{1,0:T(8,128)(2,1)} %get-tuple-element.88.w_ref.refs_6_, f32[1,1536]{1,0:T(1,128)} %reshape.203.bias_ref), custom_call_target="tpu_custom_call" | custom-call | flops 6442450944 | bytes 14680064 | tf_op jit(solution)/shard_map/pallas_call | solution.py:757
  168.9 1.3 broadcast_in_dim.11.kcode_ref
  170.2 68.6 %shard_map.197 = (bf16[2048,512]{1,0:T(8,128)(2,1)}, f32[32,2048]{1,0:T(8,128)}) custom-call(s32[4]{0:T(128)} %get-tuple-element.214.lo_ref, s32[4]{0:T(128)} %get-tuple-element.213.hi_ref, s32[4]{0:T(128)} %reduce_sum.56.pad_ref, bf16[2048,1536]{1,0:T(8,128)(2,1)} %get-tuple-element.90.q_ref.k_ref.v_ref, ...), custom_call_target="tpu_custom_call" | custom-call | flops 8589934592 | bytes 25165824 | tf_op jit(solution)/shard_map/pallas_call | solution.py:160
  238.8 2.6 constant_dynamic-slice_fusion.14
  241.4 2.6 collective-permute-start.1
  244.6 3.8 maximum_select_fusion.1.e_ref
  248.5 3.6 maximum_select_fusion.c_ref.a_ref
  252.1 8.7 %shard_map.198 = (bf16[1024,1024]{1,0:T(8,128)(2,1)}, bf16[1024,1024]{1,0:T(8,128)(2,1)}, f32[1024,1024]{1,0:T(8,128)}, f32[1024,128]{1,0:T(8,128)}) custom-call(s32[1]{0:T(128)} %bitcast.core_ref.at_ref, bf16[2048,1024]{1,0:T(8,128)(2,1)} %get-tuple-element.87.x_ref, bf16[1024,1024]{1,0:T(8,128)(2,1)} %maximum_select_fusion.c_ref.a_ref, ...), custom_call_target="tpu_custom_call" | custom-call | flops 2147483648 | bytes 12582912 | tf_op jit(solution)/shard_map/pallas_call | solution.py:325
  260.7 24.7 %shard_map.199 = (bf16[1024,4096]{1,0:T(8,128)(2,1)}, bf16[1024,4096]{1,0:T(8,128)(2,1)}) custom-call(bf16[1024,1024]{1,0:T(8,128)(2,1)} %get-tuple-element.93.h_ref, bf16[1024,4096]{1,0:T(8,128)(2,1)} %get-tuple-element.94.w_ref, f32[1,4096]{1,0:T(1,128)} %bitcast.123), custom_call_target="tpu_custom_call" | custom-call | flops 8589934592 | bytes 25165824 | tf_op jit(solution)/shard_map/pallas_call | solution.py:293
  285.4 19.2 %shard_map.200 = (bf16[1024,1024]{1,0:T(8,128)(2,1)}, f32[1024,1024]{1,0:T(8,128)}, bf16[1024,1024]{1,0:T(8,128)(2,1)}, f32[8,1024]{1,0:T(8,128)}) custom-call(bf16[1024,4096]{1,0:T(8,128)(2,1)} %get-tuple-element.102.g_ref.a_ref, bf16[4096,1024]{1,0:T(8,128)(2,1)} %get-tuple-element.96.w_ref, f32[1024,1024]{1,0:T(8,128)} %get-tuple-element.97.n_ref, ...), custom_call_target="tpu_custom_call" | custom-call | flops 8589934592 | bytes 16777216 | tf_op jit(solution)/shard_map/pallas_call | solution.py:293
  304.7 22.0 %shard_map.201 = (bf16[1024,4096]{1,0:T(8,128)(2,1)}, f32[8,4096]{1,0:T(8,128)}) custom-call(bf16[1024,1024]{1,0:T(8,128)(2,1)} %get-tuple-element.99.dz_ref.b_ref, bf16[4096,1024]{1,0:T(8,128)(2,1)} %get-tuple-element.96.w_ref, bf16[1024,4096]{1,0:T(8,128)(2,1)} %get-tuple-element.100.slope_ref), custom_call_target="tpu_custom_call" | custom-call | flops 8589934592 | bytes 25165824 | tf_op jit(solution)/shard_map/pallas_call | solution.py:293
  326.6 15.6 %shard_map.202 = (bf16[4,4,1024,128]{3,2,1,0:T(8,128)(2,1)}, bf16[4,4,1024,128]{3,2,1,0:T(8,128)(2,1)}) custom-call(bf16[1024,4096]{1,0:T(8,128)(2,1)} %get-tuple-element.102.g_ref.a_ref, bf16[1024,1024]{1,0:T(8,128)(2,1)} %get-tuple-element.99.dz_ref.b_ref), custom_call_target="tpu_custom_call" | custom-call | flops 8589934592 | bytes 16777216 | tf_op jit(solution)/shard_map/pallas_call | solution.py:426
  342.4 15.2 %shard_map.203 = (bf16[4,4,8,128,128]{4,3,2,1,0:T(8,128)(2,1)}, bf16[4,4,8,128,128]{4,3,2,1,0:T(8,128)(2,1)}) custom-call(bf16[1024,1024]{1,0:T(8,128)(2,1)} %get-tuple-element.110.a_ref, bf16[1024,4096]{1,0:T(8,128)(2,1)} %get-tuple-element.113.b_ref.du_ref), custom_call_target="tpu_custom_call" | custom-call | flops 8589934592 | bytes 16777216 | tf_op jit(solution)/shard_map/pallas_call | solution.py:426
  360.2 1.5 constant_dynamic-slice_fusion.1
  361.7 1.4 copy-done.3
  363.5 1.8 copy-done.4
  365.3 1.7 constant_dynamic-slice_fusion.6
  367.0 2.5 constant_dynamic-slice_fusion.9
  369.6 1.9 fusion.1
  371.5 1.9 fusion
  373.3 17.6 %shard_map.204 = (f32[1024,1024]{1,0:T(8,128)}, bf16[1024,1024]{1,0:T(8,128)(2,1)}, f32[8,1024]{1,0:T(8,128)}) custom-call(bf16[1024,4096]{1,0:T(8,128)(2,1)} %get-tuple-element.113.b_ref.du_ref, bf16[1024,4096]{1,0:T(8,128)(2,1)} %get-tuple-element.94.w_ref, f32[1024,1024]{1,0:T(8,128)} %get-tuple-element.114.dr_ref, f32[1024,1024]{1,0:T(8,128)} %get-tuple-element.97.n_ref, ...), custom_call_target="tpu_custom_call" | custom-call | flops 8589934592 | bytes 16777216 | tf_op jit(solution)/shard_map/pallas_call | solution.py:293
  391.0 4.6 convolution_convert_fusion
  395.6 1.2 constant_dynamic-slice_fusion.4
  396.9 6.4 shard_map.205
  403.7 1.2 collective-permute-start.5
  404.9 2.9 constant_dynamic-slice_fusion.5
  407.8 2.2 fusion.3
  410.0 2.1 fusion.2
  412.1 3.6 maximum_select_fusion.2.dc_ref
  415.6 9.4 %collective-permute-start.10 = (bf16[512,1024]{1,0:T(8,128)(2,1)}, bf16[512,1024]{1,0:T(8,128)(2,1)}, u32[]{:S(2)}, u32[]{:S(2)}) collective-permute-start(bf16[512,1024]{1,0:T(8,128)(2,1)} %get-tuple-element.123), channel_id=1, source_target_pairs={{0,0},{1,1},{4,2},{5,3},{2,4},{3,5},{6,6},{7,7},{8,8},{9,9},{12,10... | collective-permute-start | bytes 3145736 | tf_op jit(solution)/shard_map/ppermute | solution.py:1002
  425.1 0.8 collective-permute-start.8
  425.9 48.9 %shard_map.207 = (bf16[2048,256]{1,0:T(8,128)(2,1)}, bf16[2048,256]{1,0:T(8,128)(2,1)}, bf16[2048,256]{1,0:T(8,128)(2,1)}) custom-call(s32[8]{0:T(128)} %get-tuple-element.212.lo_ref, s32[8]{0:T(128)} %get-tuple-element.211.hi_ref, s32[8]{0:T(128)} %reduce_sum.62.pad_ref, bf16[2048,1536]{1,0:T(8,128)(2,1)} %get-tuple-element.90.q_ref.k_ref.v_ref, ...), custom_call_target="tpu_custom_call" | custom-call | flops 21474836480 | bytes 50331648 | tf_op jit(solution)/shard_map/pallas_call | solution.py:198
  474.8 1.6 fusion.9
  476.7 3.1 fusion.5
  479.7 4.0 maximum_select_fusion.3
  483.7 3.3 fusion.7
  487.1 2.0 collective-permute-start.13
  489.1 48.7 %shard_map.206 = (bf16[2048,256]{1,0:T(8,128)(2,1)}, bf16[2048,256]{1,0:T(8,128)(2,1)}, bf16[2048,256]{1,0:T(8,128)(2,1)}) custom-call(s32[8]{0:T(128)} %get-tuple-element.212.lo_ref, s32[8]{0:T(128)} %get-tuple-element.211.hi_ref, s32[8]{0:T(128)} %reduce_sum.62.pad_ref, bf16[2048,1536]{1,0:T(8,128)(2,1)} %get-tuple-element.90.q_ref.k_ref.v_ref, ...), custom_call_target="tpu_custom_call" | custom-call | flops 21474836480 | bytes 50331648 | tf_op jit(solution)/shard_map/pallas_call | solution.py:198
  537.8 2.0 fusion.15
  539.8 2.4 fusion.13
  542.1 2.3 fusion.11
  544.4 8.4 %shard_map.209 = bf16[1024,1024]{1,0:T(8,128)(2,1)} custom-call(s32[2]{0:T(128)} %pad_add_fusion.1.at_ref, bf16[2048,256]{1,0:T(8,128)(2,1)} %get-tuple-element.139.refs_0_.refs_2_, bf16[2048,256]{1,0:T(8,128)(2,1)} %get-tuple-element.140.refs_1_.refs_3_, bf16[2048,256]{1,0:T(8,128)(2,1)} %get-tuple-element.141.refs_2_.refs_4_, ...), custom_call_target="tpu_custom_call" | custom-call | flops 3221225472 | bytes 16777216 | tf_op jit(solution)/shard_map/pallas_call | solution.py:486
  553.4 0.8 slice.82
  554.2 0.8 slice.80
  554.9 0.9 slice.83
  555.8 0.8 slice.81
  556.6 0.8 slice.79
  558.0 2.0 collective-permute-start.17
  560.1 9.7 %shard_map.208 = f32[1024,1024]{1,0:T(8,128)} custom-call(s32[2]{0:T(128)} %pad_add_fusion.at_ref, bf16[2048,256]{1,0:T(8,128)(2,1)} %get-tuple-element.139.refs_0_.refs_2_, bf16[2048,256]{1,0:T(8,128)(2,1)} %get-tuple-element.140.refs_1_.refs_3_, bf16[2048,256]{1,0:T(8,128)(2,1)} %get-tuple-element.141.refs_2_.refs_4_, ...), custom_call_target="tpu_custom_call" | custom-call | flops 3221225472 | bytes 16777216 | tf_op jit(solution)/shard_map/pallas_call | solution.py:486
  569.7 2.7 collective-permute-done.15
  572.5 1.9 fusion.17
  574.3 4.3 add_convert_fusion.refs_0_
  578.7 4.6 collective-permute-done.17
  583.3 81.1 %shard_map.210 = (bf16[2,512,1024]{2,1,0:T(8,128)(2,1)}, f32[768,128]{1,0:T(8,128)}, f32[1024,128]{1,0:T(8,128)}, f32[256,128]{1,0:T(8,128)}, f32[96,128]{1,0:T(8,128)}) custom-call(bf16[1024,1024]{1,0:T(8,128)(2,1)} %add_convert_fusion.refs_0_, bf16[1024,2048]{1,0:T(8,128)(2,1)} %get-tuple-element.147.refs_1_, ...), custom_call_target="tpu_custom_call" | custom-call | flops 34359738368 | bytes 67108864 | tf_op jit(solution)/shard_map/pallas_call | solution.py:935
  664.5 4.1 convert_element_type.388
  668.6 0.8 copy.108
  669.5 0.8 copy.109
  672.7 0.8 convert_add_fusion
  (106 shorter events, 12.1 us)
Async XLA Ops:
  0.6 150.2 %copy-start.5 = (bf16[2,512,1024]{2,1,0:T(8,128)(2,1)S(1)}, bf16[2,512,1024]{2,1,0:T(8,128)(2,1)}, u32[]{:S(2)}) copy-start(bf16[2,512,1024]{2,1,0:T(8,128)(2,1)} %param.23) | copy-start | bytes 6291460
  1.5 165.5 %collective-permute-start = (s32[2,2048]{1,0:T(2,128)S(1)}, s32[2,2048]{1,0:T(2,128)S(1)}, u32[]{:S(2)}, u32[]{:S(2)}) collective-permute-start(s32[2,2048]{1,0:T(2,128)S(1)} %fusion.19), channel_id=1, source_target_pairs={{0,4},{4,0},{1,5},{5,1},{2,6},{6,2},{3,7},{7,3},{8,12},{12,8},{9,1... | collective-permute-start | bytes 49160 | tf_op jit(solution)/shard_map/ppermute | solution.py:956
  150.8 3.0 copy-start.15
  152.0 92.7 %collective-permute-start.2 = (bf16[512,1024]{1,0:T(8,128)(2,1)}, bf16[512,1024]{1,0:T(8,128)(2,1)S(1)}, u32[]{:S(2)}, u32[]{:S(2)}) collective-permute-start(bf16[512,1024]{1,0:T(8,128)(2,1)} %get-tuple-element.190), channel_id=1, source_target_pairs={{0,0},{1,1},{2,4},{3,5},{4,2},{5,3},{6,6},{7,7},{8,8},{9,9},{10,12... | collective-permute-start | bytes 3145736 | tf_op jit(solution)/shard_map/ppermute | solution.py:994
  153.8 90.8 %collective-permute-start.3 = (bf16[512,1024]{1,0:T(8,128)(2,1)S(1)}, bf16[512,1024]{1,0:T(8,128)(2,1)}, u32[]{:S(2)}, u32[]{:S(2)}) collective-permute-start(bf16[512,1024]{1,0:T(8,128)(2,1)S(1)} %get-tuple-element.191), channel_id=1, source_target_pairs={{0,1},{1,0},{2,5},{3,4},{4,3},{5,2},{6,7},{7,6},{8,9},{9,8},{10,13... | collective-permute-start | bytes 3145736 | tf_op jit(solution)/shard_map/ppermute | solution.py:995
  167.1 3.0 copy-start.11
  241.4 7.1 %collective-permute-start.1 = (bf16[1024,512]{1,0:T(8,128)(2,1)}, bf16[1024,512]{1,0:T(8,128)(2,1)}, u32[]{:S(2)}, u32[]{:S(2)}) collective-permute-start(bf16[1024,512]{1,0:T(8,128)(2,1)} %get-tuple-element.193), channel_id=1, source_target_pairs={{0,4},{4,0},{1,5},{5,1},{2,6},{6,2},{3,7},{7,3},{8,12},{12,8},{9,1... | collective-permute-start | bytes 3145736 | tf_op jit(solution)/shard_map/ppermute | solution.py:956
  342.2 24.8 %collective-permute-start.4 = (bf16[4,4,1024,128]{3,2,1,0:T(8,128)(2,1)}, bf16[4,4,1024,128]{3,2,1,0:T(8,128)(2,1)}, u32[]{:S(2)}, u32[]{:S(2)}) collective-permute-start(bf16[4,4,1024,128]{3,2,1,0:T(8,128)(2,1)} %get-tuple-element.106), channel_id=1, source_target_pairs={{0,4},{4,0},{1,5},{5,1},{2,6},{6,2},{3,7},{7,3},{8,12},{12,8},{9,1... | collective-permute-start | bytes 12582920 | tf_op jit(solution)/shard_map/ppermute | solution.py:956
  342.4 16.1 %copy-start.12 = (s32[1,2048]{1,0:T(1,128)S(1)}, s32[1,2048]{1,0:T(1,128)}, u32[]{:S(2)}) copy-start(s32[1,2048]{1,0:T(1,128)} %copy-done.11) | copy-start | bytes 24580
  342.4 17.7 %copy-start.6 = (bf16[1024,1024]{1,0:T(8,128)(2,1)S(1)}, bf16[1024,1024]{1,0:T(8,128)(2,1)}, u32[]{:S(2)}) copy-start(bf16[1024,1024]{1,0:T(8,128)(2,1)} %get-tuple-element.117) | copy-start | bytes 6291460
  357.6 47.3 %collective-permute-start.6 = (bf16[4,4,8,128,128]{4,3,2,1,0:T(8,128)(2,1)}, bf16[4,4,8,128,128]{4,3,2,1,0:T(8,128)(2,1)}, u32[]{:S(2)}, u32[]{:S(2)}) collective-permute-start(bf16[4,4,8,128,128]{4,3,2,1,0:T(8,128)(2,1)} %get-tuple-element.112), channel_id=1, source_target_pairs={{0,4},{4,0},{1,5},{5,1},{2,6},{6,2},{3,7},{7,3},{8,12},{12,8},{9,1... | collective-permute-start | bytes 12582920 | tf_op jit(solution)/shard_map/ppermute | solution.py:956
  360.2 2.9 copy-start.3
  363.1 2.2 copy-start.4
  396.8 15.3 %collective-permute-start.7 = (bf16[1024,512]{1,0:T(8,128)(2,1)}, bf16[1024,512]{1,0:T(8,128)(2,1)}, u32[]{:S(2)}, u32[]{:S(2)}) collective-permute-start(bf16[1024,512]{1,0:T(8,128)(2,1)} %get-tuple-element.189), channel_id=1, source_target_pairs={{0,4},{4,0},{1,5},{5,1},{2,6},{6,2},{3,7},{7,3},{8,12},{12,8},{9,1... | collective-permute-start | bytes 3145736 | tf_op jit(solution)/shard_map/ppermute | solution.py:956
  403.3 71.5 %collective-permute-start.9 = (bf16[4,4,256,128]{3,2,1,0:T(8,128)(2,1)}, bf16[4,4,256,128]{3,2,1,0:T(8,128)(2,1)}, u32[]{:S(2)}, u32[]{:S(2)}) collective-permute-start(bf16[4,4,256,128]{3,2,1,0:T(8,128)(2,1)} %get-tuple-element.121), channel_id=1, source_target_pairs={{0,4},{4,0},{1,5},{5,1},{2,6},{6,2},{3,7},{7,3},{8,12},{12,8},{9,1... | collective-permute-start | bytes 3145736 | tf_op jit(solution)/shard_map/ppermute | solution.py:956
  403.7 72.7 %collective-permute-start.5 = (bf16[2,2,2,1024,128]{4,3,1,2,0:T(8,128)(2,1)}, bf16[2,2,2,1024,128]{4,3,1,2,0:T(8,128)(2,1)}, u32[]{:S(2)}, u32[]{:S(2)}) collective-permute-start(bf16[2,2,2,1024,128]{4,3,1,2,0:T(8,128)(2,1)} %fusion.1), channel_id=1, source_target_pairs={{0,8},{8,0},{16,24},{24,16},{1,9},{9,1},{17,25},{25,17},{2,10},{10... | collective-permute-start | bytes 6291464 | tf_op jit(solution)/shard_map/ppermute | solution.py:1072
  404.9 2.9 copy-start
  412.1 13.0 %copy-start.7 = (bf16[512,1024]{1,0:T(8,128)(2,1)S(1)}, bf16[512,1024]{1,0:T(8,128)(2,1)}, u32[]{:S(2)}) copy-start(bf16[512,1024]{1,0:T(8,128)(2,1)} %get-tuple-element.124) | copy-start | bytes 3145732
  415.6 64.1 %collective-permute-start.10 = (bf16[512,1024]{1,0:T(8,128)(2,1)}, bf16[512,1024]{1,0:T(8,128)(2,1)}, u32[]{:S(2)}, u32[]{:S(2)}) collective-permute-start(bf16[512,1024]{1,0:T(8,128)(2,1)} %get-tuple-element.123), channel_id=1, source_target_pairs={{0,0},{1,1},{4,2},{5,3},{2,4},{3,5},{6,6},{7,7},{8,8},{9,9},{12,10... | collective-permute-start | bytes 3145736 | tf_op jit(solution)/shard_map/ppermute | solution.py:1002
  425.1 54.6 %collective-permute-start.11 = (bf16[512,1024]{1,0:T(8,128)(2,1)S(1)}, bf16[512,1024]{1,0:T(8,128)(2,1)}, u32[]{:S(2)}, u32[]{:S(2)}) collective-permute-start(bf16[512,1024]{1,0:T(8,128)(2,1)S(1)} %copy-done.7), channel_id=1, source_target_pairs={{1,0},{0,1},{5,2},{4,3},{3,4},{2,5},{7,6},{6,7},{9,8},{8,9},{13,10... | collective-permute-start | bytes 3145736 | tf_op jit(solution)/shard_map/ppermute | solution.py:1002
  425.1 58.6 %collective-permute-start.8 = (bf16[2,2,2,8,128,128]{5,4,3,1,2,0:T(8,128)(2,1)}, bf16[2,2,2,8,128,128]{5,4,3,1,2,0:T(8,128)(2,1)}, u32[]{:S(2)}, u32[]{:S(2)}) collective-permute-start(bf16[2,2,2,8,128,128]{5,4,3,1,2,0:T(8,128)(2,1)} %fusion.3), channel_id=1, source_target_pairs={{0,16},{8,24},{16,0},{24,8},{1,17},{9,25},{17,1},{25,9},{2,18},{10... | collective-permute-start | bytes 6291464 | tf_op jit(solution)/shard_map/ppermute | solution.py:1072
  425.9 48.9 %copy-start.8 = (bf16[4,4,256,128]{3,2,1,0:T(8,128)(2,1)S(1)}, bf16[4,4,256,128]{3,2,1,0:T(8,128)(2,1)}, u32[]{:S(2)}) copy-start(bf16[4,4,256,128]{3,2,1,0:T(8,128)(2,1)} %get-tuple-element.120) | copy-start | bytes 3145732
  474.7 1.9 copy-start.1
  479.7 4.0 copy-start.2
  487.1 50.7 %collective-permute-start.14 = (bf16[2,2,2,256,128]{4,3,2,1,0:T(8,128)(2,1)S(1)}, bf16[2,2,2,256,128]{4,3,2,1,0:T(8,128)(2,1)}, u32[]{:S(2)}, u32[]{:S(2)}) collective-permute-start(bf16[2,2,2,256,128]{4,3,2,1,0:T(8,128)(2,1)S(1)} %get-tuple-element.131), channel_id=1, source_target_pairs={{0,8},{8,0},{16,24},{24,16},{1,9},{9,1},{17,25},{25,17},{2,10},{10... | collective-permute-start | bytes 1572872 | tf_op jit(solution)/shard_map/ppermute | solution.py:1072
  487.1 52.7 %collective-permute-start.13 = (bf16[2,2,8,128,128]{4,3,2,0,1:T(8,128)(2,1)}, bf16[2,2,8,128,128]{4,3,2,0,1:T(8,128)(2,1)}, u32[]{:S(2)}, u32[]{:S(2)}) collective-permute-start(bf16[2,2,8,128,128]{4,3,2,0,1:T(8,128)(2,1)} %get-tuple-element.129), channel_id=1, source_target_pairs={{0,8},{8,0},{16,24},{24,16},{1,9},{9,1},{17,25},{25,17},{2,10},{10... | collective-permute-start | bytes 3145736 | tf_op jit(solution)/shard_map/ppermute | solution.py:1072
  489.1 53.0 %collective-permute-start.12 = (bf16[2,2,1024,128]{3,2,0,1:T(8,128)(2,1)}, bf16[2,2,1024,128]{3,2,0,1:T(8,128)(2,1)}, u32[]{:S(2)}, u32[]{:S(2)}) collective-permute-start(bf16[2,2,1024,128]{3,2,0,1:T(8,128)(2,1)} %get-tuple-element.127), channel_id=1, source_target_pairs={{0,16},{8,24},{16,0},{24,8},{1,17},{9,25},{17,1},{25,9},{2,18},{10... | collective-permute-start | bytes 3145736 | tf_op jit(solution)/shard_map/ppermute | solution.py:1072
  552.8 21.6 %collective-permute-start.16 = (bf16[1024,1024]{1,0:T(8,128)(2,1)}, bf16[1024,1024]{1,0:T(8,128)(2,1)S(1)}, u32[]{:S(2)}, u32[]{:S(2)}) collective-permute-start(bf16[1024,1024]{1,0:T(8,128)(2,1)} %shard_map.209), channel_id=1, source_target_pairs={{0,4},{4,0},{1,5},{5,1},{2,6},{6,2},{3,7},{7,3},{8,12},{12,8},{9,1... | collective-permute-start | bytes 6291464 | tf_op jit(solution)/shard_map/ppermute | solution.py:956
  557.4 15.1 %collective-permute-start.15 = (bf16[2,1024,128]{2,1,0:T(8,128)(2,1)}, bf16[2,1024,128]{2,1,0:T(8,128)(2,1)}, u32[]{:S(2)}, u32[]{:S(2)}) collective-permute-start(bf16[2,1024,128]{2,1,0:T(8,128)(2,1)} %get-tuple-element.138), channel_id=1, source_target_pairs={{0,1},{1,0},{2,3},{3,2},{4,5},{5,4},{6,7},{7,6},{8,9},{9,8},{10,11... | collective-permute-start | bytes 1572872 | tf_op jit(solution)/shard_map/ppermute | solution.py:1072
  558.0 25.3 %collective-permute-start.17 = (bf16[2,8,128,128]{3,2,1,0:T(8,128)(2,1)S(1)}, bf16[2,8,128,128]{3,2,1,0:T(8,128)(2,1)}, u32[]{:S(2)}, u32[]{:S(2)}) collective-permute-start(bf16[2,8,128,128]{3,2,1,0:T(8,128)(2,1)S(1)} %get-tuple-element.149), channel_id=1, source_target_pairs={{0,1},{1,0},{2,3},{3,2},{4,5},{5,4},{6,7},{7,6},{8,9},{9,8},{10,11... | collective-permute-start | bytes 1572872 | tf_op jit(solution)/shard_map/ppermute | solution.py:1072
  560.1 18.6 %collective-permute-start.18 = (bf16[2,2,256,128]{3,2,1,0:T(8,128)(2,1)}, bf16[2,2,256,128]{3,2,1,0:T(8,128)(2,1)}, u32[]{:S(2)}, u32[]{:S(2)}) collective-permute-start(bf16[2,2,256,128]{3,2,1,0:T(8,128)(2,1)} %get-tuple-element.151), channel_id=1, source_target_pairs={{0,16},{8,24},{16,0},{24,8},{1,17},{9,25},{17,1},{25,9},{2,18},{10... | collective-permute-start | bytes 786440 | tf_op jit(solution)/shard_map/ppermute | solution.py:1072
  578.7 94.0 %collective-permute-start.19 = (bf16[1024,128]{1,0:T(8,128)(2,1)}, bf16[1024,128]{1,0:T(8,128)(2,1)S(1)}, u32[]{:S(2)}, u32[]{:S(2)}) collective-permute-start(bf16[1024,128]{1,0:T(8,128)(2,1)} %get-tuple-element.161), channel_id=1, source_target_pairs={{0,2},{1,3},{2,0},{3,1},{4,6},{5,7},{6,4},{7,5},{8,10},{9,11},{10,... | collective-permute-start | bytes 786440 | tf_op jit(solution)/shard_map/ppermute | solution.py:1072
  664.5 4.2 copy-start.9
  664.5 5.0 copy-start.10
  664.5 5.8 copy-start.14
  668.6 4.9 copy-start.13

commit v9 on v8

--- a/solution.py
+++ b/solution.py
@@ -258,9 +258,20 @@
     slope_ref[...] = (cdf + u * (jnp.exp(-0.5 * u * u) * (1.0 / math.sqrt(2.0 * math.pi)))).astype(BF16)
 
 
-def down_kernel(g_ref, w_ref, n_ref, e_ref, bias_ref, gain_ref, out_ref, dr_ref, dz_ref, sum_ref):
+def assemble(w_ref, w_all, sem):
+    for d in range(w_ref.shape[0]):
+        for t in range(w_ref.shape[1]):
+            rows_, cols = w_ref.shape[2:]
+            pltpu.make_async_copy(
+                w_ref.at[d, t], w_all.at[pl.ds(t * rows_, rows_), pl.ds(d * cols, cols)], sem
+            ).start()
+    pltpu.make_async_copy(w_all, w_all, sem).wait()
+
+
+def down_kernel(g_ref, w_ref, n_ref, e_ref, bias_ref, gain_ref, out_ref, dr_ref, dz_ref, sum_ref, w_all, sem):
+    pl.when(pl.program_id(0) == 0)(lambda: assemble(w_ref, w_all, sem))
     hidden = n_ref[...] * gain_ref[0:1, :] + bias_ref[1:2, :]
-    normed, inverse = norm_stats(hidden + dot(g_ref[...], w_ref[...]) + bias_ref[2:3, :])
+    normed, inverse = norm_stats(hidden + dot(g_ref[...], w_all[...]) + bias_ref[2:3, :])
     out_ref[...] = (normed * gain_ref[1:2, :] + bias_ref[3:4, :]).astype(BF16)
     e = e_ref[...].astype(F32)
     dr = norm_pull(e, normed, inverse, gain_ref[1:2, :])
@@ -269,8 +280,11 @@
     add_sums(sum_ref, (e * normed, dr, e))
 
 
-def slope_kernel(dz_ref, w_ref, slope_ref, du_ref, sum_ref):
-    du = (dot(dz_ref[...], w_ref[...], NT) * slope_ref[...].astype(F32)).astype(BF16)
+def slope_kernel(dz_ref, w_ref, slope_ref, du_ref, sum_ref, w_all, sem):
+    cols = slope_ref.shape[1]
+    j = pl.program_id(0)
+    pl.when(jnp.logical_and(j == 0, pl.program_id(1) == 0))(lambda: assemble(w_ref, w_all, sem))
+    du = (dot(dz_ref[...], w_all[pl.ds(pl.multiple_of(j * cols, cols), cols), :], NT) * slope_ref[...].astype(F32)).astype(BF16)
     du_ref[...] = du
 
     @pl.when(pl.program_id(1) == 0)
@@ -289,13 +303,14 @@
     add_sums(sum_ref, (dh * normed, dm, dh))
 
 
-def call(kernel, grid, ins, outs, flops, nbytes, *args):
+def call(kernel, grid, ins, outs, flops, nbytes, *args, scratch=()):
     return pl.pallas_call(
         kernel,
         grid=grid,
         in_specs=ins,
         out_specs=outs[0],
         out_shape=outs[1],
+        scratch_shapes=list(scratch),
         compiler_params=pltpu.CompilerParams(dimension_semantics=("arbitrary",) * len(grid)),
         cost_estimate=pl.CostEstimate(flops=flops, bytes_accessed=nbytes, transcendentals=0),
     )(*args)
@@ -351,27 +366,32 @@
     )
 
 
+def assembled(w):
+    shape = (w.shape[1] * w.shape[2], w.shape[0] * w.shape[3])
+    return shape, [pltpu.VMEM(shape, BF16), pltpu.SemaphoreType.DMA]
+
+
 def down(g, w, normed, e, biases, gains, block=256):
     n, f = g.shape
-    d = w.shape[1]
+    (_, d), scratch = assembled(w)
     r = functools.partial(rows, block)
     return call(
         down_kernel, (n // block,),
-        [r(f), once(w.shape), r(d), r(d), held(biases.shape), held(gains.shape)],
+        [r(f), pl.BlockSpec(memory_space=pl.ANY), r(d), r(d), held(biases.shape), held(gains.shape)],
         ([r(d), r(d), r(d), held((8, d))], [sds((n, d)), sds((n, d), F32), sds((n, d)), sds((8, d), F32)]),
-        2 * n * d * f, 2 * n * f + 2 * d * f, g, w, normed, e, biases, gains,
+        2 * n * d * f, 2 * n * f + 2 * d * f, g, w, normed, e, biases, gains, scratch=scratch,
     )
 
 
 def slope_pull(dz, w, slope, block=256, cols=1024):
     n, d = dz.shape
-    f = w.shape[0]
+    (f, _), scratch = assembled(w)
     tile = pl.BlockSpec((block, cols), lambda j, i: (i, j))
     return call(
         slope_kernel, (f // cols, n // block),
-        [pl.BlockSpec((block, d), lambda j, i: (i, 0)), pl.BlockSpec((cols, d), lambda j, i: (j, 0)), tile],
+        [pl.BlockSpec((block, d), lambda j, i: (i, 0)), pl.BlockSpec(memory_space=pl.ANY), tile],
         ([tile, pl.BlockSpec((8, cols), lambda j, i: (0, j))], [sds((n, f)), sds((8, f), F32)]),
-        2 * n * d * f, 4 * n * f + 2 * d * f, dz, w, slope,
+        2 * n * d * f, 4 * n * f + 2 * d * f, dz, w, slope, scratch=scratch,
     )
 
 
@@ -1013,16 +1033,17 @@
     shards, kinds = [qkv_weight, up_weight], ["rows", "rows"]
     wide = out_weight.shape[1] % 128 == 0
     if wide:
-        shards, kinds = [qkv_weight, out_weight, up_weight, down_weight], ["rows", "columns", "rows", "columns"]
+        shards, kinds = [qkv_weight, out_weight, up_weight], ["rows", "columns", "rows"]
     local_bias = jnp.concatenate([qv_bias.reshape(-1), up_bias]).reshape(-1, 128)
     x_full, bias_all, *fulls = start_gather(inputs, local_bias, shards, kinds, n_p, n_t)
+    out_grad, down_weight, x_full = lax.optimization_barrier((out_grad, down_weight, x_full))
+    w_down = gathered(down_weight)
     if wide:
-        w_qkv, w_out, w_up, w_down = fulls
+        w_qkv, w_out, w_up = fulls
     else:
         w_qkv, w_up = fulls
         w_out = gathered(out_weight).transpose(1, 2, 0, 3).reshape(-1, width)
-        w_down = gathered(down_weight).transpose(1, 2, 0, 3).reshape(-1, width)
-    out_grad, x_full = lax.optimization_barrier((out_grad, x_full))
+        w_down = w_down.transpose(1, 2, 0, 3).reshape(1, 1, -1, width)
     rows = x_full.shape[0] // 2
     own = w_qkv.shape[1] // 6
     bias_all = bias_all.reshape(n_t, -1)

time: 687 us -> 662 us (0.964)
  Pallas kernels: 554 us -> 515 us
  between operations: 1.39 us -> 14.8 us
    pallas_call x1, Pallas kernels: 147 us -> 107 us  [start_gather(): pl.pallas_call(functools.partial(start_kernel, n_p, n_t, kinds), out_shap...]
  transfers between devices with their start and end apart: 20 -> 21, of which waited for: 2 -> 2; matrix products, arithmetic and copies ran while one was open for 11% -> 12% of each run, Pallas kernels for 67% -> 52%
where the time goes in v9:
time: 662 us; the launch traced here: 651 us
  Pallas kernels  515 us (78%)
  other arithmetic  54.9 us (8%)
  local copies, waits for them, and re-layouts  30.3 us (5%)
  starting transfers between devices  23.6 us (4%)
  between operations  14.8 us (2%)
  waiting for transfers between devices  7.67 us (1%)
    pallas_call x1, Pallas kernels, start_gather(): pl.pallas_call(functools.partial(start_kernel, n_p, n_t, kinds), out_shap...  107 us
    pallas_call x2, Pallas kernels, attend_bwd(): pl.pallas_call(functools.partial(attend_bwd_kernel, bq), grid_spec=pltpu....  96.5 us
    pallas_call x4, Pallas kernels, call(): pl.pallas_call(kernel, grid=grid, in_specs=ins, out_specs=outs[0], out_sh...  85 us
    pallas_call x1, Pallas kernels, finish(): pl.pallas_call(functools.partial(finish_kernel, n_p, n_t), out_shape=[sds...  82.3 us
    pallas_call x1, Pallas kernels, attend_fwd(): pl.pallas_call(functools.partial(attend_fwd_kernel, bk), grid_spec=pltpu....  68.1 us
    pallas_call x3, Pallas kernels, grad_call(): pl.pallas_call(kernel, grid=grid, in_specs=ins, out_specs=outs[0], out_sh...  37.1 us
    convert_element_type x11, other arithmetic, cut_one(): self.sum_of(lambda part: lax.dynamic_index_in_dim(part, which, at, keepdi...  24.5 us
    pallas_call x2, Pallas kernels, input_pull(): pl.pallas_call(functools.partial(input_pull_kernel, len(extra)), grid_spe...  18 us
  transfers between devices with their start and end apart: 21, of which 2 were waited for; matrix products, arithmetic and copies ran while one was open for 12% of the time, Pallas kernels for 52%

profile of v9, /device:TPU:0, one launch (start us, length us, event | category | flops | bytes accessed | tf_op | source)
XLA Modules:
  0.0 651.3 jit_solution(11348955314248750289)
XLA Ops:
  7.3 0.8 copy.94
  8.1 1.3 maximum_bitcast_fusion.1.refs_1_
  9.4 107.4 %shard_map.195 = (bf16[2048,1024]{1,0:T(8,128)(2,1)}, f32[4,12,128]{2,1,0:T(8,128)}, bf16[1024,3072]{1,0:T(8,128)(2,1)}, bf16[1024,1024]{1,0:T(8,128)(2,1)}, bf16[1024,4096]{1,0:T(8,128)(2,1)}) custom-call(bf16[2,512,1024]{2,1,0:T(8,128)(2,1)} %refs_0_.1, f32[12,128]{1,0:T(8,128)} %maximum_bitcast_fusion.1.refs_1_, bf16[3,128,256]{2,1,0:T(8,128)(2,1)} %refs_2_.1, ...), custom_call_target="tpu_custom_call" | custom-call | tf_op jit(solution)/shard_map/pallas_call | solution.py:757
  117.3 1.2 dynamic-slice_bitcast_fusion.1
  118.5 1.9 collective-permute-start.2
  121.2 12.4 %shard_map.196 = (bf16[2048,1536]{1,0:T(8,128)(2,1)}, bf16[1024,2048]{1,0:T(8,128)(2,1)}) custom-call(s32[1]{0:T(128)} %bitcast.core_ref.at_ref, bf16[2048,1024]{1,0:T(8,128)(2,1)} %get-tuple-element.87.x_ref, bf16[1024,3072]{1,0:T(8,128)(2,1)} %get-tuple-element.88.w_ref.refs_6_, f32[1,1536]{1,0:T(1,128)} %reshape.206.bias_ref), custom_call_target="tpu_custom_call" | custom-call | flops 6442450944 | bytes 14680064 | tf_op jit(solution)/shard_map/pallas_call | solution.py:777
  135.3 1.3 broadcast_in_dim.11.kcode_ref
  136.6 68.1 %shard_map.197 = (bf16[2048,512]{1,0:T(8,128)(2,1)}, f32[32,2048]{1,0:T(8,128)}) custom-call(s32[4]{0:T(128)} %get-tuple-element.214.lo_ref, s32[4]{0:T(128)} %get-tuple-element.213.hi_ref, s32[4]{0:T(128)} %reduce_sum.56.pad_ref, bf16[2048,1536]{1,0:T(8,128)(2,1)} %get-tuple-element.90.q_ref.k_ref.v_ref, ...), custom_call_target="tpu_custom_call" | custom-call | flops 8589934592 | bytes 25165824 | tf_op jit(solution)/shard_map/pallas_call | solution.py:160
  204.8 2.6 constant_dynamic-slice_fusion.14
  207.4 2.8 collective-permute-start.1
  210.9 3.8 maximum_select_fusion.1.e_ref
  214.7 3.6 maximum_select_fusion.c_ref.a_ref
  218.3 8.7 %shard_map.198 = (bf16[1024,1024]{1,0:T(8,128)(2,1)}, bf16[1024,1024]{1,0:T(8,128)(2,1)}, f32[1024,1024]{1,0:T(8,128)}, f32[1024,128]{1,0:T(8,128)}) custom-call(s32[1]{0:T(128)} %bitcast.core_ref.at_ref, bf16[2048,1024]{1,0:T(8,128)(2,1)} %get-tuple-element.87.x_ref, bf16[1024,1024]{1,0:T(8,128)(2,1)} %maximum_select_fusion.c_ref.a_ref, ...), custom_call_target="tpu_custom_call" | custom-call | flops 2147483648 | bytes 12582912 | tf_op jit(solution)/shard_map/pallas_call | solution.py:340
  227.0 24.7 %shard_map.199 = (bf16[1024,4096]{1,0:T(8,128)(2,1)}, bf16[1024,4096]{1,0:T(8,128)(2,1)}) custom-call(bf16[1024,1024]{1,0:T(8,128)(2,1)} %get-tuple-element.93.h_ref, bf16[1024,4096]{1,0:T(8,128)(2,1)} %get-tuple-element.94.w_ref, f32[1,4096]{1,0:T(1,128)} %bitcast.124), custom_call_target="tpu_custom_call" | custom-call | flops 8589934592 | bytes 25165824 | tf_op jit(solution)/shard_map/pallas_call | solution.py:307
  251.6 20.1 %shard_map.200 = (bf16[1024,1024]{1,0:T(8,128)(2,1)}, f32[1024,1024]{1,0:T(8,128)}, bf16[1024,1024]{1,0:T(8,128)(2,1)}, f32[8,1024]{1,0:T(8,128)}) custom-call(bf16[1024,4096]{1,0:T(8,128)(2,1)} %get-tuple-element.102.g_ref.a_ref, bf16[8,4,1024,128]{3,2,1,0:T(8,128)(2,1)} %bitcast.131, f32[1024,1024]{1,0:T(8,128)} %get-tuple-element.97.n_ref, ...), custom_call_target="tpu_custom_call" | custom-call | flops 8589934592 | bytes 16777216 | tf_op jit(solution)/shard_map/pallas_call | solution.py:307
  271.7 22.7 %shard_map.201 = (bf16[1024,4096]{1,0:T(8,128)(2,1)}, f32[8,4096]{1,0:T(8,128)}) custom-call(bf16[1024,1024]{1,0:T(8,128)(2,1)} %get-tuple-element.99.dz_ref.b_ref, bf16[8,4,1024,128]{3,2,1,0:T(8,128)(2,1)} %bitcast.132, bf16[1024,4096]{1,0:T(8,128)(2,1)} %get-tuple-element.100.slope_ref), custom_call_target="tpu_custom_call" | custom-call | flops 8589934592 | bytes 25165824 | tf_op jit(solution)/shard_map/pallas_call | solution.py:307
  294.4 15.5 %shard_map.202 = (bf16[4,4,1024,128]{3,2,1,0:T(8,128)(2,1)}, bf16[4,4,1024,128]{3,2,1,0:T(8,128)(2,1)}) custom-call(bf16[1024,4096]{1,0:T(8,128)(2,1)} %get-tuple-element.102.g_ref.a_ref, bf16[1024,1024]{1,0:T(8,128)(2,1)} %get-tuple-element.99.dz_ref.b_ref), custom_call_target="tpu_custom_call" | custom-call | flops 8589934592 | bytes 16777216 | tf_op jit(solution)/shard_map/pallas_call | solution.py:446
  310.0 15.2 %shard_map.203 = (bf16[4,4,8,128,128]{4,3,2,1,0:T(8,128)(2,1)}, bf16[4,4,8,128,128]{4,3,2,1,0:T(8,128)(2,1)}) custom-call(bf16[1024,1024]{1,0:T(8,128)(2,1)} %get-tuple-element.110.a_ref, bf16[1024,4096]{1,0:T(8,128)(2,1)} %get-tuple-element.113.b_ref.du_ref), custom_call_target="tpu_custom_call" | custom-call | flops 8589934592 | bytes 16777216 | tf_op jit(solution)/shard_map/pallas_call | solution.py:446
  327.9 1.5 constant_dynamic-slice_fusion.1
  329.4 1.5 copy-done.3
  331.3 1.8 copy-done.4
  333.1 1.8 constant_dynamic-slice_fusion.6
  334.8 2.5 constant_dynamic-slice_fusion.9
  337.4 1.9 fusion.1
  339.2 1.9 fusion
  341.1 17.6 %shard_map.204 = (f32[1024,1024]{1,0:T(8,128)}, bf16[1024,1024]{1,0:T(8,128)(2,1)}, f32[8,1024]{1,0:T(8,128)}) custom-call(bf16[1024,4096]{1,0:T(8,128)(2,1)} %get-tuple-element.113.b_ref.du_ref, bf16[1024,4096]{1,0:T(8,128)(2,1)} %get-tuple-element.94.w_ref, f32[1024,1024]{1,0:T(8,128)} %get-tuple-element.114.dr_ref, f32[1024,1024]{1,0:T(8,128)} %get-tuple-element.97.n_ref, ...), custom_call_target="tpu_custom_call" | custom-call | flops 8589934592 | bytes 16777216 | tf_op jit(solution)/shard_map/pallas_call | solution.py:307
  358.7 4.6 convolution_convert_fusion
  363.3 1.2 constant_dynamic-slice_fusion.4
  364.5 6.4 shard_map.205
  371.4 1.8 collective-permute-start.5
  373.3 2.9 constant_dynamic-slice_fusion.5
  376.2 2.2 fusion.3
  378.3 2.1 fusion.2
  380.4 3.6 maximum_select_fusion.2.dc_ref
  384.0 9.5 %collective-permute-start.10 = (bf16[512,1024]{1,0:T(8,128)(2,1)}, bf16[512,1024]{1,0:T(8,128)(2,1)}, u32[]{:S(2)}, u32[]{:S(2)}) collective-permute-start(bf16[512,1024]{1,0:T(8,128)(2,1)} %get-tuple-element.123), channel_id=1, source_target_pairs={{0,0},{1,1},{4,2},{5,3},{2,4},{3,5},{6,6},{7,7},{8,8},{9,9},{12,10... | collective-permute-start | bytes 3145736 | tf_op jit(solution)/shard_map/ppermute | solution.py:1022
  393.5 0.9 collective-permute-start.8
  394.4 48.4 %shard_map.207 = (bf16[2048,256]{1,0:T(8,128)(2,1)}, bf16[2048,256]{1,0:T(8,128)(2,1)}, bf16[2048,256]{1,0:T(8,128)(2,1)}) custom-call(s32[8]{0:T(128)} %get-tuple-element.212.lo_ref, s32[8]{0:T(128)} %get-tuple-element.211.hi_ref, s32[8]{0:T(128)} %reduce_sum.62.pad_ref, bf16[2048,1536]{1,0:T(8,128)(2,1)} %get-tuple-element.90.q_ref.k_ref.v_ref, ...), custom_call_target="tpu_custom_call" | custom-call | flops 21474836480 | bytes 50331648 | tf_op jit(solution)/shard_map/pallas_call | solution.py:198
  442.7 1.6 fusion.9
  444.6 3.1 fusion.5
  447.7 4.0 maximum_select_fusion.3
  451.7 3.3 fusion.7
  455.0 2.0 collective-permute-start.13
  457.1 48.1 %shard_map.206 = (bf16[2048,256]{1,0:T(8,128)(2,1)}, bf16[2048,256]{1,0:T(8,128)(2,1)}, bf16[2048,256]{1,0:T(8,128)(2,1)}) custom-call(s32[8]{0:T(128)} %get-tuple-element.212.lo_ref, s32[8]{0:T(128)} %get-tuple-element.211.hi_ref, s32[8]{0:T(128)} %reduce_sum.62.pad_ref, bf16[2048,1536]{1,0:T(8,128)(2,1)} %get-tuple-element.90.q_ref.k_ref.v_ref, ...), custom_call_target="tpu_custom_call" | custom-call | flops 21474836480 | bytes 50331648 | tf_op jit(solution)/shard_map/pallas_call | solution.py:198
  505.2 2.0 fusion.15
  507.2 2.4 fusion.13
  509.6 2.3 fusion.11
  511.8 8.4 %shard_map.209 = bf16[1024,1024]{1,0:T(8,128)(2,1)} custom-call(s32[2]{0:T(128)} %pad_add_fusion.1.at_ref, bf16[2048,256]{1,0:T(8,128)(2,1)} %get-tuple-element.139.refs_0_.refs_2_, bf16[2048,256]{1,0:T(8,128)(2,1)} %get-tuple-element.140.refs_1_.refs_3_, bf16[2048,256]{1,0:T(8,128)(2,1)} %get-tuple-element.141.refs_2_.refs_4_, ...), custom_call_target="tpu_custom_call" | custom-call | flops 3221225472 | bytes 16777216 | tf_op jit(solution)/shard_map/pallas_call | solution.py:506
  520.8 0.8 slice.82
  521.6 0.8 slice.80
  522.3 0.9 slice.83
  523.3 0.8 slice.81
  524.0 0.8 slice.79
  524.8 2.2 collective-permute-start.15
  528.3 9.7 %shard_map.208 = f32[1024,1024]{1,0:T(8,128)} custom-call(s32[2]{0:T(128)} %pad_add_fusion.at_ref, bf16[2048,256]{1,0:T(8,128)(2,1)} %get-tuple-element.139.refs_0_.refs_2_, bf16[2048,256]{1,0:T(8,128)(2,1)} %get-tuple-element.140.refs_1_.refs_3_, bf16[2048,256]{1,0:T(8,128)(2,1)} %get-tuple-element.141.refs_2_.refs_4_, ...), custom_call_target="tpu_custom_call" | custom-call | flops 3221225472 | bytes 16777216 | tf_op jit(solution)/shard_map/pallas_call | solution.py:506
  538.0 2.1 collective-permute-done.15
  540.1 1.9 fusion.17
  542.0 4.3 add_convert_fusion.refs_0_
  546.6 5.5 collective-permute-done.17
  552.1 82.3 %shard_map.210 = (bf16[2,512,1024]{2,1,0:T(8,128)(2,1)}, f32[768,128]{1,0:T(8,128)}, f32[1024,128]{1,0:T(8,128)}, f32[256,128]{1,0:T(8,128)}, f32[96,128]{1,0:T(8,128)}) custom-call(bf16[1024,1024]{1,0:T(8,128)(2,1)} %add_convert_fusion.refs_0_, bf16[1024,2048]{1,0:T(8,128)(2,1)} %get-tuple-element.147.refs_1_, ...), custom_call_target="tpu_custom_call" | custom-call | flops 34359738368 | bytes 67108864 | tf_op jit(solution)/shard_map/pallas_call | solution.py:955
  634.4 4.1 convert_element_type.388
  638.5 0.8 copy.108
  639.4 0.8 copy.109
  642.6 0.8 convert_add_fusion
  643.4 0.7 copy.112
  (113 shorter events, 12.4 us)
Async XLA Ops:
  7.2 110.1 %copy-start.5 = (bf16[2,512,1024]{2,1,0:T(8,128)(2,1)S(1)}, bf16[2,512,1024]{2,1,0:T(8,128)(2,1)}, u32[]{:S(2)}) copy-start(bf16[2,512,1024]{2,1,0:T(8,128)(2,1)} %param.23) | copy-start | bytes 6291460
  7.2 109.6 %copy-start.16 = (s32[2,1,2048]{2,1,0:T(1,128)S(1)}, s32[2,1,2048]{2,1,0:T(1,128)}, u32[]{:S(2)}) copy-start(s32[2,1,2048]{2,1,0:T(1,128)} %param.13) | copy-start | bytes 49156
  7.2 109.6 %copy-start.17 = (s32[2,1,2048]{2,1,0:T(1,128)S(1)}, s32[2,1,2048]{2,1,0:T(1,128)}, u32[]{:S(2)}) copy-start(s32[2,1,2048]{2,1,0:T(1,128)} %param.14) | copy-start | bytes 49156
  7.2 244.4 %all-gather.3.cloned.1.call-start = ((), (), s32[]{:S(2)}) async-start(), calls=%async_computation | async-start | bytes 8650752 | tf_op jit(solution)/shard_map/all_gather | solution.py:1026
  116.9 16.7 %collective-permute-start = (s32[2,2048]{1,0:T(2,128)S(1)}, s32[2,2048]{1,0:T(2,128)S(1)}, u32[]{:S(2)}, u32[]{:S(2)}) collective-permute-start(s32[2,2048]{1,0:T(2,128)S(1)} %fusion.19), channel_id=1, source_target_pairs={{0,4},{4,0},{1,5},{5,1},{2,6},{6,2},{3,7},{7,3},{8,12},{12,8},{9,1... | collective-permute-start | bytes 49160 | tf_op jit(solution)/shard_map/ppermute | solution.py:976
  117.3 3.0 copy-start.15
  118.5 92.4 %collective-permute-start.2 = (bf16[512,1024]{1,0:T(8,128)(2,1)}, bf16[512,1024]{1,0:T(8,128)(2,1)S(1)}, u32[]{:S(2)}, u32[]{:S(2)}) collective-permute-start(bf16[512,1024]{1,0:T(8,128)(2,1)} %get-tuple-element.190), channel_id=1, source_target_pairs={{0,0},{1,1},{2,4},{3,5},{4,2},{5,3},{6,6},{7,7},{8,8},{9,9},{10,12... | collective-permute-start | bytes 3145736 | tf_op jit(solution)/shard_map/ppermute | solution.py:1014
  120.3 90.5 %collective-permute-start.3 = (bf16[512,1024]{1,0:T(8,128)(2,1)S(1)}, bf16[512,1024]{1,0:T(8,128)(2,1)}, u32[]{:S(2)}, u32[]{:S(2)}) collective-permute-start(bf16[512,1024]{1,0:T(8,128)(2,1)S(1)} %get-tuple-element.191), channel_id=1, source_target_pairs={{0,1},{1,0},{2,5},{3,4},{4,3},{5,2},{6,7},{7,6},{8,9},{9,8},{10,13... | collective-permute-start | bytes 3145736 | tf_op jit(solution)/shard_map/ppermute | solution.py:1015
  133.6 3.0 copy-start.11
  207.4 7.3 %collective-permute-start.1 = (bf16[1024,512]{1,0:T(8,128)(2,1)}, bf16[1024,512]{1,0:T(8,128)(2,1)}, u32[]{:S(2)}, u32[]{:S(2)}) collective-permute-start(bf16[1024,512]{1,0:T(8,128)(2,1)} %get-tuple-element.193), channel_id=1, source_target_pairs={{0,4},{4,0},{1,5},{5,1},{2,6},{6,2},{3,7},{7,3},{8,12},{12,8},{9,1... | collective-permute-start | bytes 3145736 | tf_op jit(solution)/shard_map/ppermute | solution.py:976
  309.9 24.9 %collective-permute-start.4 = (bf16[4,4,1024,128]{3,2,1,0:T(8,128)(2,1)}, bf16[4,4,1024,128]{3,2,1,0:T(8,128)(2,1)}, u32[]{:S(2)}, u32[]{:S(2)}) collective-permute-start(bf16[4,4,1024,128]{3,2,1,0:T(8,128)(2,1)} %get-tuple-element.106), channel_id=1, source_target_pairs={{0,4},{4,0},{1,5},{5,1},{2,6},{6,2},{3,7},{7,3},{8,12},{12,8},{9,1... | collective-permute-start | bytes 12582920 | tf_op jit(solution)/shard_map/ppermute | solution.py:976
  310.0 16.3 %copy-start.12 = (s32[1,2048]{1,0:T(1,128)S(1)}, s32[1,2048]{1,0:T(1,128)}, u32[]{:S(2)}) copy-start(s32[1,2048]{1,0:T(1,128)} %copy-done.11) | copy-start | bytes 24580
  310.0 18.0 %copy-start.6 = (bf16[1024,1024]{1,0:T(8,128)(2,1)S(1)}, bf16[1024,1024]{1,0:T(8,128)(2,1)}, u32[]{:S(2)}) copy-start(bf16[1024,1024]{1,0:T(8,128)(2,1)} %get-tuple-element.117) | copy-start | bytes 6291460
  325.1 48.1 %collective-permute-start.6 = (bf16[4,4,8,128,128]{4,3,2,1,0:T(8,128)(2,1)}, bf16[4,4,8,128,128]{4,3,2,1,0:T(8,128)(2,1)}, u32[]{:S(2)}, u32[]{:S(2)}) collective-permute-start(bf16[4,4,8,128,128]{4,3,2,1,0:T(8,128)(2,1)} %get-tuple-element.112), channel_id=1, source_target_pairs={{0,4},{4,0},{1,5},{5,1},{2,6},{6,2},{3,7},{7,3},{8,12},{12,8},{9,1... | collective-permute-start | bytes 12582920 | tf_op jit(solution)/shard_map/ppermute | solution.py:976
  327.9 2.9 copy-start.3
  330.9 2.2 copy-start.4
  364.5 15.9 %collective-permute-start.7 = (bf16[1024,512]{1,0:T(8,128)(2,1)}, bf16[1024,512]{1,0:T(8,128)(2,1)}, u32[]{:S(2)}, u32[]{:S(2)}) collective-permute-start(bf16[1024,512]{1,0:T(8,128)(2,1)} %get-tuple-element.189), channel_id=1, source_target_pairs={{0,4},{4,0},{1,5},{5,1},{2,6},{6,2},{3,7},{7,3},{8,12},{12,8},{9,1... | collective-permute-start | bytes 3145736 | tf_op jit(solution)/shard_map/ppermute | solution.py:976
  370.9 71.8 %collective-permute-start.9 = (bf16[4,4,256,128]{3,2,1,0:T(8,128)(2,1)}, bf16[4,4,256,128]{3,2,1,0:T(8,128)(2,1)}, u32[]{:S(2)}, u32[]{:S(2)}) collective-permute-start(bf16[4,4,256,128]{3,2,1,0:T(8,128)(2,1)} %get-tuple-element.121), channel_id=1, source_target_pairs={{0,4},{4,0},{1,5},{5,1},{2,6},{6,2},{3,7},{7,3},{8,12},{12,8},{9,1... | collective-permute-start | bytes 3145736 | tf_op jit(solution)/shard_map/ppermute | solution.py:976
  371.4 72.9 %collective-permute-start.5 = (bf16[2,2,2,1024,128]{4,3,1,2,0:T(8,128)(2,1)}, bf16[2,2,2,1024,128]{4,3,1,2,0:T(8,128)(2,1)}, u32[]{:S(2)}, u32[]{:S(2)}) collective-permute-start(bf16[2,2,2,1024,128]{4,3,1,2,0:T(8,128)(2,1)} %fusion.1), channel_id=1, source_target_pairs={{0,8},{8,0},{16,24},{24,16},{1,9},{9,1},{17,25},{25,17},{2,10},{10... | collective-permute-start | bytes 6291464 | tf_op jit(solution)/shard_map/ppermute | solution.py:1093
  373.3 2.9 copy-start
  380.4 13.1 %copy-start.7 = (bf16[512,1024]{1,0:T(8,128)(2,1)S(1)}, bf16[512,1024]{1,0:T(8,128)(2,1)}, u32[]{:S(2)}) copy-start(bf16[512,1024]{1,0:T(8,128)(2,1)} %get-tuple-element.124) | copy-start | bytes 3145732
  384.0 63.7 %collective-permute-start.10 = (bf16[512,1024]{1,0:T(8,128)(2,1)}, bf16[512,1024]{1,0:T(8,128)(2,1)}, u32[]{:S(2)}, u32[]{:S(2)}) collective-permute-start(bf16[512,1024]{1,0:T(8,128)(2,1)} %get-tuple-element.123), channel_id=1, source_target_pairs={{0,0},{1,1},{4,2},{5,3},{2,4},{3,5},{6,6},{7,7},{8,8},{9,9},{12,10... | collective-permute-start | bytes 3145736 | tf_op jit(solution)/shard_map/ppermute | solution.py:1022
  393.5 54.2 %collective-permute-start.11 = (bf16[512,1024]{1,0:T(8,128)(2,1)S(1)}, bf16[512,1024]{1,0:T(8,128)(2,1)}, u32[]{:S(2)}, u32[]{:S(2)}) collective-permute-start(bf16[512,1024]{1,0:T(8,128)(2,1)S(1)} %copy-done.7), channel_id=1, source_target_pairs={{1,0},{0,1},{5,2},{4,3},{3,4},{2,5},{7,6},{6,7},{9,8},{8,9},{13,10... | collective-permute-start | bytes 3145736 | tf_op jit(solution)/shard_map/ppermute | solution.py:1022
  393.5 58.2 %collective-permute-start.8 = (bf16[2,2,2,8,128,128]{5,4,3,1,2,0:T(8,128)(2,1)}, bf16[2,2,2,8,128,128]{5,4,3,1,2,0:T(8,128)(2,1)}, u32[]{:S(2)}, u32[]{:S(2)}) collective-permute-start(bf16[2,2,2,8,128,128]{5,4,3,1,2,0:T(8,128)(2,1)} %fusion.3), channel_id=1, source_target_pairs={{0,16},{8,24},{16,0},{24,8},{1,17},{9,25},{17,1},{25,9},{2,18},{10... | collective-permute-start | bytes 6291464 | tf_op jit(solution)/shard_map/ppermute | solution.py:1093
  394.4 48.4 %copy-start.8 = (bf16[4,4,256,128]{3,2,1,0:T(8,128)(2,1)S(1)}, bf16[4,4,256,128]{3,2,1,0:T(8,128)(2,1)}, u32[]{:S(2)}) copy-start(bf16[4,4,256,128]{3,2,1,0:T(8,128)(2,1)} %get-tuple-element.120) | copy-start | bytes 3145732
  442.7 1.9 copy-start.1
  447.7 4.0 copy-start.2
  455.0 50.2 %collective-permute-start.14 = (bf16[2,2,2,256,128]{4,3,2,1,0:T(8,128)(2,1)S(1)}, bf16[2,2,2,256,128]{4,3,2,1,0:T(8,128)(2,1)}, u32[]{:S(2)}, u32[]{:S(2)}) collective-permute-start(bf16[2,2,2,256,128]{4,3,2,1,0:T(8,128)(2,1)S(1)} %get-tuple-element.131), channel_id=1, source_target_pairs={{0,8},{8,0},{16,24},{24,16},{1,9},{9,1},{17,25},{25,17},{2,10},{10... | collective-permute-start | bytes 1572872 | tf_op jit(solution)/shard_map/ppermute | solution.py:1093
  455.0 52.2 %collective-permute-start.13 = (bf16[2,2,8,128,128]{4,3,2,0,1:T(8,128)(2,1)}, bf16[2,2,8,128,128]{4,3,2,0,1:T(8,128)(2,1)}, u32[]{:S(2)}, u32[]{:S(2)}) collective-permute-start(bf16[2,2,8,128,128]{4,3,2,0,1:T(8,128)(2,1)} %get-tuple-element.129), channel_id=1, source_target_pairs={{0,8},{8,0},{16,24},{24,16},{1,9},{9,1},{17,25},{25,17},{2,10},{10... | collective-permute-start | bytes 3145736 | tf_op jit(solution)/shard_map/ppermute | solution.py:1093
  457.1 52.5 %collective-permute-start.12 = (bf16[2,2,1024,128]{3,2,0,1:T(8,128)(2,1)}, bf16[2,2,1024,128]{3,2,0,1:T(8,128)(2,1)}, u32[]{:S(2)}, u32[]{:S(2)}) collective-permute-start(bf16[2,2,1024,128]{3,2,0,1:T(8,128)(2,1)} %get-tuple-element.127), channel_id=1, source_target_pairs={{0,16},{8,24},{16,0},{24,8},{1,17},{9,25},{17,1},{25,9},{2,18},{10... | collective-permute-start | bytes 3145736 | tf_op jit(solution)/shard_map/ppermute | solution.py:1093
  520.2 21.8 %collective-permute-start.16 = (bf16[1024,1024]{1,0:T(8,128)(2,1)}, bf16[1024,1024]{1,0:T(8,128)(2,1)S(1)}, u32[]{:S(2)}, u32[]{:S(2)}) collective-permute-start(bf16[1024,1024]{1,0:T(8,128)(2,1)} %shard_map.209), channel_id=1, source_target_pairs={{0,4},{4,0},{1,5},{5,1},{2,6},{6,2},{3,7},{7,3},{8,12},{12,8},{9,1... | collective-permute-start | bytes 6291464 | tf_op jit(solution)/shard_map/ppermute | solution.py:976
  524.8 15.3 %collective-permute-start.15 = (bf16[2,1024,128]{2,1,0:T(8,128)(2,1)}, bf16[2,1024,128]{2,1,0:T(8,128)(2,1)}, u32[]{:S(2)}, u32[]{:S(2)}) collective-permute-start(bf16[2,1024,128]{2,1,0:T(8,128)(2,1)} %get-tuple-element.138), channel_id=1, source_target_pairs={{0,1},{1,0},{2,3},{3,2},{4,5},{5,4},{6,7},{7,6},{8,9},{9,8},{10,11... | collective-permute-start | bytes 1572872 | tf_op jit(solution)/shard_map/ppermute | solution.py:1093
  527.7 24.4 %collective-permute-start.17 = (bf16[2,8,128,128]{3,2,1,0:T(8,128)(2,1)S(1)}, bf16[2,8,128,128]{3,2,1,0:T(8,128)(2,1)}, u32[]{:S(2)}, u32[]{:S(2)}) collective-permute-start(bf16[2,8,128,128]{3,2,1,0:T(8,128)(2,1)S(1)} %get-tuple-element.149), channel_id=1, source_target_pairs={{0,1},{1,0},{2,3},{3,2},{4,5},{5,4},{6,7},{7,6},{8,9},{9,8},{10,11... | collective-permute-start | bytes 1572872 | tf_op jit(solution)/shard_map/ppermute | solution.py:1093
  527.7 18.9 %collective-permute-start.18 = (bf16[2,2,256,128]{3,2,1,0:T(8,128)(2,1)}, bf16[2,2,256,128]{3,2,1,0:T(8,128)(2,1)}, u32[]{:S(2)}, u32[]{:S(2)}) collective-permute-start(bf16[2,2,256,128]{3,2,1,0:T(8,128)(2,1)} %get-tuple-element.151), channel_id=1, source_target_pairs={{0,16},{8,24},{16,0},{24,8},{1,17},{9,25},{17,1},{25,9},{2,18},{10... | collective-permute-start | bytes 786440 | tf_op jit(solution)/shard_map/ppermute | solution.py:1093
  546.3 96.3 %collective-permute-start.19 = (bf16[1024,128]{1,0:T(8,128)(2,1)}, bf16[1024,128]{1,0:T(8,128)(2,1)S(1)}, u32[]{:S(2)}, u32[]{:S(2)}) collective-permute-start(bf16[1024,128]{1,0:T(8,128)(2,1)} %get-tuple-element.161), channel_id=1, source_target_pairs={{0,2},{1,3},{2,0},{3,1},{4,6},{5,7},{6,4},{7,5},{8,10},{9,11},{10,... | collective-permute-start | bytes 786440 | tf_op jit(solution)/shard_map/ppermute | solution.py:1093
  634.4 4.2 copy-start.9
  634.4 5.0 copy-start.10
  634.4 5.8 copy-start.14
  638.5 4.9 copy-start.13
Sparse Core Ops, SparseCore 0:
  116.9 94.0 all-gather.2
